TPU v7x, 32 devices: a whole 2x2x4 slice. The times are simulated.
32 devices in a mesh: dp: 8 (over z, core), tensor: 4 (over y, x).
Axes of the slice: x: 2, y: 2, z: 4, core: 2. Of those that a mesh axis runs over, the one named last changes fastest.
Arguments:
- layer_input: bfloat16 [8192, 2048], P(('dp', 'tensor')), may hold values from -6 to 6
- lengths: int32 [8], P('dp'), may hold values from 256 to 1024, as said below
- w_query: bfloat16 [2048, 2048], P('dp', 'tensor'), may hold values from -0.125 to 0.125
- w_keyvalue: bfloat16 [2048, 256], P('dp'), may hold values from -0.125 to 0.125
- w_project: bfloat16 [2048, 2048], P('tensor', 'dp'), may hold values from -1 to 1
- w_gate: bfloat16 [2048, 5632], P('dp', 'tensor'), may hold values from -0.125 to 0.125
- w_up: bfloat16 [2048, 5632], P('dp', 'tensor'), may hold values from -0.125 to 0.125
- w_down: bfloat16 [5632, 2048], P('tensor', 'dp'), may hold values from -0.078125 to 0.078125
- gain_attn: bfloat16 [2048], P('dp'), may hold values from 0.099609375 to 1.8984375
- gain_mlp: bfloat16 [2048], P('dp'), may hold values from 0.099609375 to 1.8984375
- out_grad: bfloat16 [8192, 2048], P(('dp', 'tensor')), may hold values from -6 to 6
- kv_grad: bfloat16 [8192, 256], P(('dp', 'tensor')), may hold values from -6 to 6
Outputs:
- output: bfloat16 [8192, 2048], P(('dp', 'tensor'))
- input_grad: float32 [8192, 2048], P(('dp', 'tensor'))
- grad_query: float32 [2048, 2048], P('dp', 'tensor')
- grad_keyvalue: float32 [2048, 256], P('dp')
- grad_project: float32 [2048, 2048], P('tensor', 'dp')
- grad_gate: float32 [2048, 5632], P('dp', 'tensor')
- grad_up: float32 [2048, 5632], P('dp', 'tensor')
- grad_down: float32 [5632, 2048], P('tensor', 'dp')
- grad_gain_attn: float32 [2048], P('dp')
- grad_gain_mlp: float32 [2048], P('dp')
Inputs may be any that keep to these rules, and one draw needn't show every extreme that they name: Each slot's sequence fills its first lengths[s] positions; one slot holds 1024 and another 256.
All inputs are finite; a program needn't handle non-finite values.
Results may differ from a plain program's by a relative error of at most 0.015.
Values may be sent and summed in bfloat16 or wider, within the bound.
No kernel may reach another device: no remote copies, remote signals or barrier semaphores. Data moves between devices by JAX's collectives and lax.ppermute only.
A program may use at most 192 MiB of HBM per device.

v0:
```python
import math

import jax
import jax.numpy as jnp
from jax import lax
from jax.sharding import PartitionSpec as P

HD = 128
QBLOCK = 512


eps = 1e-05
rope_base = 10000.0
neg_big = -1e30


def rope_tables(positions, head_size):
    half_size = head_size // 2
    frequency = rope_base ** (-(jnp.arange(half_size, dtype=jnp.float32) * 2.0 / head_size))
    angles = positions.astype(jnp.float32)[:, None] * frequency[None, :]
    return (jnp.cos(angles), jnp.sin(angles))


def rotate(values, cosine, sine_vals):
    half_size = values.shape[-1] // 2
    first_half = values[..., :half_size]
    second_half = values[..., half_size:]
    cosine = cosine[:, None, :]
    sine_vals = sine_vals[:, None, :]
    return jnp.concatenate(
        [
            first_half * cosine - second_half * sine_vals,
            second_half * cosine + first_half * sine_vals,
        ],
        axis=-1,
    )


def unrotate(values, cosine, sine_vals):
    half_size = values.shape[-1] // 2
    first_half = values[..., :half_size]
    second_half = values[..., half_size:]
    cosine = cosine[:, None, :]
    sine_vals = sine_vals[:, None, :]
    return jnp.concatenate(
        [
            first_half * cosine + second_half * sine_vals,
            second_half * cosine - first_half * sine_vals,
        ],
        axis=-1,
    )


def norm_rows(values, gain_vec):
    inv_norm = lax.rsqrt(jnp.mean(values * values, axis=-1, keepdims=True) + eps)
    return values * inv_norm * gain_vec


def swiglu(gate_act, up_act):
    return jax.nn.silu(gate_act) * up_act


def on_device(
    layer_input,
    lengths,
    w_query,
    w_keyvalue,
    w_project,
    w_gate,
    w_up,
    w_down,
    gain_attn,
    gain_mlp,
    out_grad,
    kv_grad,
):
    own_rows = layer_input.shape[0]
    model_width = layer_input.shape[1]
    slot_len = own_rows * lax.axis_size("tensor")
    local_heads = w_project.shape[0] // HD
    tensor_rank = lax.axis_index("tensor")
    length = lengths[0]
    position = jnp.arange(slot_len, dtype=jnp.int32)
    own_pos = tensor_rank * own_rows + jnp.arange(own_rows, dtype=jnp.int32)
    own_mask = (own_pos < length).astype(jnp.float32)[:, None]
    cos_table, sin_table = rope_tables(position, HD)
    cos_own, sin_own = rope_tables(own_pos, HD)
    inv_root = 1.0 / math.sqrt(HD)
    block_starts = jnp.arange(slot_len // QBLOCK, dtype=jnp.int32) * QBLOCK
    weights_fwd = (
        lax.all_gather(w_query, "dp", axis=0, tiled=True),
        lax.all_gather(w_keyvalue, "dp", axis=0, tiled=True),
        lax.all_gather(w_project, "dp", axis=1, tiled=True),
        lax.all_gather(w_gate, "dp", axis=0, tiled=True),
        lax.all_gather(w_up, "dp", axis=0, tiled=True),
        lax.all_gather(w_down, "dp", axis=1, tiled=True),
        lax.all_gather(gain_attn, "dp", axis=0, tiled=True),
        lax.all_gather(gain_mlp, "dp", axis=0, tiled=True),
    )
    query_full, keyvalue_full, project_full, gate_full, up_full, down_full, gain_one, gain_two = (
        weights_fwd
    )
    residual = layer_input.astype(jnp.float32)
    normed_one = norm_rows(residual, gain_one.astype(jnp.float32)).astype(jnp.bfloat16)
    normed_all = lax.all_gather(normed_one, "tensor", axis=0, tiled=True)
    query_raw = jnp.dot(normed_all, query_full, preferred_element_type=jnp.float32)
    keyvalue_raw = jnp.dot(normed_all, keyvalue_full, preferred_element_type=jnp.float32)
    query_rot = rotate(query_raw.reshape(slot_len, local_heads, HD), cos_table, sin_table).astype(
        jnp.bfloat16
    )
    key_rot = rotate(keyvalue_raw[:, None, :HD], cos_table, sin_table)[:, 0].astype(jnp.bfloat16)
    value_all = keyvalue_raw[:, HD:].astype(jnp.bfloat16)

    def scores_at(block_start):
        query_block = lax.dynamic_slice_in_dim(query_rot, block_start, QBLOCK, 0)
        scores = (
            jnp.einsum("qhd,kd->hqk", query_block, key_rot, preferred_element_type=jnp.float32)
            * inv_root
        )
        query_pos = block_start + jnp.arange(QBLOCK, dtype=jnp.int32)
        allowed = (position[None, :] <= query_pos[:, None]) & (position[None, :] < length)
        return (jnp.where(allowed[None], scores, neg_big), query_block)

    def attend(block_start):
        scores, query_block = scores_at(block_start)
        row_max = jnp.max(scores, axis=-1, keepdims=True)
        exp_scores = jnp.exp(scores - row_max)
        row_sum = jnp.sum(exp_scores, axis=-1, keepdims=True)
        attn_weights = (exp_scores / row_sum).astype(jnp.bfloat16)
        block_mixed = jnp.einsum(
            "hqk,kd->qhd", attn_weights, value_all, preferred_element_type=jnp.float32
        )
        return (block_mixed.astype(jnp.bfloat16), (row_max + jnp.log(row_sum))[..., 0])

    mixed_blocks, log_norms = lax.map(attend, block_starts)
    mixed_heads = mixed_blocks.reshape(slot_len, local_heads * HD)
    after_attn = residual + lax.psum_scatter(
        jnp.dot(mixed_heads, project_full, preferred_element_type=jnp.float32),
        "tensor",
        scatter_dimension=0,
        tiled=True,
    )
    normed_two = norm_rows(after_attn, gain_two.astype(jnp.float32)).astype(jnp.bfloat16)
    normed_mlp = lax.all_gather(normed_two, "tensor", axis=0, tiled=True)
    gate_act = jnp.dot(normed_mlp, gate_full, preferred_element_type=jnp.float32)
    up_act = jnp.dot(normed_mlp, up_full, preferred_element_type=jnp.float32)
    hidden = swiglu(gate_act, up_act).astype(jnp.bfloat16)
    after_mlp = after_attn + lax.psum_scatter(
        jnp.dot(hidden, down_full, preferred_element_type=jnp.float32).astype(jnp.bfloat16),
        "tensor",
        scatter_dimension=0,
        tiled=True,
    ).astype(jnp.float32)
    output = (after_mlp * own_mask).astype(jnp.bfloat16)
    weights_back = (
        lax.all_gather(w_query, "dp", axis=0, tiled=True),
        lax.all_gather(w_keyvalue, "dp", axis=0, tiled=True),
        lax.all_gather(w_project, "dp", axis=1, tiled=True),
        lax.all_gather(w_gate, "dp", axis=0, tiled=True),
        lax.all_gather(w_up, "dp", axis=0, tiled=True),
        lax.all_gather(w_down, "dp", axis=1, tiled=True),
        lax.all_gather(gain_attn, "dp", axis=0, tiled=True),
        lax.all_gather(gain_mlp, "dp", axis=0, tiled=True),
    )
    (
        query_back,
        keyvalue_back,
        project_back,
        gate_back,
        up_back,
        down_back,
        gain_back_one,
        gain_back_two,
    ) = weights_back
    top_grad = out_grad.astype(jnp.float32) * own_mask
    top_all = lax.all_gather(top_grad.astype(jnp.bfloat16), "tensor", axis=0, tiled=True)
    grad_down_part = jnp.einsum("rf,rd->fd", hidden, top_all, preferred_element_type=jnp.float32)
    hidden_grad = jnp.einsum("rd,fd->rf", top_all, down_back, preferred_element_type=jnp.float32)
    swiglu_value, swiglu_pull = jax.vjp(swiglu, gate_act, up_act)
    gate_grad, up_grad = swiglu_pull(hidden_grad)
    gate_grad = gate_grad.astype(jnp.bfloat16)
    up_grad = up_grad.astype(jnp.bfloat16)
    grad_gate_part = jnp.einsum(
        "rd,rf->df", normed_mlp, gate_grad, preferred_element_type=jnp.float32
    )
    grad_up_part = jnp.einsum("rd,rf->df", normed_mlp, up_grad, preferred_element_type=jnp.float32)
    into_gate = jnp.einsum("rf,df->rd", gate_grad, gate_back, preferred_element_type=jnp.float32)
    normed_two_grad = lax.psum_scatter(
        into_gate + jnp.einsum("rf,df->rd", up_grad, up_back, preferred_element_type=jnp.float32),
        "tensor",
        scatter_dimension=0,
        tiled=True,
    )
    norm_value, second_pull = jax.vjp(norm_rows, after_attn, gain_back_two.astype(jnp.float32))
    resid_part, gain_two_grad = second_pull(normed_two_grad)
    attn_top = top_grad + resid_part
    mlp_sums = (
        lax.psum_scatter(grad_gate_part, "dp", scatter_dimension=0, tiled=True),
        lax.psum_scatter(grad_up_part, "dp", scatter_dimension=0, tiled=True),
        lax.psum_scatter(grad_down_part, "dp", scatter_dimension=1, tiled=True),
        lax.psum_scatter(gain_two_grad, "dp", scatter_dimension=0, tiled=True),
    )
    attn_top_all = lax.all_gather(attn_top.astype(jnp.bfloat16), "tensor", axis=0, tiled=True)
    grad_project_part = jnp.einsum(
        "rc,rd->cd", mixed_heads, attn_top_all, preferred_element_type=jnp.float32
    )
    mixed_grad = jnp.einsum(
        "rd,cd->rc", attn_top_all, project_back, preferred_element_type=jnp.float32
    )
    mixed_grad = mixed_grad.astype(jnp.bfloat16).reshape(slot_len, local_heads, HD)

    def attend_back(running, block_items):
        key_acc, value_acc = running
        block_start, log_norm = block_items
        scores, query_block = scores_at(block_start)
        attn_probs = jnp.exp(scores - log_norm[..., None])
        grad_block = lax.dynamic_slice_in_dim(mixed_grad, block_start, QBLOCK, 0)
        prob_grad = jnp.einsum(
            "qhd,kd->hqk", grad_block, value_all, preferred_element_type=jnp.float32
        )
        center = jnp.sum(attn_probs * prob_grad, axis=-1, keepdims=True)
        score_grad = (attn_probs * (prob_grad - center)).astype(jnp.bfloat16)
        query_grad = (
            jnp.einsum("hqk,kd->qhd", score_grad, key_rot, preferred_element_type=jnp.float32)
            * inv_root
        )
        key_acc = (
            key_acc
            + jnp.einsum("hqk,qhd->kd", score_grad, query_block, preferred_element_type=jnp.float32)
            * inv_root
        )
        value_acc = value_acc + jnp.einsum(
            "hqk,qhd->kd",
            attn_probs.astype(jnp.bfloat16),
            grad_block,
            preferred_element_type=jnp.float32,
        )
        return ((key_acc, value_acc), query_grad)

    zero_rows = jnp.zeros((slot_len, HD), jnp.float32)
    (key_acc, value_acc), query_grads = lax.scan(
        attend_back, (zero_rows, zero_rows), (block_starts, log_norms)
    )
    query_grad_all = unrotate(query_grads.reshape(slot_len, local_heads, HD), cos_table, sin_table)
    query_grad_all = query_grad_all.astype(jnp.bfloat16).reshape(slot_len, local_heads * HD)
    grad_query_part = jnp.einsum(
        "rd,rc->dc", normed_all, query_grad_all, preferred_element_type=jnp.float32
    )
    keyvalue_part = jnp.concatenate([key_acc, value_acc], axis=1)
    into_norm = jnp.einsum(
        "rc,dc->rd", query_grad_all, query_back, preferred_element_type=jnp.float32
    )
    summed = lax.psum_scatter(
        jnp.concatenate([into_norm, keyvalue_part], axis=1),
        "tensor",
        scatter_dimension=0,
        tiled=True,
    )
    shared_grad = summed[:, model_width:] + kv_grad.astype(jnp.float32) * own_mask
    key_grad = unrotate(shared_grad[:, None, :HD], cos_own, sin_own)[:, 0]
    keyvalue_grad = jnp.concatenate([key_grad, shared_grad[:, HD:]], axis=1).astype(jnp.bfloat16)
    normed_one_grad = summed[:, :model_width] + jnp.einsum(
        "rc,dc->rd", keyvalue_grad, keyvalue_back, preferred_element_type=jnp.float32
    )
    grad_keyvalue_part = jnp.einsum(
        "rd,rc->dc", normed_one, keyvalue_grad, preferred_element_type=jnp.float32
    )
    first_value, first_pull = jax.vjp(norm_rows, residual, gain_back_one.astype(jnp.float32))
    input_part, gain_one_grad = first_pull(normed_one_grad)
    input_grad = attn_top + input_part
    attn_sums = (
        lax.psum_scatter(grad_query_part, "dp", scatter_dimension=0, tiled=True),
        lax.psum_scatter(grad_keyvalue_part, "dp", scatter_dimension=0, tiled=True),
        lax.psum_scatter(grad_project_part, "dp", scatter_dimension=1, tiled=True),
        lax.psum_scatter(gain_one_grad, "dp", scatter_dimension=0, tiled=True),
    )
    keyvalue_total, gain_one_total, gain_two_total = lax.psum(
        (attn_sums[1], attn_sums[3], mlp_sums[3]), "tensor"
    )
    return (
        output,
        input_grad,
        attn_sums[0],
        keyvalue_total,
        attn_sums[2],
        mlp_sums[0],
        mlp_sums[1],
        mlp_sums[2],
        gain_one_total,
        gain_two_total,
    )


def solution(mesh):
    placed = (
        P(("dp", "tensor"), None),
        P("dp"),
        P("dp", "tensor"),
        P("dp", None),
        P("tensor", "dp"),
        P("dp", "tensor"),
        P("dp", "tensor"),
        P("tensor", "dp"),
        P("dp"),
        P("dp"),
        P(("dp", "tensor"), None),
        P(("dp", "tensor"), None),
    )
    return jax.shard_map(
        on_device,
        mesh=mesh,
        in_specs=placed,
        out_specs=(
            P(("dp", "tensor"), None),
            P(("dp", "tensor"), None),
            P("dp", "tensor"),
            P("dp", None),
            P("tensor", "dp"),
            P("dp", "tensor"),
            P("dp", "tensor"),
            P("tensor", "dp"),
            P("dp"),
            P("dp"),
        ),
        check_vma=False,
    )
```

profile of v0, /device:TPU:0, one launch (start us, length us, event | category | flops | bytes accessed | tf_op | source)
XLA Modules:
  0.0 1494.3 jit_solution(15830499421004651365)
XLA Ops:
  8.6 13.5 all-gather
  29.7 4.8 all-gather.17.cloned.1.call-done
  34.6 54.5 %all-gather.13.cloned.1.call-done = bf16[1024,2048]{0,1:T(8,128)(2,1)} async-done(((bf16[256,2048]{0,1:T(8,128)(2,1)}), bf16[1024,2048]{0,1:T(8,128)(2,1)}) %all-gather.13.cloned.1.call-update) | async-done | bytes 4194320 | tf_op jit(solution)/shard_map/all_gather | solution.py:105
  89.1 3.8 fusion.95
  94.7 25.2 %all-gather.15.cloned.1.call-done = bf16[2048,512]{1,0:T(8,128)(2,1)} async-done(((bf16[256,512]{1,0:T(8,128)(2,1)}), bf16[2048,512]{1,0:T(8,128)(2,1)}) %all-gather.15.cloned.1.call-update) | async-done | bytes 2097168 | tf_op jit(solution)/shard_map/all_gather | solution.py:91
  119.8 5.2 fusion.94
  126.2 3.2 copy.94
  129.4 1.9 copy.93
  131.4 2.8 subtract_convert_fusion.1
  134.7 26.6 %while.30 = (s32[]{:T(128)}, bf16[2,512,4,128]{3,2,1,0:T(4,128)(2,1)}, f32[2,4,512]{2,1,0:T(4,128)S(1)}, s32[2]{0:T(128)S(1)}, s32[]{:T(128)}, /*index=5*/bf16[1...) while((s32[]{:T(128)}, ...), condition=%wide.region_4.5_spmd.clone.clone, body=%wide.region_1.4_spmd.clone.clone.sunk | while | flops 1100217856 | bytes 38344944 | solution.py:135
  139.0 1.9 bitcast_reduce_fusion.2
  140.9 2.5 fusion.159
  143.4 3.1 fusion.160
  154.1 2.5 fusion.159
  156.6 3.1 fusion.160
  161.4 7.6 fusion.66
  169.7 10.2 all-gather.1
  179.9 75.0 %reduce-scatter.11.cloned.1.call-done = f32[256,2048]{0,1:T(8,128)} async-done(((f32[1024,2048]{0,1:T(8,128)}), f32[256,2048]{0,1:T(8,128)}) %reduce-scatter.11.cloned.1.call-update) | async-done | bytes 2097168 | tf_op jit(solution)/shard_map/reduce_scatter | solution.py:137
  254.9 2.2 multiply_reduce_fusion.2
  260.1 2.3 copy.65
  262.4 2.5 fusion.63
  265.5 51.2 %all-gather.25.cloned.1.call-done = bf16[2048,1408]{1,0:T(8,128)(2,1)} async-done(((bf16[256,1408]{1,0:T(8,128)(2,1)}), bf16[2048,1408]{1,0:T(8,128)(2,1)}) %all-gather.25.cloned.1.call-update) | async-done | bytes 5767184 | tf_op jit(solution)/shard_map/all_gather | solution.py:95
  316.8 53.6 %all-gather.21.cloned.1.call-done = bf16[1024,2048]{0,1:T(8,128)(2,1)} async-done(((bf16[256,2048]{0,1:T(8,128)(2,1)}), bf16[1024,2048]{0,1:T(8,128)(2,1)}) %all-gather.21.cloned.1.call-update) | async-done | bytes 4194320 | tf_op jit(solution)/shard_map/all_gather | solution.py:144
  370.3 11.8 fusion.97
  382.1 50.3 %all-gather.23.cloned.1.call-done = bf16[2048,1408]{1,0:T(8,128)(2,1)} async-done(((bf16[256,1408]{1,0:T(8,128)(2,1)}), bf16[2048,1408]{1,0:T(8,128)(2,1)}) %all-gather.23.cloned.1.call-update) | async-done | bytes 5767184 | tf_op jit(solution)/shard_map/all_gather | solution.py:94
  432.4 11.8 fusion.96
  444.1 41.8 %all-gather.29.cloned.1.call-done = bf16[1024,2048]{0,1:T(8,128)(2,1)} async-done(((bf16[256,2048]{0,1:T(8,128)(2,1)}), bf16[1024,2048]{0,1:T(8,128)(2,1)}) %all-gather.29.cloned.1.call-update) | async-done | bytes 4194320 | tf_op jit(solution)/shard_map/all_gather | solution.py:176
  485.9 62.3 %all-gather.27.cloned.1.call-done = bf16[1408,2048]{1,0:T(8,128)(2,1)} async-done(((bf16[1408,256]{1,0:T(8,128)(2,1)}), bf16[1408,2048]{1,0:T(8,128)(2,1)}) %all-gather.27.cloned.1.call-update) | async-done | bytes 5767184 | tf_op jit(solution)/shard_map/all_gather | solution.py:96
  548.2 17.1 %multiply_convert_fusion = (bf16[1024,1408]{1,0:T(8,128)(2,1)}, bf16[1024,1408]{1,0:T(8,128)(2,1)}, bf16[1024,1408]{1,0:T(8,128)(2,1)}) fusion(f32[1024,1408]{1,0:T(8,128)} %fusion.96, f32[1024,1408]{1,0:T(8,128)} %fusion.97, bf16[1024,2048]{0,1:T(8,128)(2,1)} %all-gather.29.cloned.1.call-done, bf16[1408,2048]{1,0:T(8,128)(2,1)} %all-gather.27.cloned.1.call-done), kind=kOutput, calls=%fused_computation.67 | convolution fusion | flops 5928648704 | bytes 30146560 | tf_op jit(solution)/shard_map/rd,fd->rf/dot_general | solution.py:178
  565.3 9.1 fusion.98
  574.4 10.8 convolution_add_fusion
  585.2 84.6 %reduce-scatter.15.cloned.1.call-done = f32[256,2048]{0,1:T(8,128)} async-done(((f32[1024,2048]{0,1:T(8,128)}), f32[256,2048]{0,1:T(8,128)}) %reduce-scatter.15.cloned.1.call-update) | async-done | bytes 2097168 | tf_op jit(solution)/shard_map/reduce_scatter | solution.py:188
  669.8 3.0 multiply_reduce_fusion
  675.2 52.5 %all-gather.31.cloned.1.call-done = bf16[1024,2048]{0,1:T(8,128)(2,1)} async-done(((bf16[256,2048]{0,1:T(8,128)(2,1)}), bf16[1024,2048]{0,1:T(8,128)(2,1)}) %all-gather.31.cloned.1.call-update) | async-done | bytes 4194320 | tf_op jit(solution)/shard_map/all_gather | solution.py:203
  727.7 5.1 convolution_convert_fusion.1
  732.9 38.7 %while.31 = (s32[]{:T(128)}, f32[1024,128]{1,0:T(8,128)S(1)}, f32[1024,128]{1,0:T(8,128)}, f32[2,512,4,128]{3,1,0,2:T(8,128)}, s32[2]{0:T(128)S(1)}, /*index=5*/...) while((s32[]{:T(128)}, f32[1024,128]{1,0:T(8,128)S(1)}, ...), condition=%wide.region_12.13_spmd.clone.clone, body=%wide.region_10.12_spmd.clone.clone.sunk | while | flops 2717777408 | bytes 92076384 | solution.py:241
  738.6 3.1 fusion.174
  741.7 4.0 fusion.171
  745.7 2.4 fusion.172
  757.8 3.1 fusion.174
  760.9 4.0 fusion.171
  764.9 2.4 fusion.172
  771.6 3.2 add_convert_fusion
  776.4 3.9 fusion.103
  780.3 6.3 pad_maximum_fusion
  787.7 94.1 %reduce-scatter.17.cloned.1.call-done = f32[256,2304]{0,1:T(8,128)} async-done(((f32[1024,2304]{0,1:T(8,128)}), f32[256,2304]{0,1:T(8,128)}) %reduce-scatter.17.cloned.1.call-update) | async-done | bytes 2359312 | tf_op jit(solution)/shard_map/reduce_scatter | solution.py:253
  884.9 11.1 convolution_convert_fusion
  896.1 12.0 fusion.102
  908.2 11.8 fusion.101
  920.1 11.9 fusion.100
  932.0 6.5 fusion.99
  939.8 6.8 fusion.64
  948.5 4.0 fusion.58
  952.6 22.5 %reduce-scatter.13.cloned.1.call-done = bf16[256,2048]{0,1:T(8,128)(2,1)} async-done(((bf16[1024,2048]{0,1:T(8,128)(2,1)}), bf16[256,2048]{0,1:T(8,128)(2,1)}) %reduce-scatter.13.cloned.1.call-update) | async-done | bytes 1048592 | tf_op jit(solution)/shard_map/reduce_scatter | solution.py:148
  975.2 4.6 fusion.60
  979.8 3.0 copy.79
  982.8 30.1 %all-reduce.2 = (f32[2048]{0:T(1024)S(1)}, f32[2048]{0:T(1024)S(1)}) all-reduce(f32[2048]{0:T(1024)S(1)} %get-tuple-element.327, f32[2048]{0:T(1024)S(1)} %copy-done.22), channel_id=12, replica_groups=mesh['dp'=8,'tensor'=4] {'dp'}, use_global_device_ids=true, to_apply=%region_23.24.clone | all-reduce | flops 4096 | bytes 32768
  1014.4 9.4 all-reduce.3
  1023.9 73.9 %reduce-scatter.29.cloned.1.call-done = f32[1408,256]{1,0:T(8,128)} async-done(((f32[1408,2048]{1,0:T(8,128)}), f32[1408,256]{1,0:T(8,128)}) %reduce-scatter.29.cloned.1.call-update) | async-done | bytes 1441808 | tf_op jit(solution)/shard_map/reduce_scatter | solution.py:200
  1097.8 120.5 %reduce-scatter.27.cloned.1.call-done = f32[256,1408]{1,0:T(8,128)} async-done(((f32[2048,1408]{1,0:T(8,128)}), f32[256,1408]{1,0:T(8,128)}) %reduce-scatter.27.cloned.1.call-update) | async-done | bytes 1441808 | tf_op jit(solution)/shard_map/reduce_scatter | solution.py:199
  1218.2 120.5 %reduce-scatter.25.cloned.1.call-done = f32[256,1408]{1,0:T(8,128)} async-done(((f32[2048,1408]{1,0:T(8,128)}), f32[256,1408]{1,0:T(8,128)}) %reduce-scatter.25.cloned.1.call-update) | async-done | bytes 1441808 | tf_op jit(solution)/shard_map/reduce_scatter | solution.py:198
  1338.7 51.3 %reduce-scatter.19.cloned.1.call-done = f32[256,512]{1,0:T(8,128)} async-done(((f32[2048,512]{1,0:T(8,128)}), f32[256,512]{1,0:T(8,128)}) %reduce-scatter.19.cloned.1.call-update) | async-done | bytes 524304 | tf_op jit(solution)/shard_map/reduce_scatter | solution.py:272
  1390.0 51.1 %reduce-scatter.23.cloned.1.call-done = f32[512,256]{1,0:T(8,128)} async-done(((f32[512,2048]{1,0:T(8,128)}), f32[512,256]{1,0:T(8,128)}) %reduce-scatter.23.cloned.1.call-update) | async-done | bytes 524304 | tf_op jit(solution)/shard_map/reduce_scatter | solution.py:274
  1441.1 44.5 %all-reduce.6.cloned.1.call-done = f32[256,256]{1,0:T(8,128)} async-done(((f32[256,256]{1,0:T(8,128)}), f32[256,256]{1,0:T(8,128)}) %all-reduce.6.cloned.1.call-update) | async-done | bytes 262160 | tf_op jit(solution)/shard_map/psum | solution.py:277
  (213 shorter events, 54.8 us)
Async XLA Ops:
  7.2 27.4 %all-gather.17.cloned.1.call-start = ((), (), s32[]{:S(2)}) async-start(), calls=%async_computation.12 | async-start | bytes 1179648 | tf_op jit(solution)/shard_map/all_gather | solution.py:92
  7.9 81.1 %all-gather.13.cloned.1.call-start = ((), (), s32[]{:S(2)}) async-start(), calls=%async_computation.10 | async-start | bytes 5242880 | tf_op jit(solution)/shard_map/all_gather | solution.py:105
  22.1 67.0 %copy-start.19 = (f32[8,1,256]{2,1,0:T(1,128)}, f32[8,1,256]{2,1,0:T(1,128)S(1)}, u32[]{:S(2)}) copy-start(f32[8,1,256]{2,1,0:T(1,128)S(1)} %convert_element_type.146) | copy-start | bytes 24580
  23.6 69.3 %copy-start.2 = (bf16[256,2048]{0,1:T(8,128)(2,1)}, bf16[256,2048]{0,1:T(8,128)(2,1)S(1)}, u32[]{:S(2)}) copy-start(bf16[256,2048]{0,1:T(8,128)(2,1)S(1)} %copy.57) | copy-start | bytes 3145732
  26.4 93.4 %all-gather.15.cloned.1.call-start = ((), (), s32[]{:S(2)}) async-start(), calls=%async_computation.11 | async-start | bytes 2359296 | tf_op jit(solution)/shard_map/all_gather | solution.py:91
  27.1 134.2 %all-gather.19.cloned.1.call-start = ((), (), s32[]{:S(2)}) async-start(), calls=%async_computation.13 | async-start | bytes 2359296 | tf_op jit(solution)/shard_map/all_gather | solution.py:93
  27.7 227.2 %reduce-scatter.11.cloned.1.call-start = ((), (), s32[]{:S(2)}) async-start(), calls=%async_computation.14 | async-start | bytes 10485760 | tf_op jit(solution)/shard_map/reduce_scatter | solution.py:137
  27.8 65.2 %copy-start.31 = (f32[64]{0:T(128)}, f32[64]{0:T(128)S(1)}, u32[]{:S(2)}) copy-start(f32[64]{0:T(128)S(1)} %negate_power_fusion) | copy-start | bytes 772
  29.7 101.7 %copy-start.11 = (f32[1024,64]{1,0:T(8,128)}, f32[1024,64]{1,0:T(8,128)S(1)}, u32[]{:S(2)}) copy-start(f32[1024,64]{1,0:T(8,128)S(1)} %get-tuple-element.392) | copy-start | bytes 786436
  29.7 101.6 %copy-start.12 = (f32[1024,64]{1,0:T(8,128)}, f32[1024,64]{1,0:T(8,128)S(1)}, u32[]{:S(2)}) copy-start(f32[1024,64]{1,0:T(8,128)S(1)} %get-tuple-element.393) | copy-start | bytes 786436
  143.4 3.1 copy-start.34
  147.0 1.0 copy-start.35
  156.6 3.1 copy-start.34
  160.2 1.0 copy-start.35
  161.3 7.7 copy-start.6
  169.0 0.7 copy-start.37
  169.1 147.7 %all-gather.25.cloned.1.call-start = ((), (), s32[]{:S(2)}) async-start(), calls=%async_computation.17 | async-start | bytes 6488064 | tf_op jit(solution)/shard_map/all_gather | solution.py:95
  169.6 200.7 %all-gather.21.cloned.1.call-start = ((), (), s32[]{:S(2)}) async-start(), calls=%async_computation.15 | async-start | bytes 5242880 | tf_op jit(solution)/shard_map/all_gather | solution.py:144
  179.9 493.0 %copy-start.17 = (f32[8,1,256]{2,1,0:T(1,128)}, f32[8,1,256]{2,1,0:T(1,128)S(1)}, u32[]{:S(2)}) copy-start(f32[8,1,256]{2,1,0:T(1,128)S(1)} %convert_element_type.147) | copy-start | bytes 24580
  257.1 415.8 %copy-start = (f32[256,2048]{0,1:T(8,128)}, f32[256,2048]{0,1:T(8,128)S(1)}, u32[]{:S(2)}) copy-start(f32[256,2048]{0,1:T(8,128)S(1)} %get-tuple-element.372) | copy-start | bytes 6291460
  257.1 415.8 %copy-start.23 = (f32[256]{0:T(256)}, f32[256]{0:T(256)S(1)}, u32[]{:S(2)}) copy-start(f32[256]{0:T(256)S(1)} %fusion.89) | copy-start | bytes 3076
  258.7 173.7 %all-gather.23.cloned.1.call-start = ((), (), s32[]{:S(2)}) async-start(), calls=%async_computation.16 | async-start | bytes 6488064 | tf_op jit(solution)/shard_map/all_gather | solution.py:94
  259.5 226.5 %all-gather.29.cloned.1.call-start = ((), (), s32[]{:S(2)}) async-start(), calls=%async_computation.20 | async-start | bytes 5242880 | tf_op jit(solution)/shard_map/all_gather | solution.py:176
  264.9 283.3 %all-gather.27.cloned.1.call-start = ((), (), s32[]{:S(2)}) async-start(), calls=%async_computation.18 | async-start | bytes 6488064 | tf_op jit(solution)/shard_map/all_gather | solution.py:96
  265.5 404.3 %reduce-scatter.15.cloned.1.call-start = ((), (), s32[]{:S(2)}) async-start(), calls=%async_computation.21 | async-start | bytes 10485760 | tf_op jit(solution)/shard_map/reduce_scatter | solution.py:188
  548.2 17.1 %copy-start.33 = (bf16[2048,1408]{1,0:T(8,128)(2,1)S(1)}, bf16[2048,1408]{1,0:T(8,128)(2,1)}, u32[]{:S(2)}) copy-start(bf16[2048,1408]{1,0:T(8,128)(2,1)} %all-gather.23.cloned.1.call-done) | copy-start | bytes 17301508
  565.3 9.1 copy-start.39
  585.2 142.5 %all-gather.31.cloned.1.call-start = ((), (), s32[]{:S(2)}) async-start(), calls=%async_computation.22 | async-start | bytes 5242880 | tf_op jit(solution)/shard_map/all_gather | solution.py:203
  669.8 3.6 copy-start.4
  669.8 3.6 copy-start.5
  675.1 206.6 %reduce-scatter.17.cloned.1.call-start = ((), (), s32[]{:S(2)}) async-start(), calls=%async_computation.23 | async-start | bytes 11796480 | tf_op jit(solution)/shard_map/reduce_scatter | solution.py:253
  675.2 57.7 %copy-start.7 = (bf16[1024,128]{1,0:T(8,128)(2,1)S(1)}, bf16[1024,128]{1,0:T(8,128)(2,1)}, u32[]{:S(2)}) copy-start(bf16[1024,128]{1,0:T(8,128)(2,1)} %copy-done.6) | copy-start | bytes 786436
  737.3 1.3 copy-start.14
  741.7 4.0 copy-start.15
  748.1 1.6 copy-start.9
  750.9 1.3 copy-start.10
  756.5 1.3 copy-start.14
  760.9 4.0 copy-start.15
  767.3 1.6 copy-start.9
  770.1 1.3 copy-start.10
  774.8 1.3 copy-start.16
  786.6 0.9 copy-start.21
  786.6 96.1 %copy-start.32 = (f32[64]{0:T(128)S(1)}, f32[64]{0:T(128)}, u32[]{:S(2)}) copy-start(f32[64]{0:T(128)} %copy-done.31) | copy-start | bytes 772
  786.6 96.5 %copy-start.8 = (bf16[256,2048]{0,1:T(8,128)(2,1)S(1)}, bf16[256,2048]{0,1:T(8,128)(2,1)}, u32[]{:S(2)}) copy-start(bf16[256,2048]{0,1:T(8,128)(2,1)} %fusion.57) | copy-start | bytes 3145732
  786.7 165.9 %reduce-scatter.21.cloned.1.call-start = ((), (), s32[]{:S(2)}) async-start(), calls=%async_computation.25 | async-start | bytes 2359296 | tf_op jit(solution)/shard_map/reduce_scatter | solution.py:273
  884.9 90.3 %reduce-scatter.13.cloned.1.call-start = ((), (), s32[]{:S(2)}) async-start(), calls=%async_computation.19 | async-start | bytes 5242880 | tf_op jit(solution)/shard_map/reduce_scatter | solution.py:148
  896.0 201.7 %reduce-scatter.29.cloned.1.call-start = ((), (), s32[]{:S(2)}) async-start(), calls=%async_computation.30 | async-start | bytes 12976128 | tf_op jit(solution)/shard_map/reduce_scatter | solution.py:200
  908.1 310.1 %reduce-scatter.27.cloned.1.call-start = ((), (), s32[]{:S(2)}) async-start(), calls=%async_computation.29 | async-start | bytes 12976128 | tf_op jit(solution)/shard_map/reduce_scatter | solution.py:199
  920.0 418.7 %reduce-scatter.25.cloned.1.call-start = ((), (), s32[]{:S(2)}) async-start(), calls=%async_computation.28 | async-start | bytes 12976128 | tf_op jit(solution)/shard_map/reduce_scatter | solution.py:198
  932.0 458.0 %reduce-scatter.19.cloned.1.call-start = ((), (), s32[]{:S(2)}) async-start(), calls=%async_computation.24 | async-start | bytes 4718592 | tf_op jit(solution)/shard_map/reduce_scatter | solution.py:272
  938.5 1.2 copy-start.36
  938.6 502.6 %reduce-scatter.23.cloned.1.call-start = ((), (), s32[]{:S(2)}) async-start(), calls=%async_computation.27 | async-start | bytes 4718592 | tf_op jit(solution)/shard_map/reduce_scatter | solution.py:274
  946.6 0.7 copy-start.38
  946.6 1.9 copy-start.3
  946.6 1.9 copy-start.20
  946.6 1.9 copy-start.26
  946.7 5.9 copy-start.30
  946.7 28.5 %copy-start.1 = (f32[256,2048]{0,1:T(8,128)S(1)}, f32[256,2048]{0,1:T(8,128)}, u32[]{:S(2)}) copy-start(f32[256,2048]{0,1:T(8,128)} %copy-done) | copy-start | bytes 6291460
  946.7 28.5 %copy-start.18 = (f32[8,1,256]{2,1,0:T(1,128)S(1)}, f32[8,1,256]{2,1,0:T(1,128)}, u32[]{:S(2)}) copy-start(f32[8,1,256]{2,1,0:T(1,128)} %copy-done.17) | copy-start | bytes 24580
  946.7 28.5 %copy-start.24 = (f32[256]{0:T(256)S(1)}, f32[256]{0:T(256)}, u32[]{:S(2)}) copy-start(f32[256]{0:T(256)} %copy-done.23) | copy-start | bytes 3076
  946.7 28.5 %copy-start.28 = (f32[256]{0:T(256)S(1)}, f32[256]{0:T(256)}, u32[]{:S(2)}) copy-start(f32[256]{0:T(256)} %copy-done.27) | copy-start | bytes 3076
  946.7 538.9 %all-reduce.6.cloned.1.call-start = ((), (), s32[]{:S(2)}) async-start(), calls=%async_computation.26 | async-start | bytes 524288 | tf_op jit(solution)/shard_map/psum | solution.py:277
  979.8 3.0 copy-start.22
  979.8 33.2 %copy-start.13 = (bf16[256,2048]{0,1:T(8,128)(2,1)S(1)}, bf16[256,2048]{0,1:T(8,128)(2,1)}, u32[]{:S(2)}) copy-start(bf16[256,2048]{0,1:T(8,128)(2,1)} %get-tuple-element.385) | copy-start | bytes 3145732
  (3 other events, 1.7 us)
Sparse Core Ops, SparseCore 0:
  9.6 24.9 all-gather.16
  37.0 52.0 all-gather.12
  90.7 29.1 all-gather.14
  121.3 30.0 all-gather.18
  169.2 85.6 reduce-scatter.10
  256.4 60.3 all-gather.24
  319.2 51.1 all-gather.20
  372.0 60.3 all-gather.22
  434.8 51.1 all-gather.28
  487.4 60.7 all-gather.26
  585.3 84.4 reduce-scatter.14
  675.2 52.4 all-gather.30
  786.8 94.8 reduce-scatter.16
  885.0 36.0 reduce-scatter.20
  923.9 51.1 reduce-scatter.12
  977.9 119.8 reduce-scatter.28
  1100.5 117.6 reduce-scatter.26
  1221.0 117.6 reduce-scatter.24
  1341.6 48.3 reduce-scatter.18
  1392.7 48.3 reduce-scatter.22
  1444.1 41.5 all-reduce.5
where the time goes:
time: 1500 us; the launch traced here: 1490 us
  waiting for transfers between devices  1140 us (76%)
  matrix products  184 us (12%)
  blocking collectives  63.2 us (4%)
  other arithmetic  51.8 us (3%)
  local copies, waits for them, and re-layouts  31.2 us (2%)
  between operations  16.5 us (1%)
    reduce_scatter x1, waiting for transfers between devices, on_device(): lax.psum_scatter(grad_gate_part, 'dp', scatter_dimension=0, tiled=True)  120 us
    reduce_scatter x1, waiting for transfers between devices, on_device(): lax.psum_scatter(grad_up_part, 'dp', scatter_dimension=0, tiled=True)  120 us
    reduce_scatter x1, waiting for transfers between devices, on_device(): lax.psum_scatter(jnp.concatenate([into_norm, keyvalue_part], axis=1), 'te...  94.1 us
    reduce_scatter x1, waiting for transfers between devices, on_device(): lax.psum_scatter(into_gate + jnp.einsum('rf,df->rd', up_grad, up_back, pr...  84.6 us
    reduce_scatter x1, waiting for transfers between devices, on_device(): lax.psum_scatter(jnp.dot(mixed_heads, project_full, preferred_element_typ...  75 us
    reduce_scatter x1, waiting for transfers between devices, on_device(): lax.psum_scatter(grad_down_part, 'dp', scatter_dimension=1, tiled=True)  73.9 us
    all_gather x1, waiting for transfers between devices, on_device(): lax.all_gather(w_down, 'dp', axis=1, tiled=True)  62.3 us
    all_gather x1, waiting for transfers between devices, on_device(): normed_all = lax.all_gather(normed_one, 'tensor', axis=0, tiled=True)  54.5 us
  transfers between devices with their start and end apart: 21, of which 19 were waited for; matrix products, arithmetic and copies ran while one was open for 10% of the time, Pallas kernels for 0%

commit v1 on v0

v1 whole, which is shorter than its diff:
```python
import functools
import math

import jax
import jax.numpy as jnp
from jax import lax
from jax.experimental import pallas as pl
from jax.experimental.pallas import tpu as pltpu
from jax.sharding import PartitionSpec as P

HD = 128
eps = 1e-05
rope_base = 10000.0
neg_big = -1e30
inv_root = 1.0 / math.sqrt(HD)
f32 = jnp.float32
bf16 = jnp.bfloat16


def dot(a, b, ca, cb):
    return lax.dot_general(a, b, (((ca,), (cb,)), ((), ())), preferred_element_type=f32)


def hop(value, step):
    size = lax.axis_size("tensor")
    return lax.ppermute(value, "tensor", [(i, i ^ step) for i in range(size)])


def after(value, *others):
    return lax.optimization_barrier((value, *others))[0]


def gather_blocks(own):
    return [own] + [hop(own, j) for j in range(1, lax.axis_size("tensor"))]


def scatter_sum(blocks):
    total = blocks[0].astype(f32)
    for j in range(1, len(blocks)):
        total = total + hop(blocks[j].astype(bf16), j).astype(f32)
    return total


def gather_dp(shard):
    return lax.all_gather(shard, "dp", axis=0, tiled=True)


def scatter_dp(partial):
    return lax.psum_scatter(partial, "dp", scatter_dimension=0, tiled=True).astype(f32)


def turn(u, cos2, sin2):
    return u * cos2 + pltpu.roll(u, HD // 2, 1) * sin2


def attend_kernel(where_ref, q_ref, kv_ref, cos_ref, sin_ref, qr_ref, kvt_ref, mixed_ref, lse_ref):
    rows, width = q_ref.shape
    heads = width // HD
    ranks = kv_ref.shape[0] // rows
    j = pl.program_id(0)
    rank, length = where_ref[0], where_ref[1]
    block = jnp.bitwise_xor(rank, j)

    @pl.when(j == 0)
    def _():
        for i in range(ranks):
            here = slice(i * rows, (i + 1) * rows)
            there = pl.ds(pl.multiple_of(jnp.bitwise_xor(rank, i) * rows, rows), rows)
            key = turn(kv_ref[here, :HD], cos_ref[here, :], sin_ref[here, :])
            kvt_ref[there, :HD] = key.astype(bf16)
            kvt_ref[there, HD:] = kv_ref[here, HD:].astype(bf16)

    mine = pl.ds(pl.multiple_of(j * rows, rows), rows)
    cos2, sin2 = cos_ref[mine, :], sin_ref[mine, :]
    for h in range(heads):
        head = slice(h * HD, (h + 1) * HD)
        qr_ref[:, head] = turn(q_ref[:, head], cos2, sin2).astype(bf16)
    limit = jnp.minimum(block * rows + lax.broadcasted_iota(jnp.int32, (rows, 1), 0), length - 1)
    for w in range(ranks):

        @pl.when(block == w)
        def _(w=w):
            span = (w + 1) * rows
            allowed = lax.broadcasted_iota(jnp.int32, (rows, span), 1) <= limit
            for h in range(heads):
                head = slice(h * HD, (h + 1) * HD)
                scores = dot(qr_ref[:, head], kvt_ref[:span, :HD], 1, 1) * inv_root
                scores = jnp.where(allowed, scores, neg_big)
                top = jnp.max(scores, axis=1, keepdims=True)
                weights = jnp.exp(scores - top)
                total = jnp.sum(weights, axis=1, keepdims=True)
                probs = (weights * (1.0 / total)).astype(bf16)
                mixed_ref[:, head] = dot(probs, kvt_ref[:span, HD:], 1, 0).astype(bf16)
                lse_ref[:, h : h + 1] = top + jnp.log(total)


def attend_back_kernel(
    where_ref, qr_ref, kvt_ref, dm_ref, lse_ref, cos_ref, sin_ref, dq_ref, dkv_ref, dk_acc, dv_acc
):
    rows, width = qr_ref.shape
    heads = width // HD
    ranks = kvt_ref.shape[0] // rows
    j = pl.program_id(0)
    rank, length = where_ref[0], where_ref[1]
    block = jnp.bitwise_xor(rank, j)

    @pl.when(j == 0)
    def _():
        dk_acc[...] = jnp.zeros_like(dk_acc)
        dv_acc[...] = jnp.zeros_like(dv_acc)

    cos2, sin2 = cos_ref[...], sin_ref[...]
    limit = jnp.minimum(block * rows + lax.broadcasted_iota(jnp.int32, (rows, 1), 0), length - 1)
    for w in range(ranks):

        @pl.when(block == w)
        def _(w=w):
            span = (w + 1) * rows
            allowed = lax.broadcasted_iota(jnp.int32, (rows, span), 1) <= limit
            keys, vals = kvt_ref[:span, :HD], kvt_ref[:span, HD:]
            for h in range(heads):
                head = slice(h * HD, (h + 1) * HD)
                q, dm = qr_ref[:, head], dm_ref[:, head]
                scores = jnp.where(allowed, dot(q, keys, 1, 1) * inv_root, neg_big)
                probs = jnp.exp(scores - lse_ref[:, h : h + 1])
                dp = dot(dm, vals, 1, 1)
                center = jnp.sum(probs * dp, axis=1, keepdims=True)
                ds = (probs * (dp - center)).astype(bf16)
                dq = dot(ds, keys, 1, 0) * inv_root
                dq_ref[:, head] = turn(dq, cos2, -sin2).astype(bf16)
                dk_acc[:span, :] += dot(ds, q, 0, 0)
                dv_acc[:span, :] += dot(probs.astype(bf16), dm, 0, 0)

    @pl.when(j == ranks - 1)
    def _():
        for i in range(ranks):
            here = slice(i * rows, (i + 1) * rows)
            there = pl.ds(pl.multiple_of(jnp.bitwise_xor(rank, i) * rows, rows), rows)
            dkv_ref[here, :HD] = dk_acc[there, :] * inv_root
            dkv_ref[here, HD:] = dv_acc[there, :]


VMEM_LIMIT = 48 * 2**20


def attend(where, qkv, cos2, sin2, rows):
    slot, width = qkv.shape[0], qkv.shape[1] - 2 * HD
    heads = width // HD
    half = slot * slot * heads * HD
    return pl.pallas_call(
        attend_kernel,
        name="attend",
        grid_spec=pltpu.PrefetchScalarGridSpec(
            num_scalar_prefetch=1,
            grid=(slot // rows,),
            in_specs=[
                pl.BlockSpec((rows, width), lambda j, s: (j, 0)),
                pl.BlockSpec((slot, 2 * HD), lambda j, s: (0, width // (2 * HD))),
                pl.BlockSpec((slot, HD), lambda j, s: (0, 0)),
                pl.BlockSpec((slot, HD), lambda j, s: (0, 0)),
            ],
            out_specs=[
                pl.BlockSpec((rows, width), lambda j, s: (j, 0)),
                pl.BlockSpec((slot, 2 * HD), lambda j, s: (0, 0)),
                pl.BlockSpec((rows, width), lambda j, s: (j, 0)),
                pl.BlockSpec((rows, HD), lambda j, s: (j, 0)),
            ],
        ),
        out_shape=(
            jax.ShapeDtypeStruct((slot, width), bf16),
            jax.ShapeDtypeStruct((slot, 2 * HD), bf16),
            jax.ShapeDtypeStruct((slot, width), bf16),
            jax.ShapeDtypeStruct((slot, HD), f32),
        ),
        compiler_params=pltpu.CompilerParams(
            dimension_semantics=("arbitrary",), vmem_limit_bytes=VMEM_LIMIT
        ),
        cost_estimate=pl.CostEstimate(
            flops=4 * half, bytes_accessed=8 * 2**20, transcendentals=slot * slot * heads
        ),
    )(where, qkv, qkv, cos2, sin2)


def attend_back(where, qr, kvt, dmixed, lse, cos2, sin2, rows):
    slot, width = qr.shape
    heads = width // HD
    half = slot * slot * heads * HD
    return pl.pallas_call(
        attend_back_kernel,
        name="attend_back",
        grid_spec=pltpu.PrefetchScalarGridSpec(
            num_scalar_prefetch=1,
            grid=(slot // rows,),
            in_specs=[
                pl.BlockSpec((rows, width), lambda j, s: (j, 0)),
                pl.BlockSpec((slot, 2 * HD), lambda j, s: (0, 0)),
                pl.BlockSpec((rows, width), lambda j, s: (j, 0)),
                pl.BlockSpec((rows, HD), lambda j, s: (j, 0)),
                pl.BlockSpec((rows, HD), lambda j, s: (j, 0)),
                pl.BlockSpec((rows, HD), lambda j, s: (j, 0)),
            ],
            out_specs=[
                pl.BlockSpec((rows, width), lambda j, s: (j, 0)),
                pl.BlockSpec((slot, 2 * HD), lambda j, s: (0, 0)),
            ],
            scratch_shapes=[pltpu.VMEM((slot, HD), f32), pltpu.VMEM((slot, HD), f32)],
        ),
        out_shape=(
            jax.ShapeDtypeStruct((slot, width), bf16),
            jax.ShapeDtypeStruct((slot, 2 * HD), f32),
        ),
        compiler_params=pltpu.CompilerParams(
            dimension_semantics=("arbitrary",), vmem_limit_bytes=VMEM_LIMIT
        ),
        cost_estimate=pl.CostEstimate(
            flops=10 * half, bytes_accessed=8 * 2**20, transcendentals=slot * slot * heads
        ),
    )(where, qr, kvt, dmixed, lse, cos2, sin2)


def unrotate(values, cosine, sine_vals):
    first, second = values[:, : HD // 2], values[:, HD // 2 :]
    return jnp.concatenate(
        [first * cosine + second * sine_vals, second * cosine - first * sine_vals], axis=1
    )


def inverse_norm(values):
    return lax.rsqrt(jnp.mean(values * values, axis=-1, keepdims=True) + eps)


def rows_of(array, j, rows):
    return array[j * rows : (j + 1) * rows]


def on_device(
    layer_input,
    lengths,
    w_query,
    w_keyvalue,
    w_project,
    w_gate,
    w_up,
    w_down,
    gain_attn,
    gain_mlp,
    out_grad,
    kv_grad,
):
    rows, model_width = layer_input.shape
    ranks = lax.axis_size("tensor")
    rank = lax.axis_index("tensor").astype(jnp.int32)
    length = lengths[0]
    heads_width = w_query.shape[1]
    ff = w_gate.shape[1]
    cut = -(-ff // 256) * 128
    parts = ((0, cut), (cut, ff))

    order = jnp.bitwise_xor(rank, jnp.arange(ranks, dtype=jnp.int32))
    position = (order[:, None] * rows + jnp.arange(rows, dtype=jnp.int32)[None, :]).reshape(-1)
    frequency = rope_base ** (-(jnp.arange(HD // 2, dtype=f32) * 2.0 / HD))
    angles = position.astype(f32)[:, None] * frequency[None, :]
    cosine, sine = jnp.cos(angles), jnp.sin(angles)
    cos2 = jnp.concatenate([cosine, cosine], axis=1)
    sin2 = jnp.concatenate([-sine, sine], axis=1)
    cos_own, sin_own = cosine[:rows], sine[:rows]
    own_mask = (position[:rows] < length).astype(f32)[:, None]
    where = jnp.stack([rank, length])

    attn_shard = jnp.concatenate([w_query, w_keyvalue, w_project.T], axis=1)
    gains = lax.all_gather(jnp.stack([gain_attn, gain_mlp]), "dp", axis=1, tiled=True).astype(f32)
    gain_one, gain_two = gains[0:1], gains[1:2]
    attn_full = gather_dp(attn_shard)
    down_full = gather_dp(after(w_down.T, attn_full))
    pairs, last = [], down_full
    for a, b in parts:
        shard = jnp.concatenate([w_gate[:, a:b], w_up[:, a:b]], axis=1)
        last = gather_dp(after(shard, last))
        pairs.append(last)
    qkv_full = attn_full[:, : heads_width + 2 * HD]
    query_full = attn_full[:, :heads_width]
    keyvalue_full = attn_full[:, heads_width : heads_width + 2 * HD]
    project_full = attn_full[:, heads_width + 2 * HD :]

    residual = layer_input.astype(f32)
    inputs = gather_blocks(layer_input)

    def norm_one(block):
        block = block.astype(f32)
        return (block * inverse_norm(block) * gain_one).astype(bf16)

    normed_one = jnp.concatenate([norm_one(b) for b in inputs], axis=0)
    top = out_grad.astype(f32) * own_mask
    top_all = jnp.concatenate(gather_blocks(after(top.astype(bf16), *inputs)), axis=0)
    qkv = dot(normed_one, qkv_full, 1, 0)
    qr, kvt, mixed, lse = attend(where, qkv, cos2, sin2, rows)
    after_attn = residual + scatter_sum(
        [dot(rows_of(mixed, j, rows), project_full, 1, 1) for j in range(ranks)]
    )

    inv_two = inverse_norm(after_attn)
    normed_two_own = (after_attn * inv_two * gain_two).astype(bf16)
    normed_two = jnp.concatenate(gather_blocks(normed_two_own), axis=0)
    hidden_grad = dot(top_all, down_full, 1, 0)
    hiddens, pair_grads, pair_sums = [], [], []
    for (a, b), pair in zip(parts, pairs):
        both = dot(normed_two, pair, 1, 0)
        gate, up = both[:, : b - a], both[:, b - a :]
        sig = jax.nn.sigmoid(gate)
        grad = hidden_grad[:, a:b]
        hiddens.append((gate * sig * up).astype(bf16))
        gate_grad = (grad * up * sig * (1.0 + gate * (1.0 - sig))).astype(bf16)
        up_grad = (grad * gate * sig).astype(bf16)
        pair_grads.append(jnp.concatenate([gate_grad, up_grad], axis=1))
        pair_sums.append(scatter_dp(dot(normed_two, pair_grads[-1], 0, 0).astype(bf16)))
    hidden = jnp.concatenate(hiddens, axis=1)
    down_sum = scatter_dp(dot(top_all, hidden, 0, 0).astype(bf16))

    normed_two_grad = scatter_sum(
        [
            sum(dot(rows_of(g, j, rows), w, 1, 1) for g, w in zip(pair_grads, pairs))
            for j in range(ranks)
        ]
    )
    unit_two = after_attn * inv_two
    scaled = normed_two_grad * gain_two
    attn_top = top + inv_two * (
        scaled - unit_two * jnp.mean(scaled * unit_two, axis=-1, keepdims=True)
    )
    attn_top_all = jnp.concatenate(gather_blocks(attn_top.astype(bf16)), axis=0)
    after_mlp = after_attn + scatter_sum(
        [dot(rows_of(hidden, j, rows), down_full, 1, 1) for j in range(ranks)]
    )
    output = (after_mlp * own_mask).astype(bf16)

    mixed_grad = dot(attn_top_all, project_full, 1, 0).astype(bf16)
    project_sum = scatter_dp(dot(attn_top_all, mixed, 0, 0).astype(bf16))
    query_grad, kv_part = attend_back(where, qr, kvt, mixed_grad, lse, cos2, sin2, rows)
    shared = kv_part[:rows]
    for j in range(1, ranks):
        shared = shared + hop(rows_of(kv_part, j, rows), j)
    shared = shared + kv_grad.astype(f32) * own_mask
    kv_back = jnp.concatenate([unrotate(shared[:, :HD], cos_own, sin_own), shared[:, HD:]], axis=1)
    kv_back = kv_back.astype(bf16)
    normed_own = normed_one[:rows]
    qkv_grad = jnp.concatenate(
        [
            dot(normed_one, query_grad, 0, 0).astype(bf16),
            dot(normed_own, kv_back, 0, 0).astype(bf16),
        ],
        axis=1,
    )
    qkv_sum = scatter_dp(qkv_grad)
    normed_one_grad = scatter_sum(
        [dot(rows_of(query_grad, j, rows), query_full, 1, 1) for j in range(ranks)]
    ) + dot(kv_back, keyvalue_full, 1, 1)
    inv_one = inverse_norm(residual)
    unit_one = residual * inv_one
    scaled_one = normed_one_grad * gain_one
    input_grad = attn_top + inv_one * (
        scaled_one - unit_one * jnp.mean(scaled_one * unit_one, axis=-1, keepdims=True)
    )

    grad_query, grad_kv_part = qkv_sum[:, :heads_width], qkv_sum[:, heads_width:]
    grad_gate = jnp.concatenate([s[:, : b - a] for (a, b), s in zip(parts, pair_sums)], axis=1)
    grad_up = jnp.concatenate([s[:, b - a :] for (a, b), s in zip(parts, pair_sums)], axis=1)
    gain_one_part = jnp.sum(grad_query * w_query.astype(f32), axis=1) + jnp.sum(
        grad_kv_part * w_keyvalue.astype(f32), axis=1
    )
    gain_two_part = jnp.sum(
        grad_gate * w_gate.astype(f32) + grad_up * w_up.astype(f32), axis=1
    )
    small = jnp.concatenate(
        [grad_kv_part, gain_one_part[:, None], gain_two_part[:, None]], axis=1
    )
    step = 1
    while step < ranks:
        small = small + hop(small, step)
        step *= 2
    grad_keyvalue = small[:, : 2 * HD]
    grad_gain_one = small[:, 2 * HD] / gain_attn.astype(f32)
    grad_gain_two = small[:, 2 * HD + 1] / gain_mlp.astype(f32)
    return (
        output,
        input_grad,
        grad_query,
        grad_keyvalue,
        project_sum.T,
        grad_gate,
        grad_up,
        down_sum.T,
        grad_gain_one,
        grad_gain_two,
    )


def solution(mesh):
    placed = (
        P(("dp", "tensor"), None),
        P("dp"),
        P("dp", "tensor"),
        P("dp", None),
        P("tensor", "dp"),
        P("dp", "tensor"),
        P("dp", "tensor"),
        P("tensor", "dp"),
        P("dp"),
        P("dp"),
        P(("dp", "tensor"), None),
        P(("dp", "tensor"), None),
    )
    return jax.shard_map(
        on_device,
        mesh=mesh,
        in_specs=placed,
        out_specs=(
            P(("dp", "tensor"), None),
            P(("dp", "tensor"), None),
            P("dp", "tensor"),
            P("dp", None),
            P("tensor", "dp"),
            P("dp", "tensor"),
            P("dp", "tensor"),
            P("tensor", "dp"),
            P("dp"),
            P("dp"),
        ),
        check_vma=False,
    )
```

time: 1500 us -> 742 us (0.49)
  waiting for transfers between devices: 1140 us -> 450 us
  blocking collectives: 63.2 us -> 9.56 us
  matrix products: 184 us -> 134 us
  starting transfers between devices: 1.02 us -> 34.8 us
  Pallas kernels: 0 us -> 26.5 us
    reduce_scatter x10 -> x5, waiting for transfers between devices: 693 us -> 49.6 us  [scatter_dp(): lax.psum_scatter(partial, 'dp', scatter_dimension=0, tiled=True).astype(f32)]
    ppermute x0 -> x29, waiting for transfers between devices: none -> 281 us  [hop(): return lax.ppermute(value, 'tensor', [(i, i ^ step) for i in range(size)])]
    all_gather x10 -> x4, waiting for transfers between devices: 396 us -> 119 us  [gather_dp(): return lax.all_gather(shard, 'dp', axis=0, tiled=True)]
    dot_general x32, matrix products: 184 us -> 134 us  [dot(): lax.dot_general(a, b, (((ca,), (cb,)), ((), ())), preferred_element_type=...]
    psum x1 -> x0, waiting for transfers between devices: 44.5 us -> none  [on_device(): lax.psum((attn_sums[1], attn_sums[3], mlp_sums[3]), 'tensor')]
    ppermute x0 -> x29, starting transfers between devices: none -> 34.2 us  [hop(): return lax.ppermute(value, 'tensor', [(i, i ^ step) for i in range(size)])]
    unnamed x1 -> x0, blocking collectives: 30.1 us -> none
    pallas_call x0 -> x2, Pallas kernels: none -> 26.5 us  [the longest x1 14.6 us: attend_back(): pl.pallas_call(attend_back_kernel, name='attend_back', grid_spec=pltpu.Pr...]
  transfers between devices with their start and end apart: 21 -> 38, of which waited for: 19 -> 21; matrix products, arithmetic and copies ran while one was open for 10% -> 25% of each run, Pallas kernels for 0% -> 4%
where the time goes in v1:
time: 742 us; the launch traced here: 735 us
  waiting for transfers between devices  450 us (61%)
  matrix products  134 us (18%)
  other arithmetic  37.5 us (5%)
  starting transfers between devices  34.8 us (5%)
  local copies, waits for them, and re-layouts  27.1 us (4%)
  Pallas kernels  26.5 us (4%)
  between operations  16.1 us (2%)
  blocking collectives  9.56 us (1%)
    ppermute x29, waiting for transfers between devices, hop(): return lax.ppermute(value, 'tensor', [(i, i ^ step) for i in range(size)])  281 us
    dot_general x32, matrix products, dot(): lax.dot_general(a, b, (((ca,), (cb,)), ((), ())), preferred_element_type=...  134 us
    all_gather x4, waiting for transfers between devices, gather_dp(): return lax.all_gather(shard, 'dp', axis=0, tiled=True)  119 us
    reduce_scatter x5, waiting for transfers between devices, scatter_dp(): lax.psum_scatter(partial, 'dp', scatter_dimension=0, tiled=True).astype(f32)  49.6 us
    ppermute x29, starting transfers between devices, hop(): return lax.ppermute(value, 'tensor', [(i, i ^ step) for i in range(size)])  34.2 us
    unnamed x172, local copies, waits for them, and re-layouts  20.8 us
  transfers between devices with their start and end apart: 38, of which 21 were waited for; matrix products, arithmetic and copies ran while one was open for 25% of the time, Pallas kernels for 4%

profile of v1, /device:TPU:0, one launch (start us, length us, event | category | flops | bytes accessed | tf_op | source)
XLA Modules:
  0.0 734.7 jit_solution(16546089016646110884)
XLA Ops:
  9.5 1.9 pad_maximum_fusion.17
  11.5 59.3 %all-gather.5.cloned.1.call-done = bf16[2048,1280]{0,1:T(8,128)(2,1)} async-done(((bf16[256,1280]{0,1:T(8,128)(2,1)}), bf16[2048,1280]{0,1:T(8,128)(2,1)}) %all-gather.5.cloned.1.call-update) | async-done | bytes 5242896 | tf_op jit(solution)/shard_map/all_gather | solution.py:45
  71.8 59.6 %all-gather.7.cloned.1.call-done = bf16[2048,1408]{0,1:T(8,128)(2,1)} async-done(((bf16[256,1408]{0,1:T(8,128)(2,1)}), bf16[2048,1408]{0,1:T(8,128)(2,1)}) %all-gather.7.cloned.1.call-update) | async-done | bytes 5767184 | tf_op jit(solution)/shard_map/all_gather | solution.py:45
  135.9 9.6 %all_gather.15 = bf16[2,2048]{1,0:T(2,128)(2,1)S(1)} all-gather(bf16[2,256]{1,0:T(2,128)(2,1)S(1)} %pad_maximum_fusion.25), channel_id=1, replica_groups=mesh['dp'=8,'tensor'=4] {'dp'}, dimensions={1}, use_global_device_ids=true | all-gather | bytes 9216 | tf_op jit(solution)/shard_map/all_gather | solution.py:271
  145.4 1.9 fusion.82
  149.8 2.4 fusion.23
  152.3 5.3 collective-permute-done
  157.6 23.0 %collective-permute-done.1 = bf16[256,2048]{1,0:T(8,128)(2,1)} collective-permute-done((bf16[256,2048]{1,0:T(8,128)(2,1)S(1)}, bf16[256,2048]{1,0:T(8,128)(2,1)}, u32[]{:S(2)}, u32[]{:S(2)}) %collective-permute-start.1) | collective-permute-done | bytes 1048608 | tf_op jit(solution)/shard_map/ppermute | solution.py:26
  185.9 1.7 fusion.14
  187.7 2.7 fusion.17
  190.4 5.2 fusion.q_ref.kv_ref
  195.6 11.8 %attend.1 = (bf16[1024,512]{1,0:T(8,128)(2,1)S(1)}, bf16[1024,256]{1,0:T(8,128)(2,1)S(1)}, bf16[1024,512]{1,0:T(8,128)(2,1)S(1)}, f32[1024,128]{1,0:T(8,128)S(1)}) custom-call(s32[2]{0:T(128)S(1)} %pad_add_fusion.where_ref, f32[1024,768]{1,0:T(8,128)} %fusion.q_ref.kv_ref, f32[1024,768]{1,0:T(8,128)} %fusion.q_ref.kv_ref, ...), custom_call_target="tpu_custom_call" | custom-call | flops 2147483648 | bytes 8388608 | tf_op jit(solution)/shard_map/attend/pallas_call | solution.py:150
  208.5 1.7 convolution_convert_fusion.8
  211.8 2.3 convolution_convert_fusion.9
  215.5 2.4 convolution_convert_fusion.10
  221.3 28.7 %collective-permute-done.13 = bf16[256,2048]{1,0:T(8,128)(2,1)} collective-permute-done((bf16[256,2048]{1,0:T(8,128)(2,1)}, bf16[256,2048]{1,0:T(8,128)(2,1)}, u32[]{:S(2)}, u32[]{:S(2)}) %collective-permute-start.13) | collective-permute-done | bytes 1048608 | tf_op jit(solution)/shard_map/ppermute | solution.py:26
  252.9 20.7 %collective-permute-done.4 = bf16[256,2048]{1,0:T(8,128)(2,1)S(1)} collective-permute-done((bf16[256,2048]{1,0:T(8,128)(2,1)S(1)}, bf16[256,2048]{1,0:T(8,128)(2,1)S(1)}, u32[]{:S(2)}, u32[]{:S(2)}) %collective-permute-start.4) | collective-permute-done | bytes 1048608 | tf_op jit(solution)/shard_map/ppermute | solution.py:26
  273.6 3.1 multiply_reduce_fusion.1
  281.9 6.7 fusion.113
  288.6 16.8 %collective-permute-done.8 = bf16[256,2048]{1,0:T(8,128)(2,1)S(1)} collective-permute-done((bf16[256,2048]{1,0:T(8,128)(2,1)S(1)}, bf16[256,2048]{1,0:T(8,128)(2,1)S(1)}, u32[]{:S(2)}, u32[]{:S(2)}) %collective-permute-start.8) | collective-permute-done | bytes 1048608 | tf_op jit(solution)/shard_map/ppermute | solution.py:26
  305.4 21.4 %collective-permute-done.7 = bf16[256,2048]{1,0:T(8,128)(2,1)S(1)} collective-permute-done((bf16[256,2048]{1,0:T(8,128)(2,1)S(1)}, bf16[256,2048]{1,0:T(8,128)(2,1)S(1)}, u32[]{:S(2)}, u32[]{:S(2)}) %collective-permute-start.7) | collective-permute-done | bytes 1048608 | tf_op jit(solution)/shard_map/ppermute | solution.py:26
  327.8 8.2 %fusion.106 = f32[1024,1536]{1,0:T(8,128)S(1)} fusion(bf16[2048,1536]{1,0:T(8,128)(2,1)S(1)} %bitcast.40, bf16[256,2048]{1,0:T(8,128)(2,1)S(1)} %collective-permute-done.8, bf16[256,2048]{1,0:T(8,128)(2,1)} %copy-done.62, bf16[256,2048]{1,0:T(8,128)(2,1)} %collective-permute-done.6, bf16[256,2048]{1,0:T(8,128)(2,1)S(1)} %multiply_convert_fusion.7), kind=kOutput, calls=%fused_computation.202 | convolution fusion | flops 6459228160 | bytes 16777216 | tf_op jit(solution)/shard_map/dot_general | solution.py:21
  336.0 3.1 multiply_convert_fusion
  340.7 9.9 %convolution_convert_fusion.2 = bf16[2048,1536]{1,0:T(8,128)(2,1)} fusion(bf16[1024,768]{1,0:T(8,128)(2,1)S(1)} %get-tuple-element.45, bf16[1024,768]{1,0:T(8,128)(2,1)S(1)} %get-tuple-element.46, bf16[256,2048]{1,0:T(8,128)(2,1)S(1)} %collective-permute-done.8, bf16[256,2048]{1,0:T(8,128)(2,1)S(1)} %copy-done.63, ...), kind=kOutput, calls=%fused_computation.2 | convolution fusion | flops 6468665344 | bytes 13631488 | tf_op jit(solution)/shard_map/dot_general | solution.py:21
  350.7 6.3 fusion.51
  357.0 6.1 fusion.48
  363.1 3.2 fusion.45
  366.3 10.4 %fusion.105 = f32[1024,1280]{1,0:T(8,128)S(1)} fusion(bf16[2048,1280]{1,0:T(8,128)(2,1)} %all-gather.11.cloned.1.call-done, bf16[256,2048]{1,0:T(8,128)(2,1)} %copy-done.61, bf16[256,2048]{1,0:T(8,128)(2,1)} %copy-done.62, bf16[256,2048]{1,0:T(8,128)(2,1)} %collective-permute-done.6, bf16[256,2048]{1,0:T(8,128)(2,1)S(1)} %multiply_convert_fusion.7), kind=kOutput, calls=%fused_computation.201 | convolution fusion | flops 5385486336 | bytes 14680064 | tf_op jit(solution)/shard_map/dot_general | solution.py:21
  376.7 4.3 multiply_convert_fusion.3
  381.2 1.5 fusion.7
  384.3 1.6 fusion.6
  386.5 1.6 fusion.5
  389.6 1.8 fusion.42
  391.5 18.3 %collective-permute-done.17 = bf16[256,2048]{1,0:T(8,128)(2,1)S(1)} collective-permute-done((bf16[256,2048]{1,0:T(8,128)(2,1)S(1)}, bf16[256,2048]{1,0:T(8,128)(2,1)S(1)}, u32[]{:S(2)}, u32[]{:S(2)}) %collective-permute-start.17) | collective-permute-done | bytes 1048608 | tf_op jit(solution)/shard_map/ppermute | solution.py:26
  409.8 21.6 %collective-permute-done.16 = bf16[256,2048]{1,0:T(8,128)(2,1)S(1)} collective-permute-done((bf16[256,2048]{1,0:T(8,128)(2,1)S(1)}, bf16[256,2048]{1,0:T(8,128)(2,1)S(1)}, u32[]{:S(2)}, u32[]{:S(2)}) %collective-permute-start.16) | collective-permute-done | bytes 1048608 | tf_op jit(solution)/shard_map/ppermute | solution.py:26
  431.4 2.1 multiply_reduce_fusion
  433.5 2.0 fusion.107
  439.1 23.5 %collective-permute-done.20 = bf16[256,2048]{1,0:T(8,128)(2,1)S(1)} collective-permute-done((bf16[256,2048]{1,0:T(8,128)(2,1)S(1)}, bf16[256,2048]{1,0:T(8,128)(2,1)S(1)}, u32[]{:S(2)}, u32[]{:S(2)}) %collective-permute-start.20) | collective-permute-done | bytes 1048608 | tf_op jit(solution)/shard_map/ppermute | solution.py:26
  462.5 21.5 %collective-permute-done.19 = bf16[256,2048]{1,0:T(8,128)(2,1)S(1)} collective-permute-done((bf16[256,2048]{1,0:T(8,128)(2,1)S(1)}, bf16[256,2048]{1,0:T(8,128)(2,1)S(1)}, u32[]{:S(2)}, u32[]{:S(2)}) %collective-permute-start.19) | collective-permute-done | bytes 1048608 | tf_op jit(solution)/shard_map/ppermute | solution.py:26
  484.0 5.7 convolution_convert_fusion.15.dm_ref
  489.9 14.6 %attend_back.1 = (bf16[1024,512]{1,0:T(8,128)(2,1)S(1)}, f32[1024,256]{1,0:T(8,128)S(1)}) custom-call(s32[2]{0:T(128)S(1)} %pad_add_fusion.where_ref, bf16[1024,512]{1,0:T(8,128)(2,1)S(1)} %copy-done.1, bf16[1024,256]{1,0:T(8,128)(2,1)S(1)} %copy-done.3, bf16[1024,512]{1,0:T(8,128)(2,1)} %convolution_convert_fusion.15.dm_ref, f32[1024,128]{1,0:T(8,128)S(1)} %copy-done.5, ...), custom_call_target="tpu_custom_call" | custom-call | flops 5368709120 | bytes 8388608 | tf_op jit(solution)/shard_map/attend_back/pallas_call | solution.py:188
  508.1 2.9 convolution_convert_fusion.4
  511.0 3.7 collective-permute-done.26
  514.7 4.6 collective-permute-done.25
  521.1 2.0 pad_maximum_fusion.7
  524.4 9.7 %convolution_convert_fusion.1 = bf16[2048,1280]{1,0:T(8,128)(2,1)} fusion(bf16[1024,640]{1,0:T(8,128)(2,1)} %copy-done.13, bf16[1024,640]{1,0:T(8,128)(2,1)} %copy-done.14, bf16[256,2048]{1,0:T(8,128)(2,1)} %copy-done.61, bf16[256,2048]{1,0:T(8,128)(2,1)} %copy-done.62, bf16[256,2048]{1,0:T(8,128)(2,1)} %collective-permute-done.6, ...), kind=kOutput, calls=%fused_computation.1 | convolution fusion | flops 5393350656 | bytes 12058624 | tf_op jit(solution)/shard_map/dot_general | solution.py:21
  535.3 5.6 convolution_convert_fusion.3
  541.0 11.4 %convolution_convert_fusion = bf16[2048,1408]{1,0:T(8,128)(2,1)} fusion(bf16[1024,2048]{1,0:T(8,128)(2,1)} %copy-done.51, bf16[1024,640]{1,0:T(8,128)(2,1)} %get-tuple-element.50, bf16[1024,768]{1,0:T(8,128)(2,1)} %get-tuple-element.49), kind=kOutput, calls=%fused_computation | convolution fusion | flops 5914230784 | bytes 12845056 | tf_op jit(solution)/shard_map/dot_general | solution.py:21
  553.8 4.7 convolution_convert_fusion.12
  560.0 4.6 convolution_convert_fusion.13
  565.4 1.8 convolution_convert_fusion.14
  568.8 16.9 %collective-permute-done.11 = bf16[256,2048]{1,0:T(8,128)(2,1)S(1)} collective-permute-done((bf16[256,2048]{1,0:T(8,128)(2,1)S(1)}, bf16[256,2048]{1,0:T(8,128)(2,1)S(1)}, u32[]{:S(2)}, u32[]{:S(2)}) %collective-permute-start.11) | collective-permute-done | bytes 1048608 | tf_op jit(solution)/shard_map/ppermute | solution.py:26
  585.6 21.4 %collective-permute-done.10 = bf16[256,2048]{1,0:T(8,128)(2,1)S(1)} collective-permute-done((bf16[256,2048]{1,0:T(8,128)(2,1)S(1)}, bf16[256,2048]{1,0:T(8,128)(2,1)S(1)}, u32[]{:S(2)}, u32[]{:S(2)}) %collective-permute-start.10) | collective-permute-done | bytes 1048608 | tf_op jit(solution)/shard_map/ppermute | solution.py:26
  607.1 3.2 multiply_convert_fusion.6
  610.3 1.7 convolution_convert_fusion.5
  613.3 1.7 convolution_convert_fusion.6
  615.8 1.7 convolution_convert_fusion.7
  619.5 2.4 fusion.109
  625.9 3.0 add_reduce_fusion
  629.6 9.6 %collective-permute-done.23 = bf16[256,2048]{1,0:T(8,128)(2,1)} collective-permute-done((bf16[256,2048]{1,0:T(8,128)(2,1)}, bf16[256,2048]{1,0:T(8,128)(2,1)}, u32[]{:S(2)}, u32[]{:S(2)}) %collective-permute-start.23) | collective-permute-done | bytes 1048608 | tf_op jit(solution)/shard_map/ppermute | solution.py:26
  639.3 21.6 %collective-permute-done.22 = bf16[256,2048]{1,0:T(8,128)(2,1)} collective-permute-done((bf16[256,2048]{1,0:T(8,128)(2,1)}, bf16[256,2048]{1,0:T(8,128)(2,1)}, u32[]{:S(2)}, u32[]{:S(2)}) %collective-permute-start.22) | collective-permute-done | bytes 1048608 | tf_op jit(solution)/shard_map/ppermute | solution.py:26
  660.9 3.8 fusion.18
  667.3 1.8 fusion.21
  675.5 49.5 %reduce-scatter.14.cloned.1.call-done = bf16[256,1408]{1,0:T(8,128)(2,1)} async-done(((bf16[2048,1408]{1,0:T(8,128)(2,1)}), bf16[256,1408]{1,0:T(8,128)(2,1)}) %reduce-scatter.14.cloned.1.call-update) | async-done | bytes 720912 | tf_op jit(solution)/shard_map/reduce_scatter | solution.py:49
  (299 shorter events, 73.6 us)
Async XLA Ops:
  7.2 63.7 %slice-start.6 = ((bf16[256,1408]{1,0:T(8,128)(2,1)}), bf16[256,768]{1,0:T(8,128)(2,1)S(1)}, s32[]{:S(2)}) async-start(bf16[256,1408]{1,0:T(8,128)(2,1)} %param.18), calls=%async_computation.20 | async-start | bytes 786432 | tf_op jit(solution)/shard_map/slice | solution.py:277
  7.2 63.7 %slice-start.8 = ((bf16[256,1408]{1,0:T(8,128)(2,1)}), bf16[256,768]{1,0:T(8,128)(2,1)S(1)}, s32[]{:S(2)}) async-start(bf16[256,1408]{1,0:T(8,128)(2,1)} %param.17), calls=%async_computation.22 | async-start | bytes 786432 | tf_op jit(solution)/shard_map/slice | solution.py:277
  7.2 63.6 %all-gather.5.cloned.1.call-start = ((), (), s32[]{:S(2)}) async-start(), calls=%async_computation.5 | async-start | bytes 5898240 | tf_op jit(solution)/shard_map/all_gather | solution.py:45
  11.4 120.1 %copy-start.18 = (bf16[256,2048]{1,0:T(8,128)(2,1)S(1)}, bf16[256,2048]{1,0:T(8,128)(2,1)}, u32[]{:S(2)}) copy-start(bf16[256,2048]{1,0:T(8,128)(2,1)} %param.12) | copy-start | bytes 3145732
  11.4 120.0 %all-gather.7.cloned.1.call-start = ((), (), s32[]{:S(2)}) async-start(), calls=%async_computation.6 | async-start | bytes 6488064 | tf_op jit(solution)/shard_map/all_gather | solution.py:45
  70.8 64.9 %copy-start.59 = (bf16[256]{0:T(256)(128)(2,1)S(1)}, bf16[256]{0:T(256)(128)(2,1)}, u32[]{:S(2)}) copy-start(bf16[256]{0:T(256)(128)(2,1)} %param.21) | copy-start | bytes 1540
  70.8 64.9 %copy-start.57 = (bf16[256]{0:T(256)(128)(2,1)S(1)}, bf16[256]{0:T(256)(128)(2,1)}, u32[]{:S(2)}) copy-start(bf16[256]{0:T(256)(128)(2,1)} %param.20) | copy-start | bytes 1540
  70.8 140.7 %all-gather.9.cloned.1.call-start = ((), (), s32[]{:S(2)}) async-start(), calls=%async_computation.7 | async-start | bytes 7077888 | tf_op jit(solution)/shard_map/all_gather | solution.py:45
  131.4 234.8 %all-gather.11.cloned.1.call-start = ((), (), s32[]{:S(2)}) async-start(), calls=%async_computation.8 | async-start | bytes 5898240 | tf_op jit(solution)/shard_map/all_gather | solution.py:45
  131.5 26.1 %collective-permute-start = (bf16[256,2048]{1,0:T(8,128)(2,1)S(1)}, bf16[256,2048]{1,0:T(8,128)(2,1)S(1)}, u32[]{:S(2)}, u32[]{:S(2)}) collective-permute-start(bf16[256,2048]{1,0:T(8,128)(2,1)S(1)} %copy-done.18), channel_id=1, source_target_pairs={{0,1},{1,0},{2,3},{3,2},{4,5},{5,4},{6,7},{7,6},{8,9},{9,8},{10,11... | collective-permute-start | bytes 3145736 | tf_op jit(solution)/shard_map/ppermute | solution.py:26
  133.0 47.6 %collective-permute-start.1 = (bf16[256,2048]{1,0:T(8,128)(2,1)S(1)}, bf16[256,2048]{1,0:T(8,128)(2,1)}, u32[]{:S(2)}, u32[]{:S(2)}) collective-permute-start(bf16[256,2048]{1,0:T(8,128)(2,1)S(1)} %copy-done.18), channel_id=1, source_target_pairs={{0,2},{1,3},{2,0},{3,1},{4,6},{5,7},{6,4},{7,5},{8,10},{9,11},{10,... | collective-permute-start | bytes 3145736 | tf_op jit(solution)/shard_map/ppermute | solution.py:26
  134.5 46.1 %collective-permute-start.2 = (bf16[256,2048]{1,0:T(8,128)(2,1)S(1)}, bf16[256,2048]{1,0:T(8,128)(2,1)}, u32[]{:S(2)}, u32[]{:S(2)}) collective-permute-start(bf16[256,2048]{1,0:T(8,128)(2,1)S(1)} %copy-done.18), channel_id=1, source_target_pairs={{0,3},{1,2},{2,1},{3,0},{4,7},{5,6},{6,5},{7,4},{8,11},{9,10},{10,... | collective-permute-start | bytes 3145736 | tf_op jit(solution)/shard_map/ppermute | solution.py:26
  148.8 38.9 %copy-start.55 = (f32[256]{0:T(256)}, f32[256]{0:T(256)S(1)}, u32[]{:S(2)}) copy-start(f32[256]{0:T(256)S(1)} %add_rsqrt_fusion.4) | copy-start | bytes 3076
  149.8 37.8 %copy-start.53 = (f32[1,2048]{1,0:T(1,128)}, f32[1,2048]{1,0:T(1,128)S(1)}, u32[]{:S(2)}) copy-start(f32[1,2048]{1,0:T(1,128)S(1)} %get-tuple-element.63) | copy-start | bytes 24580
  180.6 37.3 %collective-permute-start.12 = (bf16[256,2048]{1,0:T(8,128)(2,1)}, bf16[256,2048]{1,0:T(8,128)(2,1)}, u32[]{:S(2)}, u32[]{:S(2)}) collective-permute-start(bf16[256,2048]{1,0:T(8,128)(2,1)} %fusion.23), channel_id=1, source_target_pairs={{0,1},{1,0},{2,3},{3,2},{4,5},{5,4},{6,7},{7,6},{8,9},{9,8},{10,11... | collective-permute-start | bytes 3145736 | tf_op jit(solution)/shard_map/ppermute | solution.py:26
  181.8 68.2 %collective-permute-start.13 = (bf16[256,2048]{1,0:T(8,128)(2,1)}, bf16[256,2048]{1,0:T(8,128)(2,1)}, u32[]{:S(2)}, u32[]{:S(2)}) collective-permute-start(bf16[256,2048]{1,0:T(8,128)(2,1)} %fusion.23), channel_id=1, source_target_pairs={{0,2},{1,3},{2,0},{3,1},{4,6},{5,7},{6,4},{7,5},{8,10},{9,11},{10,... | collective-permute-start | bytes 3145736 | tf_op jit(solution)/shard_map/ppermute | solution.py:26
  182.7 68.6 %collective-permute-start.14 = (bf16[256,2048]{1,0:T(8,128)(2,1)}, bf16[256,2048]{1,0:T(8,128)(2,1)}, u32[]{:S(2)}, u32[]{:S(2)}) collective-permute-start(bf16[256,2048]{1,0:T(8,128)(2,1)} %fusion.23), channel_id=1, source_target_pairs={{0,3},{1,2},{2,1},{3,0},{4,7},{5,6},{6,5},{7,4},{8,11},{9,10},{10,... | collective-permute-start | bytes 3145736 | tf_op jit(solution)/shard_map/ppermute | solution.py:26
  210.1 42.8 %collective-permute-start.5 = (bf16[256,2048]{1,0:T(8,128)(2,1)}, bf16[256,2048]{1,0:T(8,128)(2,1)}, u32[]{:S(2)}, u32[]{:S(2)}) collective-permute-start(bf16[256,2048]{1,0:T(8,128)(2,1)} %convolution_convert_fusion.8), channel_id=1, source_target_pairs={{0,3},{1,2},{2,1},{3,0},{4,7},{5,6},{6,5},{7,4},{8,11},{9,10},{10,... | collective-permute-start | bytes 3145736 | tf_op jit(solution)/shard_map/ppermute | solution.py:26
  211.6 407.8 %reduce-scatter.8.cloned.1.call-start = ((), (), s32[]{:S(2)}) async-start(), calls=%async_computation.10 | async-start | bytes 7077888 | tf_op jit(solution)/shard_map/reduce_scatter | solution.py:49
  214.2 59.5 %collective-permute-start.4 = (bf16[256,2048]{1,0:T(8,128)(2,1)S(1)}, bf16[256,2048]{1,0:T(8,128)(2,1)S(1)}, u32[]{:S(2)}, u32[]{:S(2)}) collective-permute-start(bf16[256,2048]{1,0:T(8,128)(2,1)S(1)} %convolution_convert_fusion.9), channel_id=1, source_target_pairs={{0,2},{1,3},{2,0},{3,1},{4,6},{5,7},{6,4},{7,5},{8,10},{9,11},{10,... | collective-permute-start | bytes 3145736 | tf_op jit(solution)/shard_map/ppermute | solution.py:26
  217.9 55.7 %collective-permute-start.3 = (bf16[256,2048]{1,0:T(8,128)(2,1)S(1)}, bf16[256,2048]{1,0:T(8,128)(2,1)S(1)}, u32[]{:S(2)}, u32[]{:S(2)}) collective-permute-start(bf16[256,2048]{1,0:T(8,128)(2,1)S(1)} %convolution_convert_fusion.10), channel_id=1, source_target_pairs={{0,1},{1,0},{2,3},{3,2},{4,5},{5,4},{6,7},{7,6},{8,9},{9,8},{10,11... | collective-permute-start | bytes 3145736 | tf_op jit(solution)/shard_map/ppermute | solution.py:26
  221.3 52.3 %copy-start.19 = (bf16[256,2048]{1,0:T(8,128)(2,1)S(1)}, bf16[256,2048]{1,0:T(8,128)(2,1)}, u32[]{:S(2)}) copy-start(bf16[256,2048]{1,0:T(8,128)(2,1)} %param.12) | copy-start | bytes 3145732
  278.1 49.7 %slice-start = ((s8[6291456]{0:T(1024)(128)(4,1)}), s8[4194304]{0:T(1024)(128)(4,1)S(1)}, s32[]{:S(2)}) async-start(s8[6291456]{0:T(1024)(128)(4,1)} %bitcast.39), calls=%async_computation.14 | async-start | bytes 8388608
  278.3 87.9 %copy-start.49 = (bf16[256,2048]{1,0:T(8,128)(2,1)}, bf16[256,2048]{1,0:T(8,128)(2,1)S(1)}, u32[]{:S(2)}) copy-start(bf16[256,2048]{1,0:T(8,128)(2,1)S(1)} %multiply_convert_fusion.7) | copy-start | bytes 3145732
  278.3 49.4 %slice-start.1 = ((s8[6291456]{0:T(1024)(128)(4,1)}), s8[2097152]{0:T(1024)(128)(4,1)S(1)}, s32[]{:S(2)}) async-start(s8[6291456]{0:T(1024)(128)(4,1)} %bitcast.39), calls=%async_computation.15 | async-start | bytes 4194304
  278.4 27.0 %collective-permute-start.8 = (bf16[256,2048]{1,0:T(8,128)(2,1)S(1)}, bf16[256,2048]{1,0:T(8,128)(2,1)S(1)}, u32[]{:S(2)}, u32[]{:S(2)}) collective-permute-start(bf16[256,2048]{1,0:T(8,128)(2,1)S(1)} %multiply_convert_fusion.7), channel_id=1, source_target_pairs={{0,3},{1,2},{2,1},{3,0},{4,7},{5,6},{6,5},{7,4},{8,11},{9,10},{10,... | collective-permute-start | bytes 3145736 | tf_op jit(solution)/shard_map/ppermute | solution.py:26
  279.9 46.9 %collective-permute-start.7 = (bf16[256,2048]{1,0:T(8,128)(2,1)S(1)}, bf16[256,2048]{1,0:T(8,128)(2,1)S(1)}, u32[]{:S(2)}, u32[]{:S(2)}) collective-permute-start(bf16[256,2048]{1,0:T(8,128)(2,1)S(1)} %multiply_convert_fusion.7), channel_id=1, source_target_pairs={{0,2},{1,3},{2,0},{3,1},{4,6},{5,7},{6,4},{7,5},{8,10},{9,11},{10,... | collective-permute-start | bytes 3145736 | tf_op jit(solution)/shard_map/ppermute | solution.py:26
  280.5 47.3 %collective-permute-start.6 = (bf16[256,2048]{1,0:T(8,128)(2,1)S(1)}, bf16[256,2048]{1,0:T(8,128)(2,1)}, u32[]{:S(2)}, u32[]{:S(2)}) collective-permute-start(bf16[256,2048]{1,0:T(8,128)(2,1)S(1)} %multiply_convert_fusion.7), channel_id=1, source_target_pairs={{0,1},{1,0},{2,3},{3,2},{4,5},{5,4},{6,7},{7,6},{8,9},{9,8},{10,11... | collective-permute-start | bytes 3145736 | tf_op jit(solution)/shard_map/ppermute | solution.py:26
  288.6 47.4 %copy-start.25 = (f32[1024,1408]{1,0:T(8,128)}, f32[1024,1408]{1,0:T(8,128)S(1)}, u32[]{:S(2)}) copy-start(f32[1024,1408]{1,0:T(8,128)S(1)} %fusion.113) | copy-start | bytes 17301508
  350.6 271.3 %reduce-scatter.6.cloned.1.call-start = ((), (), s32[]{:S(2)}) async-start(), calls=%async_computation.9 | async-start | bytes 3538944 | tf_op jit(solution)/shard_map/reduce_scatter | solution.py:49
  381.0 50.4 %copy-start.13 = (bf16[1024,640]{1,0:T(8,128)(2,1)}, bf16[1024,640]{1,0:T(8,128)(2,1)S(1)}, u32[]{:S(2)}) copy-start(bf16[1024,640]{1,0:T(8,128)(2,1)S(1)} %get-tuple-element.47) | copy-start | bytes 3932164
  381.0 50.3 %copy-start.14 = (bf16[1024,640]{1,0:T(8,128)(2,1)}, bf16[1024,640]{1,0:T(8,128)(2,1)S(1)}, u32[]{:S(2)}) copy-start(bf16[1024,640]{1,0:T(8,128)(2,1)S(1)} %get-tuple-element.48) | copy-start | bytes 3932164
  382.8 27.0 %collective-permute-start.17 = (bf16[256,2048]{1,0:T(8,128)(2,1)S(1)}, bf16[256,2048]{1,0:T(8,128)(2,1)S(1)}, u32[]{:S(2)}, u32[]{:S(2)}) collective-permute-start(bf16[256,2048]{1,0:T(8,128)(2,1)S(1)} %fusion.7), channel_id=1, source_target_pairs={{0,3},{1,2},{2,1},{3,0},{4,7},{5,6},{6,5},{7,4},{8,11},{9,10},{10,... | collective-permute-start | bytes 3145736 | tf_op jit(solution)/shard_map/ppermute | solution.py:26
  385.8 45.5 %collective-permute-start.16 = (bf16[256,2048]{1,0:T(8,128)(2,1)S(1)}, bf16[256,2048]{1,0:T(8,128)(2,1)S(1)}, u32[]{:S(2)}, u32[]{:S(2)}) collective-permute-start(bf16[256,2048]{1,0:T(8,128)(2,1)S(1)} %fusion.6), channel_id=1, source_target_pairs={{0,2},{1,3},{2,0},{3,1},{4,6},{5,7},{6,4},{7,5},{8,10},{9,11},{10,... | collective-permute-start | bytes 3145736 | tf_op jit(solution)/shard_map/ppermute | solution.py:26
  388.1 43.3 %copy-start.16 = (f32[256,2048]{1,0:T(8,128)S(1)}, f32[256,2048]{1,0:T(8,128)}, u32[]{:S(2)}) copy-start(f32[256,2048]{1,0:T(8,128)} %copy-done.15) | copy-start | bytes 6291460
  388.1 43.3 %collective-permute-start.15 = (bf16[256,2048]{1,0:T(8,128)(2,1)S(1)}, bf16[256,2048]{1,0:T(8,128)(2,1)S(1)}, u32[]{:S(2)}, u32[]{:S(2)}) collective-permute-start(bf16[256,2048]{1,0:T(8,128)(2,1)S(1)} %fusion.5), channel_id=1, source_target_pairs={{0,1},{1,0},{2,3},{3,2},{4,5},{5,4},{6,7},{7,6},{8,9},{9,8},{10,11... | collective-permute-start | bytes 3145736 | tf_op jit(solution)/shard_map/ppermute | solution.py:26
  391.5 42.0 %copy-start.28 = (bf16[256,2048]{1,0:T(8,128)(2,1)S(1)}, bf16[256,2048]{1,0:T(8,128)(2,1)}, u32[]{:S(2)}) copy-start(bf16[256,2048]{1,0:T(8,128)(2,1)} %param.22) | copy-start | bytes 3145732
  435.5 54.3 %copy-start.47 = (bf16[256,2048]{1,0:T(8,128)(2,1)}, bf16[256,2048]{1,0:T(8,128)(2,1)S(1)}, u32[]{:S(2)}) copy-start(bf16[256,2048]{1,0:T(8,128)(2,1)S(1)} %get-tuple-element.43) | copy-start | bytes 3145732
  435.5 54.3 %copy-start.1 = (bf16[1024,512]{1,0:T(8,128)(2,1)S(1)}, bf16[1024,512]{1,0:T(8,128)(2,1)}, u32[]{:S(2)}) copy-start(bf16[1024,512]{1,0:T(8,128)(2,1)} %copy-done) | copy-start | bytes 3145732
  435.5 54.3 %copy-start.3 = (bf16[1024,256]{1,0:T(8,128)(2,1)S(1)}, bf16[1024,256]{1,0:T(8,128)(2,1)}, u32[]{:S(2)}) copy-start(bf16[1024,256]{1,0:T(8,128)(2,1)} %copy-done.2) | copy-start | bytes 1572868
  435.5 54.3 %copy-start.5 = (f32[1024,128]{1,0:T(8,128)S(1)}, f32[1024,128]{1,0:T(8,128)}, u32[]{:S(2)}) copy-start(f32[1024,128]{1,0:T(8,128)} %copy-done.4) | copy-start | bytes 1572868
  435.5 27.0 %collective-permute-start.20 = (bf16[256,2048]{1,0:T(8,128)(2,1)S(1)}, bf16[256,2048]{1,0:T(8,128)(2,1)S(1)}, u32[]{:S(2)}, u32[]{:S(2)}) collective-permute-start(bf16[256,2048]{1,0:T(8,128)(2,1)S(1)} %get-tuple-element.43), channel_id=1, source_target_pairs={{0,3},{1,2},{2,1},{3,0},{4,7},{5,6},{6,5},{7,4},{8,11},{9,10},{10,... | collective-permute-start | bytes 3145736 | tf_op jit(solution)/shard_map/ppermute | solution.py:26
  436.9 47.1 %collective-permute-start.19 = (bf16[256,2048]{1,0:T(8,128)(2,1)S(1)}, bf16[256,2048]{1,0:T(8,128)(2,1)S(1)}, u32[]{:S(2)}, u32[]{:S(2)}) collective-permute-start(bf16[256,2048]{1,0:T(8,128)(2,1)S(1)} %get-tuple-element.43), channel_id=1, source_target_pairs={{0,2},{1,3},{2,0},{3,1},{4,6},{5,7},{6,4},{7,5},{8,10},{9,11},{10,... | collective-permute-start | bytes 3145736 | tf_op jit(solution)/shard_map/ppermute | solution.py:26
  437.6 46.4 %collective-permute-start.18 = (bf16[256,2048]{1,0:T(8,128)(2,1)S(1)}, bf16[256,2048]{1,0:T(8,128)(2,1)S(1)}, u32[]{:S(2)}, u32[]{:S(2)}) collective-permute-start(bf16[256,2048]{1,0:T(8,128)(2,1)S(1)} %get-tuple-element.43), channel_id=1, source_target_pairs={{0,1},{1,0},{2,3},{3,2},{4,5},{5,4},{6,7},{7,6},{8,9},{9,8},{10,11... | collective-permute-start | bytes 3145736 | tf_op jit(solution)/shard_map/ppermute | solution.py:26
  504.6 10.2 %collective-permute-start.26 = (f32[256,256]{1,0:T(8,128)S(1)}, f32[256,256]{1,0:T(8,128)S(1)}, u32[]{:S(2)}, u32[]{:S(2)}) collective-permute-start(f32[256,256]{1,0:T(8,128)S(1)} %get-tuple-element.54), channel_id=1, source_target_pairs={{0,3},{1,2},{2,1},{3,0},{4,7},{5,6},{6,5},{7,4},{8,11},{9,10},{10,... | collective-permute-start | bytes 786440 | tf_op jit(solution)/shard_map/ppermute | solution.py:26
  506.0 13.4 %collective-permute-start.25 = (f32[256,256]{1,0:T(8,128)S(1)}, f32[256,256]{1,0:T(8,128)S(1)}, u32[]{:S(2)}, u32[]{:S(2)}) collective-permute-start(f32[256,256]{1,0:T(8,128)S(1)} %get-tuple-element.55), channel_id=1, source_target_pairs={{0,2},{1,3},{2,0},{3,1},{4,6},{5,7},{6,4},{7,5},{8,10},{9,11},{10,... | collective-permute-start | bytes 786440 | tf_op jit(solution)/shard_map/ppermute | solution.py:26
  506.7 12.7 %collective-permute-start.24 = (f32[256,256]{1,0:T(8,128)S(1)}, f32[256,256]{1,0:T(8,128)S(1)}, u32[]{:S(2)}, u32[]{:S(2)}) collective-permute-start(f32[256,256]{1,0:T(8,128)S(1)} %get-tuple-element.53), channel_id=1, source_target_pairs={{0,1},{1,0},{2,3},{3,2},{4,5},{5,4},{6,7},{7,6},{8,9},{9,8},{10,11... | collective-permute-start | bytes 786440 | tf_op jit(solution)/shard_map/ppermute | solution.py:26
  523.2 100.9 %reduce-scatter.10.cloned.1.call-start = ((), (), s32[]{:S(2)}) async-start(), calls=%async_computation.11 | async-start | bytes 5898240 | tf_op jit(solution)/shard_map/reduce_scatter | solution.py:49
  534.1 135.0 %reduce-scatter.12.cloned.1.call-start = ((), (), s32[]{:S(2)}) async-start(), calls=%async_computation.12 | async-start | bytes 2359296 | tf_op jit(solution)/shard_map/reduce_scatter | solution.py:49
  541.0 184.1 %reduce-scatter.14.cloned.1.call-start = ((), (), s32[]{:S(2)}) async-start(), calls=%async_computation.13 | async-start | bytes 6488064 | tf_op jit(solution)/shard_map/reduce_scatter | solution.py:49
  558.6 27.0 %collective-permute-start.11 = (bf16[256,2048]{1,0:T(8,128)(2,1)S(1)}, bf16[256,2048]{1,0:T(8,128)(2,1)S(1)}, u32[]{:S(2)}, u32[]{:S(2)}) collective-permute-start(bf16[256,2048]{1,0:T(8,128)(2,1)S(1)} %convolution_convert_fusion.12), channel_id=1, source_target_pairs={{0,3},{1,2},{2,1},{3,0},{4,7},{5,6},{6,5},{7,4},{8,11},{9,10},{10,... | collective-permute-start | bytes 3145736 | tf_op jit(solution)/shard_map/ppermute | solution.py:26
  560.0 50.3 %slice-start.12 = ((s8[5242880]{0:T(1024)(128)(4,1)}), s8[4194304]{0:T(1024)(128)(4,1)S(1)}, s32[]{:S(2)}) async-start(s8[5242880]{0:T(1024)(128)(4,1)} %bitcast.47), calls=%async_computation.26 | async-start | bytes 8388608
  564.6 42.5 %copy-start.17 = (f32[256,2048]{1,0:T(8,128)S(1)}, f32[256,2048]{1,0:T(8,128)}, u32[]{:S(2)}) copy-start(f32[256,2048]{1,0:T(8,128)} %copy-done.15) | copy-start | bytes 6291460
  564.6 45.7 %slice-start.13 = ((s8[5242880]{0:T(1024)(128)(4,1)}), s8[1048576]{0:T(1024)(128)(4,1)S(1)}, s32[]{:S(2)}) async-start(s8[5242880]{0:T(1024)(128)(4,1)} %bitcast.47), calls=%async_computation.27 | async-start | bytes 2097152
  564.6 42.4 %collective-permute-start.10 = (bf16[256,2048]{1,0:T(8,128)(2,1)S(1)}, bf16[256,2048]{1,0:T(8,128)(2,1)S(1)}, u32[]{:S(2)}, u32[]{:S(2)}) collective-permute-start(bf16[256,2048]{1,0:T(8,128)(2,1)S(1)} %convolution_convert_fusion.13), channel_id=1, source_target_pairs={{0,2},{1,3},{2,0},{3,1},{4,6},{5,7},{6,4},{7,5},{8,10},{9,11},{10,... | collective-permute-start | bytes 3145736 | tf_op jit(solution)/shard_map/ppermute | solution.py:26
  567.2 39.8 %collective-permute-start.9 = (bf16[256,2048]{1,0:T(8,128)(2,1)S(1)}, bf16[256,2048]{1,0:T(8,128)(2,1)S(1)}, u32[]{:S(2)}, u32[]{:S(2)}) collective-permute-start(bf16[256,2048]{1,0:T(8,128)(2,1)S(1)} %convolution_convert_fusion.14), channel_id=1, source_target_pairs={{0,1},{1,0},{2,3},{3,2},{4,5},{5,4},{6,7},{7,6},{8,9},{9,8},{10,11... | collective-permute-start | bytes 3145736 | tf_op jit(solution)/shard_map/ppermute | solution.py:26
  612.0 27.3 %collective-permute-start.23 = (bf16[256,2048]{1,0:T(8,128)(2,1)}, bf16[256,2048]{1,0:T(8,128)(2,1)}, u32[]{:S(2)}, u32[]{:S(2)}) collective-permute-start(bf16[256,2048]{1,0:T(8,128)(2,1)} %convolution_convert_fusion.5), channel_id=1, source_target_pairs={{0,3},{1,2},{2,1},{3,0},{4,7},{5,6},{6,5},{7,4},{8,11},{9,10},{10,... | collective-permute-start | bytes 3145736 | tf_op jit(solution)/shard_map/ppermute | solution.py:26
  615.0 45.8 %collective-permute-start.22 = (bf16[256,2048]{1,0:T(8,128)(2,1)}, bf16[256,2048]{1,0:T(8,128)(2,1)}, u32[]{:S(2)}, u32[]{:S(2)}) collective-permute-start(bf16[256,2048]{1,0:T(8,128)(2,1)} %convolution_convert_fusion.6), channel_id=1, source_target_pairs={{0,2},{1,3},{2,0},{3,1},{4,6},{5,7},{6,4},{7,5},{8,10},{9,11},{10,... | collective-permute-start | bytes 3145736 | tf_op jit(solution)/shard_map/ppermute | solution.py:26
  617.5 43.4 %collective-permute-start.21 = (bf16[256,2048]{1,0:T(8,128)(2,1)}, bf16[256,2048]{1,0:T(8,128)(2,1)}, u32[]{:S(2)}, u32[]{:S(2)}) collective-permute-start(bf16[256,2048]{1,0:T(8,128)(2,1)} %convolution_convert_fusion.7), channel_id=1, source_target_pairs={{0,1},{1,0},{2,3},{3,2},{4,5},{5,4},{6,7},{7,6},{8,9},{9,8},{10,11... | collective-permute-start | bytes 3145736 | tf_op jit(solution)/shard_map/ppermute | solution.py:26
  625.9 35.0 %copy-start.54 = (f32[1,2048]{1,0:T(1,128)S(1)}, f32[1,2048]{1,0:T(1,128)}, u32[]{:S(2)}) copy-start(f32[1,2048]{1,0:T(1,128)} %copy-done.53) | copy-start | bytes 24580
  625.9 35.0 %copy-start.56 = (f32[256]{0:T(256)S(1)}, f32[256]{0:T(256)}, u32[]{:S(2)}) copy-start(f32[256]{0:T(256)} %copy-done.55) | copy-start | bytes 3076
  629.0 38.3 %copy-start.21 = (f32[256,2048]{1,0:T(8,128)S(1)}, f32[256,2048]{1,0:T(8,128)}, u32[]{:S(2)}) copy-start(f32[256,2048]{1,0:T(8,128)} %get-tuple-element.44) | copy-start | bytes 6291460
  629.0 36.7 %collective-permute-start.27 = (f32[256,258]{0,1:T(8,128)S(1)}, f32[256,258]{0,1:T(8,128)S(1)}, u32[]{:S(2)}, u32[]{:S(2)}) collective-permute-start(f32[256,258]{0,1:T(8,128)S(1)} %pad_maximum_fusion.21), channel_id=1, source_target_pairs={{0,1},{1,0},{2,3},{3,2},{4,5},{5,4},{6,7},{7,6},{8,9},{9,8},{10,11... | collective-permute-start | bytes 792584 | tf_op jit(solution)/shard_map/ppermute | solution.py:26
  665.8 7.7 %collective-permute-start.28 = (f32[256,258]{0,1:T(8,128)S(1)}, f32[256,258]{0,1:T(8,128)S(1)}, u32[]{:S(2)}, u32[]{:S(2)}) collective-permute-start(f32[256,258]{0,1:T(8,128)S(1)} %fusion.104), channel_id=1, source_target_pairs={{0,2},{1,3},{2,0},{3,1},{4,6},{5,7},{6,4},{7,5},{8,10},{9,11},{10,... | collective-permute-start | bytes 792584 | tf_op jit(solution)/shard_map/ppermute | solution.py:26
  (59 other events, 461.8 us)
Sparse Core Ops, SparseCore 0:
  11.6 59.1 all-gather.4
  72.4 58.9 all-gather.6
  133.6 62.8 all-gather.8
  211.7 53.8 all-gather.10
  350.7 67.0 reduce-scatter.7
  523.3 37.6 reduce-scatter.5
  563.3 58.9 reduce-scatter.9
  624.7 34.6 reduce-scatter.11
  661.7 63.2 reduce-scatter.13

commit v2 on v1

--- a/solution.py
+++ b/solution.py
@@ -31,14 +31,30 @@
 
 
 def gather_blocks(own):
-    return [own] + [hop(own, j) for j in range(1, lax.axis_size("tensor"))]
-
-
-def scatter_sum(blocks):
-    total = blocks[0].astype(f32)
-    for j in range(1, len(blocks)):
-        total = total + hop(blocks[j].astype(bf16), j).astype(f32)
-    return total
+    size = lax.axis_size("tensor")
+    if size != 4:
+        return [own] + [hop(own, j) for j in range(1, size)]
+    half = own.shape[0] // 2
+    near, far = hop(own, 1), hop(own, 2)
+    upper, lower = hop(far[:half], 1), hop(near[half:], 2)
+    return [own, near, far, upper, lower]
+
+
+def scatter_sum(own, rest):
+    size, rows = lax.axis_size("tensor"), own.shape[0]
+    if size != 4:
+        for j in range(1, size):
+            own = own + hop(rows_of(rest, j - 1, rows), j).astype(f32)
+        return own
+    half = rows // 2
+    one, two, three = (rows_of(rest, j, rows) for j in range(3))
+    upper = hop(jnp.concatenate([one[:half], three[:half]], axis=0), 1).astype(f32)
+    lower = hop(jnp.concatenate([two[half:], three[half:]], axis=0), 2).astype(f32)
+    upper_far = hop((two[:half].astype(f32) + upper[half:]).astype(bf16), 2).astype(f32)
+    lower_near = hop((one[half:].astype(f32) + lower[half:]).astype(bf16), 1).astype(f32)
+    return jnp.concatenate(
+        [own[:half] + upper[:half] + upper_far, own[half:] + lower[:half] + lower_near], axis=0
+    )
 
 
 def gather_dp(shard):
@@ -95,7 +111,18 @@
 
 
 def attend_back_kernel(
-    where_ref, qr_ref, kvt_ref, dm_ref, lse_ref, cos_ref, sin_ref, dq_ref, dkv_ref, dk_acc, dv_acc
+    where_ref,
+    qr_ref,
+    kvt_ref,
+    dm_ref,
+    lse_ref,
+    cos_ref,
+    sin_ref,
+    shared_ref,
+    dq_ref,
+    dkv_ref,
+    dk_acc,
+    dv_acc,
 ):
     rows, width = qr_ref.shape
     heads = width // HD
@@ -109,7 +136,8 @@
         dk_acc[...] = jnp.zeros_like(dk_acc)
         dv_acc[...] = jnp.zeros_like(dv_acc)
 
-    cos2, sin2 = cos_ref[...], sin_ref[...]
+    mine = pl.ds(pl.multiple_of(j * rows, rows), rows)
+    cos2, sin2 = cos_ref[mine, :], sin_ref[mine, :]
     limit = jnp.minimum(block * rows + lax.broadcasted_iota(jnp.int32, (rows, 1), 0), length - 1)
     for w in range(ranks):
 
@@ -136,8 +164,11 @@
         for i in range(ranks):
             here = slice(i * rows, (i + 1) * rows)
             there = pl.ds(pl.multiple_of(jnp.bitwise_xor(rank, i) * rows, rows), rows)
-            dkv_ref[here, :HD] = dk_acc[there, :] * inv_root
-            dkv_ref[here, HD:] = dv_acc[there, :]
+            dk, dv = dk_acc[there, :] * inv_root, dv_acc[there, :]
+            if i == 0:
+                dk, dv = dk + shared_ref[:, :HD], dv + shared_ref[:, HD:]
+            dkv_ref[here, :HD] = turn(dk, cos_ref[here, :], -sin_ref[here, :]).astype(bf16)
+            dkv_ref[here, HD:] = dv.astype(bf16)
 
 
 VMEM_LIMIT = 48 * 2**20
@@ -181,7 +212,7 @@
     )(where, qkv, qkv, cos2, sin2)
 
 
-def attend_back(where, qr, kvt, dmixed, lse, cos2, sin2, rows):
+def attend_back(where, qr, kvt, dmixed, lse, cos2, sin2, shared, rows):
     slot, width = qr.shape
     heads = width // HD
     half = slot * slot * heads * HD
@@ -196,8 +227,9 @@
                 pl.BlockSpec((slot, 2 * HD), lambda j, s: (0, 0)),
                 pl.BlockSpec((rows, width), lambda j, s: (j, 0)),
                 pl.BlockSpec((rows, HD), lambda j, s: (j, 0)),
-                pl.BlockSpec((rows, HD), lambda j, s: (j, 0)),
-                pl.BlockSpec((rows, HD), lambda j, s: (j, 0)),
+                pl.BlockSpec((slot, HD), lambda j, s: (0, 0)),
+                pl.BlockSpec((slot, HD), lambda j, s: (0, 0)),
+                pl.BlockSpec((rows, 2 * HD), lambda j, s: (0, 0)),
             ],
             out_specs=[
                 pl.BlockSpec((rows, width), lambda j, s: (j, 0)),
@@ -207,7 +239,7 @@
         ),
         out_shape=(
             jax.ShapeDtypeStruct((slot, width), bf16),
-            jax.ShapeDtypeStruct((slot, 2 * HD), f32),
+            jax.ShapeDtypeStruct((slot, 2 * HD), bf16),
         ),
         compiler_params=pltpu.CompilerParams(
             dimension_semantics=("arbitrary",), vmem_limit_bytes=VMEM_LIMIT
@@ -215,14 +247,7 @@
         cost_estimate=pl.CostEstimate(
             flops=10 * half, bytes_accessed=8 * 2**20, transcendentals=slot * slot * heads
         ),
-    )(where, qr, kvt, dmixed, lse, cos2, sin2)
-
-
-def unrotate(values, cosine, sine_vals):
-    first, second = values[:, : HD // 2], values[:, HD // 2 :]
-    return jnp.concatenate(
-        [first * cosine + second * sine_vals, second * cosine - first * sine_vals], axis=1
-    )
+    )(where, qr, kvt, dmixed, lse, cos2, sin2, shared)
 
 
 def inverse_norm(values):
@@ -263,44 +288,46 @@
     cosine, sine = jnp.cos(angles), jnp.sin(angles)
     cos2 = jnp.concatenate([cosine, cosine], axis=1)
     sin2 = jnp.concatenate([-sine, sine], axis=1)
-    cos_own, sin_own = cosine[:rows], sine[:rows]
     own_mask = (position[:rows] < length).astype(f32)[:, None]
     where = jnp.stack([rank, length])
 
-    attn_shard = jnp.concatenate([w_query, w_keyvalue, w_project.T], axis=1)
-    gains = lax.all_gather(jnp.stack([gain_attn, gain_mlp]), "dp", axis=1, tiled=True).astype(f32)
-    gain_one, gain_two = gains[0:1], gains[1:2]
-    attn_full = gather_dp(attn_shard)
-    down_full = gather_dp(after(w_down.T, attn_full))
-    pairs, last = [], down_full
-    for a, b in parts:
-        shard = jnp.concatenate([w_gate[:, a:b], w_up[:, a:b]], axis=1)
-        last = gather_dp(after(shard, last))
-        pairs.append(last)
-    qkv_full = attn_full[:, : heads_width + 2 * HD]
-    query_full = attn_full[:, :heads_width]
-    keyvalue_full = attn_full[:, heads_width : heads_width + 2 * HD]
-    project_full = attn_full[:, heads_width + 2 * HD :]
+    gain_one, gain_two = gain_attn.astype(f32)[:, None], gain_mlp.astype(f32)[:, None]
+    qkv_own = jnp.concatenate([w_query, w_keyvalue], axis=1).astype(f32)
+    qkv_width = qkv_own.shape[1]
+    attn_shard = jnp.concatenate([(qkv_own * gain_one).astype(bf16), w_project.T], axis=1)
+    pair_own = [
+        jnp.concatenate([w_gate[:, a:b], w_up[:, a:b]], axis=1).astype(f32) for a, b in parts
+    ]
+    pair_shards = [(own * gain_two).astype(bf16) for own in pair_own]
 
     residual = layer_input.astype(f32)
     inputs = gather_blocks(layer_input)
-
-    def norm_one(block):
+    attn_full = gather_dp(attn_shard)
+    down_full = gather_dp(after(w_down.T, *inputs))
+    qkv_full, project_full = attn_full[:, :qkv_width], attn_full[:, qkv_width:]
+    top = out_grad.astype(f32) * own_mask
+    top_blocks = gather_blocks(after(top.astype(bf16), *inputs))
+    pairs = [gather_dp(after(pair_shards[0], *top_blocks))]
+
+    def norm(block):
         block = block.astype(f32)
-        return (block * inverse_norm(block) * gain_one).astype(bf16)
-
-    normed_one = jnp.concatenate([norm_one(b) for b in inputs], axis=0)
-    top = out_grad.astype(f32) * own_mask
-    top_all = jnp.concatenate(gather_blocks(after(top.astype(bf16), *inputs)), axis=0)
+        return (block * inverse_norm(block)).astype(bf16)
+
+    normed_one = jnp.concatenate([norm(b) for b in inputs], axis=0)
     qkv = dot(normed_one, qkv_full, 1, 0)
     qr, kvt, mixed, lse = attend(where, qkv, cos2, sin2, rows)
+    top_all = jnp.concatenate(top_blocks, axis=0)
+    mixed_sent = after(mixed, top_all)
     after_attn = residual + scatter_sum(
-        [dot(rows_of(mixed, j, rows), project_full, 1, 1) for j in range(ranks)]
+        dot(mixed[:rows], project_full, 1, 1),
+        dot(mixed_sent[rows:], project_full, 1, 1).astype(bf16),
     )
 
     inv_two = inverse_norm(after_attn)
-    normed_two_own = (after_attn * inv_two * gain_two).astype(bf16)
-    normed_two = jnp.concatenate(gather_blocks(normed_two_own), axis=0)
+    unit_two = after_attn * inv_two
+    normed_blocks = gather_blocks(unit_two.astype(bf16))
+    pairs.append(gather_dp(after(pair_shards[1], *normed_blocks)))
+    normed_two = jnp.concatenate(normed_blocks, axis=0)
     hidden_grad = dot(top_all, down_full, 1, 0)
     hiddens, pair_grads, pair_sums = [], [], []
     for (a, b), pair in zip(parts, pairs):
@@ -314,83 +341,72 @@
         pair_grads.append(jnp.concatenate([gate_grad, up_grad], axis=1))
         pair_sums.append(scatter_dp(dot(normed_two, pair_grads[-1], 0, 0).astype(bf16)))
     hidden = jnp.concatenate(hiddens, axis=1)
-    down_sum = scatter_dp(dot(top_all, hidden, 0, 0).astype(bf16))
-
-    normed_two_grad = scatter_sum(
-        [
-            sum(dot(rows_of(g, j, rows), w, 1, 1) for g, w in zip(pair_grads, pairs))
-            for j in range(ranks)
-        ]
-    )
-    unit_two = after_attn * inv_two
-    scaled = normed_two_grad * gain_two
+
+    scaled = scatter_sum(
+        sum(dot(g[:rows], w, 1, 1) for g, w in zip(pair_grads, pairs)),
+        sum(dot(g[rows:], w, 1, 1) for g, w in zip(pair_grads, pairs)).astype(bf16),
+    )
     attn_top = top + inv_two * (
         scaled - unit_two * jnp.mean(scaled * unit_two, axis=-1, keepdims=True)
     )
-    attn_top_all = jnp.concatenate(gather_blocks(attn_top.astype(bf16)), axis=0)
+    attn_top_blocks = gather_blocks(attn_top.astype(bf16))
+    attn_top_all = jnp.concatenate(attn_top_blocks, axis=0)
+    down_sum = scatter_dp(dot(top_all, hidden, 0, 0).astype(bf16))
+    down_rest = dot(hidden[rows:], down_full, 1, 1).astype(bf16)
     after_mlp = after_attn + scatter_sum(
-        [dot(rows_of(hidden, j, rows), down_full, 1, 1) for j in range(ranks)]
+        dot(hidden[:rows], down_full, 1, 1), after(down_rest, *attn_top_blocks)
     )
     output = (after_mlp * own_mask).astype(bf16)
 
     mixed_grad = dot(attn_top_all, project_full, 1, 0).astype(bf16)
-    project_sum = scatter_dp(dot(attn_top_all, mixed, 0, 0).astype(bf16))
-    query_grad, kv_part = attend_back(where, qr, kvt, mixed_grad, lse, cos2, sin2, rows)
-    shared = kv_part[:rows]
-    for j in range(1, ranks):
-        shared = shared + hop(rows_of(kv_part, j, rows), j)
-    shared = shared + kv_grad.astype(f32) * own_mask
-    kv_back = jnp.concatenate([unrotate(shared[:, :HD], cos_own, sin_own), shared[:, HD:]], axis=1)
-    kv_back = kv_back.astype(bf16)
-    normed_own = normed_one[:rows]
-    qkv_grad = jnp.concatenate(
+    shared = kv_grad.astype(f32) * own_mask
+    query_grad, kv_back = attend_back(where, qr, kvt, mixed_grad, lse, cos2, sin2, shared, rows)
+    qkv_back = jnp.concatenate([query_grad, kv_back], axis=1)
+    attn_grad = jnp.concatenate(
         [
-            dot(normed_one, query_grad, 0, 0).astype(bf16),
-            dot(normed_own, kv_back, 0, 0).astype(bf16),
+            dot(normed_one, qkv_back, 0, 0).astype(bf16),
+            dot(attn_top_all, mixed, 0, 0).astype(bf16),
         ],
         axis=1,
     )
-    qkv_sum = scatter_dp(qkv_grad)
-    normed_one_grad = scatter_sum(
-        [dot(rows_of(query_grad, j, rows), query_full, 1, 1) for j in range(ranks)]
-    ) + dot(kv_back, keyvalue_full, 1, 1)
+    attn_sum = scatter_dp(attn_grad)
+    qkv_sum, project_sum = attn_sum[:, :qkv_width], attn_sum[:, qkv_width:]
+    scaled_one = scatter_sum(
+        dot(qkv_back[:rows], qkv_full, 1, 1), dot(qkv_back[rows:], qkv_full, 1, 1).astype(bf16)
+    )
     inv_one = inverse_norm(residual)
     unit_one = residual * inv_one
-    scaled_one = normed_one_grad * gain_one
     input_grad = attn_top + inv_one * (
         scaled_one - unit_one * jnp.mean(scaled_one * unit_one, axis=-1, keepdims=True)
     )
 
-    grad_query, grad_kv_part = qkv_sum[:, :heads_width], qkv_sum[:, heads_width:]
-    grad_gate = jnp.concatenate([s[:, : b - a] for (a, b), s in zip(parts, pair_sums)], axis=1)
-    grad_up = jnp.concatenate([s[:, b - a :] for (a, b), s in zip(parts, pair_sums)], axis=1)
-    gain_one_part = jnp.sum(grad_query * w_query.astype(f32), axis=1) + jnp.sum(
-        grad_kv_part * w_keyvalue.astype(f32), axis=1
-    )
-    gain_two_part = jnp.sum(
-        grad_gate * w_gate.astype(f32) + grad_up * w_up.astype(f32), axis=1
-    )
+    gain_two_part = sum(
+        jnp.sum(own * total, axis=1, keepdims=True) for own, total in zip(pair_own, pair_sums)
+    )
+    scaled_sums = [total * gain_two for total in pair_sums]
+    grad_gate = jnp.concatenate([s[:, : b - a] for (a, b), s in zip(parts, scaled_sums)], axis=1)
+    grad_up = jnp.concatenate([s[:, b - a :] for (a, b), s in zip(parts, scaled_sums)], axis=1)
+    gain_one_part = jnp.sum(
+        qkv_own[:, :heads_width] * qkv_sum[:, :heads_width], axis=1, keepdims=True
+    ) + jnp.sum(qkv_own[:, heads_width:] * qkv_sum[:, heads_width:], axis=1, keepdims=True)
     small = jnp.concatenate(
-        [grad_kv_part, gain_one_part[:, None], gain_two_part[:, None]], axis=1
+        [qkv_sum[:, heads_width:] * gain_one, gain_one_part, gain_two_part], axis=1
     )
     step = 1
     while step < ranks:
         small = small + hop(small, step)
         step *= 2
-    grad_keyvalue = small[:, : 2 * HD]
-    grad_gain_one = small[:, 2 * HD] / gain_attn.astype(f32)
-    grad_gain_two = small[:, 2 * HD + 1] / gain_mlp.astype(f32)
     return (
         output,
         input_grad,
-        grad_query,
-        grad_keyvalue,
+        qkv_sum[:, :heads_width] * gain_one,
+        small[:, : 2 * HD],
         project_sum.T,
         grad_gate,
         grad_up,
         down_sum.T,
-        grad_gain_one,
-        grad_gain_two,
+        small[:, 2 * HD],
+        small[:, 2 * HD + 1],
     )
 
 

time: 742 us -> 560 us (0.75)
  waiting for transfers between devices: 450 us -> 240 us
  local copies, waits for them, and re-layouts: 27.1 us -> 43.7 us
  starting transfers between devices: 34.8 us -> 49.6 us
  other arithmetic: 37.5 us -> 49.9 us
  blocking collectives: 9.56 us -> 0 us
    all_gather x4, waiting for transfers between devices: 119 us -> 0.04 us  [gather_dp(): return lax.all_gather(shard, 'dp', axis=0, tiled=True)]
    ppermute x29 -> x34, waiting for transfers between devices: 281 us -> 232 us  [hop(): return lax.ppermute(value, 'tensor', [(i, i ^ step) for i in range(size)])]
    reduce_scatter x5 -> x4, waiting for transfers between devices: 49.6 us -> 7.41 us  [scatter_dp(): lax.psum_scatter(partial, 'dp', scatter_dimension=0, tiled=True).astype(f32)]
    reduce_scatter x5 -> x4, starting transfers between devices: 0.38 us -> 12.6 us  [scatter_dp(): lax.psum_scatter(partial, 'dp', scatter_dimension=0, tiled=True).astype(f32)]
    all_gather x1 -> x0, blocking collectives: 9.56 us -> none  [on_device(): lax.all_gather(jnp.stack([gain_attn, gain_mlp]), 'dp', axis=1, tiled=True)]
    unnamed x7 -> x9, other arithmetic: 0.01 us -> 9.02 us
    unnamed x172 -> x147, local copies, waits for them, and re-layouts: 20.8 us -> 29.8 us
    slice x15 -> x18, local copies, waits for them, and re-layouts: 1.08 us -> 9.79 us  [the longest x8 4.07 us: gather_blocks(): upper, lower = (hop(far[:half], 1), hop(near[half:], 2))]
  transfers between devices with their start and end apart: 38 -> 42, of which waited for: 21 -> 27; matrix products, arithmetic and copies ran while one was open for 25% -> 37% of each run, Pallas kernels for 4% -> 5%
where the time goes in v2:
time: 560 us; the launch traced here: 551 us
  waiting for transfers between devices  240 us (43%)
  matrix products  127 us (23%)
  other arithmetic  49.9 us (9%)
  starting transfers between devices  49.6 us (9%)
  local copies, waits for them, and re-layouts  43.7 us (8%)
  Pallas kernels  25.4 us (5%)
  between operations  16.5 us (3%)
    ppermute x34, waiting for transfers between devices, hop(): return lax.ppermute(value, 'tensor', [(i, i ^ step) for i in range(size)])  232 us
    dot_general x20, matrix products, dot(): lax.dot_general(a, b, (((ca,), (cb,)), ((), ())), preferred_element_type=...  127 us
    ppermute x34, starting transfers between devices, hop(): return lax.ppermute(value, 'tensor', [(i, i ^ step) for i in range(size)])  36.8 us
    unnamed x147, local copies, waits for them, and re-layouts  29.8 us
    pallas_call x1, Pallas kernels, attend_back(): pl.pallas_call(attend_back_kernel, name='attend_back', grid_spec=pltpu.Pr...  13.8 us
    reduce_scatter x4, starting transfers between devices, scatter_dp(): lax.psum_scatter(partial, 'dp', scatter_dimension=0, tiled=True).astype(f32)  12.6 us
    pallas_call x1, Pallas kernels, attend(): pl.pallas_call(attend_kernel, name='attend', grid_spec=pltpu.PrefetchScal...  11.7 us
  transfers between devices with their start and end apart: 42, of which 27 were waited for; matrix products, arithmetic and copies ran while one was open for 37% of the time, Pallas kernels for 5%

profile of v2, /device:TPU:0, one launch (start us, length us, event | category | flops | bytes accessed | tf_op | source)
XLA Modules:
  0.0 551.4 jit_solution(16784391226585559243)
XLA Ops:
  10.3 1.8 pad_maximum_fusion.14
  12.2 3.1 collective-permute-start.1
  16.8 21.7 %collective-permute-done.1 = bf16[256,2048]{1,0:T(8,128)(2,1)S(1)} collective-permute-done((bf16[256,2048]{1,0:T(8,128)(2,1)S(1)}, bf16[256,2048]{1,0:T(8,128)(2,1)S(1)}, u32[]{:S(2)}, u32[]{:S(2)}) %collective-permute-start.1) | collective-permute-done | bytes 1048608 | tf_op jit(solution)/shard_map/ppermute | solution.py:26
  38.5 1.8 collective-permute-start.2
  42.9 9.0 %collective-permute-done.2 = bf16[128,2048]{1,0:T(8,128)(2,1)} collective-permute-done((bf16[128,2048]{1,0:T(8,128)(2,1)S(1)}, bf16[128,2048]{1,0:T(8,128)(2,1)}, u32[]{:S(2)}, u32[]{:S(2)}) %collective-permute-start.2) | collective-permute-done | bytes 524320 | tf_op jit(solution)/shard_map/ppermute | solution.py:26
  51.9 2.1 collective-permute-done.3
  57.2 1.9 fusion.93
  65.9 20.6 %collective-permute-done.5 = bf16[256,2048]{1,0:T(8,128)(2,1)} collective-permute-done((bf16[256,2048]{1,0:T(8,128)(2,1)}, bf16[256,2048]{1,0:T(8,128)(2,1)}, u32[]{:S(2)}, u32[]{:S(2)}) %collective-permute-start.5) | collective-permute-done | bytes 1048608 | tf_op jit(solution)/shard_map/ppermute | solution.py:26
  92.5 6.0 %collective-permute-done.6 = bf16[128,2048]{1,0:T(8,128)(2,1)} collective-permute-done((bf16[128,2048]{1,0:T(8,128)(2,1)S(1)}, bf16[128,2048]{1,0:T(8,128)(2,1)}, u32[]{:S(2)}, u32[]{:S(2)}) %collective-permute-start.6) | collective-permute-done | bytes 524320 | tf_op jit(solution)/shard_map/ppermute | solution.py:26
  98.5 1.8 collective-permute-done.7
  103.0 2.3 constant_dynamic-update-slice_fusion.4
  105.4 2.0 fusion.88
  108.3 2.3 constant_dynamic-update-slice_fusion.3
  110.6 2.3 constant_dynamic-update-slice_fusion.2
  113.0 1.9 constant_dynamic-update-slice_fusion.1
  114.8 1.9 constant_dynamic-update-slice_fusion
  116.8 8.3 %fusion.15.q_ref.kv_ref = f32[1024,768]{1,0:T(8,128)} fusion(bf16[1024,2048]{1,0:T(8,128)(2,1)} %fusion.87, bf16[2048,1280]{0,1:T(8,128)(2,1)} %all-gather.5.cloned.1.call-done), kind=kOutput, calls=%fused_computation.41 | convolution fusion | flops 3221225472 | bytes 10485760 | tf_op jit(solution)/shard_map/dot_general | solution.py:21
  125.1 11.7 %attend.1 = (bf16[1024,512]{1,0:T(8,128)(2,1)S(1)}, bf16[1024,256]{1,0:T(8,128)(2,1)S(1)}, bf16[1024,512]{1,0:T(8,128)(2,1)S(1)}, f32[1024,128]{1,0:T(8,128)S(1)}) custom-call(s32[2]{0:T(128)S(1)} %pad_add_fusion.where_ref, f32[1024,768]{1,0:T(8,128)} %fusion.15.q_ref.kv_ref, f32[1024,768]{1,0:T(8,128)} %fusion.15.q_ref.kv_ref, ...), custom_call_target="tpu_custom_call" | custom-call | flops 2147483648 | bytes 8388608 | tf_op jit(solution)/shard_map/attend/pallas_call | solution.py:181
  136.8 3.8 convolution_convert_fusion.3
  143.3 19.1 %collective-permute-done.10 = bf16[256,2048]{1,0:T(8,128)(2,1)S(1)} collective-permute-done((bf16[256,2048]{1,0:T(8,128)(2,1)S(1)}, bf16[256,2048]{1,0:T(8,128)(2,1)S(1)}, u32[]{:S(2)}, u32[]{:S(2)}) %collective-permute-start.10) | collective-permute-done | bytes 1048608 | tf_op jit(solution)/shard_map/ppermute | solution.py:26
  162.6 2.7 collective-permute-done.8
  167.6 2.4 fusion.42
  170.0 5.9 %collective-permute-done.11 = bf16[128,2048]{1,0:T(8,128)(2,1)S(1)} collective-permute-done((bf16[128,2048]{1,0:T(8,128)(2,1)S(1)}, bf16[128,2048]{1,0:T(8,128)(2,1)S(1)}, u32[]{:S(2)}, u32[]{:S(2)}) %collective-permute-start.11) | collective-permute-done | bytes 524320 | tf_op jit(solution)/shard_map/ppermute | solution.py:26
  179.3 1.8 collective-permute-start.13
  182.2 18.1 %collective-permute-done.13 = bf16[256,2048]{1,0:T(8,128)(2,1)S(1)} collective-permute-done((bf16[256,2048]{1,0:T(8,128)(2,1)S(1)}, bf16[256,2048]{1,0:T(8,128)(2,1)S(1)}, u32[]{:S(2)}, u32[]{:S(2)}) %collective-permute-start.13) | collective-permute-done | bytes 1048608 | tf_op jit(solution)/shard_map/ppermute | solution.py:26
  208.0 2.7 collective-permute-done.14
  210.6 2.6 collective-permute-done.15
  213.3 12.1 %reduce-scatter.7.cloned.1.call-start = ((), (), s32[]{:S(2)}) async-start(), calls=%async_computation.9 | async-start | bytes 7077888 | tf_op jit(solution)/shard_map/reduce_scatter | solution.py:65
  225.4 11.9 %fusion.113 = f32[1024,1408]{1,0:T(8,128)} fusion(bf16[1024,2048]{1,0:T(8,128)(2,1)} %constant_dynamic-update-slice_fusion, bf16[2048,1408]{0,1:T(8,128)(2,1)} %all-gather.11.cloned.1.call-done), kind=kOutput, calls=%fused_computation.229 | convolution fusion | flops 5905580032 | bytes 15728640 | tf_op jit(solution)/shard_map/dot_general | solution.py:21
  240.0 1.9 constant_dynamic-update-slice_fusion.6
  241.9 1.9 constant_dynamic-update-slice_fusion.5
  243.8 10.1 %fusion.111 = f32[1024,1536]{1,0:T(8,128)S(1)} fusion(bf16[1024,2048]{1,0:T(8,128)(2,1)} %constant_dynamic-update-slice_fusion.5, bf16[2048,1536]{1,0:T(8,128)(2,1)} %all-gather.7.cloned.1.call-done), kind=kOutput, calls=%fused_computation.227 | convolution fusion | flops 6442450944 | bytes 16777216 | tf_op jit(solution)/shard_map/dot_general | solution.py:21
  253.9 4.3 multiply_convert_fusion.1
  259.9 11.3 %convolution_convert_fusion.2 = bf16[2048,1536]{1,0:T(8,128)(2,1)} fusion(bf16[1024,2048]{1,0:T(8,128)(2,1)} %constant_dynamic-update-slice_fusion.5, bf16[1024,768]{1,0:T(8,128)(2,1)S(1)} %get-tuple-element.50, bf16[1024,768]{1,0:T(8,128)(2,1)S(1)} %get-tuple-element.49), kind=kOutput, calls=%fused_computation.2 | convolution fusion | flops 6451888128 | bytes 13631488 | tf_op jit(solution)/shard_map/dot_general | solution.py:21
  271.3 8.9 %fusion.112 = f32[1024,1280]{1,0:T(8,128)S(1)} fusion(bf16[1024,2048]{1,0:T(8,128)(2,1)} %constant_dynamic-update-slice_fusion.5, bf16[2048,1280]{1,0:T(8,128)(2,1)} %all-gather.9.cloned.1.call-done), kind=kOutput, calls=%fused_computation.228 | convolution fusion | flops 5368709120 | bytes 14680064 | tf_op jit(solution)/shard_map/dot_general | solution.py:21
  280.2 3.8 multiply_convert_fusion.4
  285.4 10.9 %convolution_convert_fusion.1 = bf16[2048,1280]{1,0:T(8,128)(2,1)} fusion(bf16[1024,2048]{1,0:T(8,128)(2,1)} %constant_dynamic-update-slice_fusion.5, bf16[1024,640]{1,0:T(8,128)(2,1)S(1)} %get-tuple-element.52, bf16[1024,640]{1,0:T(8,128)(2,1)S(1)} %get-tuple-element.51), kind=kOutput, calls=%fused_computation.1 | convolution fusion | flops 5376573440 | bytes 12058624 | tf_op jit(solution)/shard_map/dot_general | solution.py:21
  296.9 7.0 %fusion.35 = f32[768,2048]{1,0:T(8,128)S(1)} fusion(bf16[2048,1280]{1,0:T(8,128)(2,1)} %all-gather.9.cloned.1.call-done, bf16[1024,640]{1,0:T(8,128)(2,1)} %copy-done.23, bf16[1024,640]{1,0:T(8,128)(2,1)} %copy-done.21), kind=kOutput, calls=%fused_computation.68 | convolution fusion | flops 4030464000 | bytes 14155776 | tf_op jit(solution)/shard_map/dot_general | solution.py:21
  303.9 8.3 %add_convert_fusion = bf16[768,2048]{1,0:T(8,128)(2,1)S(1)} fusion(f32[768,2048]{1,0:T(8,128)S(1)} %fusion.35, bf16[2048,1536]{1,0:T(8,128)(2,1)} %all-gather.7.cloned.1.call-done, bf16[1024,768]{1,0:T(8,128)(2,1)S(1)} %copy-done.20, bf16[1024,768]{1,0:T(8,128)(2,1)S(1)} %copy-done.18), kind=kOutput, calls=%fused_computation.3 | convolution fusion | flops 4839702528 | bytes 18874368 | tf_op jit(solution)/shard_map/dot_general | solution.py:21
  312.9 2.0 collective-permute-start.16
  316.5 19.4 %collective-permute-done.18 = bf16[256,2048]{1,0:T(8,128)(2,1)S(1)} collective-permute-done((bf16[256,2048]{1,0:T(8,128)(2,1)S(1)}, bf16[256,2048]{1,0:T(8,128)(2,1)S(1)}, u32[]{:S(2)}, u32[]{:S(2)}) %collective-permute-start.18) | collective-permute-done | bytes 1048608 | tf_op jit(solution)/shard_map/ppermute | solution.py:26
  340.0 1.8 convolution_add_fusion
  341.8 8.4 %collective-permute-done.17 = bf16[128,2048]{1,0:T(8,128)(2,1)S(1)} collective-permute-done((bf16[128,2048]{1,0:T(8,128)(2,1)S(1)}, bf16[128,2048]{1,0:T(8,128)(2,1)S(1)}, u32[]{:S(2)}, u32[]{:S(2)}) %collective-permute-start.17) | collective-permute-done | bytes 524320 | tf_op jit(solution)/shard_map/ppermute | solution.py:26
  352.4 2.1 constant_dynamic-update-slice_fusion.14
  356.8 20.2 %collective-permute-done.21 = bf16[256,2048]{1,0:T(8,128)(2,1)S(1)} collective-permute-done((bf16[256,2048]{1,0:T(8,128)(2,1)S(1)}, bf16[256,2048]{1,0:T(8,128)(2,1)S(1)}, u32[]{:S(2)}, u32[]{:S(2)}) %collective-permute-start.21) | collective-permute-done | bytes 1048608 | tf_op jit(solution)/shard_map/ppermute | solution.py:26
  380.2 9.1 %collective-permute-done.22 = bf16[128,2048]{1,0:T(8,128)(2,1)S(1)} collective-permute-done((bf16[128,2048]{1,0:T(8,128)(2,1)S(1)}, bf16[128,2048]{1,0:T(8,128)(2,1)S(1)}, u32[]{:S(2)}, u32[]{:S(2)}) %collective-permute-start.22) | collective-permute-done | bytes 524320 | tf_op jit(solution)/shard_map/ppermute | solution.py:26
  389.4 4.0 fusion.46.dm_ref
  393.4 13.8 %attend_back.1 = (bf16[1024,512]{1,0:T(8,128)(2,1)S(1)}, bf16[1024,256]{1,0:T(8,128)(2,1)S(1)}) custom-call(s32[2]{0:T(128)S(1)} %pad_add_fusion.where_ref, bf16[1024,512]{1,0:T(8,128)(2,1)S(1)} %get-tuple-element.29.qr_ref, bf16[1024,256]{1,0:T(8,128)(2,1)S(1)} %copy-done.1, bf16[1024,512]{1,0:T(8,128)(2,1)S(1)} %fusion.46.dm_ref, ...), custom_call_target="tpu_custom_call" | custom-call | flops 5368709120 | bytes 8388608 | tf_op jit(solution)/shard_map/attend_back/pallas_call | solution.py:219
  407.3 2.5 convolution_convert_fusion.7
  410.1 3.7 convolution_convert_fusion.4
  413.8 2.8 pad_maximum_fusion
  418.0 11.0 %convolution_convert_fusion = bf16[2048,1408]{1,0:T(8,128)(2,1)} fusion(bf16[1024,2048]{1,0:T(8,128)(2,1)} %constant_dynamic-update-slice_fusion, bf16[1024,640]{1,0:T(8,128)(2,1)} %get-tuple-element.54, bf16[1024,768]{1,0:T(8,128)(2,1)S(1)} %copy-done.43), kind=kOutput, calls=%fused_computation | convolution fusion | flops 5914230784 | bytes 12845056 | tf_op jit(solution)/shard_map/dot_general | solution.py:21
  430.0 8.3 %convolution_convert_fusion.6 = bf16[768,2048]{1,0:T(8,128)(2,1)S(1)} fusion(bf16[2048,1408]{0,1:T(8,128)(2,1)} %all-gather.11.cloned.1.call-done, bf16[1024,640]{1,0:T(8,128)(2,1)} %get-tuple-element.54, bf16[1024,768]{1,0:T(8,128)(2,1)} %get-tuple-element.53), kind=kOutput, calls=%fused_computation.8 | convolution fusion | flops 4435083264 | bytes 11796480 | tf_op jit(solution)/shard_map/dot_general | solution.py:21
  440.0 5.1 convolution_convert_fusion.5
  446.7 1.8 collective-permute-start.24
  448.5 4.6 fusion.79
  454.2 29.5 %collective-permute-done.30 = bf16[256,2048]{1,0:T(8,128)(2,1)S(1)} collective-permute-done((bf16[256,2048]{1,0:T(8,128)(2,1)S(1)}, bf16[256,2048]{1,0:T(8,128)(2,1)S(1)}, u32[]{:S(2)}, u32[]{:S(2)}) %collective-permute-start.30) | collective-permute-done | bytes 1048608 | tf_op jit(solution)/shard_map/ppermute | solution.py:26
  485.5 9.3 %collective-permute-done.24 = bf16[256,2048]{1,0:T(8,128)(2,1)S(1)} collective-permute-done((bf16[256,2048]{1,0:T(8,128)(2,1)S(1)}, bf16[256,2048]{1,0:T(8,128)(2,1)S(1)}, u32[]{:S(2)}, u32[]{:S(2)}) %collective-permute-start.24) | collective-permute-done | bytes 1048608 | tf_op jit(solution)/shard_map/ppermute | solution.py:26
  496.9 2.4 collective-permute-done.29
  499.3 6.7 %collective-permute-done.31 = bf16[128,2048]{1,0:T(8,128)(2,1)S(1)} collective-permute-done((bf16[128,2048]{1,0:T(8,128)(2,1)S(1)}, bf16[128,2048]{1,0:T(8,128)(2,1)S(1)}, u32[]{:S(2)}, u32[]{:S(2)}) %collective-permute-start.31) | collective-permute-done | bytes 524320 | tf_op jit(solution)/shard_map/ppermute | solution.py:26
  507.0 5.9 %collective-permute-done.27 = bf16[128,2048]{1,0:T(8,128)(2,1)S(1)} collective-permute-done((bf16[128,2048]{1,0:T(8,128)(2,1)S(1)}, bf16[128,2048]{1,0:T(8,128)(2,1)S(1)}, u32[]{:S(2)}, u32[]{:S(2)}) %collective-permute-start.27) | collective-permute-done | bytes 524320 | tf_op jit(solution)/shard_map/ppermute | solution.py:26
  513.4 2.3 fusion.30
  525.3 4.6 collective-permute-done.32
  531.5 7.4 %reduce-scatter.11.cloned.1.call-done = bf16[256,1408]{1,0:T(8,128)(2,1)} async-done(((bf16[2048,1408]{1,0:T(8,128)(2,1)}), bf16[256,1408]{1,0:T(8,128)(2,1)}) %reduce-scatter.11.cloned.1.call-update) | async-done | bytes 720912 | tf_op jit(solution)/shard_map/reduce_scatter | solution.py:65
  (304 shorter events, 92.2 us)
Async XLA Ops:
  7.2 109.6 %all-gather.5.cloned.1.call-start = ((), (), s32[]{:S(2)}) async-start(), calls=%async_computation.4 | async-start | bytes 5898240 | tf_op jit(solution)/shard_map/all_gather | solution.py:61
  10.3 44.6 %copy-start.58 = (bf16[256]{0:T(256)(128)(2,1)S(1)}, bf16[256]{0:T(256)(128)(2,1)}, u32[]{:S(2)}) copy-start(bf16[256]{0:T(256)(128)(2,1)} %param.21) | copy-start | bytes 1540
  12.2 213.2 %all-gather.11.cloned.1.call-start = ((), (), s32[]{:S(2)}) async-start(), calls=%async_computation.7 | async-start | bytes 6488064 | tf_op jit(solution)/shard_map/all_gather | solution.py:61
  12.2 26.2 %collective-permute-start.1 = (bf16[256,2048]{1,0:T(8,128)(2,1)S(1)}, bf16[256,2048]{1,0:T(8,128)(2,1)S(1)}, u32[]{:S(2)}, u32[]{:S(2)}) collective-permute-start(bf16[256,2048]{1,0:T(8,128)(2,1)S(1)} %copy-done.4), channel_id=1, source_target_pairs={{0,2},{1,3},{2,0},{3,1},{4,6},{5,7},{6,4},{7,5},{8,10},{9,11},{10,... | collective-permute-start | bytes 3145736 | tf_op jit(solution)/shard_map/ppermute | solution.py:26
  15.3 25.0 %collective-permute-start = (bf16[256,2048]{1,0:T(8,128)(2,1)S(1)}, bf16[256,2048]{1,0:T(8,128)(2,1)S(1)}, u32[]{:S(2)}, u32[]{:S(2)}) collective-permute-start(bf16[256,2048]{1,0:T(8,128)(2,1)S(1)} %copy-done.4), channel_id=1, source_target_pairs={{0,1},{1,0},{2,3},{3,2},{4,5},{5,4},{6,7},{7,6},{8,9},{9,8},{10,11... | collective-permute-start | bytes 3145736 | tf_op jit(solution)/shard_map/ppermute | solution.py:26
  38.5 13.4 %collective-permute-start.2 = (bf16[128,2048]{1,0:T(8,128)(2,1)S(1)}, bf16[128,2048]{1,0:T(8,128)(2,1)}, u32[]{:S(2)}, u32[]{:S(2)}) collective-permute-start(bf16[128,2048]{1,0:T(8,128)(2,1)S(1)} %slice.406), channel_id=1, source_target_pairs={{0,1},{1,0},{2,3},{3,2},{4,5},{5,4},{6,7},{7,6},{8,9},{9,8},{10,11... | collective-permute-start | bytes 1572872 | tf_op jit(solution)/shard_map/ppermute | solution.py:26
  41.3 12.7 %collective-permute-start.3 = (bf16[128,2048]{1,0:T(8,128)(2,1)S(1)}, bf16[128,2048]{1,0:T(8,128)(2,1)S(1)}, u32[]{:S(2)}, u32[]{:S(2)}) collective-permute-start(bf16[128,2048]{1,0:T(8,128)(2,1)S(1)} %slice.407), channel_id=1, source_target_pairs={{0,2},{1,3},{2,0},{3,1},{4,6},{5,7},{6,4},{7,5},{8,10},{9,11},{10,... | collective-permute-start | bytes 1572872 | tf_op jit(solution)/shard_map/ppermute | solution.py:26
  54.0 189.8 %all-gather.7.cloned.1.call-start = ((), (), s32[]{:S(2)}) async-start(), calls=%async_computation.5 | async-start | bytes 7077888 | tf_op jit(solution)/shard_map/all_gather | solution.py:61
  54.9 151.3 %copy-start.54 = (f32[256]{0:T(256)}, f32[256]{0:T(256)S(1)}, u32[]{:S(2)}) copy-start(f32[256]{0:T(256)S(1)} %convert_element_type.277) | copy-start | bytes 3076
  55.9 8.4 %copy-start.27 = (bf16[256,768]{1,0:T(8,128)(2,1)}, bf16[256,768]{1,0:T(8,128)(2,1)S(1)}, u32[]{:S(2)}) copy-start(bf16[256,768]{1,0:T(8,128)(2,1)S(1)} %slice.338) | copy-start | bytes 1179652
  57.1 7.2 %copy-start.29 = (bf16[256,768]{1,0:T(8,128)(2,1)}, bf16[256,768]{1,0:T(8,128)(2,1)S(1)}, u32[]{:S(2)}) copy-start(bf16[256,768]{1,0:T(8,128)(2,1)S(1)} %slice.339) | copy-start | bytes 1179652
  62.2 26.3 %collective-permute-start.4 = (bf16[256,2048]{1,0:T(8,128)(2,1)}, bf16[256,2048]{1,0:T(8,128)(2,1)}, u32[]{:S(2)}, u32[]{:S(2)}) collective-permute-start(bf16[256,2048]{1,0:T(8,128)(2,1)} %fusion.34), channel_id=1, source_target_pairs={{0,1},{1,0},{2,3},{3,2},{4,5},{5,4},{6,7},{7,6},{8,9},{9,8},{10,11... | collective-permute-start | bytes 3145736 | tf_op jit(solution)/shard_map/ppermute | solution.py:26
  63.3 23.2 %collective-permute-start.5 = (bf16[256,2048]{1,0:T(8,128)(2,1)}, bf16[256,2048]{1,0:T(8,128)(2,1)}, u32[]{:S(2)}, u32[]{:S(2)}) collective-permute-start(bf16[256,2048]{1,0:T(8,128)(2,1)} %fusion.34), channel_id=1, source_target_pairs={{0,2},{1,3},{2,0},{3,1},{4,6},{5,7},{6,4},{7,5},{8,10},{9,11},{10,... | collective-permute-start | bytes 3145736 | tf_op jit(solution)/shard_map/ppermute | solution.py:26
  87.6 10.9 %collective-permute-start.6 = (bf16[128,2048]{1,0:T(8,128)(2,1)S(1)}, bf16[128,2048]{1,0:T(8,128)(2,1)}, u32[]{:S(2)}, u32[]{:S(2)}) collective-permute-start(bf16[128,2048]{1,0:T(8,128)(2,1)S(1)} %slice.412), channel_id=1, source_target_pairs={{0,1},{1,0},{2,3},{3,2},{4,5},{5,4},{6,7},{7,6},{8,9},{9,8},{10,11... | collective-permute-start | bytes 1572872 | tf_op jit(solution)/shard_map/ppermute | solution.py:26
  89.6 10.6 %collective-permute-start.7 = (bf16[128,2048]{1,0:T(8,128)(2,1)S(1)}, bf16[128,2048]{1,0:T(8,128)(2,1)}, u32[]{:S(2)}, u32[]{:S(2)}) collective-permute-start(bf16[128,2048]{1,0:T(8,128)(2,1)S(1)} %slice.413), channel_id=1, source_target_pairs={{0,2},{1,3},{2,0},{3,1},{4,6},{5,7},{6,4},{7,5},{8,10},{9,11},{10,... | collective-permute-start | bytes 1572872 | tf_op jit(solution)/shard_map/ppermute | solution.py:26
  92.5 10.4 %copy-start.42 = (bf16[128,2048]{1,0:T(8,128)(2,1)S(1)}, bf16[128,2048]{1,0:T(8,128)(2,1)}, u32[]{:S(2)}) copy-start(bf16[128,2048]{1,0:T(8,128)(2,1)} %copy-done.41) | copy-start | bytes 1572868
  100.3 171.0 %all-gather.9.cloned.1.call-start = ((), (), s32[]{:S(2)}) async-start(), calls=%async_computation.6 | async-start | bytes 5898240 | tf_op jit(solution)/shard_map/all_gather | solution.py:61
  141.0 21.4 %collective-permute-start.10 = (bf16[256,2048]{1,0:T(8,128)(2,1)S(1)}, bf16[256,2048]{1,0:T(8,128)(2,1)S(1)}, u32[]{:S(2)}, u32[]{:S(2)}) collective-permute-start(bf16[256,2048]{1,0:T(8,128)(2,1)S(1)} %pad_maximum_fusion.6), channel_id=1, source_target_pairs={{0,2},{1,3},{2,0},{3,1},{4,6},{5,7},{6,4},{7,5},{8,10},{9,11},{10,... | collective-permute-start | bytes 3145736 | tf_op jit(solution)/shard_map/ppermute | solution.py:26
  142.6 22.6 %collective-permute-start.8 = (bf16[256,2048]{1,0:T(8,128)(2,1)S(1)}, bf16[256,2048]{1,0:T(8,128)(2,1)S(1)}, u32[]{:S(2)}, u32[]{:S(2)}) collective-permute-start(bf16[256,2048]{1,0:T(8,128)(2,1)S(1)} %pad_maximum_fusion.5), channel_id=1, source_target_pairs={{0,1},{1,0},{2,3},{3,2},{4,5},{5,4},{6,7},{7,6},{8,9},{9,8},{10,11... | collective-permute-start | bytes 3145736 | tf_op jit(solution)/shard_map/ppermute | solution.py:26
  165.9 10.0 %collective-permute-start.11 = (bf16[128,2048]{1,0:T(8,128)(2,1)S(1)}, bf16[128,2048]{1,0:T(8,128)(2,1)S(1)}, u32[]{:S(2)}, u32[]{:S(2)}) collective-permute-start(bf16[128,2048]{1,0:T(8,128)(2,1)S(1)} %get-tuple-element.74), channel_id=1, source_target_pairs={{0,1},{1,0},{2,3},{3,2},{4,5},{5,4},{6,7},{7,6},{8,9},{9,8},{10,11... | collective-permute-start | bytes 1572872 | tf_op jit(solution)/shard_map/ppermute | solution.py:26
  166.4 10.7 %collective-permute-start.9 = (bf16[128,2048]{1,0:T(8,128)(2,1)S(1)}, bf16[128,2048]{1,0:T(8,128)(2,1)S(1)}, u32[]{:S(2)}, u32[]{:S(2)}) collective-permute-start(bf16[128,2048]{1,0:T(8,128)(2,1)S(1)} %get-tuple-element.73), channel_id=1, source_target_pairs={{0,2},{1,3},{2,0},{3,1},{4,6},{5,7},{6,4},{7,5},{8,10},{9,11},{10,... | collective-permute-start | bytes 1572872 | tf_op jit(solution)/shard_map/ppermute | solution.py:26
  170.0 7.7 %copy-start.5 = (bf16[256,2048]{1,0:T(8,128)(2,1)S(1)}, bf16[256,2048]{1,0:T(8,128)(2,1)}, u32[]{:S(2)}) copy-start(bf16[256,2048]{1,0:T(8,128)(2,1)} %param.12) | copy-start | bytes 3145732
  179.3 20.9 %collective-permute-start.13 = (bf16[256,2048]{1,0:T(8,128)(2,1)S(1)}, bf16[256,2048]{1,0:T(8,128)(2,1)S(1)}, u32[]{:S(2)}, u32[]{:S(2)}) collective-permute-start(bf16[256,2048]{1,0:T(8,128)(2,1)S(1)} %get-tuple-element.48), channel_id=1, source_target_pairs={{0,2},{1,3},{2,0},{3,1},{4,6},{5,7},{6,4},{7,5},{8,10},{9,11},{10,... | collective-permute-start | bytes 3145736 | tf_op jit(solution)/shard_map/ppermute | solution.py:26
  181.2 21.4 %collective-permute-start.12 = (bf16[256,2048]{1,0:T(8,128)(2,1)S(1)}, bf16[256,2048]{1,0:T(8,128)(2,1)S(1)}, u32[]{:S(2)}, u32[]{:S(2)}) collective-permute-start(bf16[256,2048]{1,0:T(8,128)(2,1)S(1)} %get-tuple-element.48), channel_id=1, source_target_pairs={{0,1},{1,0},{2,3},{3,2},{4,5},{5,4},{6,7},{7,6},{8,9},{9,8},{10,11... | collective-permute-start | bytes 3145736 | tf_op jit(solution)/shard_map/ppermute | solution.py:26
  201.1 9.5 %collective-permute-start.14 = (bf16[128,2048]{1,0:T(8,128)(2,1)}, bf16[128,2048]{1,0:T(8,128)(2,1)}, u32[]{:S(2)}, u32[]{:S(2)}) collective-permute-start(bf16[128,2048]{1,0:T(8,128)(2,1)} %slice.425), channel_id=1, source_target_pairs={{0,1},{1,0},{2,3},{3,2},{4,5},{5,4},{6,7},{7,6},{8,9},{9,8},{10,11... | collective-permute-start | bytes 1572872 | tf_op jit(solution)/shard_map/ppermute | solution.py:26
  203.7 9.5 %collective-permute-start.15 = (bf16[128,2048]{1,0:T(8,128)(2,1)}, bf16[128,2048]{1,0:T(8,128)(2,1)}, u32[]{:S(2)}, u32[]{:S(2)}) collective-permute-start(bf16[128,2048]{1,0:T(8,128)(2,1)} %slice.426), channel_id=1, source_target_pairs={{0,2},{1,3},{2,0},{3,1},{4,6},{5,7},{6,4},{7,5},{8,10},{9,11},{10,... | collective-permute-start | bytes 1572872 | tf_op jit(solution)/shard_map/ppermute | solution.py:26
  213.3 302.5 %reduce-scatter.7.cloned.1.call-start = ((), (), s32[]{:S(2)}) async-start(), calls=%async_computation.9 | async-start | bytes 7077888 | tf_op jit(solution)/shard_map/reduce_scatter | solution.py:65
  225.4 12.0 %copy-start.38 = (bf16[256,2048]{1,0:T(8,128)(2,1)S(1)}, bf16[256,2048]{1,0:T(8,128)(2,1)}, u32[]{:S(2)}) copy-start(bf16[256,2048]{1,0:T(8,128)(2,1)} %copy-done.37) | copy-start | bytes 3145732
  271.2 246.3 %reduce-scatter.9.cloned.1.call-start = ((), (), s32[]{:S(2)}) async-start(), calls=%async_computation.10 | async-start | bytes 5898240 | tf_op jit(solution)/shard_map/reduce_scatter | solution.py:65
  296.4 224.7 %reduce-scatter.5.cloned.1.call-start = ((), (), s32[]{:S(2)}) async-start(), calls=%async_computation.8 | async-start | bytes 5898240 | tf_op jit(solution)/shard_map/reduce_scatter | solution.py:65
  296.9 7.0 %copy-start.18 = (bf16[1024,768]{1,0:T(8,128)(2,1)S(1)}, bf16[1024,768]{1,0:T(8,128)(2,1)}, u32[]{:S(2)}) copy-start(bf16[1024,768]{1,0:T(8,128)(2,1)} %copy-done.17) | copy-start | bytes 4718596
  296.9 7.0 %copy-start.20 = (bf16[1024,768]{1,0:T(8,128)(2,1)S(1)}, bf16[1024,768]{1,0:T(8,128)(2,1)}, u32[]{:S(2)}) copy-start(bf16[1024,768]{1,0:T(8,128)(2,1)} %copy-done.19) | copy-start | bytes 4718596
  296.9 18.0 %slice-start.2 = ((s8[5242880]{0:T(1024)(128)(4,1)}), s8[4194304]{0:T(1024)(128)(4,1)S(1)}, s32[]{:S(2)}) async-start(s8[5242880]{0:T(1024)(128)(4,1)} %bitcast.40), calls=%async_computation.14 | async-start | bytes 8388608
  303.9 11.0 %slice-start.3 = ((s8[5242880]{0:T(1024)(128)(4,1)}), s8[1048576]{0:T(1024)(128)(4,1)S(1)}, s32[]{:S(2)}) async-start(s8[5242880]{0:T(1024)(128)(4,1)} %bitcast.40), calls=%async_computation.15 | async-start | bytes 2097152
  312.6 23.4 %collective-permute-start.18 = (bf16[256,2048]{1,0:T(8,128)(2,1)S(1)}, bf16[256,2048]{1,0:T(8,128)(2,1)S(1)}, u32[]{:S(2)}, u32[]{:S(2)}) collective-permute-start(bf16[256,2048]{1,0:T(8,128)(2,1)S(1)} %pad_maximum_fusion.8), channel_id=1, source_target_pairs={{0,2},{1,3},{2,0},{3,1},{4,6},{5,7},{6,4},{7,5},{8,10},{9,11},{10,... | collective-permute-start | bytes 3145736 | tf_op jit(solution)/shard_map/ppermute | solution.py:26
  312.9 24.4 %collective-permute-start.16 = (bf16[256,2048]{1,0:T(8,128)(2,1)S(1)}, bf16[256,2048]{1,0:T(8,128)(2,1)S(1)}, u32[]{:S(2)}, u32[]{:S(2)}) collective-permute-start(bf16[256,2048]{1,0:T(8,128)(2,1)S(1)} %pad_maximum_fusion.7), channel_id=1, source_target_pairs={{0,1},{1,0},{2,3},{3,2},{4,5},{5,4},{6,7},{7,6},{8,9},{9,8},{10,11... | collective-permute-start | bytes 3145736 | tf_op jit(solution)/shard_map/ppermute | solution.py:26
  314.9 25.0 %slice-start = ((s8[6291456]{0:T(1024)(128)(4,1)}), s8[4194304]{0:T(1024)(128)(4,1)S(1)}, s32[]{:S(2)}) async-start(s8[6291456]{0:T(1024)(128)(4,1)} %bitcast.38), calls=%async_computation.12 | async-start | bytes 8388608
  316.5 23.4 %slice-start.1 = ((s8[6291456]{0:T(1024)(128)(4,1)}), s8[2097152]{0:T(1024)(128)(4,1)S(1)}, s32[]{:S(2)}) async-start(s8[6291456]{0:T(1024)(128)(4,1)} %bitcast.38), calls=%async_computation.13 | async-start | bytes 4194304
  337.9 12.4 %collective-permute-start.17 = (bf16[128,2048]{1,0:T(8,128)(2,1)S(1)}, bf16[128,2048]{1,0:T(8,128)(2,1)S(1)}, u32[]{:S(2)}, u32[]{:S(2)}) collective-permute-start(bf16[128,2048]{1,0:T(8,128)(2,1)S(1)} %get-tuple-element.67), channel_id=1, source_target_pairs={{0,2},{1,3},{2,0},{3,1},{4,6},{5,7},{6,4},{7,5},{8,10},{9,11},{10,... | collective-permute-start | bytes 1572872 | tf_op jit(solution)/shard_map/ppermute | solution.py:26
  338.5 12.1 %collective-permute-start.19 = (bf16[128,2048]{1,0:T(8,128)(2,1)S(1)}, bf16[128,2048]{1,0:T(8,128)(2,1)S(1)}, u32[]{:S(2)}, u32[]{:S(2)}) collective-permute-start(bf16[128,2048]{1,0:T(8,128)(2,1)S(1)} %get-tuple-element.68), channel_id=1, source_target_pairs={{0,1},{1,0},{2,3},{3,2},{4,5},{5,4},{6,7},{7,6},{8,9},{9,8},{10,11... | collective-permute-start | bytes 1572872 | tf_op jit(solution)/shard_map/ppermute | solution.py:26
  341.8 9.3 %copy-start.6 = (bf16[256,2048]{1,0:T(8,128)(2,1)S(1)}, bf16[256,2048]{1,0:T(8,128)(2,1)}, u32[]{:S(2)}) copy-start(bf16[256,2048]{1,0:T(8,128)(2,1)} %param.12) | copy-start | bytes 3145732
  341.8 9.3 %copy-start.9 = (f32[128,2048]{1,0:T(8,128)S(1)}, f32[128,2048]{1,0:T(8,128)}, u32[]{:S(2)}) copy-start(f32[128,2048]{1,0:T(8,128)} %copy-done.8) | copy-start | bytes 3145732
  341.8 9.3 %copy-start.12 = (f32[128,2048]{1,0:T(8,128)S(1)}, f32[128,2048]{1,0:T(8,128)}, u32[]{:S(2)}) copy-start(f32[128,2048]{1,0:T(8,128)} %copy-done.11) | copy-start | bytes 3145732
  352.4 25.4 %copy-start.51 = (bf16[256,256]{1,0:T(8,128)(2,1)S(1)}, bf16[256,256]{1,0:T(8,128)(2,1)}, u32[]{:S(2)}) copy-start(bf16[256,256]{1,0:T(8,128)(2,1)} %param.23) | copy-start | bytes 393220
  354.5 22.5 %collective-permute-start.21 = (bf16[256,2048]{1,0:T(8,128)(2,1)S(1)}, bf16[256,2048]{1,0:T(8,128)(2,1)S(1)}, u32[]{:S(2)}, u32[]{:S(2)}) collective-permute-start(bf16[256,2048]{1,0:T(8,128)(2,1)S(1)} %get-tuple-element.45), channel_id=1, source_target_pairs={{0,2},{1,3},{2,0},{3,1},{4,6},{5,7},{6,4},{7,5},{8,10},{9,11},{10,... | collective-permute-start | bytes 3145736 | tf_op jit(solution)/shard_map/ppermute | solution.py:26
  355.8 23.8 %collective-permute-start.20 = (bf16[256,2048]{1,0:T(8,128)(2,1)S(1)}, bf16[256,2048]{1,0:T(8,128)(2,1)S(1)}, u32[]{:S(2)}, u32[]{:S(2)}) collective-permute-start(bf16[256,2048]{1,0:T(8,128)(2,1)S(1)} %get-tuple-element.45), channel_id=1, source_target_pairs={{0,1},{1,0},{2,3},{3,2},{4,5},{5,4},{6,7},{7,6},{8,9},{9,8},{10,11... | collective-permute-start | bytes 3145736 | tf_op jit(solution)/shard_map/ppermute | solution.py:26
  377.0 12.2 %collective-permute-start.22 = (bf16[128,2048]{1,0:T(8,128)(2,1)S(1)}, bf16[128,2048]{1,0:T(8,128)(2,1)S(1)}, u32[]{:S(2)}, u32[]{:S(2)}) collective-permute-start(bf16[128,2048]{1,0:T(8,128)(2,1)S(1)} %slice.446), channel_id=1, source_target_pairs={{0,1},{1,0},{2,3},{3,2},{4,5},{5,4},{6,7},{7,6},{8,9},{9,8},{10,11... | collective-permute-start | bytes 1572872 | tf_op jit(solution)/shard_map/ppermute | solution.py:26
  379.7 9.6 %collective-permute-start.23 = (bf16[128,2048]{1,0:T(8,128)(2,1)S(1)}, bf16[128,2048]{1,0:T(8,128)(2,1)S(1)}, u32[]{:S(2)}, u32[]{:S(2)}) collective-permute-start(bf16[128,2048]{1,0:T(8,128)(2,1)S(1)} %slice.447), channel_id=1, source_target_pairs={{0,2},{1,3},{2,0},{3,1},{4,6},{5,7},{6,4},{7,5},{8,10},{9,11},{10,... | collective-permute-start | bytes 1572872 | tf_op jit(solution)/shard_map/ppermute | solution.py:26
  416.6 122.3 %reduce-scatter.11.cloned.1.call-start = ((), (), s32[]{:S(2)}) async-start(), calls=%async_computation.11 | async-start | bytes 6488064 | tf_op jit(solution)/shard_map/reduce_scatter | solution.py:65
  438.7 46.6 %collective-permute-start.26 = (bf16[256,2048]{1,0:T(8,128)(2,1)S(1)}, bf16[256,2048]{1,0:T(8,128)(2,1)S(1)}, u32[]{:S(2)}, u32[]{:S(2)}) collective-permute-start(bf16[256,2048]{1,0:T(8,128)(2,1)S(1)} %pad_maximum_fusion.10), channel_id=1, source_target_pairs={{0,2},{1,3},{2,0},{3,1},{4,6},{5,7},{6,4},{7,5},{8,10},{9,11},{10,... | collective-permute-start | bytes 3145736 | tf_op jit(solution)/shard_map/ppermute | solution.py:26
  445.3 38.4 %collective-permute-start.30 = (bf16[256,2048]{1,0:T(8,128)(2,1)S(1)}, bf16[256,2048]{1,0:T(8,128)(2,1)S(1)}, u32[]{:S(2)}, u32[]{:S(2)}) collective-permute-start(bf16[256,2048]{1,0:T(8,128)(2,1)S(1)} %pad_maximum_fusion.12), channel_id=1, source_target_pairs={{0,2},{1,3},{2,0},{3,1},{4,6},{5,7},{6,4},{7,5},{8,10},{9,11},{10,... | collective-permute-start | bytes 3145736 | tf_op jit(solution)/shard_map/ppermute | solution.py:26
  446.3 37.7 %collective-permute-start.28 = (bf16[256,2048]{1,0:T(8,128)(2,1)S(1)}, bf16[256,2048]{1,0:T(8,128)(2,1)S(1)}, u32[]{:S(2)}, u32[]{:S(2)}) collective-permute-start(bf16[256,2048]{1,0:T(8,128)(2,1)S(1)} %pad_maximum_fusion.11), channel_id=1, source_target_pairs={{0,1},{1,0},{2,3},{3,2},{4,5},{5,4},{6,7},{7,6},{8,9},{9,8},{10,11... | collective-permute-start | bytes 3145736 | tf_op jit(solution)/shard_map/ppermute | solution.py:26
  446.6 6.6 %slice-start.4 = ((s8[5242880]{0:T(1024)(128)(4,1)}), s8[4194304]{0:T(1024)(128)(4,1)S(1)}, s32[]{:S(2)}) async-start(s8[5242880]{0:T(1024)(128)(4,1)} %bitcast.42), calls=%async_computation.16 | async-start | bytes 8388608
  446.7 6.5 %slice-start.5 = ((s8[5242880]{0:T(1024)(128)(4,1)}), s8[1048576]{0:T(1024)(128)(4,1)S(1)}, s32[]{:S(2)}) async-start(s8[5242880]{0:T(1024)(128)(4,1)} %bitcast.42), calls=%async_computation.17 | async-start | bytes 2097152
  446.7 48.1 %collective-permute-start.24 = (bf16[256,2048]{1,0:T(8,128)(2,1)S(1)}, bf16[256,2048]{1,0:T(8,128)(2,1)S(1)}, u32[]{:S(2)}, u32[]{:S(2)}) collective-permute-start(bf16[256,2048]{1,0:T(8,128)(2,1)S(1)} %pad_maximum_fusion.9), channel_id=1, source_target_pairs={{0,1},{1,0},{2,3},{3,2},{4,5},{5,4},{6,7},{7,6},{8,9},{9,8},{10,11... | collective-permute-start | bytes 3145736 | tf_op jit(solution)/shard_map/ppermute | solution.py:26
  484.5 14.9 %collective-permute-start.29 = (bf16[128,2048]{1,0:T(8,128)(2,1)S(1)}, bf16[128,2048]{1,0:T(8,128)(2,1)S(1)}, u32[]{:S(2)}, u32[]{:S(2)}) collective-permute-start(bf16[128,2048]{1,0:T(8,128)(2,1)S(1)} %get-tuple-element.55), channel_id=1, source_target_pairs={{0,2},{1,3},{2,0},{3,1},{4,6},{5,7},{6,4},{7,5},{8,10},{9,11},{10,... | collective-permute-start | bytes 1572872 | tf_op jit(solution)/shard_map/ppermute | solution.py:26
  484.8 21.2 %collective-permute-start.31 = (bf16[128,2048]{1,0:T(8,128)(2,1)S(1)}, bf16[128,2048]{1,0:T(8,128)(2,1)S(1)}, u32[]{:S(2)}, u32[]{:S(2)}) collective-permute-start(bf16[128,2048]{1,0:T(8,128)(2,1)S(1)} %get-tuple-element.56), channel_id=1, source_target_pairs={{0,1},{1,0},{2,3},{3,2},{4,5},{5,4},{6,7},{7,6},{8,9},{9,8},{10,11... | collective-permute-start | bytes 1572872 | tf_op jit(solution)/shard_map/ppermute | solution.py:26
  495.4 11.7 %collective-permute-start.25 = (bf16[128,2048]{1,0:T(8,128)(2,1)S(1)}, bf16[128,2048]{1,0:T(8,128)(2,1)S(1)}, u32[]{:S(2)}, u32[]{:S(2)}) collective-permute-start(bf16[128,2048]{1,0:T(8,128)(2,1)S(1)} %get-tuple-element.61), channel_id=1, source_target_pairs={{0,2},{1,3},{2,0},{3,1},{4,6},{5,7},{6,4},{7,5},{8,10},{9,11},{10,... | collective-permute-start | bytes 1572872 | tf_op jit(solution)/shard_map/ppermute | solution.py:26
  496.6 9.9 %copy-start.7 = (bf16[256,2048]{1,0:T(8,128)(2,1)S(1)}, bf16[256,2048]{1,0:T(8,128)(2,1)}, u32[]{:S(2)}) copy-start(bf16[256,2048]{1,0:T(8,128)(2,1)} %param.12) | copy-start | bytes 3145732
  496.6 9.9 %copy-start.53 = (f32[256]{0:T(256)S(1)}, f32[256]{0:T(256)}, u32[]{:S(2)}) copy-start(f32[256]{0:T(256)} %copy-done.52) | copy-start | bytes 3076
  496.6 16.3 %collective-permute-start.27 = (bf16[128,2048]{1,0:T(8,128)(2,1)S(1)}, bf16[128,2048]{1,0:T(8,128)(2,1)S(1)}, u32[]{:S(2)}, u32[]{:S(2)}) collective-permute-start(bf16[128,2048]{1,0:T(8,128)(2,1)S(1)} %get-tuple-element.62), channel_id=1, source_target_pairs={{0,1},{1,0},{2,3},{3,2},{4,5},{5,4},{6,7},{7,6},{8,9},{9,8},{10,11... | collective-permute-start | bytes 1572872 | tf_op jit(solution)/shard_map/ppermute | solution.py:26
  507.0 6.4 %copy-start.10 = (f32[128,2048]{1,0:T(8,128)S(1)}, f32[128,2048]{1,0:T(8,128)}, u32[]{:S(2)}) copy-start(f32[128,2048]{1,0:T(8,128)} %copy-done.8) | copy-start | bytes 3145732
  523.3 6.5 %collective-permute-start.32 = (f32[256,258]{0,1:T(8,128)S(1)}, f32[256,258]{0,1:T(8,128)S(1)}, u32[]{:S(2)}, u32[]{:S(2)}) collective-permute-start(f32[256,258]{0,1:T(8,128)S(1)} %pad_maximum_fusion.18), channel_id=1, source_target_pairs={{0,1},{1,0},{2,3},{3,2},{4,5},{5,4},{6,7},{7,6},{8,9},{9,8},{10,11... | collective-permute-start | bytes 792584 | tf_op jit(solution)/shard_map/ppermute | solution.py:26
  529.9 12.8 %collective-permute-start.33 = (f32[256,258]{0,1:T(8,128)S(1)}, f32[256,258]{0,1:T(8,128)S(1)}, u32[]{:S(2)}, u32[]{:S(2)}) collective-permute-start(f32[256,258]{0,1:T(8,128)S(1)} %fusion.103), channel_id=1, source_target_pairs={{0,2},{1,3},{2,0},{3,1},{4,6},{5,7},{6,4},{7,5},{8,10},{9,11},{10,... | collective-permute-start | bytes 792584 | tf_op jit(solution)/shard_map/ppermute | solution.py:26
  (43 other events, 104.8 us)
Sparse Core Ops, SparseCore 0:
  12.3 59.1 all-gather.4
  73.1 58.9 all-gather.10
  134.3 62.8 all-gather.6
  213.4 55.8 all-gather.8
  271.4 69.4 reduce-scatter.6
  343.1 58.2 reduce-scatter.8
  416.7 56.5 reduce-scatter.4
  475.6 63.2 reduce-scatter.10

commit v3 on v2

--- a/solution.py
+++ b/solution.py
@@ -30,26 +30,41 @@
     return lax.optimization_barrier((value, *others))[0]
 
 
-def gather_blocks(own):
+def near_blocks(own):
     size = lax.axis_size("tensor")
+    return [hop(own, j) for j in range(1, 3 if size == 4 else size)]
+
+
+def all_blocks(own, near):
+    if lax.axis_size("tensor") != 4:
+        return [own, *near]
+    half = own.shape[0] // 2
+    one, two = near
+    return [own, one, two, hop(two[:half], 1), hop(one[half:], 2)]
+
+
+def send_sums(rest):
+    size = lax.axis_size("tensor")
+    rows = rest.shape[0] // (size - 1)
+    one, *others = (rows_of(rest, j, rows) for j in range(size - 1))
     if size != 4:
-        return [own] + [hop(own, j) for j in range(1, size)]
-    half = own.shape[0] // 2
-    near, far = hop(own, 1), hop(own, 2)
-    upper, lower = hop(far[:half], 1), hop(near[half:], 2)
-    return [own, near, far, upper, lower]
-
-
-def scatter_sum(own, rest):
-    size, rows = lax.axis_size("tensor"), own.shape[0]
-    if size != 4:
-        for j in range(1, size):
-            own = own + hop(rows_of(rest, j - 1, rows), j).astype(f32)
-        return own
+        return [hop(block, j + 1) for j, block in enumerate([one, *others])]
+    two, three = others
     half = rows // 2
-    one, two, three = (rows_of(rest, j, rows) for j in range(3))
-    upper = hop(jnp.concatenate([one[:half], three[:half]], axis=0), 1).astype(f32)
-    lower = hop(jnp.concatenate([two[half:], three[half:]], axis=0), 2).astype(f32)
+    return [
+        hop(jnp.concatenate([one[:half], three[:half]], axis=0), 1),
+        hop(jnp.concatenate([two[half:], three[half:]], axis=0), 2),
+    ]
+
+
+def finish_sums(own, rest, arrived):
+    arrived = [block.astype(f32) for block in arrived]
+    if lax.axis_size("tensor") != 4:
+        return own + sum(arrived)
+    rows = own.shape[0]
+    half = rows // 2
+    one, two = rows_of(rest, 0, rows), rows_of(rest, 1, rows)
+    upper, lower = arrived
     upper_far = hop((two[:half].astype(f32) + upper[half:]).astype(bf16), 2).astype(f32)
     lower_near = hop((one[half:].astype(f32) + lower[half:]).astype(bf16), 1).astype(f32)
     return jnp.concatenate(
@@ -63,6 +78,56 @@
 
 def scatter_dp(partial):
     return lax.psum_scatter(partial, "dp", scatter_dimension=0, tiled=True).astype(f32)
+
+
+def lines_of():
+    size = lax.axis_size("dp")
+    index = lax.axis_index("dp").astype(jnp.int32)
+    return size // 2, index // 2, index % 2
+
+
+def swap_cores(value):
+    return lax.ppermute(value, "dp", [(i, i ^ 1) for i in range(lax.axis_size("dp"))])
+
+
+def shift_lines(value, step):
+    size = lax.axis_size("dp")
+    return lax.ppermute(value, "dp", [(i, (i + 2 * step) % size) for i in range(size)])
+
+
+def send_lines(shard):
+    return [shard] + [shift_lines(shard, step) for step in range(1, lines_of()[0])]
+
+
+def join_lines(pieces, *ready):
+    lines, line, core = lines_of()
+    rows = pieces[0].shape[0]
+    whole = jnp.zeros((2 * lines * rows, pieces[0].shape[1]), pieces[0].dtype)
+    for step, piece in enumerate(pieces):
+        base = 2 * ((line - step) % lines)
+        other = swap_cores(after(piece, *ready) if ready else piece)
+        whole = lax.dynamic_update_slice(whole, piece, ((base + core) * rows, 0))
+        whole = lax.dynamic_update_slice(whole, other, ((base + 1 - core) * rows, 0))
+    return whole
+
+
+pick = functools.partial(lax.dynamic_index_in_dim, keepdims=False)
+
+
+def sum_cores(partial, *ready):
+    lines, _, core = lines_of()
+    blocks = partial.reshape(lines, 2, -1, partial.shape[1])
+    other = after(swap_cores(pick(blocks, 1 - core, 1)), *ready)
+    return pick(blocks, core, 1).astype(f32) + other.astype(f32)
+
+
+def sum_lines(chip, *ready):
+    lines, line, _ = lines_of()
+    total, sent = pick(chip, line, 0), chip.astype(bf16)
+    for step in range(1, lines):
+        arrived = shift_lines(pick(sent, (line + step) % lines, 0), step)
+        total = total + after(arrived, *ready).astype(f32)
+    return total
 
 
 def turn(u, cos2, sin2):
@@ -294,85 +359,93 @@
     gain_one, gain_two = gain_attn.astype(f32)[:, None], gain_mlp.astype(f32)[:, None]
     qkv_own = jnp.concatenate([w_query, w_keyvalue], axis=1).astype(f32)
     qkv_width = qkv_own.shape[1]
-    attn_shard = jnp.concatenate([(qkv_own * gain_one).astype(bf16), w_project.T], axis=1)
     pair_own = [
         jnp.concatenate([w_gate[:, a:b], w_up[:, a:b]], axis=1).astype(f32) for a, b in parts
     ]
     pair_shards = [(own * gain_two).astype(bf16) for own in pair_own]
 
     residual = layer_input.astype(f32)
-    inputs = gather_blocks(layer_input)
-    attn_full = gather_dp(attn_shard)
-    down_full = gather_dp(after(w_down.T, *inputs))
-    qkv_full, project_full = attn_full[:, :qkv_width], attn_full[:, qkv_width:]
+    inputs = all_blocks(layer_input, near_blocks(layer_input))
+    qkv_full = gather_dp((qkv_own * gain_one).astype(bf16))
+    project_full = join_lines(send_lines(w_project.T))
+    pairs = [gather_dp(after(pair_shards[0], *inputs))]
+    down_pieces = send_lines(after(w_down.T, *inputs))
     top = out_grad.astype(f32) * own_mask
-    top_blocks = gather_blocks(after(top.astype(bf16), *inputs))
-    pairs = [gather_dp(after(pair_shards[0], *top_blocks))]
+    top_own = after(top.astype(bf16), *inputs)
+    top_near = near_blocks(top_own)
 
     def norm(block):
         block = block.astype(f32)
         return (block * inverse_norm(block)).astype(bf16)
 
     normed_one = jnp.concatenate([norm(b) for b in inputs], axis=0)
-    qkv = dot(normed_one, qkv_full, 1, 0)
+    qkv = dot(after(normed_one, project_full), qkv_full, 1, 0)
     qr, kvt, mixed, lse = attend(where, qkv, cos2, sin2, rows)
-    top_all = jnp.concatenate(top_blocks, axis=0)
-    mixed_sent = after(mixed, top_all)
-    after_attn = residual + scatter_sum(
-        dot(mixed[:rows], project_full, 1, 1),
-        dot(mixed_sent[rows:], project_full, 1, 1).astype(bf16),
+    pairs.append(gather_dp(after(pair_shards[1], mixed)))
+    mixed_rest = dot(after(mixed[rows:], *top_near), project_full, 1, 1).astype(bf16)
+    mixed_sent = send_sums(mixed_rest)
+    top_all = jnp.concatenate(all_blocks(top_own, top_near), axis=0)
+    down_full = join_lines(down_pieces, *mixed_sent)
+    after_attn = residual + finish_sums(
+        dot(mixed[:rows], project_full, 1, 1), mixed_rest, mixed_sent
     )
 
     inv_two = inverse_norm(after_attn)
     unit_two = after_attn * inv_two
-    normed_blocks = gather_blocks(unit_two.astype(bf16))
-    pairs.append(gather_dp(after(pair_shards[1], *normed_blocks)))
-    normed_two = jnp.concatenate(normed_blocks, axis=0)
-    hidden_grad = dot(top_all, down_full, 1, 0)
-    hiddens, pair_grads, pair_sums = [], [], []
-    for (a, b), pair in zip(parts, pairs):
-        both = dot(normed_two, pair, 1, 0)
+    normed_own = after(unit_two.astype(bf16), top_all)
+    grads = [dot(top_all, down_full[:, a:b], 1, 0) for a, b in parts]
+    normed_two = jnp.concatenate(all_blocks(normed_own, near_blocks(normed_own)), axis=0)
+    normed = after(normed_two, *grads)
+    hiddens, pair_grads, pair_partials = [], [], []
+    for (a, b), pair, grad in zip(parts, pairs, grads):
+        both = dot(normed, pair, 1, 0)
         gate, up = both[:, : b - a], both[:, b - a :]
         sig = jax.nn.sigmoid(gate)
-        grad = hidden_grad[:, a:b]
         hiddens.append((gate * sig * up).astype(bf16))
         gate_grad = (grad * up * sig * (1.0 + gate * (1.0 - sig))).astype(bf16)
         up_grad = (grad * gate * sig).astype(bf16)
         pair_grads.append(jnp.concatenate([gate_grad, up_grad], axis=1))
-        pair_sums.append(scatter_dp(dot(normed_two, pair_grads[-1], 0, 0).astype(bf16)))
+        if len(hiddens) == 1:
+            pair_partials.append(dot(normed_two, pair_grads[0], 0, 0).astype(bf16))
+            normed = after(normed_two, pair_partials[0])
     hidden = jnp.concatenate(hiddens, axis=1)
 
-    scaled = scatter_sum(
-        sum(dot(g[:rows], w, 1, 1) for g, w in zip(pair_grads, pairs)),
-        sum(dot(g[rows:], w, 1, 1) for g, w in zip(pair_grads, pairs)).astype(bf16),
-    )
+    rest = sum(dot(g[rows:], w, 1, 1) for g, w in zip(pair_grads, pairs)).astype(bf16)
+    rest_sent = send_sums(rest)
+    pair_partials.append(dot(normed_two, after(pair_grads[1], rest), 0, 0).astype(bf16))
+    pair_sums = [scatter_dp(partial) for partial in pair_partials]
+    own_grads = [g[:rows] for g in pair_grads]
+    own_grads[0] = after(own_grads[0], pair_partials[1])
+    scaled = finish_sums(sum(dot(g, w, 1, 1) for g, w in zip(own_grads, pairs)), rest, rest_sent)
     attn_top = top + inv_two * (
         scaled - unit_two * jnp.mean(scaled * unit_two, axis=-1, keepdims=True)
     )
-    attn_top_blocks = gather_blocks(attn_top.astype(bf16))
+    attn_top_own = attn_top.astype(bf16)
+    attn_top_blocks = all_blocks(attn_top_own, near_blocks(attn_top_own))
     attn_top_all = jnp.concatenate(attn_top_blocks, axis=0)
-    down_sum = scatter_dp(dot(top_all, hidden, 0, 0).astype(bf16))
-    down_rest = dot(hidden[rows:], down_full, 1, 1).astype(bf16)
-    after_mlp = after_attn + scatter_sum(
-        dot(hidden[:rows], down_full, 1, 1), after(down_rest, *attn_top_blocks)
+    down_chip = sum_cores(dot(top_all, hidden, 0, 0).astype(bf16))
+    down_rest = after(dot(hidden[rows:], down_full, 1, 1).astype(bf16), *attn_top_blocks)
+
+    mixed_grad = dot(after(attn_top_all, down_chip, pair_sums[0]), project_full, 1, 0).astype(bf16)
+    project_partial = dot(attn_top_all, mixed, 0, 0).astype(bf16)
+    shared = kv_grad.astype(f32) * own_mask
+    query_grad, kv_back = attend_back(
+        where, qr, kvt, after(mixed_grad, project_partial), lse, cos2, sin2, shared, rows
+    )
+    down_sum = sum_lines(down_chip, query_grad)
+    project_chip = sum_cores(project_partial, query_grad)
+    project_sum = sum_lines(project_chip)
+    down_sent = [after(block, query_grad) for block in send_sums(down_rest)]
+    after_mlp = after_attn + finish_sums(
+        dot(hidden[:rows], down_full, 1, 1), down_rest, down_sent
     )
     output = (after_mlp * own_mask).astype(bf16)
-
-    mixed_grad = dot(attn_top_all, project_full, 1, 0).astype(bf16)
-    shared = kv_grad.astype(f32) * own_mask
-    query_grad, kv_back = attend_back(where, qr, kvt, mixed_grad, lse, cos2, sin2, shared, rows)
-    qkv_back = jnp.concatenate([query_grad, kv_back], axis=1)
-    attn_grad = jnp.concatenate(
-        [
-            dot(normed_one, qkv_back, 0, 0).astype(bf16),
-            dot(attn_top_all, mixed, 0, 0).astype(bf16),
-        ],
-        axis=1,
-    )
-    attn_sum = scatter_dp(attn_grad)
-    qkv_sum, project_sum = attn_sum[:, :qkv_width], attn_sum[:, qkv_width:]
-    scaled_one = scatter_sum(
-        dot(qkv_back[:rows], qkv_full, 1, 1), dot(qkv_back[rows:], qkv_full, 1, 1).astype(bf16)
+    qkv_back = after(jnp.concatenate([query_grad, kv_back], axis=1), project_chip)
+    qkv_partial = dot(normed_one, qkv_back, 0, 0).astype(bf16)
+    qkv_sum = scatter_dp(after(qkv_partial, *pair_sums, down_sum))
+    qkv_rest = dot(after(qkv_back[rows:], qkv_partial, *down_sent), qkv_full, 1, 1).astype(bf16)
+    scaled_one = finish_sums(
+        dot(qkv_back[:rows], qkv_full, 1, 1), qkv_rest, send_sums(qkv_rest)
     )
     inv_one = inverse_norm(residual)
     unit_one = residual * inv_one

time: 560 us -> 587 us (1.048)
  the two profiles are of different devices: /device:TPU:0 before, /device:TPU:8 now
where the time goes in v3:
time: 587 us; the launch traced here: 578 us
  waiting for transfers between devices  177 us (30%)
  matrix products  133 us (23%)
  local copies, waits for them, and re-layouts  84.1 us (14%)
  other arithmetic  83.7 us (14%)
  starting transfers between devices  58.5 us (10%)
  Pallas kernels  25.4 us (4%)
  between operations  16.9 us (3%)
    dot_general x21, matrix products, dot(): lax.dot_general(a, b, (((ca,), (cb,)), ((), ())), preferred_element_type=...  133 us
    ppermute x34, waiting for transfers between devices, hop(): return lax.ppermute(value, 'tensor', [(i, i ^ step) for i in range(size)])  113 us
    ppermute x12, waiting for transfers between devices, shift_lines(): lax.ppermute(value, 'dp', [(i, (i + 2 * step) % size) for i in range(size)])  63.4 us
    ppermute x34, starting transfers between devices, hop(): return lax.ppermute(value, 'tensor', [(i, i ^ step) for i in range(size)])  39.7 us
    unnamed x184, local copies, waits for them, and re-layouts  27.2 us
    ppermute x12, starting transfers between devices, shift_lines(): lax.ppermute(value, 'dp', [(i, (i + 2 * step) % size) for i in range(size)])  17.1 us
    pallas_call x1, Pallas kernels, attend_back(): pl.pallas_call(attend_back_kernel, name='attend_back', grid_spec=pltpu.Pr...  13.8 us
  transfers between devices with their start and end apart: 62, of which 23 were waited for; matrix products, arithmetic and copies ran while one was open for 48% of the time, Pallas kernels for 4%

profile of v3, /device:TPU:8, one launch (start us, length us, event | category | flops | bytes accessed | tf_op | source)
XLA Modules:
  0.0 578.4 jit_solution(12934821751333783448)
XLA Ops:
  13.5 2.6 collective-permute-start.7
  16.9 3.2 fusion.81
  20.0 15.6 %collective-permute-done.1 = bf16[256,2048]{1,0:T(8,128)(2,1)S(1)} collective-permute-done((bf16[256,2048]{1,0:T(8,128)(2,1)}, bf16[256,2048]{1,0:T(8,128)(2,1)S(1)}, u32[]{:S(2)}, u32[]{:S(2)}) %collective-permute-start.1) | collective-permute-done | bytes 1048608 | tf_op jit(solution)/shard_map/ppermute | solution.py:26
  46.1 2.1 fusion.34
  51.8 2.1 fusion.38
  58.2 5.2 collective-permute-done.9
  75.4 2.8 collective-permute-start.26
  81.9 2.0 fusion.71
  83.9 2.0 fusion.70
  85.9 8.3 %fusion.97.q_ref.kv_ref = f32[1024,768]{1,0:T(8,128)} fusion(bf16[1024,2048]{1,0:T(8,128)(2,1)} %fusion.70, bf16[2048,768]{1,0:T(8,128)(2,1)} %all-gather.4.cloned.1.call-done), kind=kOutput, calls=%fused_computation.247 | convolution fusion | flops 3221225472 | bytes 10485760 | tf_op jit(solution)/shard_map/dot_general | solution.py:21
  94.2 11.5 %attend.1 = (bf16[1024,512]{1,0:T(8,128)(2,1)S(1)}, bf16[1024,256]{1,0:T(8,128)(2,1)S(1)}, bf16[1024,512]{1,0:T(8,128)(2,1)S(1)}, f32[1024,128]{1,0:T(8,128)S(1)}) custom-call(s32[2]{0:T(128)S(1)} %pad_add_fusion.where_ref, f32[1024,768]{1,0:T(8,128)} %fusion.97.q_ref.kv_ref, f32[1024,768]{1,0:T(8,128)} %fusion.97.q_ref.kv_ref, ...), custom_call_target="tpu_custom_call" | custom-call | flops 2147483648 | bytes 8388608 | tf_op jit(solution)/shard_map/attend/pallas_call | solution.py:246
  111.1 2.4 constant_dynamic-update-slice_fusion.4
  118.7 3.0 constant_dynamic-update-slice_fusion.3
  121.7 2.3 constant_dynamic-update-slice_fusion.2
  124.0 20.0 %collective-permute-done.17 = bf16[128,2048]{1,0:T(8,128)(2,1)S(1)} collective-permute-done((bf16[128,2048]{1,0:T(8,128)(2,1)S(1)}, bf16[128,2048]{1,0:T(8,128)(2,1)S(1)}, u32[]{:S(2)}, u32[]{:S(2)}) %collective-permute-start.17) | collective-permute-done | bytes 524320 | tf_op jit(solution)/shard_map/ppermute | solution.py:26
  144.0 2.7 collective-permute-start.24
  152.1 10.2 %collective-permute-done.18 = bf16[128,2048]{1,0:T(8,128)(2,1)S(1)} collective-permute-done((bf16[128,2048]{1,0:T(8,128)(2,1)S(1)}, bf16[128,2048]{1,0:T(8,128)(2,1)S(1)}, u32[]{:S(2)}, u32[]{:S(2)}) %collective-permute-start.18) | collective-permute-done | bytes 524320 | tf_op jit(solution)/shard_map/ppermute | solution.py:26
  165.2 2.4 fusion.79
  167.7 20.5 %collective-permute-done.24 = bf16[256,1408]{0,1:T(8,128)(2,1)} collective-permute-done((bf16[256,1408]{0,1:T(8,128)(2,1)}, bf16[256,1408]{0,1:T(8,128)(2,1)}, u32[]{:S(2)}, u32[]{:S(2)}) %collective-permute-start.24) | collective-permute-done | bytes 720928 | tf_op jit(solution)/shard_map/ppermute | solution.py:95
  200.8 9.4 %fusion = f32[1024,768]{0,1:T(8,128)} fusion(bf16[1024,2048]{1,0:T(8,128)(2,1)} %constant_dynamic-update-slice_fusion, bf16[2048,1408]{0,1:T(8,128)(2,1)S(1)} %constant_dynamic-update-slice_fusion.15), kind=kOutput, calls=%fused_computation.14 | convolution fusion | flops 3221225472 | bytes 10485760 | tf_op jit(solution)/shard_map/dot_general | solution.py:21
  210.2 7.3 %collective-permute-done.20 = bf16[256,2048]{1,0:T(8,128)(2,1)S(1)} collective-permute-done((bf16[256,2048]{1,0:T(8,128)(2,1)S(1)}, bf16[256,2048]{1,0:T(8,128)(2,1)S(1)}, u32[]{:S(2)}, u32[]{:S(2)}) %collective-permute-start.20) | collective-permute-done | bytes 1048608 | tf_op jit(solution)/shard_map/ppermute | solution.py:26
  219.3 6.6 %fusion.11 = f32[1024,640]{0,1:T(8,128)} fusion(bf16[1024,2048]{1,0:T(8,128)(2,1)} %constant_dynamic-update-slice_fusion, bf16[2048,1408]{0,1:T(8,128)(2,1)S(1)} %constant_dynamic-update-slice_fusion.15), kind=kOutput, calls=%fused_computation.38 | convolution fusion | flops 2684354560 | bytes 9437184 | tf_op jit(solution)/shard_map/dot_general | solution.py:21
  232.1 6.6 %collective-permute-done.22 = bf16[128,2048]{1,0:T(8,128)(2,1)S(1)} collective-permute-done((bf16[128,2048]{1,0:T(8,128)(2,1)S(1)}, bf16[128,2048]{1,0:T(8,128)(2,1)S(1)}, u32[]{:S(2)}, u32[]{:S(2)}) %collective-permute-start.22) | collective-permute-done | bytes 524320 | tf_op jit(solution)/shard_map/ppermute | solution.py:26
  239.5 10.5 %fusion.98 = f32[1024,1536]{0,1:T(8,128)S(1)} fusion(bf16[1024,2048]{1,0:T(8,128)(2,1)} %constant_dynamic-update-slice_fusion.5, bf16[2048,1536]{1,0:T(8,128)(2,1)} %all-gather.6.cloned.1.call-done), kind=kOutput, calls=%fused_computation.248 | convolution fusion | flops 6442450944 | bytes 16777216 | tf_op jit(solution)/shard_map/dot_general | solution.py:21
  250.0 3.2 multiply_convert_fusion.1
  254.4 11.3 %convolution_convert_fusion.2 = bf16[2048,1536]{1,0:T(8,128)(2,1)} fusion(bf16[1024,2048]{1,0:T(8,128)(2,1)} %constant_dynamic-update-slice_fusion.5, bf16[1024,768]{0,1:T(8,128)(2,1)} %get-tuple-element.86, bf16[1024,768]{0,1:T(8,128)(2,1)S(1)} %get-tuple-element.85), kind=kOutput, calls=%fused_computation.2 | convolution fusion | flops 6451888128 | bytes 13631488 | tf_op jit(solution)/shard_map/dot_general | solution.py:21
  270.6 9.9 %fusion.99 = f32[1024,1280]{0,1:T(8,128)S(1)} fusion(bf16[1024,2048]{1,0:T(8,128)(2,1)} %constant_dynamic-update-slice_fusion.5, bf16[2048,1280]{1,0:T(8,128)(2,1)} %all-gather.8.cloned.1.call-done), kind=kOutput, calls=%fused_computation.249 | convolution fusion | flops 5368709120 | bytes 14680064 | tf_op jit(solution)/shard_map/dot_general | solution.py:21
  280.5 2.7 multiply_convert_fusion.3
  284.7 2.0 copy-done.39
  286.7 4.3 fusion.32
  291.0 7.8 %add_convert_fusion = bf16[768,2048]{1,0:T(8,128)(2,1)} fusion(f32[768,2048]{1,0:T(8,128)S(1)} %fusion.32, bf16[2048,1536]{1,0:T(8,128)(2,1)S(1)} %bitcast.106, bf16[1024,768]{0,1:T(8,128)(2,1)} %get-tuple-element.86, bf16[1024,768]{0,1:T(8,128)(2,1)S(1)} %copy-done.34), kind=kOutput, calls=%fused_computation.3 | convolution fusion | flops 4839702528 | bytes 18874368 | tf_op jit(solution)/shard_map/dot_general | solution.py:21
  298.9 10.9 %convolution_convert_fusion.1 = bf16[2048,1280]{1,0:T(8,128)(2,1)} fusion(bf16[1024,2048]{1,0:T(8,128)(2,1)} %constant_dynamic-update-slice_fusion.5, bf16[1024,1280]{0,1:T(8,128)(2,1)S(1)} %pad_maximum_fusion), kind=kOutput, calls=%fused_computation.1 | convolution fusion | flops 5371330560 | bytes 12058624 | tf_op jit(solution)/shard_map/dot_general | solution.py:21
  309.8 2.9 fusion.93
  316.2 11.4 %convolution_convert_fusion = bf16[2048,1408]{1,0:T(8,128)(2,1)S(1)} fusion(bf16[1024,2048]{1,0:T(8,128)(2,1)} %constant_dynamic-update-slice_fusion, bf16[1024,640]{0,1:T(8,128)(2,1)S(1)} %copy-done.41, bf16[1024,768]{0,1:T(8,128)(2,1)S(1)} %copy-done.35), kind=kOutput, calls=%fused_computation | convolution fusion | flops 5914230784 | bytes 12845056 | tf_op jit(solution)/shard_map/dot_general | solution.py:21
  332.0 4.8 collective-permute-done.32
  341.1 5.1 convolution_add_fusion
  346.3 4.1 collective-permute-done.31
  352.7 2.1 constant_dynamic-update-slice_fusion.14
  357.0 3.1 fusion.63
  360.2 6.8 %convolution_convert_fusion.6 = bf16[768,2048]{1,0:T(8,128)(2,1)} fusion(bf16[2048,1408]{0,1:T(8,128)(2,1)S(1)} %bitcast.83, bf16[1024,640]{0,1:T(8,128)(2,1)S(1)} %copy-done.41, bf16[1024,768]{0,1:T(8,128)(2,1)S(1)} %copy-done.35), kind=kOutput, calls=%fused_computation.8 | convolution fusion | flops 4435083264 | bytes 11796480 | tf_op jit(solution)/shard_map/dot_general | solution.py:21
  367.0 8.4 %collective-permute-done.35 = bf16[256,2048]{1,0:T(8,128)(2,1)S(1)} collective-permute-done((bf16[256,2048]{1,0:T(8,128)(2,1)S(1)}, bf16[256,2048]{1,0:T(8,128)(2,1)S(1)}, u32[]{:S(2)}, u32[]{:S(2)}) %collective-permute-start.35) | collective-permute-done | bytes 1048608 | tf_op jit(solution)/shard_map/ppermute | solution.py:26
  380.9 6.6 %fusion.90 = (bf16[4,256,1408]{2,1,0:T(8,128)(2,1)S(1)}, f32[4,256,1408]{2,1,0:T(8,128)}) fusion(bf16[4,256,1408]{2,1,0:T(8,128)(2,1)} %collective-permute-done.39, bf16[4,2,256,1408]{3,2,1,0:T(8,128)(2,1)S(1)} %bitcast.85, s32[]{:T(128)S(6)} %select_n.138), kind=kLoop, calls=%fused_computation.240 | loop fusion | flops 5767168 | bytes 14417924 | tf_op jit(solution)/shard_map/convert_element_type | solution.py:126
  388.8 2.3 copy.39
  391.1 2.3 copy.41
  393.3 2.3 copy.40
  395.6 5.7 collective-permute-start.50
  402.1 2.6 constant_dynamic-slice_fusion.7
  404.6 2.9 copy.38
  411.3 4.7 convolution_convert_fusion.7
  420.8 5.3 convolution_convert_fusion.8.dm_ref
  426.1 13.8 %attend_back.1 = (bf16[1024,512]{1,0:T(8,128)(2,1)S(1)}, bf16[1024,256]{1,0:T(8,128)(2,1)S(1)}) custom-call(s32[2]{0:T(128)S(1)} %copy-done.1, bf16[1024,512]{1,0:T(8,128)(2,1)S(1)} %get-tuple-element.60.qr_ref, bf16[1024,256]{1,0:T(8,128)(2,1)S(1)} %copy-done.3, bf16[1024,512]{1,0:T(8,128)(2,1)S(1)} %convolution_convert_fusion.8.dm_ref, ...), custom_call_target="tpu_custom_call" | custom-call | flops 5368709120 | bytes 8388608 | tf_op jit(solution)/shard_map/attend_back/pallas_call | solution.py:284
  440.0 16.6 %collective-permute-done.50 = bf16[256,1408]{0,1:T(8,128)(2,1)} collective-permute-done((bf16[256,1408]{0,1:T(8,128)(2,1)}, bf16[256,1408]{0,1:T(8,128)(2,1)}, u32[]{:S(2)}, u32[]{:S(2)}) %collective-permute-start.50) | collective-permute-done | bytes 720928 | tf_op jit(solution)/shard_map/ppermute | solution.py:95
  458.2 3.9 fusion.89
  462.1 7.6 %convolution_convert_fusion.5 = bf16[2048,768]{1,0:T(8,128)(2,1)} fusion(bf16[1024,2048]{1,0:T(8,128)(2,1)} %fusion.70, bf16[1024,768]{1,0:T(8,128)(2,1)S(1)} %pad_maximum_fusion.3), kind=kOutput, calls=%fused_computation.7 | convolution fusion | flops 3222798336 | bytes 8912896 | tf_op jit(solution)/shard_map/dot_general | solution.py:21
  469.6 2.9 fusion.37
  473.6 2.5 convert_multiply_fusion.16
  486.9 3.1 convolution_convert_fusion.4
  498.4 8.7 %collective-permute-done.54 = bf16[256,512]{0,1:T(8,128)(2,1)S(1)} collective-permute-done((bf16[256,512]{0,1:T(8,128)(2,1)}, bf16[256,512]{0,1:T(8,128)(2,1)S(1)}, u32[]{:S(2)}, u32[]{:S(2)}) %collective-permute-start.54) | collective-permute-done | bytes 262176 | tf_op jit(solution)/shard_map/ppermute | solution.py:95
  508.7 12.4 %collective-permute-done.55 = bf16[256,512]{0,1:T(8,128)(2,1)} collective-permute-done((bf16[256,512]{0,1:T(8,128)(2,1)}, bf16[256,512]{0,1:T(8,128)(2,1)}, u32[]{:S(2)}, u32[]{:S(2)}) %collective-permute-start.55) | collective-permute-done | bytes 262176 | tf_op jit(solution)/shard_map/ppermute | solution.py:95
  527.3 8.6 %collective-permute-done.42 = bf16[128,2048]{1,0:T(8,128)(2,1)S(1)} collective-permute-done((bf16[128,2048]{1,0:T(8,128)(2,1)S(1)}, bf16[128,2048]{1,0:T(8,128)(2,1)S(1)}, u32[]{:S(2)}, u32[]{:S(2)}) %collective-permute-start.42) | collective-permute-done | bytes 524320 | tf_op jit(solution)/shard_map/ppermute | solution.py:26
  537.7 7.8 %collective-permute-done.47 = bf16[128,2048]{1,0:T(8,128)(2,1)S(1)} collective-permute-done((bf16[128,2048]{1,0:T(8,128)(2,1)S(1)}, bf16[128,2048]{1,0:T(8,128)(2,1)S(1)}, u32[]{:S(2)}, u32[]{:S(2)}) %collective-permute-start.47) | collective-permute-done | bytes 524320 | tf_op jit(solution)/shard_map/ppermute | solution.py:26
  552.0 8.7 %collective-permute-done.51 = f32[256,258]{1,0:T(8,128)S(1)} collective-permute-done((f32[256,258]{1,0:T(8,128)S(1)}, f32[256,258]{1,0:T(8,128)S(1)}, u32[]{:S(2)}, u32[]{:S(2)}) %collective-permute-start.51) | collective-permute-done | bytes 264224 | tf_op jit(solution)/shard_map/ppermute | solution.py:26
  562.2 3.6 fusion.26
  565.8 3.8 collective-permute-done.52
  (421 shorter events, 160.7 us)
Async XLA Ops:
  7.2 78.7 %all-gather.4.cloned.1.call-start = ((), (), s32[]{:S(2)}) async-start(), calls=%async_computation.3 | async-start | bytes 3538944 | tf_op jit(solution)/shard_map/all_gather | solution.py:76
  10.4 229.1 %all-gather.6.cloned.1.call-start = ((), (), s32[]{:S(2)}) async-start(), calls=%async_computation.4 | async-start | bytes 7077888 | tf_op jit(solution)/shard_map/all_gather | solution.py:76
  10.4 25.2 %collective-permute-start.1 = (bf16[256,2048]{1,0:T(8,128)(2,1)}, bf16[256,2048]{1,0:T(8,128)(2,1)S(1)}, u32[]{:S(2)}, u32[]{:S(2)}) collective-permute-start(bf16[256,2048]{1,0:T(8,128)(2,1)} %param.12), channel_id=1, source_target_pairs={{0,2},{1,3},{2,0},{3,1},{4,6},{5,7},{6,4},{7,5},{8,10},{9,11},{10,... | collective-permute-start | bytes 3145736 | tf_op jit(solution)/shard_map/ppermute | solution.py:26
  12.0 25.9 %collective-permute-start = (bf16[256,2048]{1,0:T(8,128)(2,1)}, bf16[256,2048]{1,0:T(8,128)(2,1)S(1)}, u32[]{:S(2)}, u32[]{:S(2)}) collective-permute-start(bf16[256,2048]{1,0:T(8,128)(2,1)} %param.12), channel_id=1, source_target_pairs={{0,1},{1,0},{2,3},{3,2},{4,5},{5,4},{6,7},{7,6},{8,9},{9,8},{10,11... | collective-permute-start | bytes 3145736 | tf_op jit(solution)/shard_map/ppermute | solution.py:26
  13.5 44.6 %collective-permute-start.7 = (bf16[256,512]{0,1:T(8,128)(2,1)}, bf16[256,512]{0,1:T(8,128)(2,1)}, u32[]{:S(2)}, u32[]{:S(2)}) collective-permute-start(bf16[256,512]{0,1:T(8,128)(2,1)} %bitcast.94), channel_id=1, source_target_pairs={{0,16},{4,20},{8,24},{12,28},{16,0},{20,4},{24,8},{28,12},{1,17},{... | collective-permute-start | bytes 786440 | tf_op jit(solution)/shard_map/ppermute | solution.py:95
  16.1 41.2 %collective-permute-start.5 = (bf16[256,512]{0,1:T(8,128)(2,1)}, bf16[256,512]{0,1:T(8,128)(2,1)}, u32[]{:S(2)}, u32[]{:S(2)}) collective-permute-start(bf16[256,512]{0,1:T(8,128)(2,1)} %bitcast.95), channel_id=1, source_target_pairs={{0,8},{4,12},{8,16},{12,20},{16,24},{20,28},{24,0},{28,4},{1,9},{5... | collective-permute-start | bytes 786440 | tf_op jit(solution)/shard_map/ppermute | solution.py:95
  16.1 47.3 %collective-permute-start.4 = (bf16[256,512]{0,1:T(8,128)(2,1)}, bf16[256,512]{0,1:T(8,128)(2,1)}, u32[]{:S(2)}, u32[]{:S(2)}) collective-permute-start(bf16[256,512]{0,1:T(8,128)(2,1)} %bitcast.96), channel_id=1, source_target_pairs={{0,4},{4,0},{8,12},{12,8},{16,20},{20,16},{24,28},{28,24},{1,5},{5... | collective-permute-start | bytes 786440 | tf_op jit(solution)/shard_map/ppermute | solution.py:90
  36.4 13.2 %collective-permute-start.2 = (bf16[128,2048]{1,0:T(8,128)(2,1)}, bf16[128,2048]{1,0:T(8,128)(2,1)}, u32[]{:S(2)}, u32[]{:S(2)}) collective-permute-start(bf16[128,2048]{1,0:T(8,128)(2,1)} %slice.399), channel_id=1, source_target_pairs={{0,1},{1,0},{2,3},{3,2},{4,5},{5,4},{6,7},{7,6},{8,9},{9,8},{10,11... | collective-permute-start | bytes 1572872 | tf_op jit(solution)/shard_map/ppermute | solution.py:26
  38.8 12.9 %collective-permute-start.3 = (bf16[128,2048]{1,0:T(8,128)(2,1)}, bf16[128,2048]{1,0:T(8,128)(2,1)}, u32[]{:S(2)}, u32[]{:S(2)}) collective-permute-start(bf16[128,2048]{1,0:T(8,128)(2,1)} %slice.400), channel_id=1, source_target_pairs={{0,2},{1,3},{2,0},{3,1},{4,6},{5,7},{6,4},{7,5},{8,10},{9,11},{10,... | collective-permute-start | bytes 1572872 | tf_op jit(solution)/shard_map/ppermute | solution.py:26
  49.7 13.7 %collective-permute-start.9 = (bf16[256,512]{0,1:T(8,128)(2,1)}, bf16[256,512]{0,1:T(8,128)(2,1)}, u32[]{:S(2)}, u32[]{:S(2)}) collective-permute-start(bf16[256,512]{0,1:T(8,128)(2,1)} %bitcast.97), channel_id=1, source_target_pairs={{0,24},{4,28},{8,0},{12,4},{16,8},{20,12},{24,16},{28,20},{1,25},{... | collective-permute-start | bytes 786440 | tf_op jit(solution)/shard_map/ppermute | solution.py:95
  51.8 218.8 %all-gather.8.cloned.1.call-start = ((), (), s32[]{:S(2)}) async-start(), calls=%async_computation.5 | async-start | bytes 5898240 | tf_op jit(solution)/shard_map/all_gather | solution.py:76
  57.3 9.5 %collective-permute-start.6 = (bf16[256,512]{0,1:T(8,128)(2,1)}, bf16[256,512]{0,1:T(8,128)(2,1)S(1)}, u32[]{:S(2)}, u32[]{:S(2)}) collective-permute-start(bf16[256,512]{0,1:T(8,128)(2,1)} %collective-permute-done.5), channel_id=1, source_target_pairs={{0,4},{4,0},{8,12},{12,8},{16,20},{20,16},{24,28},{28,24},{1,5},{5... | collective-permute-start | bytes 786440 | tf_op jit(solution)/shard_map/ppermute | solution.py:90
  58.1 36.1 %copy-start = (s32[2]{0:T(128)}, s32[2]{0:T(128)S(1)}, u32[]{:S(2)}) copy-start(s32[2]{0:T(128)S(1)} %pad_add_fusion.where_ref) | copy-start | bytes 28
  58.1 11.1 %collective-permute-start.8 = (bf16[256,512]{0,1:T(8,128)(2,1)}, bf16[256,512]{0,1:T(8,128)(2,1)S(1)}, u32[]{:S(2)}, u32[]{:S(2)}) collective-permute-start(bf16[256,512]{0,1:T(8,128)(2,1)} %collective-permute-done.7), channel_id=1, source_target_pairs={{0,4},{4,0},{8,12},{12,8},{16,20},{20,16},{24,28},{28,24},{1,5},{5... | collective-permute-start | bytes 786440 | tf_op jit(solution)/shard_map/ppermute | solution.py:90
  63.4 8.2 %collective-permute-start.10 = (bf16[256,512]{0,1:T(8,128)(2,1)}, bf16[256,512]{0,1:T(8,128)(2,1)S(1)}, u32[]{:S(2)}, u32[]{:S(2)}) collective-permute-start(bf16[256,512]{0,1:T(8,128)(2,1)} %collective-permute-done.9), channel_id=1, source_target_pairs={{0,4},{4,0},{8,12},{12,8},{16,20},{20,16},{24,28},{28,24},{1,5},{5... | collective-permute-start | bytes 786440 | tf_op jit(solution)/shard_map/ppermute | solution.py:90
  75.4 92.3 %collective-permute-start.28 = (bf16[256,1408]{0,1:T(8,128)(2,1)}, bf16[256,1408]{0,1:T(8,128)(2,1)}, u32[]{:S(2)}, u32[]{:S(2)}) collective-permute-start(bf16[256,1408]{0,1:T(8,128)(2,1)} %bitcast.4), channel_id=1, source_target_pairs={{0,24},{4,28},{8,0},{12,4},{16,8},{20,12},{24,16},{28,20},{1,25},{... | collective-permute-start | bytes 2162696 | tf_op jit(solution)/shard_map/ppermute | solution.py:95
  75.4 92.3 %collective-permute-start.26 = (bf16[256,1408]{0,1:T(8,128)(2,1)}, bf16[256,1408]{0,1:T(8,128)(2,1)}, u32[]{:S(2)}, u32[]{:S(2)}) collective-permute-start(bf16[256,1408]{0,1:T(8,128)(2,1)} %bitcast.4), channel_id=1, source_target_pairs={{0,16},{4,20},{8,24},{12,28},{16,0},{20,4},{24,8},{28,12},{1,17},{... | collective-permute-start | bytes 2162696 | tf_op jit(solution)/shard_map/ppermute | solution.py:95
  78.2 27.7 %collective-permute-start.12 = (bf16[256,2048]{1,0:T(8,128)(2,1)}, bf16[256,2048]{1,0:T(8,128)(2,1)}, u32[]{:S(2)}, u32[]{:S(2)}) collective-permute-start(bf16[256,2048]{1,0:T(8,128)(2,1)} %fusion.30), channel_id=1, source_target_pairs={{0,2},{1,3},{2,0},{3,1},{4,6},{5,7},{6,4},{7,5},{8,10},{9,11},{10,... | collective-permute-start | bytes 3145736 | tf_op jit(solution)/shard_map/ppermute | solution.py:26
  78.9 27.0 %collective-permute-start.11 = (bf16[256,2048]{1,0:T(8,128)(2,1)}, bf16[256,2048]{1,0:T(8,128)(2,1)}, u32[]{:S(2)}, u32[]{:S(2)}) collective-permute-start(bf16[256,2048]{1,0:T(8,128)(2,1)} %fusion.30), channel_id=1, source_target_pairs={{0,1},{1,0},{2,3},{3,2},{4,5},{5,4},{6,7},{7,6},{8,9},{9,8},{10,11... | collective-permute-start | bytes 3145736 | tf_op jit(solution)/shard_map/ppermute | solution.py:26
  108.0 41.3 %collective-permute-start.13 = (bf16[256,2048]{1,0:T(8,128)(2,1)S(1)}, bf16[256,2048]{1,0:T(8,128)(2,1)S(1)}, u32[]{:S(2)}, u32[]{:S(2)}) collective-permute-start(bf16[256,2048]{1,0:T(8,128)(2,1)S(1)} %pad_maximum_fusion.6), channel_id=1, source_target_pairs={{0,1},{1,0},{2,3},{3,2},{4,5},{5,4},{6,7},{7,6},{8,9},{9,8},{10,11... | collective-permute-start | bytes 3145736 | tf_op jit(solution)/shard_map/ppermute | solution.py:26
  109.7 37.9 %collective-permute-start.15 = (bf16[256,2048]{1,0:T(8,128)(2,1)S(1)}, bf16[256,2048]{1,0:T(8,128)(2,1)S(1)}, u32[]{:S(2)}, u32[]{:S(2)}) collective-permute-start(bf16[256,2048]{1,0:T(8,128)(2,1)S(1)} %pad_maximum_fusion.7), channel_id=1, source_target_pairs={{0,2},{1,3},{2,0},{3,1},{4,6},{5,7},{6,4},{7,5},{8,10},{9,11},{10,... | collective-permute-start | bytes 3145736 | tf_op jit(solution)/shard_map/ppermute | solution.py:26
  114.6 29.5 %collective-permute-start.17 = (bf16[128,2048]{1,0:T(8,128)(2,1)S(1)}, bf16[128,2048]{1,0:T(8,128)(2,1)S(1)}, u32[]{:S(2)}, u32[]{:S(2)}) collective-permute-start(bf16[128,2048]{1,0:T(8,128)(2,1)S(1)} %slice.414), channel_id=1, source_target_pairs={{0,1},{1,0},{2,3},{3,2},{4,5},{5,4},{6,7},{7,6},{8,9},{9,8},{10,11... | collective-permute-start | bytes 1572872 | tf_op jit(solution)/shard_map/ppermute | solution.py:26
  117.2 32.4 %copy-start.16 = (bf16[2048,1408]{0,1:T(8,128)(2,1)}, bf16[2048,1408]{0,1:T(8,128)(2,1)S(1)}, u32[]{:S(2)}) copy-start(bf16[2048,1408]{0,1:T(8,128)(2,1)S(1)} %constant_dynamic-update-slice_fusion.22) | copy-start | bytes 17301508
  144.0 44.1 %collective-permute-start.24 = (bf16[256,1408]{0,1:T(8,128)(2,1)}, bf16[256,1408]{0,1:T(8,128)(2,1)}, u32[]{:S(2)}, u32[]{:S(2)}) collective-permute-start(bf16[256,1408]{0,1:T(8,128)(2,1)} %bitcast.4), channel_id=1, source_target_pairs={{0,8},{4,12},{8,16},{12,20},{16,24},{20,28},{24,0},{28,4},{1,9},{5... | collective-permute-start | bytes 2162696 | tf_op jit(solution)/shard_map/ppermute | solution.py:95
  147.6 14.8 %collective-permute-start.18 = (bf16[128,2048]{1,0:T(8,128)(2,1)S(1)}, bf16[128,2048]{1,0:T(8,128)(2,1)S(1)}, u32[]{:S(2)}, u32[]{:S(2)}) collective-permute-start(bf16[128,2048]{1,0:T(8,128)(2,1)S(1)} %slice.415), channel_id=1, source_target_pairs={{0,2},{1,3},{2,0},{3,1},{4,6},{5,7},{6,4},{7,5},{8,10},{9,11},{10,... | collective-permute-start | bytes 1572872 | tf_op jit(solution)/shard_map/ppermute | solution.py:26
  151.7 37.1 %collective-permute-start.14 = (bf16[128,2048]{1,0:T(8,128)(2,1)}, bf16[128,2048]{1,0:T(8,128)(2,1)}, u32[]{:S(2)}, u32[]{:S(2)}) collective-permute-start(bf16[128,2048]{1,0:T(8,128)(2,1)} %get-tuple-element.109), channel_id=1, source_target_pairs={{0,2},{1,3},{2,0},{3,1},{4,6},{5,7},{6,4},{7,5},{8,10},{9,11},{10,... | collective-permute-start | bytes 1572872 | tf_op jit(solution)/shard_map/ppermute | solution.py:26
  162.4 26.9 %collective-permute-start.16 = (bf16[128,2048]{1,0:T(8,128)(2,1)}, bf16[128,2048]{1,0:T(8,128)(2,1)}, u32[]{:S(2)}, u32[]{:S(2)}) collective-permute-start(bf16[128,2048]{1,0:T(8,128)(2,1)} %get-tuple-element.110), channel_id=1, source_target_pairs={{0,1},{1,0},{2,3},{3,2},{4,5},{5,4},{6,7},{7,6},{8,9},{9,8},{10,11... | collective-permute-start | bytes 1572872 | tf_op jit(solution)/shard_map/ppermute | solution.py:26
  164.8 256.0 %reduce-scatter.4.cloned.1.call-start = ((), (), s32[]{:S(2)}) async-start(), calls=%async_computation.6 | async-start | bytes 7077888 | tf_op jit(solution)/shard_map/reduce_scatter | solution.py:80
  188.2 7.0 %collective-permute-start.23 = (bf16[256,1408]{0,1:T(8,128)(2,1)}, bf16[256,1408]{0,1:T(8,128)(2,1)S(1)}, u32[]{:S(2)}, u32[]{:S(2)}) collective-permute-start(bf16[256,1408]{0,1:T(8,128)(2,1)} %bitcast.4), channel_id=1, source_target_pairs={{0,4},{4,0},{8,12},{12,8},{16,20},{20,16},{24,28},{28,24},{1,5},{5... | collective-permute-start | bytes 2162696 | tf_op jit(solution)/shard_map/ppermute | solution.py:90
  188.2 9.8 %collective-permute-start.25 = (bf16[256,1408]{0,1:T(8,128)(2,1)}, bf16[256,1408]{0,1:T(8,128)(2,1)S(1)}, u32[]{:S(2)}, u32[]{:S(2)}) collective-permute-start(bf16[256,1408]{0,1:T(8,128)(2,1)} %collective-permute-done.24), channel_id=1, source_target_pairs={{0,4},{4,0},{8,12},{12,8},{16,20},{20,16},{24,28},{28,24},{1,5},{5... | collective-permute-start | bytes 2162696 | tf_op jit(solution)/shard_map/ppermute | solution.py:90
  188.7 10.6 %collective-permute-start.27 = (bf16[256,1408]{0,1:T(8,128)(2,1)}, bf16[256,1408]{0,1:T(8,128)(2,1)S(1)}, u32[]{:S(2)}, u32[]{:S(2)}) collective-permute-start(bf16[256,1408]{0,1:T(8,128)(2,1)} %collective-permute-done.26), channel_id=1, source_target_pairs={{0,4},{4,0},{8,12},{12,8},{16,20},{20,16},{24,28},{28,24},{1,5},{5... | collective-permute-start | bytes 2162696 | tf_op jit(solution)/shard_map/ppermute | solution.py:90
  188.7 11.9 %collective-permute-start.29 = (bf16[256,1408]{0,1:T(8,128)(2,1)}, bf16[256,1408]{0,1:T(8,128)(2,1)S(1)}, u32[]{:S(2)}, u32[]{:S(2)}) collective-permute-start(bf16[256,1408]{0,1:T(8,128)(2,1)} %collective-permute-done.28), channel_id=1, source_target_pairs={{0,4},{4,0},{8,12},{12,8},{16,20},{20,16},{24,28},{28,24},{1,5},{5... | collective-permute-start | bytes 2162696 | tf_op jit(solution)/shard_map/ppermute | solution.py:90
  192.4 25.1 %collective-permute-start.20 = (bf16[256,2048]{1,0:T(8,128)(2,1)S(1)}, bf16[256,2048]{1,0:T(8,128)(2,1)S(1)}, u32[]{:S(2)}, u32[]{:S(2)}) collective-permute-start(bf16[256,2048]{1,0:T(8,128)(2,1)S(1)} %multiply_convert_fusion.6), channel_id=1, source_target_pairs={{0,2},{1,3},{2,0},{3,1},{4,6},{5,7},{6,4},{7,5},{8,10},{9,11},{10,... | collective-permute-start | bytes 3145736 | tf_op jit(solution)/shard_map/ppermute | solution.py:26
  195.2 30.7 %collective-permute-start.19 = (bf16[256,2048]{1,0:T(8,128)(2,1)S(1)}, bf16[256,2048]{1,0:T(8,128)(2,1)S(1)}, u32[]{:S(2)}, u32[]{:S(2)}) collective-permute-start(bf16[256,2048]{1,0:T(8,128)(2,1)S(1)} %multiply_convert_fusion.6), channel_id=1, source_target_pairs={{0,1},{1,0},{2,3},{3,2},{4,5},{5,4},{6,7},{7,6},{8,9},{9,8},{10,11... | collective-permute-start | bytes 3145736 | tf_op jit(solution)/shard_map/ppermute | solution.py:26
  217.5 13.7 %collective-permute-start.21 = (bf16[128,2048]{1,0:T(8,128)(2,1)S(1)}, bf16[128,2048]{1,0:T(8,128)(2,1)S(1)}, u32[]{:S(2)}, u32[]{:S(2)}) collective-permute-start(bf16[128,2048]{1,0:T(8,128)(2,1)S(1)} %slice.416), channel_id=1, source_target_pairs={{0,1},{1,0},{2,3},{3,2},{4,5},{5,4},{6,7},{7,6},{8,9},{9,8},{10,11... | collective-permute-start | bytes 1572872 | tf_op jit(solution)/shard_map/ppermute | solution.py:26
  226.0 12.7 %collective-permute-start.22 = (bf16[128,2048]{1,0:T(8,128)(2,1)S(1)}, bf16[128,2048]{1,0:T(8,128)(2,1)S(1)}, u32[]{:S(2)}, u32[]{:S(2)}) collective-permute-start(bf16[128,2048]{1,0:T(8,128)(2,1)S(1)} %slice.417), channel_id=1, source_target_pairs={{0,2},{1,3},{2,0},{3,1},{4,6},{5,7},{6,4},{7,5},{8,10},{9,11},{10,... | collective-permute-start | bytes 1572872 | tf_op jit(solution)/shard_map/ppermute | solution.py:26
  265.7 206.9 %reduce-scatter.6.cloned.1.call-start = ((), (), s32[]{:S(2)}) async-start(), calls=%async_computation.7 | async-start | bytes 5898240 | tf_op jit(solution)/shard_map/reduce_scatter | solution.py:80
  312.7 233.3 %reduce-scatter.8.cloned.1.call-start = ((), (), s32[]{:S(2)}) async-start(), calls=%async_computation.8 | async-start | bytes 3538944 | tf_op jit(solution)/shard_map/reduce_scatter | solution.py:80
  314.3 22.5 %collective-permute-start.32 = (bf16[256,2048]{1,0:T(8,128)(2,1)S(1)}, bf16[256,2048]{1,0:T(8,128)(2,1)S(1)}, u32[]{:S(2)}, u32[]{:S(2)}) collective-permute-start(bf16[256,2048]{1,0:T(8,128)(2,1)S(1)} %pad_maximum_fusion.9), channel_id=1, source_target_pairs={{0,2},{1,3},{2,0},{3,1},{4,6},{5,7},{6,4},{7,5},{8,10},{9,11},{10,... | collective-permute-start | bytes 3145736 | tf_op jit(solution)/shard_map/ppermute | solution.py:26
  316.1 22.3 %collective-permute-start.30 = (bf16[256,2048]{1,0:T(8,128)(2,1)S(1)}, bf16[256,2048]{1,0:T(8,128)(2,1)S(1)}, u32[]{:S(2)}, u32[]{:S(2)}) collective-permute-start(bf16[256,2048]{1,0:T(8,128)(2,1)S(1)} %pad_maximum_fusion.8), channel_id=1, source_target_pairs={{0,1},{1,0},{2,3},{3,2},{4,5},{5,4},{6,7},{7,6},{8,9},{9,8},{10,11... | collective-permute-start | bytes 3145736 | tf_op jit(solution)/shard_map/ppermute | solution.py:26
  329.4 51.5 %collective-permute-start.39 = (bf16[4,256,1408]{2,1,0:T(8,128)(2,1)}, bf16[4,256,1408]{2,1,0:T(8,128)(2,1)}, u32[]{:S(2)}, u32[]{:S(2)}) collective-permute-start(bf16[4,256,1408]{2,1,0:T(8,128)(2,1)} %dynamic-slice_bitcast_fusion), channel_id=1, source_target_pairs={{0,4},{4,0},{8,12},{12,8},{16,20},{20,16},{24,28},{28,24},{1,5},{5... | collective-permute-start | bytes 8650760 | tf_op jit(solution)/shard_map/ppermute | solution.py:90
  340.2 10.2 %collective-permute-start.31 = (bf16[128,2048]{1,0:T(8,128)(2,1)S(1)}, bf16[128,2048]{1,0:T(8,128)(2,1)S(1)}, u32[]{:S(2)}, u32[]{:S(2)}) collective-permute-start(bf16[128,2048]{1,0:T(8,128)(2,1)S(1)} %get-tuple-element.103), channel_id=1, source_target_pairs={{0,2},{1,3},{2,0},{3,1},{4,6},{5,7},{6,4},{7,5},{8,10},{9,11},{10,... | collective-permute-start | bytes 1572872 | tf_op jit(solution)/shard_map/ppermute | solution.py:26
  340.6 10.2 %collective-permute-start.33 = (bf16[128,2048]{1,0:T(8,128)(2,1)S(1)}, bf16[128,2048]{1,0:T(8,128)(2,1)S(1)}, u32[]{:S(2)}, u32[]{:S(2)}) collective-permute-start(bf16[128,2048]{1,0:T(8,128)(2,1)S(1)} %get-tuple-element.104), channel_id=1, source_target_pairs={{0,1},{1,0},{2,3},{3,2},{4,5},{5,4},{6,7},{7,6},{8,9},{9,8},{10,11... | collective-permute-start | bytes 1572872 | tf_op jit(solution)/shard_map/ppermute | solution.py:26
  354.8 20.7 %collective-permute-start.35 = (bf16[256,2048]{1,0:T(8,128)(2,1)S(1)}, bf16[256,2048]{1,0:T(8,128)(2,1)S(1)}, u32[]{:S(2)}, u32[]{:S(2)}) collective-permute-start(bf16[256,2048]{1,0:T(8,128)(2,1)S(1)} %get-tuple-element.83), channel_id=1, source_target_pairs={{0,2},{1,3},{2,0},{3,1},{4,6},{5,7},{6,4},{7,5},{8,10},{9,11},{10,... | collective-permute-start | bytes 3145736 | tf_op jit(solution)/shard_map/ppermute | solution.py:26
  356.2 22.3 %collective-permute-start.34 = (bf16[256,2048]{1,0:T(8,128)(2,1)S(1)}, bf16[256,2048]{1,0:T(8,128)(2,1)S(1)}, u32[]{:S(2)}, u32[]{:S(2)}) collective-permute-start(bf16[256,2048]{1,0:T(8,128)(2,1)S(1)} %get-tuple-element.83), channel_id=1, source_target_pairs={{0,1},{1,0},{2,3},{3,2},{4,5},{5,4},{6,7},{7,6},{8,9},{9,8},{10,11... | collective-permute-start | bytes 3145736 | tf_op jit(solution)/shard_map/ppermute | solution.py:26
  376.3 31.2 %collective-permute-start.36 = (bf16[128,2048]{1,0:T(8,128)(2,1)}, bf16[128,2048]{1,0:T(8,128)(2,1)}, u32[]{:S(2)}, u32[]{:S(2)}) collective-permute-start(bf16[128,2048]{1,0:T(8,128)(2,1)} %slice.441), channel_id=1, source_target_pairs={{0,1},{1,0},{2,3},{3,2},{4,5},{5,4},{6,7},{7,6},{8,9},{9,8},{10,11... | collective-permute-start | bytes 1572872 | tf_op jit(solution)/shard_map/ppermute | solution.py:26
  379.3 28.2 %collective-permute-start.37 = (bf16[128,2048]{1,0:T(8,128)(2,1)}, bf16[128,2048]{1,0:T(8,128)(2,1)}, u32[]{:S(2)}, u32[]{:S(2)}) collective-permute-start(bf16[128,2048]{1,0:T(8,128)(2,1)} %slice.442), channel_id=1, source_target_pairs={{0,2},{1,3},{2,0},{3,1},{4,6},{5,7},{6,4},{7,5},{8,10},{9,11},{10,... | collective-permute-start | bytes 1572872 | tf_op jit(solution)/shard_map/ppermute | solution.py:26
  395.6 62.5 %collective-permute-start.49 = (bf16[256,1408]{0,1:T(8,128)(2,1)}, bf16[256,1408]{0,1:T(8,128)(2,1)}, u32[]{:S(2)}, u32[]{:S(2)}) collective-permute-start(bf16[256,1408]{0,1:T(8,128)(2,1)} %bitcast.92), channel_id=1, source_target_pairs={{0,16},{4,20},{8,24},{12,28},{16,0},{20,4},{24,8},{28,12},{1,17},{... | collective-permute-start | bytes 2162696 | tf_op jit(solution)/shard_map/ppermute | solution.py:95
  395.6 61.0 %collective-permute-start.50 = (bf16[256,1408]{0,1:T(8,128)(2,1)}, bf16[256,1408]{0,1:T(8,128)(2,1)}, u32[]{:S(2)}, u32[]{:S(2)}) collective-permute-start(bf16[256,1408]{0,1:T(8,128)(2,1)} %bitcast.93), channel_id=1, source_target_pairs={{0,24},{4,28},{8,0},{12,4},{16,8},{20,12},{24,16},{28,20},{1,25},{... | collective-permute-start | bytes 2162696 | tf_op jit(solution)/shard_map/ppermute | solution.py:95
  401.3 56.8 %collective-permute-start.48 = (bf16[256,1408]{0,1:T(8,128)(2,1)}, bf16[256,1408]{0,1:T(8,128)(2,1)}, u32[]{:S(2)}, u32[]{:S(2)}) collective-permute-start(bf16[256,1408]{0,1:T(8,128)(2,1)} %bitcast.91), channel_id=1, source_target_pairs={{0,8},{4,12},{8,16},{12,20},{16,24},{20,28},{24,0},{28,4},{1,9},{5... | collective-permute-start | bytes 2162696 | tf_op jit(solution)/shard_map/ppermute | solution.py:95
  417.2 40.8 %collective-permute-start.43 = (bf16[4,256,512]{2,1,0:T(8,128)(2,1)}, bf16[4,256,512]{2,1,0:T(8,128)(2,1)}, u32[]{:S(2)}, u32[]{:S(2)}) collective-permute-start(bf16[4,256,512]{2,1,0:T(8,128)(2,1)} %dynamic-slice_bitcast_fusion.1), channel_id=1, source_target_pairs={{0,4},{4,0},{8,12},{12,8},{16,20},{20,16},{24,28},{28,24},{1,5},{5... | collective-permute-start | bytes 3145736 | tf_op jit(solution)/shard_map/ppermute | solution.py:90
  418.8 64.7 %collective-permute-start.41 = (bf16[256,2048]{1,0:T(8,128)(2,1)}, bf16[256,2048]{1,0:T(8,128)(2,1)}, u32[]{:S(2)}, u32[]{:S(2)}) collective-permute-start(bf16[256,2048]{1,0:T(8,128)(2,1)} %pad_maximum_fusion.11), channel_id=1, source_target_pairs={{0,2},{1,3},{2,0},{3,1},{4,6},{5,7},{6,4},{7,5},{8,10},{9,11},{10,... | collective-permute-start | bytes 3145736 | tf_op jit(solution)/shard_map/ppermute | solution.py:26
  456.6 26.9 %collective-permute-start.38 = (bf16[256,2048]{1,0:T(8,128)(2,1)}, bf16[256,2048]{1,0:T(8,128)(2,1)}, u32[]{:S(2)}, u32[]{:S(2)}) collective-permute-start(bf16[256,2048]{1,0:T(8,128)(2,1)} %pad_maximum_fusion.10), channel_id=1, source_target_pairs={{0,1},{1,0},{2,3},{3,2},{4,5},{5,4},{6,7},{7,6},{8,9},{9,8},{10,11... | collective-permute-start | bytes 3145736 | tf_op jit(solution)/shard_map/ppermute | solution.py:26
  480.2 26.9 %collective-permute-start.54 = (bf16[256,512]{0,1:T(8,128)(2,1)}, bf16[256,512]{0,1:T(8,128)(2,1)S(1)}, u32[]{:S(2)}, u32[]{:S(2)}) collective-permute-start(bf16[256,512]{0,1:T(8,128)(2,1)} %bitcast.19), channel_id=1, source_target_pairs={{0,16},{4,20},{8,24},{12,28},{16,0},{20,4},{24,8},{28,12},{1,17},{... | collective-permute-start | bytes 786440 | tf_op jit(solution)/shard_map/ppermute | solution.py:95
  480.2 40.9 %collective-permute-start.55 = (bf16[256,512]{0,1:T(8,128)(2,1)}, bf16[256,512]{0,1:T(8,128)(2,1)}, u32[]{:S(2)}, u32[]{:S(2)}) collective-permute-start(bf16[256,512]{0,1:T(8,128)(2,1)} %bitcast.20), channel_id=1, source_target_pairs={{0,24},{4,28},{8,0},{12,4},{16,8},{20,12},{24,16},{28,20},{1,25},{... | collective-permute-start | bytes 786440 | tf_op jit(solution)/shard_map/ppermute | solution.py:95
  481.0 40.2 %collective-permute-start.53 = (bf16[256,512]{0,1:T(8,128)(2,1)}, bf16[256,512]{0,1:T(8,128)(2,1)}, u32[]{:S(2)}, u32[]{:S(2)}) collective-permute-start(bf16[256,512]{0,1:T(8,128)(2,1)} %bitcast.18), channel_id=1, source_target_pairs={{0,8},{4,12},{8,16},{12,20},{16,24},{20,28},{24,0},{28,4},{1,9},{5... | collective-permute-start | bytes 786440 | tf_op jit(solution)/shard_map/ppermute | solution.py:95
  490.4 32.8 %collective-permute-start.46 = (bf16[256,2048]{1,0:T(8,128)(2,1)S(1)}, bf16[256,2048]{1,0:T(8,128)(2,1)S(1)}, u32[]{:S(2)}, u32[]{:S(2)}) collective-permute-start(bf16[256,2048]{1,0:T(8,128)(2,1)S(1)} %pad_maximum_fusion.13), channel_id=1, source_target_pairs={{0,2},{1,3},{2,0},{3,1},{4,6},{5,7},{6,4},{7,5},{8,10},{9,11},{10,... | collective-permute-start | bytes 3145736 | tf_op jit(solution)/shard_map/ppermute | solution.py:26
  492.0 31.4 %collective-permute-start.44 = (bf16[256,2048]{1,0:T(8,128)(2,1)S(1)}, bf16[256,2048]{1,0:T(8,128)(2,1)S(1)}, u32[]{:S(2)}, u32[]{:S(2)}) collective-permute-start(bf16[256,2048]{1,0:T(8,128)(2,1)S(1)} %pad_maximum_fusion.12), channel_id=1, source_target_pairs={{0,1},{1,0},{2,3},{3,2},{4,5},{5,4},{6,7},{7,6},{8,9},{9,8},{10,11... | collective-permute-start | bytes 3145736 | tf_op jit(solution)/shard_map/ppermute | solution.py:26
  507.1 20.2 %collective-permute-start.40 = (bf16[128,2048]{1,0:T(8,128)(2,1)S(1)}, bf16[128,2048]{1,0:T(8,128)(2,1)S(1)}, u32[]{:S(2)}, u32[]{:S(2)}) collective-permute-start(bf16[128,2048]{1,0:T(8,128)(2,1)S(1)} %get-tuple-element.97), channel_id=1, source_target_pairs={{0,2},{1,3},{2,0},{3,1},{4,6},{5,7},{6,4},{7,5},{8,10},{9,11},{10,... | collective-permute-start | bytes 1572872 | tf_op jit(solution)/shard_map/ppermute | solution.py:26
  521.1 14.8 %collective-permute-start.42 = (bf16[128,2048]{1,0:T(8,128)(2,1)S(1)}, bf16[128,2048]{1,0:T(8,128)(2,1)S(1)}, u32[]{:S(2)}, u32[]{:S(2)}) collective-permute-start(bf16[128,2048]{1,0:T(8,128)(2,1)S(1)} %get-tuple-element.98), channel_id=1, source_target_pairs={{0,1},{1,0},{2,3},{3,2},{4,5},{5,4},{6,7},{7,6},{8,9},{9,8},{10,11... | collective-permute-start | bytes 1572872 | tf_op jit(solution)/shard_map/ppermute | solution.py:26
  524.0 13.7 %collective-permute-start.45 = (bf16[128,2048]{1,0:T(8,128)(2,1)S(1)}, bf16[128,2048]{1,0:T(8,128)(2,1)S(1)}, u32[]{:S(2)}, u32[]{:S(2)}) collective-permute-start(bf16[128,2048]{1,0:T(8,128)(2,1)S(1)} %get-tuple-element.91), channel_id=1, source_target_pairs={{0,2},{1,3},{2,0},{3,1},{4,6},{5,7},{6,4},{7,5},{8,10},{9,11},{10,... | collective-permute-start | bytes 1572872 | tf_op jit(solution)/shard_map/ppermute | solution.py:26
  525.5 20.0 %collective-permute-start.47 = (bf16[128,2048]{1,0:T(8,128)(2,1)S(1)}, bf16[128,2048]{1,0:T(8,128)(2,1)S(1)}, u32[]{:S(2)}, u32[]{:S(2)}) collective-permute-start(bf16[128,2048]{1,0:T(8,128)(2,1)S(1)} %get-tuple-element.92), channel_id=1, source_target_pairs={{0,1},{1,0},{2,3},{3,2},{4,5},{5,4},{6,7},{7,6},{8,9},{9,8},{10,11... | collective-permute-start | bytes 1572872 | tf_op jit(solution)/shard_map/ppermute | solution.py:26
  551.2 9.5 %collective-permute-start.51 = (f32[256,258]{1,0:T(8,128)S(1)}, f32[256,258]{1,0:T(8,128)S(1)}, u32[]{:S(2)}, u32[]{:S(2)}) collective-permute-start(f32[256,258]{1,0:T(8,128)S(1)} %pad_maximum_fusion.19), channel_id=1, source_target_pairs={{0,1},{1,0},{2,3},{3,2},{4,5},{5,4},{6,7},{7,6},{8,9},{9,8},{10,11... | collective-permute-start | bytes 792584 | tf_op jit(solution)/shard_map/ppermute | solution.py:26
  560.9 8.7 %collective-permute-start.52 = (f32[256,258]{1,0:T(8,128)S(1)}, f32[256,258]{1,0:T(8,128)S(1)}, u32[]{:S(2)}, u32[]{:S(2)}) collective-permute-start(f32[256,258]{1,0:T(8,128)S(1)} %fusion.131), channel_id=1, source_target_pairs={{0,2},{1,3},{2,0},{3,1},{4,6},{5,7},{6,4},{7,5},{8,10},{9,11},{10,... | collective-permute-start | bytes 792584 | tf_op jit(solution)/shard_map/ppermute | solution.py:26
  (85 other events, 531.3 us)
Sparse Core Ops, SparseCore 0:
  10.5 53.9 all-gather.3
  66.7 114.4 all-gather.5
  183.4 59.4 all-gather.7
  265.8 67.3 reduce-scatter.3
  335.3 58.2 reduce-scatter.5
  472.7 60.4 reduce-scatter.7

commit v4 on v3

--- a/solution.py
+++ b/solution.py
@@ -78,56 +78,6 @@
 
 def scatter_dp(partial):
     return lax.psum_scatter(partial, "dp", scatter_dimension=0, tiled=True).astype(f32)
-
-
-def lines_of():
-    size = lax.axis_size("dp")
-    index = lax.axis_index("dp").astype(jnp.int32)
-    return size // 2, index // 2, index % 2
-
-
-def swap_cores(value):
-    return lax.ppermute(value, "dp", [(i, i ^ 1) for i in range(lax.axis_size("dp"))])
-
-
-def shift_lines(value, step):
-    size = lax.axis_size("dp")
-    return lax.ppermute(value, "dp", [(i, (i + 2 * step) % size) for i in range(size)])
-
-
-def send_lines(shard):
-    return [shard] + [shift_lines(shard, step) for step in range(1, lines_of()[0])]
-
-
-def join_lines(pieces, *ready):
-    lines, line, core = lines_of()
-    rows = pieces[0].shape[0]
-    whole = jnp.zeros((2 * lines * rows, pieces[0].shape[1]), pieces[0].dtype)
-    for step, piece in enumerate(pieces):
-        base = 2 * ((line - step) % lines)
-        other = swap_cores(after(piece, *ready) if ready else piece)
-        whole = lax.dynamic_update_slice(whole, piece, ((base + core) * rows, 0))
-        whole = lax.dynamic_update_slice(whole, other, ((base + 1 - core) * rows, 0))
-    return whole
-
-
-pick = functools.partial(lax.dynamic_index_in_dim, keepdims=False)
-
-
-def sum_cores(partial, *ready):
-    lines, _, core = lines_of()
-    blocks = partial.reshape(lines, 2, -1, partial.shape[1])
-    other = after(swap_cores(pick(blocks, 1 - core, 1)), *ready)
-    return pick(blocks, core, 1).astype(f32) + other.astype(f32)
-
-
-def sum_lines(chip, *ready):
-    lines, line, _ = lines_of()
-    total, sent = pick(chip, line, 0), chip.astype(bf16)
-    for step in range(1, lines):
-        arrived = shift_lines(pick(sent, (line + step) % lines, 0), step)
-        total = total + after(arrived, *ready).astype(f32)
-    return total
 
 
 def turn(u, cos2, sin2):
@@ -359,17 +309,21 @@
     gain_one, gain_two = gain_attn.astype(f32)[:, None], gain_mlp.astype(f32)[:, None]
     qkv_own = jnp.concatenate([w_query, w_keyvalue], axis=1).astype(f32)
     qkv_width = qkv_own.shape[1]
+    attn_shard = jnp.concatenate([(qkv_own * gain_one).astype(bf16), w_project.T], axis=1)
     pair_own = [
         jnp.concatenate([w_gate[:, a:b], w_up[:, a:b]], axis=1).astype(f32) for a, b in parts
     ]
-    pair_shards = [(own * gain_two).astype(bf16) for own in pair_own]
+    ff_shards = [
+        jnp.concatenate([(own * gain_two).astype(bf16), w_down[a:b].T], axis=1)
+        for (a, b), own in zip(parts, pair_own)
+    ]
 
     residual = layer_input.astype(f32)
-    inputs = all_blocks(layer_input, near_blocks(layer_input))
-    qkv_full = gather_dp((qkv_own * gain_one).astype(bf16))
-    project_full = join_lines(send_lines(w_project.T))
-    pairs = [gather_dp(after(pair_shards[0], *inputs))]
-    down_pieces = send_lines(after(w_down.T, *inputs))
+    near = near_blocks(layer_input)
+    inputs = all_blocks(layer_input, near)
+    attn_full = gather_dp(attn_shard)
+    ff_full = [gather_dp(after(ff_shards[0], *near))]
+    qkv_full, project_full = attn_full[:, :qkv_width], attn_full[:, qkv_width:]
     top = out_grad.astype(f32) * own_mask
     top_own = after(top.astype(bf16), *inputs)
     top_near = near_blocks(top_own)
@@ -379,13 +333,12 @@
         return (block * inverse_norm(block)).astype(bf16)
 
     normed_one = jnp.concatenate([norm(b) for b in inputs], axis=0)
-    qkv = dot(after(normed_one, project_full), qkv_full, 1, 0)
+    qkv = dot(normed_one, qkv_full, 1, 0)
     qr, kvt, mixed, lse = attend(where, qkv, cos2, sin2, rows)
-    pairs.append(gather_dp(after(pair_shards[1], mixed)))
+    ff_full.append(gather_dp(after(ff_shards[1], mixed)))
     mixed_rest = dot(after(mixed[rows:], *top_near), project_full, 1, 1).astype(bf16)
     mixed_sent = send_sums(mixed_rest)
     top_all = jnp.concatenate(all_blocks(top_own, top_near), axis=0)
-    down_full = join_lines(down_pieces, *mixed_sent)
     after_attn = residual + finish_sums(
         dot(mixed[:rows], project_full, 1, 1), mixed_rest, mixed_sent
     )
@@ -393,57 +346,69 @@
     inv_two = inverse_norm(after_attn)
     unit_two = after_attn * inv_two
     normed_own = after(unit_two.astype(bf16), top_all)
-    grads = [dot(top_all, down_full[:, a:b], 1, 0) for a, b in parts]
     normed_two = jnp.concatenate(all_blocks(normed_own, near_blocks(normed_own)), axis=0)
-    normed = after(normed_two, *grads)
-    hiddens, pair_grads, pair_partials = [], [], []
-    for (a, b), pair, grad in zip(parts, pairs, grads):
-        both = dot(normed, pair, 1, 0)
-        gate, up = both[:, : b - a], both[:, b - a :]
+
+    def feed(part, normed, full):
+        width = part[1] - part[0]
+        grad = dot(top_all, full[:, 2 * width :], 1, 0)
+        both = dot(after(normed, grad), full[:, : 2 * width], 1, 0)
+        gate, up = both[:, :width], both[:, width:]
         sig = jax.nn.sigmoid(gate)
-        hiddens.append((gate * sig * up).astype(bf16))
+        hidden = (gate * sig * up).astype(bf16)
         gate_grad = (grad * up * sig * (1.0 + gate * (1.0 - sig))).astype(bf16)
         up_grad = (grad * gate * sig).astype(bf16)
-        pair_grads.append(jnp.concatenate([gate_grad, up_grad], axis=1))
-        if len(hiddens) == 1:
-            pair_partials.append(dot(normed_two, pair_grads[0], 0, 0).astype(bf16))
-            normed = after(normed_two, pair_partials[0])
-    hidden = jnp.concatenate(hiddens, axis=1)
-
-    rest = sum(dot(g[rows:], w, 1, 1) for g, w in zip(pair_grads, pairs)).astype(bf16)
+        return hidden, jnp.concatenate([gate_grad, up_grad], axis=1)
+
+    def partial(hidden, grads):
+        return jnp.concatenate(
+            [
+                dot(normed_two, grads, 0, 0).astype(bf16),
+                dot(top_all, hidden, 0, 0).astype(bf16),
+            ],
+            axis=1,
+        )
+
+    pairs = [full[:, : 2 * (b - a)] for (a, b), full in zip(parts, ff_full)]
+    downs = [full[:, 2 * (b - a) :] for (a, b), full in zip(parts, ff_full)]
+    hidden0, grads0 = feed(parts[0], normed_two, ff_full[0])
+    partial0 = partial(hidden0, grads0)
+    rest0 = dot(after(grads0[rows:], partial0), pairs[0], 1, 1)
+    hidden1, grads1 = feed(parts[1], after(normed_two, rest0), ff_full[1])
+    rest = (rest0 + dot(grads1[rows:], pairs[1], 1, 1)).astype(bf16)
     rest_sent = send_sums(rest)
-    pair_partials.append(dot(normed_two, after(pair_grads[1], rest), 0, 0).astype(bf16))
-    pair_sums = [scatter_dp(partial) for partial in pair_partials]
-    own_grads = [g[:rows] for g in pair_grads]
-    own_grads[0] = after(own_grads[0], pair_partials[1])
-    scaled = finish_sums(sum(dot(g, w, 1, 1) for g, w in zip(own_grads, pairs)), rest, rest_sent)
+    partial1 = partial(after(hidden1, rest), after(grads1, rest))
+    ff_sums = [scatter_dp(partial0), scatter_dp(partial1)]
+    own = dot(after(grads0[:rows], partial1), pairs[0], 1, 1) + dot(grads1[:rows], pairs[1], 1, 1)
+    scaled = finish_sums(own, rest, rest_sent)
     attn_top = top + inv_two * (
         scaled - unit_two * jnp.mean(scaled * unit_two, axis=-1, keepdims=True)
     )
     attn_top_own = attn_top.astype(bf16)
     attn_top_blocks = all_blocks(attn_top_own, near_blocks(attn_top_own))
     attn_top_all = jnp.concatenate(attn_top_blocks, axis=0)
-    down_chip = sum_cores(dot(top_all, hidden, 0, 0).astype(bf16))
-    down_rest = after(dot(hidden[rows:], down_full, 1, 1).astype(bf16), *attn_top_blocks)
-
-    mixed_grad = dot(after(attn_top_all, down_chip, pair_sums[0]), project_full, 1, 0).astype(bf16)
-    project_partial = dot(attn_top_all, mixed, 0, 0).astype(bf16)
+    hidden = [hidden0, hidden1]
+    down_rest = sum(dot(h[rows:], w, 1, 1) for h, w in zip(hidden, downs)).astype(bf16)
+    down_rest = after(down_rest, *attn_top_blocks)
+
+    mixed_grad = dot(after(attn_top_all, down_rest, ff_sums[0]), project_full, 1, 0).astype(bf16)
     shared = kv_grad.astype(f32) * own_mask
     query_grad, kv_back = attend_back(
-        where, qr, kvt, after(mixed_grad, project_partial), lse, cos2, sin2, shared, rows
-    )
-    down_sum = sum_lines(down_chip, query_grad)
-    project_chip = sum_cores(project_partial, query_grad)
-    project_sum = sum_lines(project_chip)
+        where, qr, kvt, mixed_grad, lse, cos2, sin2, shared, rows
+    )
     down_sent = [after(block, query_grad) for block in send_sums(down_rest)]
-    after_mlp = after_attn + finish_sums(
-        dot(hidden[:rows], down_full, 1, 1), down_rest, down_sent
-    )
+    qkv_back = after(jnp.concatenate([query_grad, kv_back], axis=1), *down_sent)
+    attn_partial = jnp.concatenate(
+        [
+            dot(normed_one, qkv_back, 0, 0).astype(bf16),
+            dot(attn_top_all, mixed, 0, 0).astype(bf16),
+        ],
+        axis=1,
+    )
+    attn_sum = scatter_dp(after(attn_partial, ff_sums[1]))
+    own_down = sum(dot(h[:rows], w, 1, 1) for h, w in zip(hidden, downs))
+    after_mlp = after_attn + finish_sums(own_down, down_rest, down_sent)
     output = (after_mlp * own_mask).astype(bf16)
-    qkv_back = after(jnp.concatenate([query_grad, kv_back], axis=1), project_chip)
-    qkv_partial = dot(normed_one, qkv_back, 0, 0).astype(bf16)
-    qkv_sum = scatter_dp(after(qkv_partial, *pair_sums, down_sum))
-    qkv_rest = dot(after(qkv_back[rows:], qkv_partial, *down_sent), qkv_full, 1, 1).astype(bf16)
+    qkv_rest = dot(after(qkv_back[rows:], attn_partial), qkv_full, 1, 1).astype(bf16)
     scaled_one = finish_sums(
         dot(qkv_back[:rows], qkv_full, 1, 1), qkv_rest, send_sums(qkv_rest)
     )
@@ -453,6 +418,11 @@
         scaled_one - unit_one * jnp.mean(scaled_one * unit_one, axis=-1, keepdims=True)
     )
 
+    qkv_sum, project_sum = attn_sum[:, :qkv_width], attn_sum[:, qkv_width:]
+    pair_sums = [total[:, : own.shape[1]] for own, total in zip(pair_own, ff_sums)]
+    down_sum = jnp.concatenate(
+        [total[:, own.shape[1] :] for own, total in zip(pair_own, ff_sums)], axis=1
+    )
     gain_two_part = sum(
         jnp.sum(own * total, axis=1, keepdims=True) for own, total in zip(pair_own, pair_sums)
     )

time: 587 us -> 534 us (0.910)
  local copies, waits for them, and re-layouts: 84.1 us -> 50.5 us
  starting transfers between devices: 58.5 us -> 32.3 us
  waiting for transfers between devices: 177 us -> 183 us
    ppermute x22 -> x0, waiting for transfers between devices: 63.4 us -> none  [the longest x12 63.4 us: shift_lines(): lax.ppermute(value, 'dp', [(i, (i + 2 * step) % size) for i in range(size)])]
    ppermute x34, waiting for transfers between devices: 113 us -> 171 us  [hop(): return lax.ppermute(value, 'tensor', [(i, i ^ step) for i in range(size)])]
    concatenate x2 -> x10, other arithmetic: 0.34 us -> 28.7 us  [the longest x2 19.6 us: partial(): jnp.concatenate([dot(normed_two, grads, 0, 0).astype(bf16), dot(top_all,...]
    ppermute x22 -> x0, starting transfers between devices: 18.2 us -> none  [the longest x12 17.1 us: shift_lines(): lax.ppermute(value, 'dp', [(i, (i + 2 * step) % size) for i in range(size)])]
    dynamic_slice x12 -> x0, local copies, waits for them, and re-layouts: 17.4 us -> none  [the longest x8 10.7 us: sum_lines(): arrived = shift_lines(pick(sent, (line + step) % lines, 0), step)]
    convert_element_type x7 -> x5, other arithmetic: 22.4 us -> 5.44 us  [the longest x2 4.08 us: feed(): up_grad = (grad * gate * sig).astype(bf16)]
    dynamic_update_slice x16 -> x0, local copies, waits for them, and re-layouts: 14.2 us -> none  [the longest x8 9.98 us: join_lines(): whole = lax.dynamic_update_slice(whole, piece, ((base + core) * rows, 0))]
    reduce_scatter x3, waiting for transfers between devices: 0.04 us -> 12 us  [scatter_dp(): lax.psum_scatter(partial, 'dp', scatter_dimension=0, tiled=True).astype(f32)]
  transfers between devices with their start and end apart: 62 -> 40, of which waited for: 23 -> 26; matrix products, arithmetic and copies ran while one was open for 48% -> 47% of each run, Pallas kernels for 4% -> 5%
where the time goes in v4:
time: 534 us; the launch traced here: 525 us
  waiting for transfers between devices  183 us (34%)
  matrix products  137 us (26%)
  other arithmetic  80.3 us (15%)
  local copies, waits for them, and re-layouts  50.5 us (9%)
  starting transfers between devices  32.3 us (6%)
  Pallas kernels  25.3 us (5%)
  between operations  16.7 us (3%)
    ppermute x34, waiting for transfers between devices, hop(): return lax.ppermute(value, 'tensor', [(i, i ^ step) for i in range(size)])  171 us
    dot_general x24, matrix products, dot(): lax.dot_general(a, b, (((ca,), (cb,)), ((), ())), preferred_element_type=...  137 us
    ppermute x34, starting transfers between devices, hop(): return lax.ppermute(value, 'tensor', [(i, i ^ step) for i in range(size)])  32.1 us
    unnamed x178, local copies, waits for them, and re-layouts  30.8 us
    concatenate x2, other arithmetic, partial(): jnp.concatenate([dot(normed_two, grads, 0, 0).astype(bf16), dot(top_all,...  19.6 us
    pallas_call x1, Pallas kernels, attend_back(): pl.pallas_call(attend_back_kernel, name='attend_back', grid_spec=pltpu.Pr...  13.5 us
    reduce_scatter x3, waiting for transfers between devices, scatter_dp(): lax.psum_scatter(partial, 'dp', scatter_dimension=0, tiled=True).astype(f32)  12 us
    pallas_call x1, Pallas kernels, attend(): pl.pallas_call(attend_kernel, name='attend', grid_spec=pltpu.PrefetchScal...  11.8 us
  transfers between devices with their start and end apart: 40, of which 26 were waited for; matrix products, arithmetic and copies ran while one was open for 47% of the time, Pallas kernels for 5%

profile of v4, /device:TPU:8, one launch (start us, length us, event | category | flops | bytes accessed | tf_op | source)
XLA Modules:
  0.0 525.1 jit_solution(9112675046795822100)
XLA Ops:
  10.2 1.8 pad_maximum_fusion.22
  15.3 1.8 slice.380
  18.2 1.9 slice.381
  20.1 1.9 copy.39
  25.4 11.8 %collective-permute-done = bf16[256,2048]{1,0:T(8,128)(2,1)S(1)} collective-permute-done((bf16[256,2048]{1,0:T(8,128)(2,1)S(1)}, bf16[256,2048]{1,0:T(8,128)(2,1)S(1)}, u32[]{:S(2)}, u32[]{:S(2)}) %collective-permute-start) | collective-permute-done | bytes 1048608 | tf_op jit(solution)/shard_map/ppermute | solution.py:26
  38.4 1.7 slice.389
  40.2 1.7 slice.390
  43.8 2.0 copy.41
  45.9 1.9 fusion.98
  58.6 7.4 %collective-permute-done.3 = bf16[128,2048]{1,0:T(8,128)(2,1)S(1)} collective-permute-done((bf16[128,2048]{1,0:T(8,128)(2,1)S(1)}, bf16[128,2048]{1,0:T(8,128)(2,1)S(1)}, u32[]{:S(2)}, u32[]{:S(2)}) %collective-permute-start.3) | collective-permute-done | bytes 524320 | tf_op jit(solution)/shard_map/ppermute | solution.py:26
  71.0 8.3 %fusion.29.q_ref.kv_ref = f32[1024,768]{1,0:T(8,128)} fusion(bf16[1024,2048]{1,0:T(8,128)(2,1)} %fusion.90, bf16[2048,1280]{0,1:T(8,128)(2,1)} %all-gather.4.cloned.1.call-done), kind=kOutput, calls=%fused_computation.64 | convolution fusion | flops 3221225472 | bytes 10485760 | tf_op jit(solution)/shard_map/dot_general | solution.py:21
  79.4 11.8 %attend.1 = (bf16[1024,512]{1,0:T(8,128)(2,1)S(1)}, bf16[1024,256]{1,0:T(8,128)(2,1)S(1)}, bf16[1024,512]{1,0:T(8,128)(2,1)S(1)}, f32[1024,128]{1,0:T(8,128)S(1)}) custom-call(s32[2]{0:T(128)S(1)} %pad_add_fusion.where_ref, f32[1024,768]{1,0:T(8,128)} %fusion.29.q_ref.kv_ref, f32[1024,768]{1,0:T(8,128)} %fusion.29.q_ref.kv_ref, ...), custom_call_target="tpu_custom_call" | custom-call | flops 2147483648 | bytes 8388608 | tf_op jit(solution)/shard_map/attend/pallas_call | solution.py:196
  91.3 3.7 convolution_convert_fusion.2
  109.3 24.9 %collective-permute-done.10 = bf16[128,2048]{1,0:T(8,128)(2,1)S(1)} collective-permute-done((bf16[128,2048]{1,0:T(8,128)(2,1)S(1)}, bf16[128,2048]{1,0:T(8,128)(2,1)S(1)}, u32[]{:S(2)}, u32[]{:S(2)}) %collective-permute-start.10) | collective-permute-done | bytes 524320 | tf_op jit(solution)/shard_map/ppermute | solution.py:26
  139.1 3.8 fusion.53
  142.9 5.1 collective-permute-done.7
  152.4 20.1 %collective-permute-done.13 = bf16[256,2048]{1,0:T(8,128)(2,1)S(1)} collective-permute-done((bf16[256,2048]{1,0:T(8,128)(2,1)S(1)}, bf16[256,2048]{1,0:T(8,128)(2,1)S(1)}, u32[]{:S(2)}, u32[]{:S(2)}) %collective-permute-start.13) | collective-permute-done | bytes 1048608 | tf_op jit(solution)/shard_map/ppermute | solution.py:26
  178.4 4.9 collective-permute-done.14
  185.4 6.5 %fusion.24 = f32[1024,768]{0,1:T(8,128)S(1)} fusion(bf16[1024,2048]{1,0:T(8,128)(2,1)} %copy-done.59, bf16[2048,2304]{0,1:T(8,128)(2,1)} %all-gather.6.cloned.1.call-done), kind=kOutput, calls=%fused_computation.59 | convolution fusion | flops 3221225472 | bytes 10485760 | tf_op jit(solution)/shard_map/dot_general | solution.py:21
  192.0 10.8 %fusion.4 = f32[1024,1536]{0,1:T(8,128)S(1)} fusion(bf16[1024,2048]{1,0:T(8,128)(2,1)} %constant_dynamic-update-slice_fusion.5, bf16[2048,2304]{0,1:T(8,128)(2,1)S(1)} %copy-done.71), kind=kOutput, calls=%fused_computation.11 | convolution fusion | flops 6442450944 | bytes 16777216 | tf_op jit(solution)/shard_map/dot_general | solution.py:21
  202.8 2.2 multiply_convert_fusion
  205.0 3.6 convolution_convert_fusion.3
  208.7 10.7 %convolution_convert_fusion.1 = bf16[2048,1536]{0,1:T(8,128)(2,1)S(1)} fusion(bf16[1024,2048]{1,0:T(8,128)(2,1)} %constant_dynamic-update-slice_fusion.5, bf16[1024,768]{0,1:T(8,128)(2,1)S(1)} %get-tuple-element.73, bf16[1024,768]{0,1:T(8,128)(2,1)S(1)} %get-tuple-element.74), kind=kOutput, calls=%fused_computation.3 | convolution fusion | flops 6451888128 | bytes 13631488 | tf_op jit(solution)/shard_map/dot_general | solution.py:21
  219.4 11.5 %pad_maximum_fusion = bf16[2048,2304]{0,1:T(8,128)(2,1)} fusion(bf16[2048,768]{0,1:T(8,128)(2,1)S(1)} %convolution_convert_fusion.3, bf16[2048,1536]{0,1:T(8,128)(2,1)S(1)} %convolution_convert_fusion.1), kind=kLoop, calls=%fused_computation | loop fusion | flops 18874368 | bytes 18874368 | tf_op jit(solution)/shard_map/concatenate | solution.py:363
  231.0 1.8 fusion.31
  232.8 10.0 %fusion.2 = f32[768,2048]{1,0:T(8,128)} fusion(bf16[768,1536]{0,1:T(8,128)(2,1)S(1)} %fusion.31, bf16[2048,2304]{0,1:T(8,128)(2,1)} %all-gather.6.cloned.1.call-done), kind=kOutput, calls=%fused_computation.9 | convolution fusion | flops 4831838208 | bytes 14942208 | tf_op jit(solution)/shard_map/dot_general | solution.py:21
  242.8 5.7 %fusion.46 = f32[1024,640]{0,1:T(8,128)S(1)} fusion(bf16[1024,2048]{1,0:T(8,128)(2,1)} %copy-done.59, bf16[2048,1920]{0,1:T(8,128)(2,1)} %all-gather.8.cloned.1.call-done), kind=kOutput, calls=%fused_computation.88 | convolution fusion | flops 2684354560 | bytes 9437184 | tf_op jit(solution)/shard_map/dot_general | solution.py:21
  248.9 8.7 %fusion.10 = f32[1024,1280]{0,1:T(8,128)S(1)} fusion(bf16[1024,2048]{1,0:T(8,128)(2,1)} %constant_dynamic-update-slice_fusion.5, bf16[2048,1920]{0,1:T(8,128)(2,1)S(1)} %copy-done.57), kind=kOutput, calls=%fused_computation.17 | convolution fusion | flops 5368709120 | bytes 14680064 | tf_op jit(solution)/shard_map/dot_general | solution.py:21
  257.6 1.9 multiply_convert_fusion.3
  261.0 7.9 %add_convert_fusion = bf16[768,2048]{1,0:T(8,128)(2,1)} fusion(f32[768,2048]{1,0:T(8,128)} %fusion.2, bf16[2048,1920]{0,1:T(8,128)(2,1)S(1)} %copy-done.57, bf16[1024,640]{0,1:T(8,128)(2,1)S(1)} %get-tuple-element.76, bf16[1024,640]{0,1:T(8,128)(2,1)S(1)} %get-tuple-element.75), kind=kOutput, calls=%fused_computation.4 | convolution fusion | flops 4033609728 | bytes 17301504 | tf_op jit(solution)/shard_map/dot_general | solution.py:21
  268.9 4.2 convolution_convert_fusion.6
  273.1 9.9 %convolution_convert_fusion = bf16[2048,1280]{0,1:T(8,128)(2,1)} fusion(bf16[1024,1280]{0,1:T(8,128)(2,1)S(1)} %pad_maximum_fusion.4, bf16[1024,2048]{1,0:T(8,128)(2,1)} %constant_dynamic-update-slice_fusion.5), kind=kOutput, calls=%fused_computation.2 | convolution fusion | flops 5371330560 | bytes 12058624 | tf_op jit(solution)/shard_map/dot_general | solution.py:21
  283.1 8.1 %pad_maximum_fusion.1 = bf16[2048,1920]{0,1:T(8,128)(2,1)} fusion(bf16[2048,640]{0,1:T(8,128)(2,1)} %convolution_convert_fusion.6, bf16[2048,1280]{0,1:T(8,128)(2,1)} %convolution_convert_fusion), kind=kLoop, calls=%fused_computation.1 | loop fusion | flops 15728640 | bytes 15728640 | tf_op jit(solution)/shard_map/concatenate | solution.py:363
  291.2 1.8 fusion.105
  295.9 4.3 fusion.6
  300.2 14.0 %collective-permute-done.18 = bf16[256,2048]{1,0:T(8,128)(2,1)S(1)} collective-permute-done((bf16[256,2048]{1,0:T(8,128)(2,1)S(1)}, bf16[256,2048]{1,0:T(8,128)(2,1)S(1)}, u32[]{:S(2)}, u32[]{:S(2)}) %collective-permute-start.18) | collective-permute-done | bytes 1048608 | tf_op jit(solution)/shard_map/ppermute | solution.py:26
  318.0 1.8 fusion.17
  319.8 5.7 %collective-permute-done.17 = bf16[128,2048]{1,0:T(8,128)(2,1)S(1)} collective-permute-done((bf16[128,2048]{1,0:T(8,128)(2,1)S(1)}, bf16[128,2048]{1,0:T(8,128)(2,1)S(1)}, u32[]{:S(2)}, u32[]{:S(2)}) %collective-permute-start.17) | collective-permute-done | bytes 524320 | tf_op jit(solution)/shard_map/ppermute | solution.py:26
  328.3 2.1 constant_dynamic-update-slice_fusion.14
  332.4 4.8 fusion.20
  337.2 14.2 %collective-permute-done.21 = bf16[256,2048]{1,0:T(8,128)(2,1)S(1)} collective-permute-done((bf16[256,2048]{1,0:T(8,128)(2,1)S(1)}, bf16[256,2048]{1,0:T(8,128)(2,1)S(1)}, u32[]{:S(2)}, u32[]{:S(2)}) %collective-permute-start.21) | collective-permute-done | bytes 1048608 | tf_op jit(solution)/shard_map/ppermute | solution.py:26
  351.4 2.2 collective-permute-start.22
  355.5 5.7 %add_convert_fusion.1 = bf16[768,2048]{1,0:T(8,128)(2,1)S(1)} fusion(f32[768,2048]{1,0:T(8,128)} %fusion.20, bf16[2048,1920]{0,1:T(8,128)(2,1)} %all-gather.8.cloned.1.call-done, bf16[1024,640]{0,1:T(8,128)(2,1)S(1)} %copy-done.52), kind=kOutput, calls=%fused_computation.5 | convolution fusion | flops 2016411648 | bytes 13041664 | tf_op jit(solution)/shard_map/dot_general | solution.py:21
  361.4 7.9 %collective-permute-done.23 = bf16[128,2048]{1,0:T(8,128)(2,1)S(1)} collective-permute-done((bf16[128,2048]{1,0:T(8,128)(2,1)S(1)}, bf16[128,2048]{1,0:T(8,128)(2,1)S(1)}, u32[]{:S(2)}, u32[]{:S(2)}) %collective-permute-start.23) | collective-permute-done | bytes 524320 | tf_op jit(solution)/shard_map/ppermute | solution.py:26
  372.4 2.1 copy-done.58
  374.5 3.9 convolution_convert_fusion.7
  378.3 2.9 convert_element_type.304
  381.2 5.4 %fusion.57.dm_ref = bf16[1024,512]{1,0:T(8,128)(2,1)S(1)} fusion(bf16[1024,2048]{1,0:T(8,128)(2,1)} %copy-done.58, bf16[2048,1280]{0,1:T(8,128)(2,1)} %all-gather.4.cloned.1.call-done), kind=kOutput, calls=%fused_computation.104 | convolution fusion | flops 2148007936 | bytes 7340032 | tf_op jit(solution)/shard_map/dot_general | solution.py:21
  386.6 13.5 %attend_back.1 = (bf16[1024,512]{1,0:T(8,128)(2,1)S(1)}, bf16[1024,256]{1,0:T(8,128)(2,1)S(1)}) custom-call(s32[2]{0:T(128)S(1)} %copy-done.1, bf16[1024,512]{1,0:T(8,128)(2,1)S(1)} %get-tuple-element.49.qr_ref, bf16[1024,256]{1,0:T(8,128)(2,1)S(1)} %copy-done.3, bf16[1024,512]{1,0:T(8,128)(2,1)S(1)} %fusion.57.dm_ref, f32[1024,128]{1,0:T(8,128)S(1)} %copy-done.5, ...), custom_call_target="tpu_custom_call" | custom-call | flops 5368709120 | bytes 8388608 | tf_op jit(solution)/shard_map/attend_back/pallas_call | solution.py:234
  400.3 7.0 %convolution_convert_fusion.5 = bf16[2048,768]{0,1:T(8,128)(2,1)S(1)} fusion(bf16[1024,2048]{1,0:T(8,128)(2,1)} %fusion.90, bf16[1024,768]{1,0:T(8,128)(2,1)S(1)} %pad_maximum_fusion.8), kind=kOutput, calls=%fused_computation.27 | convolution fusion | flops 3222798336 | bytes 8912896 | tf_op jit(solution)/shard_map/dot_general | solution.py:21
  407.3 2.9 pad_maximum_fusion.2
  410.2 12.0 %reduce-scatter.6.cloned.1.call-done = bf16[256,1920]{0,1:T(8,128)(2,1)} async-done(((bf16[2048,1920]{0,1:T(8,128)(2,1)}), bf16[256,1920]{0,1:T(8,128)(2,1)}) %reduce-scatter.6.cloned.1.call-update) | async-done | bytes 983056 | tf_op jit(solution)/shard_map/reduce_scatter | solution.py:80
  425.5 3.2 fusion.22
  428.6 2.9 convolution_add_fusion
  434.8 2.8 convolution_convert_fusion.4
  447.5 16.1 %collective-permute-done.30 = bf16[256,2048]{1,0:T(8,128)(2,1)S(1)} collective-permute-done((bf16[256,2048]{1,0:T(8,128)(2,1)S(1)}, bf16[256,2048]{1,0:T(8,128)(2,1)S(1)}, u32[]{:S(2)}, u32[]{:S(2)}) %collective-permute-start.30) | collective-permute-done | bytes 1048608 | tf_op jit(solution)/shard_map/ppermute | solution.py:26
  463.9 1.7 collective-permute-done.28
  468.2 6.7 %collective-permute-done.25 = bf16[128,2048]{1,0:T(8,128)(2,1)S(1)} collective-permute-done((bf16[128,2048]{1,0:T(8,128)(2,1)S(1)}, bf16[128,2048]{1,0:T(8,128)(2,1)S(1)}, u32[]{:S(2)}, u32[]{:S(2)}) %collective-permute-start.25) | collective-permute-done | bytes 524320 | tf_op jit(solution)/shard_map/ppermute | solution.py:26
  474.9 2.0 collective-permute-done.27
  477.4 8.7 %collective-permute-done.29 = bf16[128,2048]{1,0:T(8,128)(2,1)S(1)} collective-permute-done((bf16[128,2048]{1,0:T(8,128)(2,1)S(1)}, bf16[128,2048]{1,0:T(8,128)(2,1)S(1)}, u32[]{:S(2)}, u32[]{:S(2)}) %collective-permute-start.29) | collective-permute-done | bytes 524320 | tf_op jit(solution)/shard_map/ppermute | solution.py:26
  486.1 2.0 collective-permute-done.31
  490.4 2.3 fusion.39
  502.0 5.6 %collective-permute-done.32 = f32[256,258]{0,1:T(8,128)} collective-permute-done((f32[256,258]{0,1:T(8,128)}, f32[256,258]{0,1:T(8,128)}, u32[]{:S(2)}, u32[]{:S(2)}) %collective-permute-start.32) | collective-permute-done | bytes 264224 | tf_op jit(solution)/shard_map/ppermute | solution.py:26
  511.4 5.0 collective-permute-done.33
  (348 shorter events, 115.3 us)
Async XLA Ops:
  7.2 8.1 %copy-start.72 = (bf16[256]{0:T(256)(128)(2,1)S(1)}, bf16[256]{0:T(256)(128)(2,1)}, u32[]{:S(2)}) copy-start(bf16[256]{0:T(256)(128)(2,1)} %param.21) | copy-start | bytes 1540
  7.2 63.8 %all-gather.4.cloned.1.call-start = ((), (), s32[]{:S(2)}) async-start(), calls=%async_computation.3 | async-start | bytes 5898240 | tf_op jit(solution)/shard_map/all_gather | solution.py:76
  12.1 173.3 %all-gather.6.cloned.1.call-start = ((), (), s32[]{:S(2)}) async-start(), calls=%async_computation.4 | async-start | bytes 10616832 | tf_op jit(solution)/shard_map/all_gather | solution.py:76
  12.2 25.0 %collective-permute-start = (bf16[256,2048]{1,0:T(8,128)(2,1)S(1)}, bf16[256,2048]{1,0:T(8,128)(2,1)S(1)}, u32[]{:S(2)}, u32[]{:S(2)}) collective-permute-start(bf16[256,2048]{1,0:T(8,128)(2,1)S(1)} %copy-done.6), channel_id=1, source_target_pairs={{0,1},{1,0},{2,3},{3,2},{4,5},{5,4},{6,7},{7,6},{8,9},{9,8},{10,11... | collective-permute-start | bytes 3145736 | tf_op jit(solution)/shard_map/ppermute | solution.py:26
  13.7 24.6 %collective-permute-start.1 = (bf16[256,2048]{1,0:T(8,128)(2,1)S(1)}, bf16[256,2048]{1,0:T(8,128)(2,1)S(1)}, u32[]{:S(2)}, u32[]{:S(2)}) collective-permute-start(bf16[256,2048]{1,0:T(8,128)(2,1)S(1)} %copy-done.6), channel_id=1, source_target_pairs={{0,2},{1,3},{2,0},{3,1},{4,6},{5,7},{6,4},{7,5},{8,10},{9,11},{10,... | collective-permute-start | bytes 3145736 | tf_op jit(solution)/shard_map/ppermute | solution.py:26
  15.3 34.2 %copy-start.67 = (f32[256]{0:T(256)}, f32[256]{0:T(256)S(1)}, u32[]{:S(2)}) copy-start(f32[256]{0:T(256)S(1)} %convert_element_type.279) | copy-start | bytes 3076
  18.2 7.2 %copy-start.32 = (bf16[256,768]{0,1:T(8,128)(2,1)}, bf16[256,768]{0,1:T(8,128)(2,1)S(1)}, u32[]{:S(2)}) copy-start(bf16[256,768]{0,1:T(8,128)(2,1)S(1)} %copy.38) | copy-start | bytes 1179652
  37.2 10.7 %copy-start.22 = (bf16[256,2048]{1,0:T(8,128)(2,1)}, bf16[256,2048]{1,0:T(8,128)(2,1)S(1)}, u32[]{:S(2)}) copy-start(bf16[256,2048]{1,0:T(8,128)(2,1)S(1)} %collective-permute-done) | copy-start | bytes 3145732
  38.4 204.4 %all-gather.8.cloned.1.call-start = ((), (), s32[]{:S(2)}) async-start(), calls=%async_computation.5 | async-start | bytes 8847360 | tf_op jit(solution)/shard_map/all_gather | solution.py:76
  45.9 33.5 %copy-start = (s32[2]{0:T(128)}, s32[2]{0:T(128)S(1)}, u32[]{:S(2)}) copy-start(s32[2]{0:T(128)S(1)} %pad_add_fusion.where_ref) | copy-start | bytes 28
  53.3 12.7 %collective-permute-start.3 = (bf16[128,2048]{1,0:T(8,128)(2,1)S(1)}, bf16[128,2048]{1,0:T(8,128)(2,1)S(1)}, u32[]{:S(2)}, u32[]{:S(2)}) collective-permute-start(bf16[128,2048]{1,0:T(8,128)(2,1)S(1)} %slice.459), channel_id=1, source_target_pairs={{0,2},{1,3},{2,0},{3,1},{4,6},{5,7},{6,4},{7,5},{8,10},{9,11},{10,... | collective-permute-start | bytes 1572872 | tf_op jit(solution)/shard_map/ppermute | solution.py:26
  54.9 12.5 %collective-permute-start.2 = (bf16[128,2048]{1,0:T(8,128)(2,1)S(1)}, bf16[128,2048]{1,0:T(8,128)(2,1)S(1)}, u32[]{:S(2)}, u32[]{:S(2)}) collective-permute-start(bf16[128,2048]{1,0:T(8,128)(2,1)S(1)} %slice.458), channel_id=1, source_target_pairs={{0,1},{1,0},{2,3},{3,2},{4,5},{5,4},{6,7},{7,6},{8,9},{9,8},{10,11... | collective-permute-start | bytes 1572872 | tf_op jit(solution)/shard_map/ppermute | solution.py:26
  67.4 23.9 %collective-permute-start.5 = (bf16[256,2048]{1,0:T(8,128)(2,1)}, bf16[256,2048]{1,0:T(8,128)(2,1)}, u32[]{:S(2)}, u32[]{:S(2)}) collective-permute-start(bf16[256,2048]{1,0:T(8,128)(2,1)} %fusion.43), channel_id=1, source_target_pairs={{0,2},{1,3},{2,0},{3,1},{4,6},{5,7},{6,4},{7,5},{8,10},{9,11},{10,... | collective-permute-start | bytes 3145736 | tf_op jit(solution)/shard_map/ppermute | solution.py:26
  67.9 23.4 %collective-permute-start.4 = (bf16[256,2048]{1,0:T(8,128)(2,1)}, bf16[256,2048]{1,0:T(8,128)(2,1)}, u32[]{:S(2)}, u32[]{:S(2)}) collective-permute-start(bf16[256,2048]{1,0:T(8,128)(2,1)} %fusion.43), channel_id=1, source_target_pairs={{0,1},{1,0},{2,3},{3,2},{4,5},{5,4},{6,7},{7,6},{8,9},{9,8},{10,11... | collective-permute-start | bytes 3145736 | tf_op jit(solution)/shard_map/ppermute | solution.py:26
  97.5 36.7 %collective-permute-start.8 = (bf16[256,2048]{1,0:T(8,128)(2,1)}, bf16[256,2048]{1,0:T(8,128)(2,1)}, u32[]{:S(2)}, u32[]{:S(2)}) collective-permute-start(bf16[256,2048]{1,0:T(8,128)(2,1)} %pad_maximum_fusion.13), channel_id=1, source_target_pairs={{0,2},{1,3},{2,0},{3,1},{4,6},{5,7},{6,4},{7,5},{8,10},{9,11},{10,... | collective-permute-start | bytes 3145736 | tf_op jit(solution)/shard_map/ppermute | solution.py:26
  99.1 279.2 %reduce-scatter.4.cloned.1.call-start = ((), (), s32[]{:S(2)}) async-start(), calls=%async_computation.6 | async-start | bytes 10616832 | tf_op jit(solution)/shard_map/reduce_scatter | solution.py:80
  100.4 35.3 %collective-permute-start.6 = (bf16[256,2048]{1,0:T(8,128)(2,1)S(1)}, bf16[256,2048]{1,0:T(8,128)(2,1)S(1)}, u32[]{:S(2)}, u32[]{:S(2)}) collective-permute-start(bf16[256,2048]{1,0:T(8,128)(2,1)S(1)} %pad_maximum_fusion.12), channel_id=1, source_target_pairs={{0,1},{1,0},{2,3},{3,2},{4,5},{5,4},{6,7},{7,6},{8,9},{9,8},{10,11... | collective-permute-start | bytes 3145736 | tf_op jit(solution)/shard_map/ppermute | solution.py:26
  102.9 31.3 %collective-permute-start.10 = (bf16[128,2048]{1,0:T(8,128)(2,1)S(1)}, bf16[128,2048]{1,0:T(8,128)(2,1)S(1)}, u32[]{:S(2)}, u32[]{:S(2)}) collective-permute-start(bf16[128,2048]{1,0:T(8,128)(2,1)S(1)} %slice.475), channel_id=1, source_target_pairs={{0,1},{1,0},{2,3},{3,2},{4,5},{5,4},{6,7},{7,6},{8,9},{9,8},{10,11... | collective-permute-start | bytes 1572872 | tf_op jit(solution)/shard_map/ppermute | solution.py:26
  106.1 33.0 %collective-permute-start.11 = (bf16[128,2048]{1,0:T(8,128)(2,1)S(1)}, bf16[128,2048]{1,0:T(8,128)(2,1)S(1)}, u32[]{:S(2)}, u32[]{:S(2)}) collective-permute-start(bf16[128,2048]{1,0:T(8,128)(2,1)S(1)} %slice.476), channel_id=1, source_target_pairs={{0,2},{1,3},{2,0},{3,1},{4,6},{5,7},{6,4},{7,5},{8,10},{9,11},{10,... | collective-permute-start | bytes 1572872 | tf_op jit(solution)/shard_map/ppermute | solution.py:26
  137.5 10.5 %collective-permute-start.7 = (bf16[128,2048]{1,0:T(8,128)(2,1)S(1)}, bf16[128,2048]{1,0:T(8,128)(2,1)S(1)}, u32[]{:S(2)}, u32[]{:S(2)}) collective-permute-start(bf16[128,2048]{1,0:T(8,128)(2,1)S(1)} %get-tuple-element.97), channel_id=1, source_target_pairs={{0,2},{1,3},{2,0},{3,1},{4,6},{5,7},{6,4},{7,5},{8,10},{9,11},{10,... | collective-permute-start | bytes 1572872 | tf_op jit(solution)/shard_map/ppermute | solution.py:26
  138.1 10.3 %collective-permute-start.9 = (bf16[128,2048]{1,0:T(8,128)(2,1)S(1)}, bf16[128,2048]{1,0:T(8,128)(2,1)S(1)}, u32[]{:S(2)}, u32[]{:S(2)}) collective-permute-start(bf16[128,2048]{1,0:T(8,128)(2,1)S(1)} %get-tuple-element.98), channel_id=1, source_target_pairs={{0,1},{1,0},{2,3},{3,2},{4,5},{5,4},{6,7},{7,6},{8,9},{9,8},{10,11... | collective-permute-start | bytes 1572872 | tf_op jit(solution)/shard_map/ppermute | solution.py:26
  139.1 8.9 %copy-start.59 = (bf16[1024,2048]{1,0:T(8,128)(2,1)}, bf16[1024,2048]{1,0:T(8,128)(2,1)S(1)}, u32[]{:S(2)}) copy-start(bf16[1024,2048]{1,0:T(8,128)(2,1)S(1)} %constant_dynamic-update-slice_fusion) | copy-start | bytes 12582916
  150.4 22.0 %collective-permute-start.13 = (bf16[256,2048]{1,0:T(8,128)(2,1)S(1)}, bf16[256,2048]{1,0:T(8,128)(2,1)S(1)}, u32[]{:S(2)}, u32[]{:S(2)}) collective-permute-start(bf16[256,2048]{1,0:T(8,128)(2,1)S(1)} %multiply_convert_fusion.6), channel_id=1, source_target_pairs={{0,2},{1,3},{2,0},{3,1},{4,6},{5,7},{6,4},{7,5},{8,10},{9,11},{10,... | collective-permute-start | bytes 3145736 | tf_op jit(solution)/shard_map/ppermute | solution.py:26
  151.7 23.6 %collective-permute-start.12 = (bf16[256,2048]{1,0:T(8,128)(2,1)S(1)}, bf16[256,2048]{1,0:T(8,128)(2,1)S(1)}, u32[]{:S(2)}, u32[]{:S(2)}) collective-permute-start(bf16[256,2048]{1,0:T(8,128)(2,1)S(1)} %multiply_convert_fusion.6), channel_id=1, source_target_pairs={{0,1},{1,0},{2,3},{3,2},{4,5},{5,4},{6,7},{7,6},{8,9},{9,8},{10,11... | collective-permute-start | bytes 3145736 | tf_op jit(solution)/shard_map/ppermute | solution.py:26
  172.5 10.8 %collective-permute-start.14 = (bf16[128,2048]{1,0:T(8,128)(2,1)S(1)}, bf16[128,2048]{1,0:T(8,128)(2,1)S(1)}, u32[]{:S(2)}, u32[]{:S(2)}) collective-permute-start(bf16[128,2048]{1,0:T(8,128)(2,1)S(1)} %slice.477), channel_id=1, source_target_pairs={{0,1},{1,0},{2,3},{3,2},{4,5},{5,4},{6,7},{7,6},{8,9},{9,8},{10,11... | collective-permute-start | bytes 1572872 | tf_op jit(solution)/shard_map/ppermute | solution.py:26
  175.3 9.2 %collective-permute-start.15 = (bf16[128,2048]{1,0:T(8,128)(2,1)S(1)}, bf16[128,2048]{1,0:T(8,128)(2,1)S(1)}, u32[]{:S(2)}, u32[]{:S(2)}) collective-permute-start(bf16[128,2048]{1,0:T(8,128)(2,1)S(1)} %slice.478), channel_id=1, source_target_pairs={{0,2},{1,3},{2,0},{3,1},{4,6},{5,7},{6,4},{7,5},{8,10},{9,11},{10,... | collective-permute-start | bytes 1572872 | tf_op jit(solution)/shard_map/ppermute | solution.py:26
  185.4 6.6 %copy-start.71 = (bf16[2048,2304]{0,1:T(8,128)(2,1)S(1)}, bf16[2048,2304]{0,1:T(8,128)(2,1)}, u32[]{:S(2)}) copy-start(bf16[2048,2304]{0,1:T(8,128)(2,1)} %all-gather.6.cloned.1.call-done) | copy-start | bytes 28311556
  230.9 191.2 %reduce-scatter.6.cloned.1.call-start = ((), (), s32[]{:S(2)}) async-start(), calls=%async_computation.7 | async-start | bytes 8847360 | tf_op jit(solution)/shard_map/reduce_scatter | solution.py:80
  259.6 9.4 %copy-start.51 = (bf16[1024,640]{0,1:T(8,128)(2,1)}, bf16[1024,640]{0,1:T(8,128)(2,1)S(1)}, u32[]{:S(2)}) copy-start(bf16[1024,640]{0,1:T(8,128)(2,1)S(1)} %get-tuple-element.46) | copy-start | bytes 3932164
  261.0 7.9 %copy-start.61 = (bf16[1024,2048]{1,0:T(8,128)(2,1)S(1)}, bf16[1024,2048]{1,0:T(8,128)(2,1)}, u32[]{:S(2)}) copy-start(bf16[1024,2048]{1,0:T(8,128)(2,1)} %copy-done.59) | copy-start | bytes 12582916
  291.1 204.5 %reduce-scatter.8.cloned.1.call-start = ((), (), s32[]{:S(2)}) async-start(), calls=%async_computation.8 | async-start | bytes 5898240 | tf_op jit(solution)/shard_map/reduce_scatter | solution.py:80
  293.1 21.2 %collective-permute-start.18 = (bf16[256,2048]{1,0:T(8,128)(2,1)S(1)}, bf16[256,2048]{1,0:T(8,128)(2,1)S(1)}, u32[]{:S(2)}, u32[]{:S(2)}) collective-permute-start(bf16[256,2048]{1,0:T(8,128)(2,1)S(1)} %pad_maximum_fusion.15), channel_id=1, source_target_pairs={{0,2},{1,3},{2,0},{3,1},{4,6},{5,7},{6,4},{7,5},{8,10},{9,11},{10,... | collective-permute-start | bytes 3145736 | tf_op jit(solution)/shard_map/ppermute | solution.py:26
  293.9 24.1 %slice-start.3 = ((s8[9437184]{0:T(1024)(128)(4,1)}), s8[4194304]{0:T(1024)(128)(4,1)S(1)}, s32[]{:S(2)}) async-start(s8[9437184]{0:T(1024)(128)(4,1)} %bitcast.55), calls=%async_computation.12 | async-start | bytes 8388608
  294.0 20.5 %collective-permute-start.16 = (bf16[256,2048]{1,0:T(8,128)(2,1)S(1)}, bf16[256,2048]{1,0:T(8,128)(2,1)S(1)}, u32[]{:S(2)}, u32[]{:S(2)}) collective-permute-start(bf16[256,2048]{1,0:T(8,128)(2,1)S(1)} %pad_maximum_fusion.14), channel_id=1, source_target_pairs={{0,1},{1,0},{2,3},{3,2},{4,5},{5,4},{6,7},{7,6},{8,9},{9,8},{10,11... | collective-permute-start | bytes 3145736 | tf_op jit(solution)/shard_map/ppermute | solution.py:26
  295.9 22.0 %slice-start.4 = ((s8[9437184]{0:T(1024)(128)(4,1)}), s8[4194304]{0:T(1024)(128)(4,1)S(1)}, s32[]{:S(2)}) async-start(s8[9437184]{0:T(1024)(128)(4,1)} %bitcast.55), calls=%async_computation.13 | async-start | bytes 8388608
  300.2 17.7 %slice-start.5 = ((s8[9437184]{0:T(1024)(128)(4,1)}), s8[1048576]{0:T(1024)(128)(4,1)S(1)}, s32[]{:S(2)}) async-start(s8[9437184]{0:T(1024)(128)(4,1)} %bitcast.55), calls=%async_computation.14 | async-start | bytes 2097152
  316.3 9.2 %collective-permute-start.17 = (bf16[128,2048]{1,0:T(8,128)(2,1)S(1)}, bf16[128,2048]{1,0:T(8,128)(2,1)S(1)}, u32[]{:S(2)}, u32[]{:S(2)}) collective-permute-start(bf16[128,2048]{1,0:T(8,128)(2,1)S(1)} %get-tuple-element.91), channel_id=1, source_target_pairs={{0,2},{1,3},{2,0},{3,1},{4,6},{5,7},{6,4},{7,5},{8,10},{9,11},{10,... | collective-permute-start | bytes 1572872 | tf_op jit(solution)/shard_map/ppermute | solution.py:26
  317.3 9.2 %collective-permute-start.19 = (bf16[128,2048]{1,0:T(8,128)(2,1)S(1)}, bf16[128,2048]{1,0:T(8,128)(2,1)S(1)}, u32[]{:S(2)}, u32[]{:S(2)}) collective-permute-start(bf16[128,2048]{1,0:T(8,128)(2,1)S(1)} %get-tuple-element.92), channel_id=1, source_target_pairs={{0,1},{1,0},{2,3},{3,2},{4,5},{5,4},{6,7},{7,6},{8,9},{9,8},{10,11... | collective-permute-start | bytes 1572872 | tf_op jit(solution)/shard_map/ppermute | solution.py:26
  319.8 7.2 %copy-start.8 = (bf16[256,2048]{1,0:T(8,128)(2,1)S(1)}, bf16[256,2048]{1,0:T(8,128)(2,1)}, u32[]{:S(2)}) copy-start(bf16[256,2048]{1,0:T(8,128)(2,1)} %param.12) | copy-start | bytes 3145732
  319.8 7.2 %copy-start.11 = (f32[128,2048]{1,0:T(8,128)S(1)}, f32[128,2048]{1,0:T(8,128)}, u32[]{:S(2)}) copy-start(f32[128,2048]{1,0:T(8,128)} %copy-done.10) | copy-start | bytes 3145732
  319.8 7.2 %copy-start.14 = (f32[128,2048]{1,0:T(8,128)S(1)}, f32[128,2048]{1,0:T(8,128)}, u32[]{:S(2)}) copy-start(f32[128,2048]{1,0:T(8,128)} %copy-done.13) | copy-start | bytes 3145732
  330.4 21.0 %collective-permute-start.21 = (bf16[256,2048]{1,0:T(8,128)(2,1)S(1)}, bf16[256,2048]{1,0:T(8,128)(2,1)S(1)}, u32[]{:S(2)}, u32[]{:S(2)}) collective-permute-start(bf16[256,2048]{1,0:T(8,128)(2,1)S(1)} %get-tuple-element.71), channel_id=1, source_target_pairs={{0,2},{1,3},{2,0},{3,1},{4,6},{5,7},{6,4},{7,5},{8,10},{9,11},{10,... | collective-permute-start | bytes 3145736 | tf_op jit(solution)/shard_map/ppermute | solution.py:26
  331.4 23.7 %collective-permute-start.20 = (bf16[256,2048]{1,0:T(8,128)(2,1)S(1)}, bf16[256,2048]{1,0:T(8,128)(2,1)S(1)}, u32[]{:S(2)}, u32[]{:S(2)}) collective-permute-start(bf16[256,2048]{1,0:T(8,128)(2,1)S(1)} %get-tuple-element.71), channel_id=1, source_target_pairs={{0,1},{1,0},{2,3},{3,2},{4,5},{5,4},{6,7},{7,6},{8,9},{9,8},{10,11... | collective-permute-start | bytes 3145736 | tf_op jit(solution)/shard_map/ppermute | solution.py:26
  332.4 23.0 %copy-start.52 = (bf16[1024,640]{0,1:T(8,128)(2,1)S(1)}, bf16[1024,640]{0,1:T(8,128)(2,1)}, u32[]{:S(2)}) copy-start(bf16[1024,640]{0,1:T(8,128)(2,1)} %copy-done.51) | copy-start | bytes 3932164
  351.4 9.9 %collective-permute-start.22 = (bf16[128,2048]{1,0:T(8,128)(2,1)S(1)}, bf16[128,2048]{1,0:T(8,128)(2,1)S(1)}, u32[]{:S(2)}, u32[]{:S(2)}) collective-permute-start(bf16[128,2048]{1,0:T(8,128)(2,1)S(1)} %slice.512), channel_id=1, source_target_pairs={{0,1},{1,0},{2,3},{3,2},{4,5},{5,4},{6,7},{7,6},{8,9},{9,8},{10,11... | collective-permute-start | bytes 1572872 | tf_op jit(solution)/shard_map/ppermute | solution.py:26
  355.2 14.1 %collective-permute-start.23 = (bf16[128,2048]{1,0:T(8,128)(2,1)S(1)}, bf16[128,2048]{1,0:T(8,128)(2,1)S(1)}, u32[]{:S(2)}, u32[]{:S(2)}) collective-permute-start(bf16[128,2048]{1,0:T(8,128)(2,1)S(1)} %slice.513), channel_id=1, source_target_pairs={{0,2},{1,3},{2,0},{3,1},{4,6},{5,7},{6,4},{7,5},{8,10},{9,11},{10,... | collective-permute-start | bytes 1572872 | tf_op jit(solution)/shard_map/ppermute | solution.py:26
  361.2 8.4 %copy-start.38 = (bf16[768,2048]{1,0:T(8,128)(2,1)}, bf16[768,2048]{1,0:T(8,128)(2,1)S(1)}, u32[]{:S(2)}) copy-start(bf16[768,2048]{1,0:T(8,128)(2,1)S(1)} %add_convert_fusion.1) | copy-start | bytes 9437188
  370.6 29.5 %collective-permute-start.26 = (bf16[256,2048]{1,0:T(8,128)(2,1)}, bf16[256,2048]{1,0:T(8,128)(2,1)}, u32[]{:S(2)}, u32[]{:S(2)}) collective-permute-start(bf16[256,2048]{1,0:T(8,128)(2,1)} %pad_maximum_fusion.17), channel_id=1, source_target_pairs={{0,2},{1,3},{2,0},{3,1},{4,6},{5,7},{6,4},{7,5},{8,10},{9,11},{10,... | collective-permute-start | bytes 3145736 | tf_op jit(solution)/shard_map/ppermute | solution.py:26
  371.6 28.5 %collective-permute-start.24 = (bf16[256,2048]{1,0:T(8,128)(2,1)}, bf16[256,2048]{1,0:T(8,128)(2,1)}, u32[]{:S(2)}, u32[]{:S(2)}) collective-permute-start(bf16[256,2048]{1,0:T(8,128)(2,1)} %pad_maximum_fusion.16), channel_id=1, source_target_pairs={{0,1},{1,0},{2,3},{3,2},{4,5},{5,4},{6,7},{7,6},{8,9},{9,8},{10,11... | collective-permute-start | bytes 3145736 | tf_op jit(solution)/shard_map/ppermute | solution.py:26
  400.3 7.0 %copy-start.28 = (bf16[1024,768]{1,0:T(8,128)(2,1)}, bf16[1024,768]{1,0:T(8,128)(2,1)S(1)}, u32[]{:S(2)}) copy-start(bf16[1024,768]{1,0:T(8,128)(2,1)S(1)} %pad_maximum_fusion.8) | copy-start | bytes 4718596
  400.3 7.0 %copy-start.49 = (bf16[2048,512]{0,1:T(8,128)(2,1)S(1)}, bf16[2048,512]{0,1:T(8,128)(2,1)}, u32[]{:S(2)}) copy-start(bf16[2048,512]{0,1:T(8,128)(2,1)} %convolution_convert_fusion.7) | copy-start | bytes 6291460
  425.4 9.3 %slice-start.1 = ((s8[5242880]{0:T(1024)(128)(4,1)}), s8[4194304]{0:T(1024)(128)(4,1)S(1)}, s32[]{:S(2)}) async-start(s8[5242880]{0:T(1024)(128)(4,1)} %bitcast.41), calls=%async_computation.10 | async-start | bytes 8388608
  437.9 25.8 %collective-permute-start.30 = (bf16[256,2048]{1,0:T(8,128)(2,1)S(1)}, bf16[256,2048]{1,0:T(8,128)(2,1)S(1)}, u32[]{:S(2)}, u32[]{:S(2)}) collective-permute-start(bf16[256,2048]{1,0:T(8,128)(2,1)S(1)} %pad_maximum_fusion.19), channel_id=1, source_target_pairs={{0,2},{1,3},{2,0},{3,1},{4,6},{5,7},{6,4},{7,5},{8,10},{9,11},{10,... | collective-permute-start | bytes 3145736 | tf_op jit(solution)/shard_map/ppermute | solution.py:26
  439.6 26.1 %collective-permute-start.28 = (bf16[256,2048]{1,0:T(8,128)(2,1)S(1)}, bf16[256,2048]{1,0:T(8,128)(2,1)S(1)}, u32[]{:S(2)}, u32[]{:S(2)}) collective-permute-start(bf16[256,2048]{1,0:T(8,128)(2,1)S(1)} %pad_maximum_fusion.18), channel_id=1, source_target_pairs={{0,1},{1,0},{2,3},{3,2},{4,5},{5,4},{6,7},{7,6},{8,9},{9,8},{10,11... | collective-permute-start | bytes 3145736 | tf_op jit(solution)/shard_map/ppermute | solution.py:26
  442.6 32.3 %collective-permute-start.25 = (bf16[128,2048]{1,0:T(8,128)(2,1)S(1)}, bf16[128,2048]{1,0:T(8,128)(2,1)S(1)}, u32[]{:S(2)}, u32[]{:S(2)}) collective-permute-start(bf16[128,2048]{1,0:T(8,128)(2,1)S(1)} %get-tuple-element.85), channel_id=1, source_target_pairs={{0,2},{1,3},{2,0},{3,1},{4,6},{5,7},{6,4},{7,5},{8,10},{9,11},{10,... | collective-permute-start | bytes 1572872 | tf_op jit(solution)/shard_map/ppermute | solution.py:26
  443.2 33.7 %collective-permute-start.27 = (bf16[128,2048]{1,0:T(8,128)(2,1)S(1)}, bf16[128,2048]{1,0:T(8,128)(2,1)S(1)}, u32[]{:S(2)}, u32[]{:S(2)}) collective-permute-start(bf16[128,2048]{1,0:T(8,128)(2,1)S(1)} %get-tuple-element.86), channel_id=1, source_target_pairs={{0,1},{1,0},{2,3},{3,2},{4,5},{5,4},{6,7},{7,6},{8,9},{9,8},{10,11... | collective-permute-start | bytes 1572872 | tf_op jit(solution)/shard_map/ppermute | solution.py:26
  466.2 20.0 %collective-permute-start.29 = (bf16[128,2048]{1,0:T(8,128)(2,1)S(1)}, bf16[128,2048]{1,0:T(8,128)(2,1)S(1)}, u32[]{:S(2)}, u32[]{:S(2)}) collective-permute-start(bf16[128,2048]{1,0:T(8,128)(2,1)S(1)} %get-tuple-element.79), channel_id=1, source_target_pairs={{0,2},{1,3},{2,0},{3,1},{4,6},{5,7},{6,4},{7,5},{8,10},{9,11},{10,... | collective-permute-start | bytes 1572872 | tf_op jit(solution)/shard_map/ppermute | solution.py:26
  466.7 21.4 %collective-permute-start.31 = (bf16[128,2048]{1,0:T(8,128)(2,1)S(1)}, bf16[128,2048]{1,0:T(8,128)(2,1)S(1)}, u32[]{:S(2)}, u32[]{:S(2)}) collective-permute-start(bf16[128,2048]{1,0:T(8,128)(2,1)S(1)} %get-tuple-element.80), channel_id=1, source_target_pairs={{0,1},{1,0},{2,3},{3,2},{4,5},{5,4},{6,7},{7,6},{8,9},{9,8},{10,11... | collective-permute-start | bytes 1572872 | tf_op jit(solution)/shard_map/ppermute | solution.py:26
  477.4 11.3 %copy-start.9 = (bf16[256,2048]{1,0:T(8,128)(2,1)S(1)}, bf16[256,2048]{1,0:T(8,128)(2,1)}, u32[]{:S(2)}) copy-start(bf16[256,2048]{1,0:T(8,128)(2,1)} %param.12) | copy-start | bytes 3145732
  477.4 11.3 %copy-start.66 = (f32[256]{0:T(256)S(1)}, f32[256]{0:T(256)}, u32[]{:S(2)}) copy-start(f32[256]{0:T(256)} %copy-done.65) | copy-start | bytes 3076
  498.8 8.8 %collective-permute-start.32 = (f32[256,258]{0,1:T(8,128)}, f32[256,258]{0,1:T(8,128)}, u32[]{:S(2)}, u32[]{:S(2)}) collective-permute-start(f32[256,258]{0,1:T(8,128)} %pad_maximum_fusion.26), channel_id=1, source_target_pairs={{0,1},{1,0},{2,3},{3,2},{4,5},{5,4},{6,7},{7,6},{8,9},{9,8},{10,11... | collective-permute-start | bytes 792584 | tf_op jit(solution)/shard_map/ppermute | solution.py:26
  500.4 8.8 %copy-start.37 = (f32[256,768]{0,1:T(8,128)S(1)}, f32[256,768]{0,1:T(8,128)}, u32[]{:S(2)}) copy-start(f32[256,768]{0,1:T(8,128)} %slice.543) | copy-start | bytes 2359300
  502.0 8.4 %copy-start.50 = (f32[256,512]{0,1:T(8,128)S(1)}, f32[256,512]{0,1:T(8,128)}, u32[]{:S(2)}) copy-start(f32[256,512]{0,1:T(8,128)} %get-tuple-element.121) | copy-start | bytes 1572868
  508.6 7.7 %collective-permute-start.33 = (f32[256,258]{0,1:T(8,128)S(1)}, f32[256,258]{0,1:T(8,128)S(1)}, u32[]{:S(2)}, u32[]{:S(2)}) collective-permute-start(f32[256,258]{0,1:T(8,128)S(1)} %fusion.102), channel_id=1, source_target_pairs={{0,2},{1,3},{2,0},{3,1},{4,6},{5,7},{6,4},{7,5},{8,10},{9,11},{10,... | collective-permute-start | bytes 792584 | tf_op jit(solution)/shard_map/ppermute | solution.py:26
  (55 other events, 176.5 us)
Sparse Core Ops, SparseCore 0:
  12.2 54.6 all-gather.3
  69.1 89.3 all-gather.5
  160.6 76.3 all-gather.7
  239.2 97.7 reduce-scatter.3
  339.1 83.0 reduce-scatter.5
  424.3 58.2 reduce-scatter.7

commit v5 on v4

--- a/solution.py
+++ b/solution.py
@@ -78,6 +78,9 @@
 
 def scatter_dp(partial):
     return lax.psum_scatter(partial, "dp", scatter_dimension=0, tiled=True).astype(f32)
+
+
+pick = functools.partial(lax.dynamic_index_in_dim, keepdims=False)
 
 
 def turn(u, cos2, sin2):
@@ -308,8 +311,13 @@
 
     gain_one, gain_two = gain_attn.astype(f32)[:, None], gain_mlp.astype(f32)[:, None]
     qkv_own = jnp.concatenate([w_query, w_keyvalue], axis=1).astype(f32)
-    qkv_width = qkv_own.shape[1]
-    attn_shard = jnp.concatenate([(qkv_own * gain_one).astype(bf16), w_project.T], axis=1)
+    shard_rows = qkv_own.shape[0]
+    kv_rows = shard_rows // ranks
+    scaled_own = (qkv_own * gain_one).astype(bf16)
+    kv_part = lax.dynamic_slice_in_dim(scaled_own[:, heads_width:], rank * kv_rows, kv_rows)
+    attn_shard = jnp.concatenate(
+        [scaled_own[:, :heads_width], w_project.T, kv_part.reshape(-1, heads_width)], axis=0
+    )
     pair_own = [
         jnp.concatenate([w_gate[:, a:b], w_up[:, a:b]], axis=1).astype(f32) for a, b in parts
     ]
@@ -323,9 +331,17 @@
     inputs = all_blocks(layer_input, near)
     attn_full = gather_dp(attn_shard)
     ff_full = [gather_dp(after(ff_shards[0], *near))]
-    qkv_full, project_full = attn_full[:, :qkv_width], attn_full[:, qkv_width:]
+    attn_full = attn_full.reshape(-1, *attn_shard.shape)
+    query_full = attn_full[:, :shard_rows].reshape(model_width, heads_width)
+    project_full = attn_full[:, shard_rows : 2 * shard_rows].reshape(model_width, heads_width)
+    kv_part = attn_full[:, 2 * shard_rows :].reshape(-1, 2 * HD)
+    kv_near = near_blocks(kv_part)
+    kv_blocks = jnp.concatenate(all_blocks(kv_part, kv_near), axis=0)
+    kv_blocks = kv_blocks.reshape(ranks, -1, kv_rows, 2 * HD)
+    keyvalue_full = jnp.stack([pick(kv_blocks, order[j], 0) for j in range(ranks)], axis=1)
+    qkv_full = jnp.concatenate([query_full, keyvalue_full.reshape(model_width, 2 * HD)], axis=1)
     top = out_grad.astype(f32) * own_mask
-    top_own = after(top.astype(bf16), *inputs)
+    top_own = after(top.astype(bf16), keyvalue_full)
     top_near = near_blocks(top_own)
 
     def norm(block):
@@ -338,6 +354,7 @@
     ff_full.append(gather_dp(after(ff_shards[1], mixed)))
     mixed_rest = dot(after(mixed[rows:], *top_near), project_full, 1, 1).astype(bf16)
     mixed_sent = send_sums(mixed_rest)
+    top_near = [after(block, *mixed_sent) for block in top_near]
     top_all = jnp.concatenate(all_blocks(top_own, top_near), axis=0)
     after_attn = residual + finish_sums(
         dot(mixed[:rows], project_full, 1, 1), mixed_rest, mixed_sent
@@ -346,12 +363,15 @@
     inv_two = inverse_norm(after_attn)
     unit_two = after_attn * inv_two
     normed_own = after(unit_two.astype(bf16), top_all)
-    normed_two = jnp.concatenate(all_blocks(normed_own, near_blocks(normed_own)), axis=0)
-
-    def feed(part, normed, full):
-        width = part[1] - part[0]
-        grad = dot(top_all, full[:, 2 * width :], 1, 0)
-        both = dot(after(normed, grad), full[:, : 2 * width], 1, 0)
+    pairs = [full[:, : 2 * (b - a)] for (a, b), full in zip(parts, ff_full)]
+    downs = [full[:, 2 * (b - a) :] for (a, b), full in zip(parts, ff_full)]
+    first_grad = dot(top_all, downs[0], 1, 0)
+    normed_near = [after(block, first_grad) for block in near_blocks(normed_own)]
+    normed_two = jnp.concatenate(all_blocks(normed_own, normed_near), axis=0)
+
+    def feed(normed, pair, grad):
+        width = grad.shape[1]
+        both = dot(after(normed, grad), pair, 1, 0)
         gate, up = both[:, :width], both[:, width:]
         sig = jax.nn.sigmoid(gate)
         hidden = (gate * sig * up).astype(bf16)
@@ -368,12 +388,10 @@
             axis=1,
         )
 
-    pairs = [full[:, : 2 * (b - a)] for (a, b), full in zip(parts, ff_full)]
-    downs = [full[:, 2 * (b - a) :] for (a, b), full in zip(parts, ff_full)]
-    hidden0, grads0 = feed(parts[0], normed_two, ff_full[0])
+    hidden0, grads0 = feed(normed_two, pairs[0], first_grad)
     partial0 = partial(hidden0, grads0)
     rest0 = dot(after(grads0[rows:], partial0), pairs[0], 1, 1)
-    hidden1, grads1 = feed(parts[1], after(normed_two, rest0), ff_full[1])
+    hidden1, grads1 = feed(after(normed_two, rest0), pairs[1], dot(top_all, downs[1], 1, 0))
     rest = (rest0 + dot(grads1[rows:], pairs[1], 1, 1)).astype(bf16)
     rest_sent = send_sums(rest)
     partial1 = partial(after(hidden1, rest), after(grads1, rest))
@@ -397,13 +415,21 @@
     )
     down_sent = [after(block, query_grad) for block in send_sums(down_rest)]
     qkv_back = after(jnp.concatenate([query_grad, kv_back], axis=1), *down_sent)
+    kv_grads = dot(normed_one, qkv_back[:, heads_width:], 0, 0).astype(bf16)
+    kv_grads = kv_grads.reshape(-1, ranks, kv_rows, 2 * HD)
+    kv_own, *kv_rest = (pick(kv_grads, order[j], 1).reshape(-1, 2 * HD) for j in range(ranks))
+    kv_rest = jnp.concatenate(kv_rest, axis=0)
+    kv_sum = finish_sums(kv_own.astype(f32), kv_rest, send_sums(kv_rest)).astype(bf16)
     attn_partial = jnp.concatenate(
         [
-            dot(normed_one, qkv_back, 0, 0).astype(bf16),
-            dot(attn_top_all, mixed, 0, 0).astype(bf16),
+            dot(normed_one, qkv_back[:, :heads_width], 0, 0)
+            .astype(bf16)
+            .reshape(-1, shard_rows, heads_width),
+            dot(attn_top_all, mixed, 0, 0).astype(bf16).reshape(-1, shard_rows, heads_width),
+            kv_sum.reshape(model_width // shard_rows, -1, heads_width),
         ],
         axis=1,
-    )
+    ).reshape(-1, heads_width)
     attn_sum = scatter_dp(after(attn_partial, ff_sums[1]))
     own_down = sum(dot(h[:rows], w, 1, 1) for h, w in zip(hidden, downs))
     after_mlp = after_attn + finish_sums(own_down, down_rest, down_sent)
@@ -418,7 +444,8 @@
         scaled_one - unit_one * jnp.mean(scaled_one * unit_one, axis=-1, keepdims=True)
     )
 
-    qkv_sum, project_sum = attn_sum[:, :qkv_width], attn_sum[:, qkv_width:]
+    query_sum, project_sum = attn_sum[:shard_rows], attn_sum[shard_rows : 2 * shard_rows]
+    kv_sum = attn_sum[2 * shard_rows :].reshape(kv_rows, 2 * HD)
     pair_sums = [total[:, : own.shape[1]] for own, total in zip(pair_own, ff_sums)]
     down_sum = jnp.concatenate(
         [total[:, own.shape[1] :] for own, total in zip(pair_own, ff_sums)], axis=1
@@ -429,27 +456,31 @@
     scaled_sums = [total * gain_two for total in pair_sums]
     grad_gate = jnp.concatenate([s[:, : b - a] for (a, b), s in zip(parts, scaled_sums)], axis=1)
     grad_up = jnp.concatenate([s[:, b - a :] for (a, b), s in zip(parts, scaled_sums)], axis=1)
-    gain_one_part = jnp.sum(
-        qkv_own[:, :heads_width] * qkv_sum[:, :heads_width], axis=1, keepdims=True
-    ) + jnp.sum(qkv_own[:, heads_width:] * qkv_sum[:, heads_width:], axis=1, keepdims=True)
+    query_part = jnp.sum(qkv_own[:, :heads_width] * query_sum, axis=1, keepdims=True)
+    kv_here = lax.dynamic_slice_in_dim(qkv_own[:, heads_width:], rank * kv_rows, kv_rows)
+    gain_here = lax.dynamic_slice_in_dim(gain_one, rank * kv_rows, kv_rows)
     small = jnp.concatenate(
-        [qkv_sum[:, heads_width:] * gain_one, gain_one_part, gain_two_part], axis=1
-    )
-    step = 1
-    while step < ranks:
-        small = small + hop(small, step)
-        step *= 2
+        [
+            kv_sum * gain_here,
+            jnp.sum(kv_here * kv_sum, axis=1, keepdims=True),
+            jnp.concatenate([query_part, gain_two_part], axis=1).reshape(kv_rows, -1),
+        ],
+        axis=1,
+    )
+    blocks = jnp.stack([small] + [hop(small, j) for j in range(1, ranks)], axis=0)
+    sums = jnp.sum(blocks[:, :, 2 * HD + 1 :], axis=0).reshape(shard_rows, 2)
+    placed = jnp.concatenate([pick(blocks, order[j], 0) for j in range(ranks)], axis=0)
     return (
         output,
         input_grad,
-        qkv_sum[:, :heads_width] * gain_one,
-        small[:, : 2 * HD],
+        query_sum * gain_one,
+        placed[:, : 2 * HD],
         project_sum.T,
         grad_gate,
         grad_up,
         down_sum.T,
-        small[:, 2 * HD],
-        small[:, 2 * HD + 1],
+        sums[:, 0] + placed[:, 2 * HD],
+        sums[:, 1],
     )
 
 

time: 534 us -> 532 us (level)
  the two profiles are of different devices: /device:TPU:8 before, /device:TPU:0 now
where the time goes in v5:
time: 532 us; the launch traced here: 522 us
  waiting for transfers between devices  138 us (26%)
  matrix products  127 us (24%)
  other arithmetic  87.1 us (16%)
  local copies, waits for them, and re-layouts  67.7 us (13%)
  starting transfers between devices  52.8 us (10%)
  Pallas kernels  25.3 us (5%)
  between operations  24.3 us (5%)
    ppermute x43, waiting for transfers between devices, hop(): return lax.ppermute(value, 'tensor', [(i, i ^ step) for i in range(size)])  138 us
    dot_general x25, matrix products, dot(): lax.dot_general(a, b, (((ca,), (cb,)), ((), ())), preferred_element_type=...  127 us
    ppermute x43, starting transfers between devices, hop(): return lax.ppermute(value, 'tensor', [(i, i ^ step) for i in range(size)])  52.5 us
    unnamed x188, local copies, waits for them, and re-layouts  39.1 us
    concatenate x2, other arithmetic, partial(): jnp.concatenate([dot(normed_two, grads, 0, 0).astype(bf16), dot(top_all,...  19.5 us
    pallas_call x1, Pallas kernels, attend_back(): pl.pallas_call(attend_back_kernel, name='attend_back', grid_spec=pltpu.Pr...  13.7 us
    pallas_call x1, Pallas kernels, attend(): pl.pallas_call(attend_kernel, name='attend', grid_spec=pltpu.PrefetchScal...  11.6 us
  transfers between devices with their start and end apart: 49, of which 33 were waited for; matrix products, arithmetic and copies ran while one was open for 49% of the time, Pallas kernels for 5%

profile of v5, /device:TPU:0, one launch (start us, length us, event | category | flops | bytes accessed | tf_op | source)
XLA Modules:
  0.0 521.9 jit_solution(6417230493907159632)
XLA Ops:
  11.3 3.0 collective-permute-start
  20.7 1.9 copy.54
  25.9 11.5 %collective-permute-done = bf16[256,2048]{1,0:T(8,128)(2,1)S(1)} collective-permute-done((bf16[256,2048]{1,0:T(8,128)(2,1)S(1)}, bf16[256,2048]{1,0:T(8,128)(2,1)S(1)}, u32[]{:S(2)}, u32[]{:S(2)}) %collective-permute-start) | collective-permute-done | bytes 1048608 | tf_op jit(solution)/shard_map/ppermute | solution.py:26
  49.9 2.0 copy.56
  67.2 7.4 %collective-permute-done.2 = bf16[128,2048]{1,0:T(8,128)(2,1)S(1)} collective-permute-done((bf16[128,2048]{1,0:T(8,128)(2,1)S(1)}, bf16[128,2048]{1,0:T(8,128)(2,1)S(1)}, u32[]{:S(2)}, u32[]{:S(2)}) %collective-permute-start.2) | collective-permute-done | bytes 524320 | tf_op jit(solution)/shard_map/ppermute | solution.py:26
  81.3 3.9 collective-permute-done.5
  87.7 2.7 collective-permute-done.6
  98.0 7.4 %fusion.76.q_ref.kv_ref = f32[1024,768]{1,0:T(8,128)} fusion(bf16[1024,2048]{1,0:T(8,128)(2,1)} %fusion.80, bf16[2048,256]{1,0:T(8,128)(2,1)S(1)} %bitcast.104, bf16[2048,512]{1,0:T(8,128)(2,1)S(1)} %bitcast.99), kind=kOutput, calls=%fused_computation.162 | convolution fusion | flops 3227516928 | bytes 10485760 | tf_op jit(solution)/shard_map/dot_general | solution.py:21
  105.4 11.6 %attend.1 = (bf16[1024,512]{1,0:T(8,128)(2,1)S(1)}, bf16[1024,256]{1,0:T(8,128)(2,1)S(1)}, bf16[1024,512]{1,0:T(8,128)(2,1)S(1)}, f32[1024,128]{1,0:T(8,128)S(1)}) custom-call(s32[2]{0:T(128)S(1)} %pad_add_fusion.where_ref, f32[1024,768]{1,0:T(8,128)} %fusion.76.q_ref.kv_ref, f32[1024,768]{1,0:T(8,128)} %fusion.76.q_ref.kv_ref, ...), custom_call_target="tpu_custom_call" | custom-call | flops 2147483648 | bytes 8388608 | tf_op jit(solution)/shard_map/attend/pallas_call | solution.py:199
  119.7 3.7 convolution_convert_fusion.2
  125.9 20.2 %collective-permute-done.12 = bf16[256,2048]{1,0:T(8,128)(2,1)S(1)} collective-permute-done((bf16[256,2048]{1,0:T(8,128)(2,1)S(1)}, bf16[256,2048]{1,0:T(8,128)(2,1)S(1)}, u32[]{:S(2)}, u32[]{:S(2)}) %collective-permute-start.12) | collective-permute-done | bytes 1048608 | tf_op jit(solution)/shard_map/ppermute | solution.py:26
  157.3 2.8 collective-permute-done.11
  161.4 5.4 %collective-permute-done.14 = bf16[128,2048]{1,0:T(8,128)(2,1)S(1)} collective-permute-done((bf16[128,2048]{1,0:T(8,128)(2,1)S(1)}, bf16[128,2048]{1,0:T(8,128)(2,1)S(1)}, u32[]{:S(2)}, u32[]{:S(2)}) %collective-permute-start.14) | collective-permute-done | bytes 524320 | tf_op jit(solution)/shard_map/ppermute | solution.py:26
  169.9 2.1 collective-permute-start.17
  172.6 6.6 %fusion.24 = f32[1024,768]{0,1:T(8,128)S(1)} fusion(bf16[1024,2048]{1,0:T(8,128)(2,1)} %copy-done.63, bf16[2048,2304]{0,1:T(8,128)(2,1)} %all-gather.6.cloned.1.call-done), kind=kOutput, calls=%fused_computation.61 | convolution fusion | flops 3221225472 | bytes 10485760 | tf_op jit(solution)/shard_map/dot_general | solution.py:21
  179.2 9.0 %collective-permute-done.17 = bf16[256,2048]{1,0:T(8,128)(2,1)} collective-permute-done((bf16[256,2048]{1,0:T(8,128)(2,1)}, bf16[256,2048]{1,0:T(8,128)(2,1)}, u32[]{:S(2)}, u32[]{:S(2)}) %collective-permute-start.17) | collective-permute-done | bytes 1048608 | tf_op jit(solution)/shard_map/ppermute | solution.py:26
  194.1 2.9 collective-permute-start.19
  199.8 4.3 collective-permute-done.19
  204.2 6.8 %fusion.4 = f32[1024,1536]{0,1:T(8,128)S(1)} fusion(bf16[1024,2048]{1,0:T(8,128)(2,1)S(1)} %constant_dynamic-update-slice_fusion.10, bf16[2048,2304]{0,1:T(8,128)(2,1)S(1)} %copy-done.79), kind=kOutput, calls=%fused_computation.10 | convolution fusion | flops 6442450944 | bytes 16777216 | tf_op jit(solution)/shard_map/dot_general | solution.py:21
  211.0 2.2 multiply_convert_fusion
  213.4 3.6 convolution_convert_fusion.3
  217.0 8.7 %convolution_convert_fusion.1 = bf16[2048,1536]{0,1:T(8,128)(2,1)S(1)} fusion(bf16[1024,2048]{1,0:T(8,128)(2,1)S(1)} %constant_dynamic-update-slice_fusion.10, bf16[1024,768]{0,1:T(8,128)(2,1)S(1)} %get-tuple-element.93, bf16[1024,768]{0,1:T(8,128)(2,1)S(1)} %get-tuple-element.94), kind=kOutput, calls=%fused_computation.3 | convolution fusion | flops 6451888128 | bytes 13631488 | tf_op jit(solution)/shard_map/dot_general | solution.py:21
  225.7 11.5 %pad_maximum_fusion = bf16[2048,2304]{0,1:T(8,128)(2,1)} fusion(bf16[2048,768]{0,1:T(8,128)(2,1)S(1)} %convolution_convert_fusion.3, bf16[2048,1536]{0,1:T(8,128)(2,1)S(1)} %convolution_convert_fusion.1), kind=kLoop, calls=%fused_computation | loop fusion | flops 18874368 | bytes 18874368 | tf_op jit(solution)/shard_map/concatenate | solution.py:383
  239.1 9.8 %fusion.2 = f32[768,2048]{1,0:T(8,128)} fusion(bf16[768,1536]{0,1:T(8,128)(2,1)S(1)} %fusion.26, bf16[2048,2304]{0,1:T(8,128)(2,1)} %all-gather.6.cloned.1.call-done), kind=kOutput, calls=%fused_computation.8 | convolution fusion | flops 4831838208 | bytes 14942208 | tf_op jit(solution)/shard_map/dot_general | solution.py:21
  248.9 5.7 %fusion.41 = f32[1024,640]{0,1:T(8,128)S(1)} fusion(bf16[1024,2048]{1,0:T(8,128)(2,1)} %copy-done.63, bf16[2048,1920]{0,1:T(8,128)(2,1)} %all-gather.8.cloned.1.call-done), kind=kOutput, calls=%fused_computation.85 | convolution fusion | flops 2684354560 | bytes 9437184 | tf_op jit(solution)/shard_map/dot_general | solution.py:21
  255.4 5.7 %fusion.10 = f32[1024,1280]{0,1:T(8,128)S(1)} fusion(bf16[1024,2048]{1,0:T(8,128)(2,1)S(1)} %copy-done.67, bf16[2048,1920]{0,1:T(8,128)(2,1)S(1)} %copy-done.60), kind=kOutput, calls=%fused_computation.17 | convolution fusion | flops 5368709120 | bytes 14680064 | tf_op jit(solution)/shard_map/dot_general | solution.py:21
  264.5 7.9 %add_convert_fusion = bf16[768,2048]{1,0:T(8,128)(2,1)} fusion(f32[768,2048]{1,0:T(8,128)} %fusion.2, bf16[2048,1920]{0,1:T(8,128)(2,1)S(1)} %copy-done.60, bf16[1024,640]{0,1:T(8,128)(2,1)S(1)} %get-tuple-element.96, bf16[1024,640]{0,1:T(8,128)(2,1)S(1)} %get-tuple-element.95), kind=kOutput, calls=%fused_computation.4 | convolution fusion | flops 4033609728 | bytes 17301504 | tf_op jit(solution)/shard_map/dot_general | solution.py:21
  272.4 4.6 convolution_convert_fusion.5
  277.0 7.4 %convolution_convert_fusion = bf16[2048,1280]{0,1:T(8,128)(2,1)} fusion(bf16[1024,1280]{0,1:T(8,128)(2,1)S(1)} %pad_maximum_fusion.4, bf16[1024,2048]{1,0:T(8,128)(2,1)S(1)} %copy-done.68), kind=kOutput, calls=%fused_computation.2 | convolution fusion | flops 5371330560 | bytes 12058624 | tf_op jit(solution)/shard_map/dot_general | solution.py:21
  284.4 8.0 %pad_maximum_fusion.1 = bf16[2048,1920]{0,1:T(8,128)(2,1)} fusion(bf16[2048,640]{0,1:T(8,128)(2,1)} %convolution_convert_fusion.5, bf16[2048,1280]{0,1:T(8,128)(2,1)} %convolution_convert_fusion), kind=kLoop, calls=%fused_computation.1 | loop fusion | flops 15728640 | bytes 15728640 | tf_op jit(solution)/shard_map/concatenate | solution.py:383
  294.3 2.1 collective-permute-start.22
  298.3 4.1 fusion.6
  302.4 13.1 %collective-permute-done.22 = bf16[256,2048]{1,0:T(8,128)(2,1)S(1)} collective-permute-done((bf16[256,2048]{1,0:T(8,128)(2,1)S(1)}, bf16[256,2048]{1,0:T(8,128)(2,1)S(1)}, u32[]{:S(2)}, u32[]{:S(2)}) %collective-permute-start.22) | collective-permute-done | bytes 1048608 | tf_op jit(solution)/shard_map/ppermute | solution.py:26
  317.5 1.9 collective-permute-start.21
  320.0 4.6 fusion.17
  324.7 3.9 collective-permute-done.21
  328.6 2.3 collective-permute-done.23
  332.7 2.8 constant_dynamic-update-slice_fusion.19
  336.9 5.2 fusion.20
  342.1 14.0 %collective-permute-done.25 = bf16[256,2048]{1,0:T(8,128)(2,1)S(1)} collective-permute-done((bf16[256,2048]{1,0:T(8,128)(2,1)}, bf16[256,2048]{1,0:T(8,128)(2,1)S(1)}, u32[]{:S(2)}, u32[]{:S(2)}) %collective-permute-start.25) | collective-permute-done | bytes 1048608 | tf_op jit(solution)/shard_map/ppermute | solution.py:26
  359.4 4.8 add_convert_fusion.1
  364.3 2.1 constant_dynamic-update-slice_fusion.18
  366.5 3.2 collective-permute-done.26
  369.7 3.2 collective-permute-done.27
  377.3 2.0 copy-done.62
  379.3 3.8 convolution_convert_fusion.6
  383.1 3.1 convert_element_type.346
  386.1 4.6 convolution_convert_fusion.9.dm_ref
  390.8 13.7 %attend_back.1 = (bf16[1024,512]{1,0:T(8,128)(2,1)S(1)}, bf16[1024,256]{1,0:T(8,128)(2,1)S(1)}) custom-call(s32[2]{0:T(128)S(1)} %pad_add_fusion.where_ref, bf16[1024,512]{1,0:T(8,128)(2,1)S(1)} %get-tuple-element.57.qr_ref, bf16[1024,256]{1,0:T(8,128)(2,1)S(1)} %copy-done.3, bf16[1024,512]{1,0:T(8,128)(2,1)S(1)} %convolution_convert_fusion.9.dm_ref, ...), custom_call_target="tpu_custom_call" | custom-call | flops 5368709120 | bytes 8388608 | tf_op jit(solution)/shard_map/attend_back/pallas_call | solution.py:237
  405.6 3.5 convolution_convert_fusion.8
  410.7 5.9 %convolution_convert_fusion.7 = bf16[2048,512]{1,0:T(8,128)(2,1)} fusion(bf16[1024,2048]{1,0:T(8,128)(2,1)} %fusion.80, bf16[1024,768]{1,0:T(8,128)(2,1)S(1)} %pad_maximum_fusion.9), kind=kOutput, calls=%fused_computation.42 | convolution fusion | flops 2148532224 | bytes 7340032 | tf_op jit(solution)/shard_map/dot_general | solution.py:21
  418.9 4.1 collective-permute-done.34
  424.5 3.7 collective-permute-done.35
  428.4 3.9 pad_maximum_fusion.2
  436.8 3.0 fusion.22
  439.9 3.0 convolution_add_fusion
  452.3 2.4 fusion.75
  454.6 3.1 convolution_convert_fusion.4
  467.3 10.8 %collective-permute-done.38 = bf16[256,2048]{1,0:T(8,128)(2,1)S(1)} collective-permute-done((bf16[256,2048]{1,0:T(8,128)(2,1)}, bf16[256,2048]{1,0:T(8,128)(2,1)S(1)}, u32[]{:S(2)}, u32[]{:S(2)}) %collective-permute-start.38) | collective-permute-done | bytes 1048608 | tf_op jit(solution)/shard_map/ppermute | solution.py:26
  481.9 2.6 fusion.59
  489.4 2.5 maximum_bitcast_fusion
  491.9 2.1 collective-permute-done.37
  498.9 2.3 fusion.34
  510.4 2.3 collective-permute-done.42
  (414 shorter events, 157.7 us)
Async XLA Ops:
  7.2 8.6 %copy-start.80 = (bf16[256]{0:T(256)(128)(2,1)S(1)}, bf16[256]{0:T(256)(128)(2,1)}, u32[]{:S(2)}) copy-start(bf16[256]{0:T(256)(128)(2,1)} %param.21) | copy-start | bytes 1540
  7.2 69.2 %all-gather.4.cloned.1.call-start = ((), (), s32[]{:S(2)}) async-start(), calls=%async_computation.3 | async-start | bytes 5013504 | tf_op jit(solution)/shard_map/all_gather | solution.py:76
  11.2 161.4 %all-gather.6.cloned.1.call-start = ((), (), s32[]{:S(2)}) async-start(), calls=%async_computation.4 | async-start | bytes 10616832 | tf_op jit(solution)/shard_map/all_gather | solution.py:76
  11.3 26.2 %collective-permute-start = (bf16[256,2048]{1,0:T(8,128)(2,1)S(1)}, bf16[256,2048]{1,0:T(8,128)(2,1)S(1)}, u32[]{:S(2)}, u32[]{:S(2)}) collective-permute-start(bf16[256,2048]{1,0:T(8,128)(2,1)S(1)} %copy-done.6), channel_id=1, source_target_pairs={{0,1},{1,0},{2,3},{3,2},{4,5},{5,4},{6,7},{7,6},{8,9},{9,8},{10,11... | collective-permute-start | bytes 3145736 | tf_op jit(solution)/shard_map/ppermute | solution.py:26
  14.3 24.6 %collective-permute-start.1 = (bf16[256,2048]{1,0:T(8,128)(2,1)S(1)}, bf16[256,2048]{1,0:T(8,128)(2,1)S(1)}, u32[]{:S(2)}, u32[]{:S(2)}) collective-permute-start(bf16[256,2048]{1,0:T(8,128)(2,1)S(1)} %copy-done.6), channel_id=1, source_target_pairs={{0,2},{1,3},{2,0},{3,1},{4,6},{5,7},{6,4},{7,5},{8,10},{9,11},{10,... | collective-permute-start | bytes 3145736 | tf_op jit(solution)/shard_map/ppermute | solution.py:26
  15.8 42.3 %copy-start.74 = (f32[256]{0:T(256)}, f32[256]{0:T(256)S(1)}, u32[]{:S(2)}) copy-start(f32[256]{0:T(256)S(1)} %convert_element_type.321) | copy-start | bytes 3076
  18.8 7.2 %copy-start.36 = (bf16[256,768]{0,1:T(8,128)(2,1)}, bf16[256,768]{0,1:T(8,128)(2,1)S(1)}, u32[]{:S(2)}) copy-start(bf16[256,768]{0,1:T(8,128)(2,1)S(1)} %copy.53) | copy-start | bytes 1179652
  37.5 16.9 %copy-start.25 = (bf16[256,2048]{1,0:T(8,128)(2,1)}, bf16[256,2048]{1,0:T(8,128)(2,1)S(1)}, u32[]{:S(2)}) copy-start(bf16[256,2048]{1,0:T(8,128)(2,1)S(1)} %collective-permute-done) | copy-start | bytes 3145732
  38.9 209.9 %all-gather.8.cloned.1.call-start = ((), (), s32[]{:S(2)}) async-start(), calls=%async_computation.5 | async-start | bytes 8847360 | tf_op jit(solution)/shard_map/all_gather | solution.py:76
  49.9 8.3 %copy-start.45 = (bf16[256,640]{0,1:T(8,128)(2,1)}, bf16[256,640]{0,1:T(8,128)(2,1)S(1)}, u32[]{:S(2)}) copy-start(bf16[256,640]{0,1:T(8,128)(2,1)S(1)} %copy.55) | copy-start | bytes 983044
  62.0 12.6 %collective-permute-start.2 = (bf16[128,2048]{1,0:T(8,128)(2,1)S(1)}, bf16[128,2048]{1,0:T(8,128)(2,1)S(1)}, u32[]{:S(2)}, u32[]{:S(2)}) collective-permute-start(bf16[128,2048]{1,0:T(8,128)(2,1)S(1)} %slice.583), channel_id=1, source_target_pairs={{0,1},{1,0},{2,3},{3,2},{4,5},{5,4},{6,7},{7,6},{8,9},{9,8},{10,11... | collective-permute-start | bytes 1572872 | tf_op jit(solution)/shard_map/ppermute | solution.py:26
  62.5 12.7 %collective-permute-start.3 = (bf16[128,2048]{1,0:T(8,128)(2,1)S(1)}, bf16[128,2048]{1,0:T(8,128)(2,1)S(1)}, u32[]{:S(2)}, u32[]{:S(2)}) collective-permute-start(bf16[128,2048]{1,0:T(8,128)(2,1)S(1)} %slice.584), channel_id=1, source_target_pairs={{0,2},{1,3},{2,0},{3,1},{4,6},{5,7},{6,4},{7,5},{8,10},{9,11},{10,... | collective-permute-start | bytes 1572872 | tf_op jit(solution)/shard_map/ppermute | solution.py:26
  77.5 8.5 %collective-permute-start.4 = (bf16[512,256]{1,0:T(8,128)(2,1)S(1)}, bf16[512,256]{1,0:T(8,128)(2,1)S(1)}, u32[]{:S(2)}, u32[]{:S(2)}) collective-permute-start(bf16[512,256]{1,0:T(8,128)(2,1)S(1)} %reshape.205), channel_id=1, source_target_pairs={{0,1},{1,0},{2,3},{3,2},{4,5},{5,4},{6,7},{7,6},{8,9},{9,8},{10,11... | collective-permute-start | bytes 786440 | tf_op jit(solution)/shard_map/ppermute | solution.py:26
  78.8 6.4 %collective-permute-start.5 = (bf16[512,256]{1,0:T(8,128)(2,1)S(1)}, bf16[512,256]{1,0:T(8,128)(2,1)S(1)}, u32[]{:S(2)}, u32[]{:S(2)}) collective-permute-start(bf16[512,256]{1,0:T(8,128)(2,1)S(1)} %reshape.205), channel_id=1, source_target_pairs={{0,2},{1,3},{2,0},{3,1},{4,6},{5,7},{6,4},{7,5},{8,10},{9,11},{10,... | collective-permute-start | bytes 786440 | tf_op jit(solution)/shard_map/ppermute | solution.py:26
  85.2 5.2 collective-permute-start.6
  86.0 5.4 %collective-permute-start.7 = (bf16[256,256]{1,0:T(8,128)(2,1)S(1)}, bf16[256,256]{1,0:T(8,128)(2,1)S(1)}, u32[]{:S(2)}, u32[]{:S(2)}) collective-permute-start(bf16[256,256]{1,0:T(8,128)(2,1)S(1)} %slice.590), channel_id=1, source_target_pairs={{0,2},{1,3},{2,0},{3,1},{4,6},{5,7},{6,4},{7,5},{8,10},{9,11},{10,... | collective-permute-start | bytes 393224 | tf_op jit(solution)/shard_map/ppermute | solution.py:26
  87.7 7.0 %copy-start.31 = (bf16[4352,512]{1,0:T(8,128)(2,1)S(1)}, bf16[4352,512]{1,0:T(8,128)(2,1)}, u32[]{:S(2)}) copy-start(bf16[4352,512]{1,0:T(8,128)(2,1)} %all-gather.4.cloned.1.call-done) | copy-start | bytes 13369348
  91.7 28.0 %collective-permute-start.8 = (bf16[256,2048]{1,0:T(8,128)(2,1)}, bf16[256,2048]{1,0:T(8,128)(2,1)}, u32[]{:S(2)}, u32[]{:S(2)}) collective-permute-start(bf16[256,2048]{1,0:T(8,128)(2,1)} %fusion.38), channel_id=1, source_target_pairs={{0,1},{1,0},{2,3},{3,2},{4,5},{5,4},{6,7},{7,6},{8,9},{9,8},{10,11... | collective-permute-start | bytes 3145736 | tf_op jit(solution)/shard_map/ppermute | solution.py:26
  93.1 26.5 %collective-permute-start.9 = (bf16[256,2048]{1,0:T(8,128)(2,1)}, bf16[256,2048]{1,0:T(8,128)(2,1)}, u32[]{:S(2)}, u32[]{:S(2)}) collective-permute-start(bf16[256,2048]{1,0:T(8,128)(2,1)} %fusion.38), channel_id=1, source_target_pairs={{0,2},{1,3},{2,0},{3,1},{4,6},{5,7},{6,4},{7,5},{8,10},{9,11},{10,... | collective-permute-start | bytes 3145736 | tf_op jit(solution)/shard_map/ppermute | solution.py:26
  119.6 263.5 %reduce-scatter.4.cloned.1.call-start = ((), (), s32[]{:S(2)}) async-start(), calls=%async_computation.6 | async-start | bytes 10616832 | tf_op jit(solution)/shard_map/reduce_scatter | solution.py:80
  123.6 22.4 %collective-permute-start.12 = (bf16[256,2048]{1,0:T(8,128)(2,1)S(1)}, bf16[256,2048]{1,0:T(8,128)(2,1)S(1)}, u32[]{:S(2)}, u32[]{:S(2)}) collective-permute-start(bf16[256,2048]{1,0:T(8,128)(2,1)S(1)} %pad_maximum_fusion.15), channel_id=1, source_target_pairs={{0,2},{1,3},{2,0},{3,1},{4,6},{5,7},{6,4},{7,5},{8,10},{9,11},{10,... | collective-permute-start | bytes 3145736 | tf_op jit(solution)/shard_map/ppermute | solution.py:26
  124.3 22.0 %collective-permute-start.10 = (bf16[256,2048]{1,0:T(8,128)(2,1)S(1)}, bf16[256,2048]{1,0:T(8,128)(2,1)S(1)}, u32[]{:S(2)}, u32[]{:S(2)}) collective-permute-start(bf16[256,2048]{1,0:T(8,128)(2,1)S(1)} %pad_maximum_fusion.14), channel_id=1, source_target_pairs={{0,1},{1,0},{2,3},{3,2},{4,5},{5,4},{6,7},{7,6},{8,9},{9,8},{10,11... | collective-permute-start | bytes 3145736 | tf_op jit(solution)/shard_map/ppermute | solution.py:26
  146.8 13.2 %collective-permute-start.11 = (bf16[128,2048]{1,0:T(8,128)(2,1)S(1)}, bf16[128,2048]{1,0:T(8,128)(2,1)S(1)}, u32[]{:S(2)}, u32[]{:S(2)}) collective-permute-start(bf16[128,2048]{1,0:T(8,128)(2,1)S(1)} %get-tuple-element.119), channel_id=1, source_target_pairs={{0,2},{1,3},{2,0},{3,1},{4,6},{5,7},{6,4},{7,5},{8,10},{9,11},{10,... | collective-permute-start | bytes 1572872 | tf_op jit(solution)/shard_map/ppermute | solution.py:26
  148.7 11.7 %collective-permute-start.13 = (bf16[128,2048]{1,0:T(8,128)(2,1)S(1)}, bf16[128,2048]{1,0:T(8,128)(2,1)S(1)}, u32[]{:S(2)}, u32[]{:S(2)}) collective-permute-start(bf16[128,2048]{1,0:T(8,128)(2,1)S(1)} %get-tuple-element.120), channel_id=1, source_target_pairs={{0,1},{1,0},{2,3},{3,2},{4,5},{5,4},{6,7},{7,6},{8,9},{9,8},{10,11... | collective-permute-start | bytes 1572872 | tf_op jit(solution)/shard_map/ppermute | solution.py:26
  151.7 15.1 %collective-permute-start.14 = (bf16[128,2048]{1,0:T(8,128)(2,1)S(1)}, bf16[128,2048]{1,0:T(8,128)(2,1)S(1)}, u32[]{:S(2)}, u32[]{:S(2)}) collective-permute-start(bf16[128,2048]{1,0:T(8,128)(2,1)S(1)} %slice.479), channel_id=1, source_target_pairs={{0,1},{1,0},{2,3},{3,2},{4,5},{5,4},{6,7},{7,6},{8,9},{9,8},{10,11... | collective-permute-start | bytes 1572872 | tf_op jit(solution)/shard_map/ppermute | solution.py:26
  154.3 13.2 %collective-permute-start.15 = (bf16[128,2048]{1,0:T(8,128)(2,1)S(1)}, bf16[128,2048]{1,0:T(8,128)(2,1)S(1)}, u32[]{:S(2)}, u32[]{:S(2)}) collective-permute-start(bf16[128,2048]{1,0:T(8,128)(2,1)S(1)} %slice.480), channel_id=1, source_target_pairs={{0,2},{1,3},{2,0},{3,1},{4,6},{5,7},{6,4},{7,5},{8,10},{9,11},{10,... | collective-permute-start | bytes 1572872 | tf_op jit(solution)/shard_map/ppermute | solution.py:26
  169.9 18.4 %collective-permute-start.17 = (bf16[256,2048]{1,0:T(8,128)(2,1)}, bf16[256,2048]{1,0:T(8,128)(2,1)}, u32[]{:S(2)}, u32[]{:S(2)}) collective-permute-start(bf16[256,2048]{1,0:T(8,128)(2,1)} %multiply_convert_fusion.6), channel_id=1, source_target_pairs={{0,2},{1,3},{2,0},{3,1},{4,6},{5,7},{6,4},{7,5},{8,10},{9,11},{10,... | collective-permute-start | bytes 3145736 | tf_op jit(solution)/shard_map/ppermute | solution.py:26
  172.0 20.9 %collective-permute-start.16 = (bf16[256,2048]{1,0:T(8,128)(2,1)}, bf16[256,2048]{1,0:T(8,128)(2,1)}, u32[]{:S(2)}, u32[]{:S(2)}) collective-permute-start(bf16[256,2048]{1,0:T(8,128)(2,1)} %multiply_convert_fusion.6), channel_id=1, source_target_pairs={{0,1},{1,0},{2,3},{3,2},{4,5},{5,4},{6,7},{7,6},{8,9},{9,8},{10,11... | collective-permute-start | bytes 3145736 | tf_op jit(solution)/shard_map/ppermute | solution.py:26
  188.2 15.9 %copy-start.79 = (bf16[2048,2304]{0,1:T(8,128)(2,1)S(1)}, bf16[2048,2304]{0,1:T(8,128)(2,1)}, u32[]{:S(2)}) copy-start(bf16[2048,2304]{0,1:T(8,128)(2,1)} %all-gather.6.cloned.1.call-done) | copy-start | bytes 28311556
  189.5 10.3 %collective-permute-start.18 = (bf16[128,2048]{1,0:T(8,128)(2,1)S(1)}, bf16[128,2048]{1,0:T(8,128)(2,1)S(1)}, u32[]{:S(2)}, u32[]{:S(2)}) collective-permute-start(bf16[128,2048]{1,0:T(8,128)(2,1)S(1)} %slice.485), channel_id=1, source_target_pairs={{0,1},{1,0},{2,3},{3,2},{4,5},{5,4},{6,7},{7,6},{8,9},{9,8},{10,11... | collective-permute-start | bytes 1572872 | tf_op jit(solution)/shard_map/ppermute | solution.py:26
  194.1 10.0 %collective-permute-start.19 = (bf16[128,2048]{1,0:T(8,128)(2,1)S(1)}, bf16[128,2048]{1,0:T(8,128)(2,1)S(1)}, u32[]{:S(2)}, u32[]{:S(2)}) collective-permute-start(bf16[128,2048]{1,0:T(8,128)(2,1)S(1)} %slice.486), channel_id=1, source_target_pairs={{0,2},{1,3},{2,0},{3,1},{4,6},{5,7},{6,4},{7,5},{8,10},{9,11},{10,... | collective-permute-start | bytes 1572872 | tf_op jit(solution)/shard_map/ppermute | solution.py:26
  204.1 12.9 %copy-start.66 = (bf16[1024,2048]{1,0:T(8,128)(2,1)}, bf16[1024,2048]{1,0:T(8,128)(2,1)S(1)}, u32[]{:S(2)}) copy-start(bf16[1024,2048]{1,0:T(8,128)(2,1)S(1)} %constant_dynamic-update-slice_fusion.10) | copy-start | bytes 12582916
  237.2 195.0 %reduce-scatter.6.cloned.1.call-start = ((), (), s32[]{:S(2)}) async-start(), calls=%async_computation.7 | async-start | bytes 8847360 | tf_op jit(solution)/shard_map/reduce_scatter | solution.py:80
  263.1 9.3 %copy-start.53 = (bf16[1024,640]{0,1:T(8,128)(2,1)}, bf16[1024,640]{0,1:T(8,128)(2,1)S(1)}, u32[]{:S(2)}) copy-start(bf16[1024,640]{0,1:T(8,128)(2,1)S(1)} %get-tuple-element.54) | copy-start | bytes 3932164
  264.5 7.9 %copy-start.65 = (bf16[1024,2048]{1,0:T(8,128)(2,1)S(1)}, bf16[1024,2048]{1,0:T(8,128)(2,1)}, u32[]{:S(2)}) copy-start(bf16[1024,2048]{1,0:T(8,128)(2,1)} %copy-done.63) | copy-start | bytes 12582916
  292.4 208.9 %reduce-scatter.8.cloned.1.call-start = ((), (), s32[]{:S(2)}) async-start(), calls=%async_computation.8 | async-start | bytes 5013504 | tf_op jit(solution)/shard_map/reduce_scatter | solution.py:80
  294.3 21.2 %collective-permute-start.22 = (bf16[256,2048]{1,0:T(8,128)(2,1)S(1)}, bf16[256,2048]{1,0:T(8,128)(2,1)S(1)}, u32[]{:S(2)}, u32[]{:S(2)}) collective-permute-start(bf16[256,2048]{1,0:T(8,128)(2,1)S(1)} %pad_maximum_fusion.17), channel_id=1, source_target_pairs={{0,2},{1,3},{2,0},{3,1},{4,6},{5,7},{6,4},{7,5},{8,10},{9,11},{10,... | collective-permute-start | bytes 3145736 | tf_op jit(solution)/shard_map/ppermute | solution.py:26
  296.5 19.2 %collective-permute-start.20 = (bf16[256,2048]{1,0:T(8,128)(2,1)S(1)}, bf16[256,2048]{1,0:T(8,128)(2,1)S(1)}, u32[]{:S(2)}, u32[]{:S(2)}) collective-permute-start(bf16[256,2048]{1,0:T(8,128)(2,1)S(1)} %pad_maximum_fusion.16), channel_id=1, source_target_pairs={{0,1},{1,0},{2,3},{3,2},{4,5},{5,4},{6,7},{7,6},{8,9},{9,8},{10,11... | collective-permute-start | bytes 3145736 | tf_op jit(solution)/shard_map/ppermute | solution.py:26
  317.5 11.0 %collective-permute-start.21 = (bf16[128,2048]{1,0:T(8,128)(2,1)S(1)}, bf16[128,2048]{1,0:T(8,128)(2,1)S(1)}, u32[]{:S(2)}, u32[]{:S(2)}) collective-permute-start(bf16[128,2048]{1,0:T(8,128)(2,1)S(1)} %get-tuple-element.113), channel_id=1, source_target_pairs={{0,2},{1,3},{2,0},{3,1},{4,6},{5,7},{6,4},{7,5},{8,10},{9,11},{10,... | collective-permute-start | bytes 1572872 | tf_op jit(solution)/shard_map/ppermute | solution.py:26
  319.5 11.4 %collective-permute-start.23 = (bf16[128,2048]{1,0:T(8,128)(2,1)S(1)}, bf16[128,2048]{1,0:T(8,128)(2,1)S(1)}, u32[]{:S(2)}, u32[]{:S(2)}) collective-permute-start(bf16[128,2048]{1,0:T(8,128)(2,1)S(1)} %get-tuple-element.114), channel_id=1, source_target_pairs={{0,1},{1,0},{2,3},{3,2},{4,5},{5,4},{6,7},{7,6},{8,9},{9,8},{10,11... | collective-permute-start | bytes 1572872 | tf_op jit(solution)/shard_map/ppermute | solution.py:26
  324.6 6.8 %copy-start.10 = (f32[128,2048]{1,0:T(8,128)S(1)}, f32[128,2048]{1,0:T(8,128)}, u32[]{:S(2)}) copy-start(f32[128,2048]{1,0:T(8,128)} %copy-done.9) | copy-start | bytes 3145732
  335.5 20.6 %collective-permute-start.25 = (bf16[256,2048]{1,0:T(8,128)(2,1)}, bf16[256,2048]{1,0:T(8,128)(2,1)S(1)}, u32[]{:S(2)}, u32[]{:S(2)}) collective-permute-start(bf16[256,2048]{1,0:T(8,128)(2,1)} %get-tuple-element.91), channel_id=1, source_target_pairs={{0,2},{1,3},{2,0},{3,1},{4,6},{5,7},{6,4},{7,5},{8,10},{9,11},{10,... | collective-permute-start | bytes 3145736 | tf_op jit(solution)/shard_map/ppermute | solution.py:26
  335.5 21.4 %collective-permute-start.24 = (bf16[256,2048]{1,0:T(8,128)(2,1)}, bf16[256,2048]{1,0:T(8,128)(2,1)}, u32[]{:S(2)}, u32[]{:S(2)}) collective-permute-start(bf16[256,2048]{1,0:T(8,128)(2,1)} %get-tuple-element.91), channel_id=1, source_target_pairs={{0,1},{1,0},{2,3},{3,2},{4,5},{5,4},{6,7},{7,6},{8,9},{9,8},{10,11... | collective-permute-start | bytes 3145736 | tf_op jit(solution)/shard_map/ppermute | solution.py:26
  336.9 22.5 %copy-start.54 = (bf16[1024,640]{0,1:T(8,128)(2,1)S(1)}, bf16[1024,640]{0,1:T(8,128)(2,1)}, u32[]{:S(2)}) copy-start(bf16[1024,640]{0,1:T(8,128)(2,1)} %copy-done.53) | copy-start | bytes 3932164
  356.1 13.5 %collective-permute-start.26 = (bf16[128,2048]{1,0:T(8,128)(2,1)S(1)}, bf16[128,2048]{1,0:T(8,128)(2,1)S(1)}, u32[]{:S(2)}, u32[]{:S(2)}) collective-permute-start(bf16[128,2048]{1,0:T(8,128)(2,1)S(1)} %slice.638), channel_id=1, source_target_pairs={{0,1},{1,0},{2,3},{3,2},{4,5},{5,4},{6,7},{7,6},{8,9},{9,8},{10,11... | collective-permute-start | bytes 1572872 | tf_op jit(solution)/shard_map/ppermute | solution.py:26
  358.0 14.9 %collective-permute-start.27 = (bf16[128,2048]{1,0:T(8,128)(2,1)S(1)}, bf16[128,2048]{1,0:T(8,128)(2,1)S(1)}, u32[]{:S(2)}, u32[]{:S(2)}) collective-permute-start(bf16[128,2048]{1,0:T(8,128)(2,1)S(1)} %slice.639), channel_id=1, source_target_pairs={{0,2},{1,3},{2,0},{3,1},{4,6},{5,7},{6,4},{7,5},{8,10},{9,11},{10,... | collective-permute-start | bytes 1572872 | tf_op jit(solution)/shard_map/ppermute | solution.py:26
  364.2 8.8 %copy-start.40 = (bf16[768,2048]{1,0:T(8,128)(2,1)}, bf16[768,2048]{1,0:T(8,128)(2,1)S(1)}, u32[]{:S(2)}) copy-start(bf16[768,2048]{1,0:T(8,128)(2,1)S(1)} %add_convert_fusion.1) | copy-start | bytes 9437188
  374.1 30.4 %collective-permute-start.30 = (bf16[256,2048]{1,0:T(8,128)(2,1)}, bf16[256,2048]{1,0:T(8,128)(2,1)S(1)}, u32[]{:S(2)}, u32[]{:S(2)}) collective-permute-start(bf16[256,2048]{1,0:T(8,128)(2,1)} %pad_maximum_fusion.19), channel_id=1, source_target_pairs={{0,2},{1,3},{2,0},{3,1},{4,6},{5,7},{6,4},{7,5},{8,10},{9,11},{10,... | collective-permute-start | bytes 3145736 | tf_op jit(solution)/shard_map/ppermute | solution.py:26
  376.5 28.0 %collective-permute-start.28 = (bf16[256,2048]{1,0:T(8,128)(2,1)}, bf16[256,2048]{1,0:T(8,128)(2,1)}, u32[]{:S(2)}, u32[]{:S(2)}) collective-permute-start(bf16[256,2048]{1,0:T(8,128)(2,1)} %pad_maximum_fusion.18), channel_id=1, source_target_pairs={{0,1},{1,0},{2,3},{3,2},{4,5},{5,4},{6,7},{7,6},{8,9},{9,8},{10,11... | collective-permute-start | bytes 3145736 | tf_op jit(solution)/shard_map/ppermute | solution.py:26
  409.2 8.2 %collective-permute-start.32 = (bf16[512,256]{1,0:T(8,128)(2,1)S(1)}, bf16[512,256]{1,0:T(8,128)(2,1)S(1)}, u32[]{:S(2)}, u32[]{:S(2)}) collective-permute-start(bf16[512,256]{1,0:T(8,128)(2,1)S(1)} %pad_maximum_fusion.33), channel_id=1, source_target_pairs={{0,1},{1,0},{2,3},{3,2},{4,5},{5,4},{6,7},{7,6},{8,9},{9,8},{10,11... | collective-permute-start | bytes 786440 | tf_op jit(solution)/shard_map/ppermute | solution.py:26
  416.6 6.4 %collective-permute-start.34 = (bf16[512,256]{1,0:T(8,128)(2,1)S(1)}, bf16[512,256]{1,0:T(8,128)(2,1)S(1)}, u32[]{:S(2)}, u32[]{:S(2)}) collective-permute-start(bf16[512,256]{1,0:T(8,128)(2,1)S(1)} %pad_maximum_fusion.34), channel_id=1, source_target_pairs={{0,2},{1,3},{2,0},{3,1},{4,6},{5,7},{6,4},{7,5},{8,10},{9,11},{10,... | collective-permute-start | bytes 786440 | tf_op jit(solution)/shard_map/ppermute | solution.py:26
  417.5 6.9 %collective-permute-start.33 = (bf16[256,256]{1,0:T(8,128)(2,1)S(1)}, bf16[256,256]{1,0:T(8,128)(2,1)S(1)}, u32[]{:S(2)}, u32[]{:S(2)}) collective-permute-start(bf16[256,256]{1,0:T(8,128)(2,1)S(1)} %fusion.90), channel_id=1, source_target_pairs={{0,2},{1,3},{2,0},{3,1},{4,6},{5,7},{6,4},{7,5},{8,10},{9,11},{10,... | collective-permute-start | bytes 393224 | tf_op jit(solution)/shard_map/ppermute | solution.py:26
  423.2 5.0 collective-permute-start.35
  446.4 16.2 %collective-permute-start.29 = (bf16[128,2048]{1,0:T(8,128)(2,1)S(1)}, bf16[128,2048]{1,0:T(8,128)(2,1)S(1)}, u32[]{:S(2)}, u32[]{:S(2)}) collective-permute-start(bf16[128,2048]{1,0:T(8,128)(2,1)S(1)} %get-tuple-element.107), channel_id=1, source_target_pairs={{0,2},{1,3},{2,0},{3,1},{4,6},{5,7},{6,4},{7,5},{8,10},{9,11},{10,... | collective-permute-start | bytes 1572872 | tf_op jit(solution)/shard_map/ppermute | solution.py:26
  447.4 15.2 %collective-permute-start.31 = (bf16[128,2048]{1,0:T(8,128)(2,1)S(1)}, bf16[128,2048]{1,0:T(8,128)(2,1)S(1)}, u32[]{:S(2)}, u32[]{:S(2)}) collective-permute-start(bf16[128,2048]{1,0:T(8,128)(2,1)S(1)} %get-tuple-element.108), channel_id=1, source_target_pairs={{0,1},{1,0},{2,3},{3,2},{4,5},{5,4},{6,7},{7,6},{8,9},{9,8},{10,11... | collective-permute-start | bytes 1572872 | tf_op jit(solution)/shard_map/ppermute | solution.py:26
  459.8 18.3 %collective-permute-start.38 = (bf16[256,2048]{1,0:T(8,128)(2,1)}, bf16[256,2048]{1,0:T(8,128)(2,1)S(1)}, u32[]{:S(2)}, u32[]{:S(2)}) collective-permute-start(bf16[256,2048]{1,0:T(8,128)(2,1)} %pad_maximum_fusion.21), channel_id=1, source_target_pairs={{0,2},{1,3},{2,0},{3,1},{4,6},{5,7},{6,4},{7,5},{8,10},{9,11},{10,... | collective-permute-start | bytes 3145736 | tf_op jit(solution)/shard_map/ppermute | solution.py:26
  461.4 17.7 %collective-permute-start.36 = (bf16[256,2048]{1,0:T(8,128)(2,1)}, bf16[256,2048]{1,0:T(8,128)(2,1)}, u32[]{:S(2)}, u32[]{:S(2)}) collective-permute-start(bf16[256,2048]{1,0:T(8,128)(2,1)} %pad_maximum_fusion.20), channel_id=1, source_target_pairs={{0,1},{1,0},{2,3},{3,2},{4,5},{5,4},{6,7},{7,6},{8,9},{9,8},{10,11... | collective-permute-start | bytes 3145736 | tf_op jit(solution)/shard_map/ppermute | solution.py:26
  484.5 9.5 %collective-permute-start.37 = (bf16[128,2048]{1,0:T(8,128)(2,1)}, bf16[128,2048]{1,0:T(8,128)(2,1)}, u32[]{:S(2)}, u32[]{:S(2)}) collective-permute-start(bf16[128,2048]{1,0:T(8,128)(2,1)} %get-tuple-element.101), channel_id=1, source_target_pairs={{0,2},{1,3},{2,0},{3,1},{4,6},{5,7},{6,4},{7,5},{8,10},{9,11},{10,... | collective-permute-start | bytes 1572872 | tf_op jit(solution)/shard_map/ppermute | solution.py:26
  485.6 9.5 %collective-permute-start.39 = (bf16[128,2048]{1,0:T(8,128)(2,1)}, bf16[128,2048]{1,0:T(8,128)(2,1)}, u32[]{:S(2)}, u32[]{:S(2)}) collective-permute-start(bf16[128,2048]{1,0:T(8,128)(2,1)} %get-tuple-element.102), channel_id=1, source_target_pairs={{0,1},{1,0},{2,3},{3,2},{4,5},{5,4},{6,7},{7,6},{8,9},{9,8},{10,11... | collective-permute-start | bytes 1572872 | tf_op jit(solution)/shard_map/ppermute | solution.py:26
  488.2 6.9 %copy-start.20 = (f32[256,2048]{1,0:T(8,128)S(1)}, f32[256,2048]{1,0:T(8,128)}, u32[]{:S(2)}) copy-start(f32[256,2048]{1,0:T(8,128)} %copy-done.19) | copy-start | bytes 6291460
  488.2 6.9 %copy-start.50 = (f32[256,2048]{1,0:T(8,128)S(1)}, f32[256,2048]{1,0:T(8,128)}, u32[]{:S(2)}) copy-start(f32[256,2048]{1,0:T(8,128)} %fusion.75) | copy-start | bytes 6291460
  504.9 4.6 collective-permute-start.40
  505.8 4.6 collective-permute-start.41
  507.2 5.5 %collective-permute-start.42 = (f32[64,265]{1,0:T(8,128)S(1)}, f32[64,265]{1,0:T(8,128)S(1)}, u32[]{:S(2)}, u32[]{:S(2)}) collective-permute-start(f32[64,265]{1,0:T(8,128)S(1)} %pad_maximum_fusion.36), channel_id=1, source_target_pairs={{0,3},{1,2},{2,1},{3,0},{4,7},{5,6},{6,5},{7,4},{8,11},{9,10},{10,... | collective-permute-start | bytes 203528 | tf_op jit(solution)/shard_map/ppermute | solution.py:26
  (68 other events, 219.3 us)
Sparse Core Ops, SparseCore 0:
  11.3 51.7 all-gather.3
  65.3 89.9 all-gather.5
  157.4 76.3 all-gather.7
  237.4 100.7 reduce-scatter.3
  340.3 83.0 reduce-scatter.5
  433.8 52.1 reduce-scatter.7

commit v6 on v5

--- a/solution.py
+++ b/solution.py
@@ -330,7 +330,7 @@
     near = near_blocks(layer_input)
     inputs = all_blocks(layer_input, near)
     attn_full = gather_dp(attn_shard)
-    ff_full = [gather_dp(after(ff_shards[0], *near))]
+    ff_full = [gather_dp(after(ff_shards[0], *inputs))]
     attn_full = attn_full.reshape(-1, *attn_shard.shape)
     query_full = attn_full[:, :shard_rows].reshape(model_width, heads_width)
     project_full = attn_full[:, shard_rows : 2 * shard_rows].reshape(model_width, heads_width)
@@ -419,25 +419,27 @@
     kv_grads = kv_grads.reshape(-1, ranks, kv_rows, 2 * HD)
     kv_own, *kv_rest = (pick(kv_grads, order[j], 1).reshape(-1, 2 * HD) for j in range(ranks))
     kv_rest = jnp.concatenate(kv_rest, axis=0)
-    kv_sum = finish_sums(kv_own.astype(f32), kv_rest, send_sums(kv_rest)).astype(bf16)
+    kv_sent = send_sums(kv_rest)
+    qkv_rest = dot(after(qkv_back[rows:], kv_rest), qkv_full, 1, 1).astype(bf16)
+    qkv_sent = send_sums(after(qkv_rest, *kv_sent, ff_sums[1]))
+    query_back = after(qkv_back[:, :heads_width], qkv_rest)
+    kv_sum = finish_sums(kv_own.astype(f32), kv_rest, kv_sent).astype(bf16)
     attn_partial = jnp.concatenate(
         [
-            dot(normed_one, qkv_back[:, :heads_width], 0, 0)
-            .astype(bf16)
-            .reshape(-1, shard_rows, heads_width),
+            dot(normed_one, query_back, 0, 0).astype(bf16).reshape(-1, shard_rows, heads_width),
             dot(attn_top_all, mixed, 0, 0).astype(bf16).reshape(-1, shard_rows, heads_width),
             kv_sum.reshape(model_width // shard_rows, -1, heads_width),
         ],
         axis=1,
     ).reshape(-1, heads_width)
-    attn_sum = scatter_dp(after(attn_partial, ff_sums[1]))
-    own_down = sum(dot(h[:rows], w, 1, 1) for h, w in zip(hidden, downs))
+    attn_sum = scatter_dp(attn_partial)
+    down_sent = [after(block, *kv_sent) for block in down_sent]
+    own_down = sum(
+        dot(after(h[:rows], attn_partial), w, 1, 1) for h, w in zip(hidden, downs)
+    )
     after_mlp = after_attn + finish_sums(own_down, down_rest, down_sent)
     output = (after_mlp * own_mask).astype(bf16)
-    qkv_rest = dot(after(qkv_back[rows:], attn_partial), qkv_full, 1, 1).astype(bf16)
-    scaled_one = finish_sums(
-        dot(qkv_back[:rows], qkv_full, 1, 1), qkv_rest, send_sums(qkv_rest)
-    )
+    scaled_one = finish_sums(dot(qkv_back[:rows], qkv_full, 1, 1), qkv_rest, qkv_sent)
     inv_one = inverse_norm(residual)
     unit_one = residual * inv_one
     input_grad = attn_top + inv_one * (

time: 532 us -> 525 us (0.987)
  other arithmetic: 87.1 us -> 81.3 us
    unnamed x188 -> x196, local copies, waits for them, and re-layouts: 39.1 us -> 38.8 us
  transfers between devices with their start and end apart: 49 -> 49, of which waited for: 33 -> 32; matrix products, arithmetic and copies ran while one was open for 49% -> 48% of each run, Pallas kernels for 5% -> 5%
where the time goes in v6:
time: 525 us; the launch traced here: 515 us
  waiting for transfers between devices  138 us (26%)
  matrix products  128 us (24%)
  other arithmetic  81.3 us (15%)
  local copies, waits for them, and re-layouts  67.7 us (13%)
  starting transfers between devices  49.3 us (9%)
  Pallas kernels  25.3 us (5%)
  between operations  24.7 us (5%)
    ppermute x43, waiting for transfers between devices, hop(): return lax.ppermute(value, 'tensor', [(i, i ^ step) for i in range(size)])  138 us
    dot_general x25, matrix products, dot(): lax.dot_general(a, b, (((ca,), (cb,)), ((), ())), preferred_element_type=...  128 us
    ppermute x43, starting transfers between devices, hop(): return lax.ppermute(value, 'tensor', [(i, i ^ step) for i in range(size)])  49 us
    unnamed x196, local copies, waits for them, and re-layouts  38.8 us
    concatenate x2, other arithmetic, partial(): jnp.concatenate([dot(normed_two, grads, 0, 0).astype(bf16), dot(top_all,...  19.5 us
    pallas_call x1, Pallas kernels, attend_back(): pl.pallas_call(attend_back_kernel, name='attend_back', grid_spec=pltpu.Pr...  13.7 us
    pallas_call x1, Pallas kernels, attend(): pl.pallas_call(attend_kernel, name='attend', grid_spec=pltpu.PrefetchScal...  11.6 us
  transfers between devices with their start and end apart: 49, of which 32 were waited for; matrix products, arithmetic and copies ran while one was open for 48% of the time, Pallas kernels for 5%

profile of v6, /device:TPU:0, one launch (start us, length us, event | category | flops | bytes accessed | tf_op | source)
XLA Modules:
  0.0 514.7 jit_solution(3797757340514561591)
XLA Ops:
  11.3 3.0 collective-permute-start
  23.9 13.6 %collective-permute-done = bf16[256,2048]{1,0:T(8,128)(2,1)S(1)} collective-permute-done((bf16[256,2048]{1,0:T(8,128)(2,1)S(1)}, bf16[256,2048]{1,0:T(8,128)(2,1)S(1)}, u32[]{:S(2)}, u32[]{:S(2)}) %collective-permute-start) | collective-permute-done | bytes 1048608 | tf_op jit(solution)/shard_map/ppermute | solution.py:26
  43.6 8.2 %collective-permute-done.3 = bf16[128,2048]{1,0:T(8,128)(2,1)} collective-permute-done((bf16[128,2048]{1,0:T(8,128)(2,1)}, bf16[128,2048]{1,0:T(8,128)(2,1)}, u32[]{:S(2)}, u32[]{:S(2)}) %collective-permute-start.3) | collective-permute-done | bytes 524320 | tf_op jit(solution)/shard_map/ppermute | solution.py:26
  51.8 2.1 collective-permute-done.2
  79.5 2.0 fusion.81
  84.6 2.0 fusion.80
  86.7 2.4 collective-permute-done.5
  94.1 2.7 collective-permute-done.7
  97.1 2.2 collective-permute-start.9
  104.0 7.4 %fusion.77.q_ref.kv_ref = f32[1024,768]{1,0:T(8,128)} fusion(bf16[1024,2048]{1,0:T(8,128)(2,1)} %fusion.80, bf16[2048,256]{1,0:T(8,128)(2,1)S(1)} %bitcast.107, bf16[2048,512]{1,0:T(8,128)(2,1)S(1)} %bitcast.102), kind=kOutput, calls=%fused_computation.159 | convolution fusion | flops 3227516928 | bytes 10485760 | tf_op jit(solution)/shard_map/dot_general | solution.py:21
  111.4 11.6 %attend.1 = (bf16[1024,512]{1,0:T(8,128)(2,1)S(1)}, bf16[1024,256]{1,0:T(8,128)(2,1)S(1)}, bf16[1024,512]{1,0:T(8,128)(2,1)S(1)}, f32[1024,128]{1,0:T(8,128)S(1)}) custom-call(s32[2]{0:T(128)S(1)} %pad_add_fusion.where_ref, f32[1024,768]{1,0:T(8,128)} %fusion.77.q_ref.kv_ref, f32[1024,768]{1,0:T(8,128)} %fusion.77.q_ref.kv_ref, ...), custom_call_target="tpu_custom_call" | custom-call | flops 2147483648 | bytes 8388608 | tf_op jit(solution)/shard_map/attend/pallas_call | solution.py:199
  125.7 3.7 convolution_convert_fusion.2
  131.9 18.0 %collective-permute-done.10 = bf16[256,2048]{1,0:T(8,128)(2,1)S(1)} collective-permute-done((bf16[256,2048]{1,0:T(8,128)(2,1)S(1)}, bf16[256,2048]{1,0:T(8,128)(2,1)S(1)}, u32[]{:S(2)}, u32[]{:S(2)}) %collective-permute-start.10) | collective-permute-done | bytes 1048608 | tf_op jit(solution)/shard_map/ppermute | solution.py:26
  150.1 2.5 collective-permute-done.12
  166.0 5.2 %collective-permute-done.14 = bf16[128,2048]{1,0:T(8,128)(2,1)S(1)} collective-permute-done((bf16[128,2048]{1,0:T(8,128)(2,1)S(1)}, bf16[128,2048]{1,0:T(8,128)(2,1)S(1)}, u32[]{:S(2)}, u32[]{:S(2)}) %collective-permute-start.14) | collective-permute-done | bytes 524320 | tf_op jit(solution)/shard_map/ppermute | solution.py:26
  171.2 2.7 collective-permute-done.15
  178.4 6.7 %fusion.27 = f32[1024,768]{0,1:T(8,128)S(1)} fusion(bf16[1024,2048]{1,0:T(8,128)(2,1)} %copy-done.68, bf16[2048,2304]{0,1:T(8,128)(2,1)} %all-gather.6.cloned.1.call-done), kind=kOutput, calls=%fused_computation.59 | convolution fusion | flops 3221225472 | bytes 10485760 | tf_op jit(solution)/shard_map/dot_general | solution.py:21
  185.1 10.2 %collective-permute-done.17 = bf16[256,2048]{1,0:T(8,128)(2,1)} collective-permute-done((bf16[256,2048]{1,0:T(8,128)(2,1)}, bf16[256,2048]{1,0:T(8,128)(2,1)}, u32[]{:S(2)}, u32[]{:S(2)}) %collective-permute-start.17) | collective-permute-done | bytes 1048608 | tf_op jit(solution)/shard_map/ppermute | solution.py:26
  203.7 2.2 collective-permute-done.18
  205.9 4.0 collective-permute-done.19
  209.9 6.8 %fusion.4 = f32[1024,1536]{0,1:T(8,128)S(1)} fusion(bf16[1024,2048]{1,0:T(8,128)(2,1)S(1)} %constant_dynamic-update-slice_fusion.10, bf16[2048,2304]{0,1:T(8,128)(2,1)S(1)} %copy-done.83), kind=kOutput, calls=%fused_computation.10 | convolution fusion | flops 6442450944 | bytes 16777216 | tf_op jit(solution)/shard_map/dot_general | solution.py:21
  216.7 2.2 multiply_convert_fusion.1
  218.9 3.6 convolution_convert_fusion.3
  222.6 8.7 %convolution_convert_fusion.1 = bf16[2048,1536]{0,1:T(8,128)(2,1)S(1)} fusion(bf16[1024,2048]{1,0:T(8,128)(2,1)S(1)} %constant_dynamic-update-slice_fusion.10, bf16[1024,768]{0,1:T(8,128)(2,1)S(1)} %get-tuple-element.102, bf16[1024,768]{0,1:T(8,128)(2,1)S(1)} %get-tuple-element.101), kind=kOutput, calls=%fused_computation.3 | convolution fusion | flops 6451888128 | bytes 13631488 | tf_op jit(solution)/shard_map/dot_general | solution.py:21
  231.3 11.5 %pad_maximum_fusion = bf16[2048,2304]{0,1:T(8,128)(2,1)} fusion(bf16[2048,768]{0,1:T(8,128)(2,1)S(1)} %convolution_convert_fusion.3, bf16[2048,1536]{0,1:T(8,128)(2,1)S(1)} %convolution_convert_fusion.1), kind=kLoop, calls=%fused_computation | loop fusion | flops 18874368 | bytes 18874368 | tf_op jit(solution)/shard_map/concatenate | solution.py:383
  244.7 9.8 %fusion.2 = f32[768,2048]{1,0:T(8,128)} fusion(bf16[768,1536]{0,1:T(8,128)(2,1)S(1)} %pad_maximum_fusion.5, bf16[2048,2304]{0,1:T(8,128)(2,1)} %all-gather.6.cloned.1.call-done), kind=kOutput, calls=%fused_computation.8 | convolution fusion | flops 4831838208 | bytes 14942208 | tf_op jit(solution)/shard_map/dot_general | solution.py:21
  254.5 5.7 %fusion.43 = f32[1024,640]{0,1:T(8,128)S(1)} fusion(bf16[1024,2048]{1,0:T(8,128)(2,1)} %copy-done.68, bf16[2048,1920]{0,1:T(8,128)(2,1)} %all-gather.8.cloned.1.call-done), kind=kOutput, calls=%fused_computation.83 | convolution fusion | flops 2684354560 | bytes 9437184 | tf_op jit(solution)/shard_map/dot_general | solution.py:21
  261.1 5.7 %fusion.10 = f32[1024,1280]{0,1:T(8,128)S(1)} fusion(bf16[1024,2048]{1,0:T(8,128)(2,1)S(1)} %copy-done.72, bf16[2048,1920]{0,1:T(8,128)(2,1)S(1)} %copy-done.62), kind=kOutput, calls=%fused_computation.17 | convolution fusion | flops 5368709120 | bytes 14680064 | tf_op jit(solution)/shard_map/dot_general | solution.py:21
  268.8 9.0 %add_convert_fusion.1 = bf16[768,2048]{1,0:T(8,128)(2,1)} fusion(f32[768,2048]{1,0:T(8,128)} %fusion.2, bf16[2048,1920]{0,1:T(8,128)(2,1)S(1)} %copy-done.62, bf16[1024,640]{0,1:T(8,128)(2,1)S(1)} %get-tuple-element.104, bf16[1024,640]{0,1:T(8,128)(2,1)S(1)} %get-tuple-element.103), kind=kOutput, calls=%fused_computation.5 | convolution fusion | flops 4033609728 | bytes 17301504 | tf_op jit(solution)/shard_map/dot_general | solution.py:21
  278.1 2.0 copy-done.70
  280.1 4.6 convolution_convert_fusion.5
  284.7 7.4 %convolution_convert_fusion = bf16[2048,1280]{0,1:T(8,128)(2,1)} fusion(bf16[1024,1280]{0,1:T(8,128)(2,1)S(1)} %pad_maximum_fusion.3, bf16[1024,2048]{1,0:T(8,128)(2,1)S(1)} %copy-done.72), kind=kOutput, calls=%fused_computation.2 | convolution fusion | flops 5371330560 | bytes 12058624 | tf_op jit(solution)/shard_map/dot_general | solution.py:21
  292.0 8.0 %pad_maximum_fusion.1 = bf16[2048,1920]{0,1:T(8,128)(2,1)} fusion(bf16[2048,640]{0,1:T(8,128)(2,1)} %convolution_convert_fusion.5, bf16[2048,1280]{0,1:T(8,128)(2,1)} %convolution_convert_fusion), kind=kLoop, calls=%fused_computation.1 | loop fusion | flops 15728640 | bytes 15728640 | tf_op jit(solution)/shard_map/concatenate | solution.py:383
  304.8 4.1 fusion.6
  308.9 12.7 %collective-permute-done.22 = bf16[256,2048]{1,0:T(8,128)(2,1)S(1)} collective-permute-done((bf16[256,2048]{1,0:T(8,128)(2,1)S(1)}, bf16[256,2048]{1,0:T(8,128)(2,1)S(1)}, u32[]{:S(2)}, u32[]{:S(2)}) %collective-permute-start.22) | collective-permute-done | bytes 1048608 | tf_op jit(solution)/shard_map/ppermute | solution.py:26
  327.7 4.6 fusion.20
  332.3 5.3 %collective-permute-done.21 = bf16[128,2048]{1,0:T(8,128)(2,1)S(1)} collective-permute-done((bf16[128,2048]{1,0:T(8,128)(2,1)S(1)}, bf16[128,2048]{1,0:T(8,128)(2,1)S(1)}, u32[]{:S(2)}, u32[]{:S(2)}) %collective-permute-start.21) | collective-permute-done | bytes 524320 | tf_op jit(solution)/shard_map/ppermute | solution.py:26
  340.2 2.8 constant_dynamic-update-slice_fusion.19
  345.7 5.1 fusion.25
  350.7 13.0 %collective-permute-done.25 = bf16[256,2048]{1,0:T(8,128)(2,1)S(1)} collective-permute-done((bf16[256,2048]{1,0:T(8,128)(2,1)}, bf16[256,2048]{1,0:T(8,128)(2,1)S(1)}, u32[]{:S(2)}, u32[]{:S(2)}) %collective-permute-start.25) | collective-permute-done | bytes 1048608 | tf_op jit(solution)/shard_map/ppermute | solution.py:26
  363.7 2.5 collective-permute-start.26
  367.5 4.9 add_convert_fusion
  372.4 2.1 constant_dynamic-update-slice_fusion.18
  374.6 4.4 collective-permute-done.26
  379.0 3.2 collective-permute-done.27
  388.0 3.8 convolution_convert_fusion.6
  391.8 3.1 convert_element_type.346
  394.8 4.7 convolution_convert_fusion.9.dm_ref
  399.5 13.7 %attend_back.1 = (bf16[1024,512]{1,0:T(8,128)(2,1)S(1)}, bf16[1024,256]{1,0:T(8,128)(2,1)S(1)}) custom-call(s32[2]{0:T(128)S(1)} %pad_add_fusion.where_ref, bf16[1024,512]{1,0:T(8,128)(2,1)S(1)} %get-tuple-element.53.qr_ref, bf16[1024,256]{1,0:T(8,128)(2,1)S(1)} %copy-done.3, bf16[1024,512]{1,0:T(8,128)(2,1)S(1)} %convolution_convert_fusion.9.dm_ref, ...), custom_call_target="tpu_custom_call" | custom-call | flops 5368709120 | bytes 8388608 | tf_op jit(solution)/shard_map/attend_back/pallas_call | solution.py:237
  414.2 3.7 convolution_convert_fusion.8
  418.9 2.1 collective-permute-start.30
  420.9 4.0 convolution_convert_fusion.4
  425.0 5.9 %convolution_convert_fusion.7 = bf16[2048,512]{1,0:T(8,128)(2,1)} fusion(bf16[1024,2048]{1,0:T(8,128)(2,1)} %fusion.80, bf16[1024,512]{1,0:T(8,128)(2,1)S(1)} %slice-done), kind=kOutput, calls=%fused_computation.40 | convolution fusion | flops 2148532224 | bytes 7340032 | tf_op jit(solution)/shard_map/dot_general | solution.py:21
  432.7 3.4 collective-permute-done.31
  436.5 3.6 pad_maximum_fusion.2
  441.5 2.1 slice.609
  447.7 2.3 fusion.76
  467.9 2.9 fusion.23
  470.8 2.8 convolution_add_fusion
  473.6 3.3 collective-permute-done.38
  482.5 2.0 collective-permute-done.35
  485.1 3.7 collective-permute-done.37
  492.5 2.3 fusion.36
  499.8 2.2 collective-permute-start.42
  (427 shorter events, 156.3 us)
Async XLA Ops:
  7.2 8.6 %copy-start.84 = (bf16[256]{0:T(256)(128)(2,1)S(1)}, bf16[256]{0:T(256)(128)(2,1)}, u32[]{:S(2)}) copy-start(bf16[256]{0:T(256)(128)(2,1)} %param.21) | copy-start | bytes 1540
  7.2 74.3 %all-gather.4.cloned.1.call-start = ((), (), s32[]{:S(2)}) async-start(), calls=%async_computation.3 | async-start | bytes 5013504 | tf_op jit(solution)/shard_map/all_gather | solution.py:76
  11.2 167.2 %all-gather.6.cloned.1.call-start = ((), (), s32[]{:S(2)}) async-start(), calls=%async_computation.4 | async-start | bytes 10616832 | tf_op jit(solution)/shard_map/all_gather | solution.py:76
  11.3 26.2 %collective-permute-start = (bf16[256,2048]{1,0:T(8,128)(2,1)S(1)}, bf16[256,2048]{1,0:T(8,128)(2,1)S(1)}, u32[]{:S(2)}, u32[]{:S(2)}) collective-permute-start(bf16[256,2048]{1,0:T(8,128)(2,1)S(1)} %copy-done.6), channel_id=1, source_target_pairs={{0,1},{1,0},{2,3},{3,2},{4,5},{5,4},{6,7},{7,6},{8,9},{9,8},{10,11... | collective-permute-start | bytes 3145736 | tf_op jit(solution)/shard_map/ppermute | solution.py:26
  14.3 25.8 %collective-permute-start.1 = (bf16[256,2048]{1,0:T(8,128)(2,1)S(1)}, bf16[256,2048]{1,0:T(8,128)(2,1)S(1)}, u32[]{:S(2)}, u32[]{:S(2)}) collective-permute-start(bf16[256,2048]{1,0:T(8,128)(2,1)S(1)} %copy-done.6), channel_id=1, source_target_pairs={{0,2},{1,3},{2,0},{3,1},{4,6},{5,7},{6,4},{7,5},{8,10},{9,11},{10,... | collective-permute-start | bytes 3145736 | tf_op jit(solution)/shard_map/ppermute | solution.py:26
  15.8 54.1 %copy-start.78 = (f32[256]{0:T(256)}, f32[256]{0:T(256)S(1)}, u32[]{:S(2)}) copy-start(f32[256]{0:T(256)S(1)} %convert_element_type.321) | copy-start | bytes 3076
  18.8 22.2 %copy-start.34 = (bf16[256,768]{0,1:T(8,128)(2,1)}, bf16[256,768]{0,1:T(8,128)(2,1)S(1)}, u32[]{:S(2)}) copy-start(bf16[256,768]{0,1:T(8,128)(2,1)S(1)} %copy.53) | copy-start | bytes 1179652
  22.6 19.8 %copy-start.63 = (bf16[1408,256]{1,0:T(8,128)(2,1)S(1)}, bf16[1408,256]{1,0:T(8,128)(2,1)}, u32[]{:S(2)}) copy-start(bf16[1408,256]{1,0:T(8,128)(2,1)} %param.19) | copy-start | bytes 2162692
  38.3 13.5 %collective-permute-start.3 = (bf16[128,2048]{1,0:T(8,128)(2,1)}, bf16[128,2048]{1,0:T(8,128)(2,1)}, u32[]{:S(2)}, u32[]{:S(2)}) collective-permute-start(bf16[128,2048]{1,0:T(8,128)(2,1)} %slice.584), channel_id=1, source_target_pairs={{0,2},{1,3},{2,0},{3,1},{4,6},{5,7},{6,4},{7,5},{8,10},{9,11},{10,... | collective-permute-start | bytes 1572872 | tf_op jit(solution)/shard_map/ppermute | solution.py:26
  40.1 13.9 %copy-start.25 = (bf16[256,2048]{1,0:T(8,128)(2,1)}, bf16[256,2048]{1,0:T(8,128)(2,1)S(1)}, u32[]{:S(2)}) copy-start(bf16[256,2048]{1,0:T(8,128)(2,1)S(1)} %collective-permute-done.1) | copy-start | bytes 3145732
  40.9 12.9 %collective-permute-start.2 = (bf16[128,2048]{1,0:T(8,128)(2,1)}, bf16[128,2048]{1,0:T(8,128)(2,1)}, u32[]{:S(2)}, u32[]{:S(2)}) collective-permute-start(bf16[128,2048]{1,0:T(8,128)(2,1)} %slice.583), channel_id=1, source_target_pairs={{0,1},{1,0},{2,3},{3,2},{4,5},{5,4},{6,7},{7,6},{8,9},{9,8},{10,11... | collective-permute-start | bytes 1572872 | tf_op jit(solution)/shard_map/ppermute | solution.py:26
  53.9 200.5 %all-gather.8.cloned.1.call-start = ((), (), s32[]{:S(2)}) async-start(), calls=%async_computation.5 | async-start | bytes 8847360 | tf_op jit(solution)/shard_map/all_gather | solution.py:76
  82.6 6.4 %collective-permute-start.5 = (bf16[512,256]{1,0:T(8,128)(2,1)S(1)}, bf16[512,256]{1,0:T(8,128)(2,1)S(1)}, u32[]{:S(2)}, u32[]{:S(2)}) collective-permute-start(bf16[512,256]{1,0:T(8,128)(2,1)S(1)} %reshape.205), channel_id=1, source_target_pairs={{0,2},{1,3},{2,0},{3,1},{4,6},{5,7},{6,4},{7,5},{8,10},{9,11},{10,... | collective-permute-start | bytes 786440 | tf_op jit(solution)/shard_map/ppermute | solution.py:26
  83.2 7.5 %collective-permute-start.4 = (bf16[512,256]{1,0:T(8,128)(2,1)S(1)}, bf16[512,256]{1,0:T(8,128)(2,1)S(1)}, u32[]{:S(2)}, u32[]{:S(2)}) collective-permute-start(bf16[512,256]{1,0:T(8,128)(2,1)S(1)} %reshape.205), channel_id=1, source_target_pairs={{0,1},{1,0},{2,3},{3,2},{4,5},{5,4},{6,7},{7,6},{8,9},{9,8},{10,11... | collective-permute-start | bytes 786440 | tf_op jit(solution)/shard_map/ppermute | solution.py:26
  89.0 5.0 collective-permute-start.6
  90.7 6.1 %collective-permute-start.7 = (bf16[256,256]{1,0:T(8,128)(2,1)S(1)}, bf16[256,256]{1,0:T(8,128)(2,1)S(1)}, u32[]{:S(2)}, u32[]{:S(2)}) collective-permute-start(bf16[256,256]{1,0:T(8,128)(2,1)S(1)} %slice.590), channel_id=1, source_target_pairs={{0,2},{1,3},{2,0},{3,1},{4,6},{5,7},{6,4},{7,5},{8,10},{9,11},{10,... | collective-permute-start | bytes 393224 | tf_op jit(solution)/shard_map/ppermute | solution.py:26
  97.1 28.6 %collective-permute-start.9 = (bf16[256,2048]{1,0:T(8,128)(2,1)}, bf16[256,2048]{1,0:T(8,128)(2,1)}, u32[]{:S(2)}, u32[]{:S(2)}) collective-permute-start(bf16[256,2048]{1,0:T(8,128)(2,1)} %fusion.40), channel_id=1, source_target_pairs={{0,2},{1,3},{2,0},{3,1},{4,6},{5,7},{6,4},{7,5},{8,10},{9,11},{10,... | collective-permute-start | bytes 3145736 | tf_op jit(solution)/shard_map/ppermute | solution.py:26
  99.2 26.5 %collective-permute-start.8 = (bf16[256,2048]{1,0:T(8,128)(2,1)}, bf16[256,2048]{1,0:T(8,128)(2,1)}, u32[]{:S(2)}, u32[]{:S(2)}) collective-permute-start(bf16[256,2048]{1,0:T(8,128)(2,1)} %fusion.40), channel_id=1, source_target_pairs={{0,1},{1,0},{2,3},{3,2},{4,5},{5,4},{6,7},{7,6},{8,9},{9,8},{10,11... | collective-permute-start | bytes 3145736 | tf_op jit(solution)/shard_map/ppermute | solution.py:26
  125.6 266.1 %reduce-scatter.4.cloned.1.call-start = ((), (), s32[]{:S(2)}) async-start(), calls=%async_computation.6 | async-start | bytes 10616832 | tf_op jit(solution)/shard_map/reduce_scatter | solution.py:80
  129.6 20.3 %collective-permute-start.10 = (bf16[256,2048]{1,0:T(8,128)(2,1)S(1)}, bf16[256,2048]{1,0:T(8,128)(2,1)S(1)}, u32[]{:S(2)}, u32[]{:S(2)}) collective-permute-start(bf16[256,2048]{1,0:T(8,128)(2,1)S(1)} %pad_maximum_fusion.13), channel_id=1, source_target_pairs={{0,1},{1,0},{2,3},{3,2},{4,5},{5,4},{6,7},{7,6},{8,9},{9,8},{10,11... | collective-permute-start | bytes 3145736 | tf_op jit(solution)/shard_map/ppermute | solution.py:26
  130.4 22.3 %collective-permute-start.12 = (bf16[256,2048]{1,0:T(8,128)(2,1)S(1)}, bf16[256,2048]{1,0:T(8,128)(2,1)S(1)}, u32[]{:S(2)}, u32[]{:S(2)}) collective-permute-start(bf16[256,2048]{1,0:T(8,128)(2,1)S(1)} %pad_maximum_fusion.14), channel_id=1, source_target_pairs={{0,2},{1,3},{2,0},{3,1},{4,6},{5,7},{6,4},{7,5},{8,10},{9,11},{10,... | collective-permute-start | bytes 3145736 | tf_op jit(solution)/shard_map/ppermute | solution.py:26
  153.2 11.8 %collective-permute-start.11 = (bf16[128,2048]{1,0:T(8,128)(2,1)S(1)}, bf16[128,2048]{1,0:T(8,128)(2,1)S(1)}, u32[]{:S(2)}, u32[]{:S(2)}) collective-permute-start(bf16[128,2048]{1,0:T(8,128)(2,1)S(1)} %get-tuple-element.127), channel_id=1, source_target_pairs={{0,2},{1,3},{2,0},{3,1},{4,6},{5,7},{6,4},{7,5},{8,10},{9,11},{10,... | collective-permute-start | bytes 1572872 | tf_op jit(solution)/shard_map/ppermute | solution.py:26
  153.7 11.2 %collective-permute-start.13 = (bf16[128,2048]{1,0:T(8,128)(2,1)S(1)}, bf16[128,2048]{1,0:T(8,128)(2,1)S(1)}, u32[]{:S(2)}, u32[]{:S(2)}) collective-permute-start(bf16[128,2048]{1,0:T(8,128)(2,1)S(1)} %get-tuple-element.128), channel_id=1, source_target_pairs={{0,1},{1,0},{2,3},{3,2},{4,5},{5,4},{6,7},{7,6},{8,9},{9,8},{10,11... | collective-permute-start | bytes 1572872 | tf_op jit(solution)/shard_map/ppermute | solution.py:26
  158.8 12.4 %collective-permute-start.14 = (bf16[128,2048]{1,0:T(8,128)(2,1)S(1)}, bf16[128,2048]{1,0:T(8,128)(2,1)S(1)}, u32[]{:S(2)}, u32[]{:S(2)}) collective-permute-start(bf16[128,2048]{1,0:T(8,128)(2,1)S(1)} %slice.479), channel_id=1, source_target_pairs={{0,1},{1,0},{2,3},{3,2},{4,5},{5,4},{6,7},{7,6},{8,9},{9,8},{10,11... | collective-permute-start | bytes 1572872 | tf_op jit(solution)/shard_map/ppermute | solution.py:26
  159.3 14.6 %collective-permute-start.15 = (bf16[128,2048]{1,0:T(8,128)(2,1)S(1)}, bf16[128,2048]{1,0:T(8,128)(2,1)S(1)}, u32[]{:S(2)}, u32[]{:S(2)}) collective-permute-start(bf16[128,2048]{1,0:T(8,128)(2,1)S(1)} %slice.480), channel_id=1, source_target_pairs={{0,2},{1,3},{2,0},{3,1},{4,6},{5,7},{6,4},{7,5},{8,10},{9,11},{10,... | collective-permute-start | bytes 1572872 | tf_op jit(solution)/shard_map/ppermute | solution.py:26
  165.6 8.4 %copy-start.9 = (f32[128,2048]{1,0:T(8,128)}, f32[128,2048]{1,0:T(8,128)S(1)}, u32[]{:S(2)}) copy-start(f32[128,2048]{1,0:T(8,128)S(1)} %get-tuple-element.141) | copy-start | bytes 3145732
  165.6 8.4 %copy-start.12 = (f32[128,2048]{1,0:T(8,128)}, f32[128,2048]{1,0:T(8,128)S(1)}, u32[]{:S(2)}) copy-start(f32[128,2048]{1,0:T(8,128)S(1)} %get-tuple-element.142) | copy-start | bytes 3145732
  176.3 19.0 %collective-permute-start.17 = (bf16[256,2048]{1,0:T(8,128)(2,1)}, bf16[256,2048]{1,0:T(8,128)(2,1)}, u32[]{:S(2)}, u32[]{:S(2)}) collective-permute-start(bf16[256,2048]{1,0:T(8,128)(2,1)} %multiply_convert_fusion.6), channel_id=1, source_target_pairs={{0,2},{1,3},{2,0},{3,1},{4,6},{5,7},{6,4},{7,5},{8,10},{9,11},{10,... | collective-permute-start | bytes 3145736 | tf_op jit(solution)/shard_map/ppermute | solution.py:26
  176.8 22.7 %collective-permute-start.16 = (bf16[256,2048]{1,0:T(8,128)(2,1)}, bf16[256,2048]{1,0:T(8,128)(2,1)}, u32[]{:S(2)}, u32[]{:S(2)}) collective-permute-start(bf16[256,2048]{1,0:T(8,128)(2,1)} %multiply_convert_fusion.6), channel_id=1, source_target_pairs={{0,1},{1,0},{2,3},{3,2},{4,5},{5,4},{6,7},{7,6},{8,9},{9,8},{10,11... | collective-permute-start | bytes 3145736 | tf_op jit(solution)/shard_map/ppermute | solution.py:26
  195.3 14.5 %copy-start.83 = (bf16[2048,2304]{0,1:T(8,128)(2,1)S(1)}, bf16[2048,2304]{0,1:T(8,128)(2,1)}, u32[]{:S(2)}) copy-start(bf16[2048,2304]{0,1:T(8,128)(2,1)} %all-gather.6.cloned.1.call-done) | copy-start | bytes 28311556
  196.6 9.2 %collective-permute-start.18 = (bf16[128,2048]{1,0:T(8,128)(2,1)S(1)}, bf16[128,2048]{1,0:T(8,128)(2,1)S(1)}, u32[]{:S(2)}, u32[]{:S(2)}) collective-permute-start(bf16[128,2048]{1,0:T(8,128)(2,1)S(1)} %slice.485), channel_id=1, source_target_pairs={{0,1},{1,0},{2,3},{3,2},{4,5},{5,4},{6,7},{7,6},{8,9},{9,8},{10,11... | collective-permute-start | bytes 1572872 | tf_op jit(solution)/shard_map/ppermute | solution.py:26
  200.6 9.2 %collective-permute-start.19 = (bf16[128,2048]{1,0:T(8,128)(2,1)S(1)}, bf16[128,2048]{1,0:T(8,128)(2,1)S(1)}, u32[]{:S(2)}, u32[]{:S(2)}) collective-permute-start(bf16[128,2048]{1,0:T(8,128)(2,1)S(1)} %slice.486), channel_id=1, source_target_pairs={{0,2},{1,3},{2,0},{3,1},{4,6},{5,7},{6,4},{7,5},{8,10},{9,11},{10,... | collective-permute-start | bytes 1572872 | tf_op jit(solution)/shard_map/ppermute | solution.py:26
  209.9 12.7 %copy-start.71 = (bf16[1024,2048]{1,0:T(8,128)(2,1)}, bf16[1024,2048]{1,0:T(8,128)(2,1)S(1)}, u32[]{:S(2)}) copy-start(bf16[1024,2048]{1,0:T(8,128)(2,1)S(1)} %constant_dynamic-update-slice_fusion.10) | copy-start | bytes 12582916
  242.8 207.2 %reduce-scatter.6.cloned.1.call-start = ((), (), s32[]{:S(2)}) async-start(), calls=%async_computation.7 | async-start | bytes 8847360 | tf_op jit(solution)/shard_map/reduce_scatter | solution.py:80
  268.7 9.1 %copy-start.27 = (bf16[1024,640]{0,1:T(8,128)(2,1)}, bf16[1024,640]{0,1:T(8,128)(2,1)S(1)}, u32[]{:S(2)}) copy-start(bf16[1024,640]{0,1:T(8,128)(2,1)S(1)} %get-tuple-element.103) | copy-start | bytes 3932164
  268.7 9.1 %copy-start.29 = (bf16[1024,640]{0,1:T(8,128)(2,1)}, bf16[1024,640]{0,1:T(8,128)(2,1)S(1)}, u32[]{:S(2)}) copy-start(bf16[1024,640]{0,1:T(8,128)(2,1)S(1)} %get-tuple-element.104) | copy-start | bytes 3932164
  268.8 9.3 %copy-start.54 = (bf16[1024,640]{0,1:T(8,128)(2,1)}, bf16[1024,640]{0,1:T(8,128)(2,1)S(1)}, u32[]{:S(2)}) copy-start(bf16[1024,640]{0,1:T(8,128)(2,1)S(1)} %get-tuple-element.60) | copy-start | bytes 3932164
  300.1 194.8 %reduce-scatter.8.cloned.1.call-start = ((), (), s32[]{:S(2)}) async-start(), calls=%async_computation.8 | async-start | bytes 5013504 | tf_op jit(solution)/shard_map/reduce_scatter | solution.py:80
  302.1 19.5 %collective-permute-start.22 = (bf16[256,2048]{1,0:T(8,128)(2,1)S(1)}, bf16[256,2048]{1,0:T(8,128)(2,1)S(1)}, u32[]{:S(2)}, u32[]{:S(2)}) collective-permute-start(bf16[256,2048]{1,0:T(8,128)(2,1)S(1)} %pad_maximum_fusion.16), channel_id=1, source_target_pairs={{0,2},{1,3},{2,0},{3,1},{4,6},{5,7},{6,4},{7,5},{8,10},{9,11},{10,... | collective-permute-start | bytes 3145736 | tf_op jit(solution)/shard_map/ppermute | solution.py:26
  302.4 21.1 %collective-permute-start.20 = (bf16[256,2048]{1,0:T(8,128)(2,1)S(1)}, bf16[256,2048]{1,0:T(8,128)(2,1)S(1)}, u32[]{:S(2)}, u32[]{:S(2)}) collective-permute-start(bf16[256,2048]{1,0:T(8,128)(2,1)S(1)} %pad_maximum_fusion.15), channel_id=1, source_target_pairs={{0,1},{1,0},{2,3},{3,2},{4,5},{5,4},{6,7},{7,6},{8,9},{9,8},{10,11... | collective-permute-start | bytes 3145736 | tf_op jit(solution)/shard_map/ppermute | solution.py:26
  325.2 12.4 %collective-permute-start.21 = (bf16[128,2048]{1,0:T(8,128)(2,1)S(1)}, bf16[128,2048]{1,0:T(8,128)(2,1)S(1)}, u32[]{:S(2)}, u32[]{:S(2)}) collective-permute-start(bf16[128,2048]{1,0:T(8,128)(2,1)S(1)} %get-tuple-element.121), channel_id=1, source_target_pairs={{0,2},{1,3},{2,0},{3,1},{4,6},{5,7},{6,4},{7,5},{8,10},{9,11},{10,... | collective-permute-start | bytes 1572872 | tf_op jit(solution)/shard_map/ppermute | solution.py:26
  326.1 12.4 %collective-permute-start.23 = (bf16[128,2048]{1,0:T(8,128)(2,1)S(1)}, bf16[128,2048]{1,0:T(8,128)(2,1)S(1)}, u32[]{:S(2)}, u32[]{:S(2)}) collective-permute-start(bf16[128,2048]{1,0:T(8,128)(2,1)S(1)} %get-tuple-element.122), channel_id=1, source_target_pairs={{0,1},{1,0},{2,3},{3,2},{4,5},{5,4},{6,7},{7,6},{8,9},{9,8},{10,11... | collective-permute-start | bytes 1572872 | tf_op jit(solution)/shard_map/ppermute | solution.py:26
  343.0 20.6 %collective-permute-start.25 = (bf16[256,2048]{1,0:T(8,128)(2,1)}, bf16[256,2048]{1,0:T(8,128)(2,1)S(1)}, u32[]{:S(2)}, u32[]{:S(2)}) collective-permute-start(bf16[256,2048]{1,0:T(8,128)(2,1)} %get-tuple-element.99), channel_id=1, source_target_pairs={{0,2},{1,3},{2,0},{3,1},{4,6},{5,7},{6,4},{7,5},{8,10},{9,11},{10,... | collective-permute-start | bytes 3145736 | tf_op jit(solution)/shard_map/ppermute | solution.py:26
  344.6 21.7 %collective-permute-start.24 = (bf16[256,2048]{1,0:T(8,128)(2,1)}, bf16[256,2048]{1,0:T(8,128)(2,1)}, u32[]{:S(2)}, u32[]{:S(2)}) collective-permute-start(bf16[256,2048]{1,0:T(8,128)(2,1)} %get-tuple-element.99), channel_id=1, source_target_pairs={{0,1},{1,0},{2,3},{3,2},{4,5},{5,4},{6,7},{7,6},{8,9},{9,8},{10,11... | collective-permute-start | bytes 3145736 | tf_op jit(solution)/shard_map/ppermute | solution.py:26
  345.6 21.8 %copy-start.55 = (bf16[1024,640]{0,1:T(8,128)(2,1)S(1)}, bf16[1024,640]{0,1:T(8,128)(2,1)}, u32[]{:S(2)}) copy-start(bf16[1024,640]{0,1:T(8,128)(2,1)} %copy-done.54) | copy-start | bytes 3932164
  363.7 15.3 %collective-permute-start.26 = (bf16[128,2048]{1,0:T(8,128)(2,1)S(1)}, bf16[128,2048]{1,0:T(8,128)(2,1)S(1)}, u32[]{:S(2)}, u32[]{:S(2)}) collective-permute-start(bf16[128,2048]{1,0:T(8,128)(2,1)S(1)} %slice.630), channel_id=1, source_target_pairs={{0,1},{1,0},{2,3},{3,2},{4,5},{5,4},{6,7},{7,6},{8,9},{9,8},{10,11... | collective-permute-start | bytes 1572872 | tf_op jit(solution)/shard_map/ppermute | solution.py:26
  367.4 14.9 %collective-permute-start.27 = (bf16[128,2048]{1,0:T(8,128)(2,1)S(1)}, bf16[128,2048]{1,0:T(8,128)(2,1)S(1)}, u32[]{:S(2)}, u32[]{:S(2)}) collective-permute-start(bf16[128,2048]{1,0:T(8,128)(2,1)S(1)} %slice.631), channel_id=1, source_target_pairs={{0,2},{1,3},{2,0},{3,1},{4,6},{5,7},{6,4},{7,5},{8,10},{9,11},{10,... | collective-permute-start | bytes 1572872 | tf_op jit(solution)/shard_map/ppermute | solution.py:26
  372.4 10.1 %copy-start.38 = (bf16[768,2048]{1,0:T(8,128)(2,1)}, bf16[768,2048]{1,0:T(8,128)(2,1)S(1)}, u32[]{:S(2)}) copy-start(bf16[768,2048]{1,0:T(8,128)(2,1)S(1)} %add_convert_fusion) | copy-start | bytes 9437188
  383.5 29.7 %collective-permute-start.29 = (bf16[256,2048]{1,0:T(8,128)(2,1)}, bf16[256,2048]{1,0:T(8,128)(2,1)S(1)}, u32[]{:S(2)}, u32[]{:S(2)}) collective-permute-start(bf16[256,2048]{1,0:T(8,128)(2,1)} %pad_maximum_fusion.18), channel_id=1, source_target_pairs={{0,2},{1,3},{2,0},{3,1},{4,6},{5,7},{6,4},{7,5},{8,10},{9,11},{10,... | collective-permute-start | bytes 3145736 | tf_op jit(solution)/shard_map/ppermute | solution.py:26
  384.6 28.7 %collective-permute-start.28 = (bf16[256,2048]{1,0:T(8,128)(2,1)}, bf16[256,2048]{1,0:T(8,128)(2,1)}, u32[]{:S(2)}, u32[]{:S(2)}) collective-permute-start(bf16[256,2048]{1,0:T(8,128)(2,1)} %pad_maximum_fusion.17), channel_id=1, source_target_pairs={{0,1},{1,0},{2,3},{3,2},{4,5},{5,4},{6,7},{7,6},{8,9},{9,8},{10,11... | collective-permute-start | bytes 3145736 | tf_op jit(solution)/shard_map/ppermute | solution.py:26
  418.0 13.2 %collective-permute-start.32 = (bf16[512,256]{1,0:T(8,128)(2,1)S(1)}, bf16[512,256]{1,0:T(8,128)(2,1)S(1)}, u32[]{:S(2)}, u32[]{:S(2)}) collective-permute-start(bf16[512,256]{1,0:T(8,128)(2,1)S(1)} %pad_maximum_fusion.34), channel_id=1, source_target_pairs={{0,2},{1,3},{2,0},{3,1},{4,6},{5,7},{6,4},{7,5},{8,10},{9,11},{10,... | collective-permute-start | bytes 786440 | tf_op jit(solution)/shard_map/ppermute | solution.py:26
  418.9 12.1 %collective-permute-start.30 = (bf16[512,256]{1,0:T(8,128)(2,1)S(1)}, bf16[512,256]{1,0:T(8,128)(2,1)S(1)}, u32[]{:S(2)}, u32[]{:S(2)}) collective-permute-start(bf16[512,256]{1,0:T(8,128)(2,1)S(1)} %pad_maximum_fusion.33), channel_id=1, source_target_pairs={{0,1},{1,0},{2,3},{3,2},{4,5},{5,4},{6,7},{7,6},{8,9},{9,8},{10,11... | collective-permute-start | bytes 786440 | tf_op jit(solution)/shard_map/ppermute | solution.py:26
  431.1 5.0 collective-permute-start.31
  431.3 5.0 collective-permute-start.33
  462.0 14.9 %collective-permute-start.38 = (bf16[256,2048]{1,0:T(8,128)(2,1)S(1)}, bf16[256,2048]{1,0:T(8,128)(2,1)S(1)}, u32[]{:S(2)}, u32[]{:S(2)}) collective-permute-start(bf16[256,2048]{1,0:T(8,128)(2,1)S(1)} %pad_maximum_fusion.20), channel_id=1, source_target_pairs={{0,2},{1,3},{2,0},{3,1},{4,6},{5,7},{6,4},{7,5},{8,10},{9,11},{10,... | collective-permute-start | bytes 3145736 | tf_op jit(solution)/shard_map/ppermute | solution.py:26
  464.1 14.9 %collective-permute-start.36 = (bf16[256,2048]{1,0:T(8,128)(2,1)S(1)}, bf16[256,2048]{1,0:T(8,128)(2,1)S(1)}, u32[]{:S(2)}, u32[]{:S(2)}) collective-permute-start(bf16[256,2048]{1,0:T(8,128)(2,1)S(1)} %pad_maximum_fusion.19), channel_id=1, source_target_pairs={{0,1},{1,0},{2,3},{3,2},{4,5},{5,4},{6,7},{7,6},{8,9},{9,8},{10,11... | collective-permute-start | bytes 3145736 | tf_op jit(solution)/shard_map/ppermute | solution.py:26
  465.8 16.8 %collective-permute-start.34 = (bf16[128,2048]{1,0:T(8,128)(2,1)S(1)}, bf16[128,2048]{1,0:T(8,128)(2,1)S(1)}, u32[]{:S(2)}, u32[]{:S(2)}) collective-permute-start(bf16[128,2048]{1,0:T(8,128)(2,1)S(1)} %get-tuple-element.115), channel_id=1, source_target_pairs={{0,2},{1,3},{2,0},{3,1},{4,6},{5,7},{6,4},{7,5},{8,10},{9,11},{10,... | collective-permute-start | bytes 1572872 | tf_op jit(solution)/shard_map/ppermute | solution.py:26
  466.9 17.7 %collective-permute-start.35 = (bf16[128,2048]{1,0:T(8,128)(2,1)S(1)}, bf16[128,2048]{1,0:T(8,128)(2,1)S(1)}, u32[]{:S(2)}, u32[]{:S(2)}) collective-permute-start(bf16[128,2048]{1,0:T(8,128)(2,1)S(1)} %get-tuple-element.116), channel_id=1, source_target_pairs={{0,1},{1,0},{2,3},{3,2},{4,5},{5,4},{6,7},{7,6},{8,9},{9,8},{10,11... | collective-permute-start | bytes 1572872 | tf_op jit(solution)/shard_map/ppermute | solution.py:26
  479.6 9.2 %collective-permute-start.37 = (bf16[128,2048]{1,0:T(8,128)(2,1)S(1)}, bf16[128,2048]{1,0:T(8,128)(2,1)S(1)}, u32[]{:S(2)}, u32[]{:S(2)}) collective-permute-start(bf16[128,2048]{1,0:T(8,128)(2,1)S(1)} %get-tuple-element.109), channel_id=1, source_target_pairs={{0,2},{1,3},{2,0},{3,1},{4,6},{5,7},{6,4},{7,5},{8,10},{9,11},{10,... | collective-permute-start | bytes 1572872 | tf_op jit(solution)/shard_map/ppermute | solution.py:26
  479.8 10.4 %copy-start.49 = (f32[256,2048]{1,0:T(8,128)S(1)}, f32[256,2048]{1,0:T(8,128)}, u32[]{:S(2)}) copy-start(f32[256,2048]{1,0:T(8,128)} %fusion.76) | copy-start | bytes 6291460
  479.8 10.4 %collective-permute-start.39 = (bf16[128,2048]{1,0:T(8,128)(2,1)S(1)}, bf16[128,2048]{1,0:T(8,128)(2,1)S(1)}, u32[]{:S(2)}, u32[]{:S(2)}) collective-permute-start(bf16[128,2048]{1,0:T(8,128)(2,1)S(1)} %get-tuple-element.110), channel_id=1, source_target_pairs={{0,1},{1,0},{2,3},{3,2},{4,5},{5,4},{6,7},{7,6},{8,9},{9,8},{10,11... | collective-permute-start | bytes 1572872 | tf_op jit(solution)/shard_map/ppermute | solution.py:26
  498.5 4.6 collective-permute-start.41
  499.1 4.6 collective-permute-start.40
  499.8 5.8 %collective-permute-start.42 = (f32[64,265]{1,0:T(8,128)S(1)}, f32[64,265]{1,0:T(8,128)S(1)}, u32[]{:S(2)}, u32[]{:S(2)}) collective-permute-start(f32[64,265]{1,0:T(8,128)S(1)} %pad_maximum_fusion.36), channel_id=1, source_target_pairs={{0,3},{1,2},{2,1},{3,0},{4,7},{5,6},{6,5},{7,4},{8,11},{9,10},{10,... | collective-permute-start | bytes 203528 | tf_op jit(solution)/shard_map/ppermute | solution.py:26
  (74 other events, 235.0 us)
Sparse Core Ops, SparseCore 0:
  11.3 51.7 all-gather.3
  65.3 89.9 all-gather.5
  157.4 76.3 all-gather.7
  242.9 98.8 reduce-scatter.3
  344.0 83.0 reduce-scatter.5
  440.3 52.9 reduce-scatter.7

commit v7 on v6

--- a/solution.py
+++ b/solution.py
@@ -330,7 +330,15 @@
     near = near_blocks(layer_input)
     inputs = all_blocks(layer_input, near)
     attn_full = gather_dp(attn_shard)
-    ff_full = [gather_dp(after(ff_shards[0], *inputs))]
+
+    def norm(block):
+        block = block.astype(f32)
+        return (block * inverse_norm(block)).astype(bf16)
+
+    normed_one = jnp.concatenate([norm(b) for b in inputs], axis=0)
+    top = out_grad.astype(f32) * own_mask
+    ready = normed_one, ff_shards[1], top.astype(bf16), cos2, sin2
+    ff_full = [gather_dp(after(ff_shards[0], *ready))]
     attn_full = attn_full.reshape(-1, *attn_shard.shape)
     query_full = attn_full[:, :shard_rows].reshape(model_width, heads_width)
     project_full = attn_full[:, shard_rows : 2 * shard_rows].reshape(model_width, heads_width)
@@ -340,15 +348,8 @@
     kv_blocks = kv_blocks.reshape(ranks, -1, kv_rows, 2 * HD)
     keyvalue_full = jnp.stack([pick(kv_blocks, order[j], 0) for j in range(ranks)], axis=1)
     qkv_full = jnp.concatenate([query_full, keyvalue_full.reshape(model_width, 2 * HD)], axis=1)
-    top = out_grad.astype(f32) * own_mask
     top_own = after(top.astype(bf16), keyvalue_full)
     top_near = near_blocks(top_own)
-
-    def norm(block):
-        block = block.astype(f32)
-        return (block * inverse_norm(block)).astype(bf16)
-
-    normed_one = jnp.concatenate([norm(b) for b in inputs], axis=0)
     qkv = dot(normed_one, qkv_full, 1, 0)
     qr, kvt, mixed, lse = attend(where, qkv, cos2, sin2, rows)
     ff_full.append(gather_dp(after(ff_shards[1], mixed)))
@@ -394,7 +395,7 @@
     hidden1, grads1 = feed(after(normed_two, rest0), pairs[1], dot(top_all, downs[1], 1, 0))
     rest = (rest0 + dot(grads1[rows:], pairs[1], 1, 1)).astype(bf16)
     rest_sent = send_sums(rest)
-    partial1 = partial(after(hidden1, rest), after(grads1, rest))
+    partial1 = partial(after(hidden1, *rest_sent), after(grads1, *rest_sent))
     ff_sums = [scatter_dp(partial0), scatter_dp(partial1)]
     own = dot(after(grads0[:rows], partial1), pairs[0], 1, 1) + dot(grads1[:rows], pairs[1], 1, 1)
     scaled = finish_sums(own, rest, rest_sent)
@@ -448,6 +449,7 @@
 
     query_sum, project_sum = attn_sum[:shard_rows], attn_sum[shard_rows : 2 * shard_rows]
     kv_sum = attn_sum[2 * shard_rows :].reshape(kv_rows, 2 * HD)
+    ff_sums = [after(total, *qkv_sent) for total in ff_sums]
     pair_sums = [total[:, : own.shape[1]] for own, total in zip(pair_own, ff_sums)]
     down_sum = jnp.concatenate(
         [total[:, own.shape[1] :] for own, total in zip(pair_own, ff_sums)], axis=1

time: 525 us -> 521 us (level)
  other arithmetic: 81.3 us -> 94.4 us
  local copies, waits for them, and re-layouts: 67.7 us -> 60.2 us
  matrix products: 128 us -> 122 us
    ppermute x43, waiting for transfers between devices: 138 us -> 124 us  [hop(): return lax.ppermute(value, 'tensor', [(i, i ^ step) for i in range(size)])]
    all_gather x3, waiting for transfers between devices: 0.01 us -> 12.7 us  [gather_dp(): return lax.all_gather(shard, 'dp', axis=0, tiled=True)]
    dot_general x25, matrix products: 128 us -> 122 us  [dot(): lax.dot_general(a, b, (((ca,), (cb,)), ((), ())), preferred_element_type=...]
    unnamed x196 -> x226, local copies, waits for them, and re-layouts: 38.8 us -> 36.3 us
  transfers between devices with their start and end apart: 49 -> 49, of which waited for: 32 -> 30; matrix products, arithmetic and copies ran while one was open for 48% -> 50% of each run, Pallas kernels for 5% -> 5%
where the time goes in v7:
time: 521 us; the launch traced here: 515 us
  waiting for transfers between devices  136 us (26%)
  matrix products  122 us (23%)
  other arithmetic  94.4 us (18%)
  local copies, waits for them, and re-layouts  60.2 us (12%)
  starting transfers between devices  51.9 us (10%)
  Pallas kernels  25 us (5%)
  between operations  24.6 us (5%)
    ppermute x43, waiting for transfers between devices, hop(): return lax.ppermute(value, 'tensor', [(i, i ^ step) for i in range(size)])  124 us
    dot_general x25, matrix products, dot(): lax.dot_general(a, b, (((ca,), (cb,)), ((), ())), preferred_element_type=...  122 us
    ppermute x43, starting transfers between devices, hop(): return lax.ppermute(value, 'tensor', [(i, i ^ step) for i in range(size)])  51.1 us
    unnamed x226, local copies, waits for them, and re-layouts  36.3 us
    concatenate x2, other arithmetic, partial(): jnp.concatenate([dot(normed_two, grads, 0, 0).astype(bf16), dot(top_all,...  19.6 us
    pallas_call x1, Pallas kernels, attend_back(): pl.pallas_call(attend_back_kernel, name='attend_back', grid_spec=pltpu.Pr...  13.7 us
    all_gather x3, waiting for transfers between devices, gather_dp(): return lax.all_gather(shard, 'dp', axis=0, tiled=True)  12.7 us
    pallas_call x1, Pallas kernels, attend(): pl.pallas_call(attend_kernel, name='attend', grid_spec=pltpu.PrefetchScal...  11.4 us
  transfers between devices with their start and end apart: 49, of which 30 were waited for; matrix products, arithmetic and copies ran while one was open for 50% of the time, Pallas kernels for 5%

profile of v7, /device:TPU:0, one launch (start us, length us, event | category | flops | bytes accessed | tf_op | source)
XLA Modules:
  0.0 514.6 jit_solution(1604369679955956040)
XLA Ops:
  7.2 3.1 collective-permute-start.1
  20.8 3.1 fusion.93
  26.5 2.1 pad_maximum_fusion.11
  40.0 2.4 fusion.57
  43.6 3.3 collective-permute-done.2
  47.1 2.1 collective-permute-done.3
  51.6 12.7 %all-gather.4.cloned.1.call-done = bf16[4352,512]{1,0:T(8,128)(2,1)} async-done(((bf16[544,512]{1,0:T(8,128)(2,1)}), bf16[4352,512]{1,0:T(8,128)(2,1)}) %all-gather.4.cloned.1.call-update) | async-done | bytes 4456464 | tf_op jit(solution)/shard_map/all_gather | solution.py:76
  78.2 3.8 collective-permute-done.6
  88.1 7.3 %fusion.77.q_ref.kv_ref = f32[1024,768]{1,0:T(8,128)} fusion(bf16[1024,2048]{1,0:T(8,128)(2,1)} %fusion.80, bf16[2048,256]{1,0:T(8,128)(2,1)S(1)} %bitcast.109, bf16[2048,512]{1,0:T(8,128)(2,1)S(1)} %bitcast.104), kind=kOutput, calls=%fused_computation.159 | convolution fusion | flops 3227516928 | bytes 10485760 | tf_op jit(solution)/shard_map/dot_general | solution.py:21
  95.4 11.4 %attend.1 = (bf16[1024,512]{1,0:T(8,128)(2,1)S(1)}, bf16[1024,256]{1,0:T(8,128)(2,1)S(1)}, bf16[1024,512]{1,0:T(8,128)(2,1)S(1)}, f32[1024,128]{1,0:T(8,128)S(1)}) custom-call(s32[2]{0:T(128)S(1)} %pad_add_fusion.where_ref, f32[1024,768]{1,0:T(8,128)} %fusion.77.q_ref.kv_ref, f32[1024,768]{1,0:T(8,128)} %fusion.77.q_ref.kv_ref, ...), custom_call_target="tpu_custom_call" | custom-call | flops 2147483648 | bytes 8388608 | tf_op jit(solution)/shard_map/attend/pallas_call | solution.py:199
  109.9 3.7 convolution_convert_fusion.2
  116.9 20.2 %collective-permute-done.10 = bf16[256,2048]{1,0:T(8,128)(2,1)S(1)} collective-permute-done((bf16[256,2048]{1,0:T(8,128)(2,1)S(1)}, bf16[256,2048]{1,0:T(8,128)(2,1)S(1)}, u32[]{:S(2)}, u32[]{:S(2)}) %collective-permute-start.10) | collective-permute-done | bytes 1048608 | tf_op jit(solution)/shard_map/ppermute | solution.py:26
  148.4 4.5 collective-permute-done.11
  155.5 6.1 %collective-permute-done.14 = bf16[128,2048]{1,0:T(8,128)(2,1)S(1)} collective-permute-done((bf16[128,2048]{1,0:T(8,128)(2,1)S(1)}, bf16[128,2048]{1,0:T(8,128)(2,1)S(1)}, u32[]{:S(2)}, u32[]{:S(2)}) %collective-permute-start.14) | collective-permute-done | bytes 524320 | tf_op jit(solution)/shard_map/ppermute | solution.py:26
  165.9 6.4 %fusion.27 = f32[1024,768]{0,1:T(8,128)S(1)} fusion(bf16[1024,2048]{1,0:T(8,128)(2,1)} %copy-done.79, bf16[2048,2304]{0,1:T(8,128)(2,1)} %all-gather.6.cloned.1.call-done), kind=kOutput, calls=%fused_computation.59 | convolution fusion | flops 3221225472 | bytes 10485760 | tf_op jit(solution)/shard_map/dot_general | solution.py:21
  172.3 13.1 %collective-permute-done.17 = bf16[256,2048]{1,0:T(8,128)(2,1)} collective-permute-done((bf16[256,2048]{1,0:T(8,128)(2,1)}, bf16[256,2048]{1,0:T(8,128)(2,1)}, u32[]{:S(2)}, u32[]{:S(2)}) %collective-permute-start.17) | collective-permute-done | bytes 1048608 | tf_op jit(solution)/shard_map/ppermute | solution.py:26
  193.9 2.9 collective-permute-done.18
  196.8 3.0 collective-permute-done.19
  199.9 6.8 %fusion.4 = f32[1024,1536]{0,1:T(8,128)S(1)} fusion(bf16[1024,2048]{1,0:T(8,128)(2,1)S(1)} %constant_dynamic-update-slice_fusion.10, bf16[2048,2304]{0,1:T(8,128)(2,1)S(1)} %copy-done.94), kind=kOutput, calls=%fused_computation.10 | convolution fusion | flops 6442450944 | bytes 16777216 | tf_op jit(solution)/shard_map/dot_general | solution.py:21
  206.7 2.2 multiply_convert_fusion.1
  208.9 3.6 convolution_convert_fusion.3
  212.6 8.7 %convolution_convert_fusion.1 = bf16[2048,1536]{0,1:T(8,128)(2,1)S(1)} fusion(bf16[1024,2048]{1,0:T(8,128)(2,1)S(1)} %constant_dynamic-update-slice_fusion.10, bf16[1024,768]{0,1:T(8,128)(2,1)S(1)} %get-tuple-element.106, bf16[1024,768]{0,1:T(8,128)(2,1)S(1)} %get-tuple-element.105), kind=kOutput, calls=%fused_computation.3 | convolution fusion | flops 6451888128 | bytes 13631488 | tf_op jit(solution)/shard_map/dot_general | solution.py:21
  221.3 11.5 %pad_maximum_fusion = bf16[2048,2304]{0,1:T(8,128)(2,1)} fusion(bf16[2048,768]{0,1:T(8,128)(2,1)S(1)} %convolution_convert_fusion.3, bf16[2048,1536]{0,1:T(8,128)(2,1)S(1)} %convolution_convert_fusion.1), kind=kLoop, calls=%fused_computation | loop fusion | flops 18874368 | bytes 18874368 | tf_op jit(solution)/shard_map/concatenate | solution.py:384
  234.8 9.8 %fusion.2 = f32[768,2048]{1,0:T(8,128)} fusion(bf16[768,1536]{0,1:T(8,128)(2,1)S(1)} %pad_maximum_fusion.5, bf16[2048,2304]{0,1:T(8,128)(2,1)} %all-gather.6.cloned.1.call-done), kind=kOutput, calls=%fused_computation.8 | convolution fusion | flops 4831838208 | bytes 14942208 | tf_op jit(solution)/shard_map/dot_general | solution.py:21
  244.6 5.7 %fusion.43 = f32[1024,640]{0,1:T(8,128)S(1)} fusion(bf16[1024,2048]{1,0:T(8,128)(2,1)} %copy-done.79, bf16[2048,1920]{0,1:T(8,128)(2,1)} %all-gather.8.cloned.1.call-done), kind=kOutput, calls=%fused_computation.83 | convolution fusion | flops 2684354560 | bytes 9437184 | tf_op jit(solution)/shard_map/dot_general | solution.py:21
  251.2 5.8 %fusion.10 = f32[1024,1280]{0,1:T(8,128)S(1)} fusion(bf16[1024,2048]{1,0:T(8,128)(2,1)S(1)} %copy-done.83, bf16[2048,1920]{0,1:T(8,128)(2,1)S(1)} %copy-done.33), kind=kOutput, calls=%fused_computation.17 | convolution fusion | flops 5368709120 | bytes 14680064 | tf_op jit(solution)/shard_map/dot_general | solution.py:21
  256.9 1.9 multiply_convert_fusion.4
  258.9 4.5 add_convert_fusion.1
  267.1 18.2 %collective-permute-done.21 = bf16[256,2048]{1,0:T(8,128)(2,1)S(1)} collective-permute-done((bf16[256,2048]{1,0:T(8,128)(2,1)S(1)}, bf16[256,2048]{1,0:T(8,128)(2,1)S(1)}, u32[]{:S(2)}, u32[]{:S(2)}) %collective-permute-start.21) | collective-permute-done | bytes 1048608 | tf_op jit(solution)/shard_map/ppermute | solution.py:26
  285.9 4.6 convolution_convert_fusion.5
  290.5 7.3 %convolution_convert_fusion = bf16[2048,1280]{0,1:T(8,128)(2,1)} fusion(bf16[1024,1280]{0,1:T(8,128)(2,1)S(1)} %pad_maximum_fusion.3, bf16[1024,2048]{1,0:T(8,128)(2,1)S(1)} %copy-done.84), kind=kOutput, calls=%fused_computation.2 | convolution fusion | flops 5371330560 | bytes 12058624 | tf_op jit(solution)/shard_map/dot_general | solution.py:21
  297.8 8.0 %pad_maximum_fusion.1 = bf16[2048,1920]{0,1:T(8,128)(2,1)} fusion(bf16[2048,640]{0,1:T(8,128)(2,1)} %convolution_convert_fusion.5, bf16[2048,1280]{0,1:T(8,128)(2,1)} %convolution_convert_fusion), kind=kLoop, calls=%fused_computation.1 | loop fusion | flops 15728640 | bytes 15728640 | tf_op jit(solution)/shard_map/concatenate | solution.py:384
  312.7 4.9 fusion
  323.0 2.8 constant_dynamic-update-slice_fusion.19
  327.6 5.1 fusion.25
  332.7 13.7 %collective-permute-done.25 = bf16[256,2048]{1,0:T(8,128)(2,1)S(1)} collective-permute-done((bf16[256,2048]{1,0:T(8,128)(2,1)}, bf16[256,2048]{1,0:T(8,128)(2,1)S(1)}, u32[]{:S(2)}, u32[]{:S(2)}) %collective-permute-start.25) | collective-permute-done | bytes 1048608 | tf_op jit(solution)/shard_map/ppermute | solution.py:26
  346.4 2.2 collective-permute-start.26
  352.8 4.8 add_convert_fusion
  357.6 2.1 constant_dynamic-update-slice_fusion.18
  359.8 6.4 %collective-permute-done.27 = bf16[128,2048]{1,0:T(8,128)(2,1)S(1)} collective-permute-done((bf16[128,2048]{1,0:T(8,128)(2,1)S(1)}, bf16[128,2048]{1,0:T(8,128)(2,1)S(1)}, u32[]{:S(2)}, u32[]{:S(2)}) %collective-permute-start.27) | collective-permute-done | bytes 524320 | tf_op jit(solution)/shard_map/ppermute | solution.py:26
  371.2 1.9 copy-done.78
  373.2 3.8 convolution_convert_fusion.6
  376.9 3.0 convert_element_type.347
  380.0 4.7 convolution_convert_fusion.9.dm_ref
  384.7 13.7 %attend_back.1 = (bf16[1024,512]{1,0:T(8,128)(2,1)S(1)}, bf16[1024,256]{1,0:T(8,128)(2,1)S(1)}) custom-call(s32[2]{0:T(128)S(1)} %copy-done.3, bf16[1024,512]{1,0:T(8,128)(2,1)S(1)} %get-tuple-element.55.qr_ref, bf16[1024,256]{1,0:T(8,128)(2,1)S(1)} %copy-done.5, bf16[1024,512]{1,0:T(8,128)(2,1)S(1)} %convolution_convert_fusion.9.dm_ref, ...), custom_call_target="tpu_custom_call" | custom-call | flops 5368709120 | bytes 8388608 | tf_op jit(solution)/shard_map/attend_back/pallas_call | solution.py:237
  399.5 4.2 convolution_convert_fusion.8
  405.3 4.0 convolution_convert_fusion.4
  409.3 5.9 %convolution_convert_fusion.7 = bf16[2048,512]{1,0:T(8,128)(2,1)} fusion(bf16[1024,2048]{1,0:T(8,128)(2,1)} %fusion.80, bf16[1024,512]{1,0:T(8,128)(2,1)S(1)} %slice-done.1), kind=kOutput, calls=%fused_computation.40 | convolution fusion | flops 2148532224 | bytes 7340032 | tf_op jit(solution)/shard_map/dot_general | solution.py:21
  418.3 2.1 collective-permute-done.31
  422.2 3.5 pad_maximum_fusion.2
  426.8 2.4 slice.609
  430.2 2.3 fusion.76
  435.6 2.5 fusion.65
  442.7 2.0 collective-permute-start.38
  445.6 2.9 fusion.23
  448.6 2.9 convolution_add_fusion
  451.5 3.1 fusion.66
  454.6 8.2 %collective-permute-done.38 = bf16[256,2048]{1,0:T(8,128)(2,1)S(1)} collective-permute-done((bf16[256,2048]{1,0:T(8,128)(2,1)S(1)}, bf16[256,2048]{1,0:T(8,128)(2,1)S(1)}, u32[]{:S(2)}, u32[]{:S(2)}) %collective-permute-start.38) | collective-permute-done | bytes 1048608 | tf_op jit(solution)/shard_map/ppermute | solution.py:26
  471.9 3.3 fusion.61
  479.3 2.9 copy.49
  482.2 2.4 maximum_bitcast_fusion
  484.6 2.1 collective-permute-done.37
  488.0 2.5 fusion.62
  492.4 2.3 fusion.36
  (463 shorter events, 149.5 us)
Async XLA Ops:
  7.2 57.2 %all-gather.4.cloned.1.call-start = ((), (), s32[]{:S(2)}) async-start(), calls=%async_computation.3 | async-start | bytes 5013504 | tf_op jit(solution)/shard_map/all_gather | solution.py:76
  7.2 26.4 %collective-permute-start.1 = (bf16[256,2048]{1,0:T(8,128)(2,1)}, bf16[256,2048]{1,0:T(8,128)(2,1)S(1)}, u32[]{:S(2)}, u32[]{:S(2)}) collective-permute-start(bf16[256,2048]{1,0:T(8,128)(2,1)} %param.12), channel_id=1, source_target_pairs={{0,2},{1,3},{2,0},{3,1},{4,6},{5,7},{6,4},{7,5},{8,10},{9,11},{10,... | collective-permute-start | bytes 3145736 | tf_op jit(solution)/shard_map/ppermute | solution.py:26
  10.3 25.2 %collective-permute-start = (bf16[256,2048]{1,0:T(8,128)(2,1)}, bf16[256,2048]{1,0:T(8,128)(2,1)}, u32[]{:S(2)}, u32[]{:S(2)}) collective-permute-start(bf16[256,2048]{1,0:T(8,128)(2,1)} %param.12), channel_id=1, source_target_pairs={{0,1},{1,0},{2,3},{3,2},{4,5},{5,4},{6,7},{7,6},{8,9},{9,8},{10,11... | collective-permute-start | bytes 3145736 | tf_op jit(solution)/shard_map/ppermute | solution.py:26
  15.8 150.1 %all-gather.6.cloned.1.call-start = ((), (), s32[]{:S(2)}) async-start(), calls=%async_computation.4 | async-start | bytes 10616832 | tf_op jit(solution)/shard_map/all_gather | solution.py:76
  17.3 9.1 %copy-start.90 = (f32[256]{0:T(256)}, f32[256]{0:T(256)S(1)}, u32[]{:S(2)}) copy-start(f32[256]{0:T(256)S(1)} %convert_element_type.322) | copy-start | bytes 3076
  33.7 13.3 %collective-permute-start.2 = (bf16[128,2048]{1,0:T(8,128)(2,1)S(1)}, bf16[128,2048]{1,0:T(8,128)(2,1)S(1)}, u32[]{:S(2)}, u32[]{:S(2)}) collective-permute-start(bf16[128,2048]{1,0:T(8,128)(2,1)S(1)} %slice.583), channel_id=1, source_target_pairs={{0,1},{1,0},{2,3},{3,2},{4,5},{5,4},{6,7},{7,6},{8,9},{9,8},{10,11... | collective-permute-start | bytes 1572872 | tf_op jit(solution)/shard_map/ppermute | solution.py:26
  36.6 12.7 %collective-permute-start.3 = (bf16[128,2048]{1,0:T(8,128)(2,1)S(1)}, bf16[128,2048]{1,0:T(8,128)(2,1)S(1)}, u32[]{:S(2)}, u32[]{:S(2)}) collective-permute-start(bf16[128,2048]{1,0:T(8,128)(2,1)S(1)} %slice.584), channel_id=1, source_target_pairs={{0,2},{1,3},{2,0},{3,1},{4,6},{5,7},{6,4},{7,5},{8,10},{9,11},{10,... | collective-permute-start | bytes 1572872 | tf_op jit(solution)/shard_map/ppermute | solution.py:26
  51.4 193.2 %all-gather.8.cloned.1.call-start = ((), (), s32[]{:S(2)}) async-start(), calls=%async_computation.5 | async-start | bytes 8847360 | tf_op jit(solution)/shard_map/all_gather | solution.py:76
  65.4 11.4 %collective-permute-start.5 = (bf16[512,256]{1,0:T(8,128)(2,1)S(1)}, bf16[512,256]{1,0:T(8,128)(2,1)S(1)}, u32[]{:S(2)}, u32[]{:S(2)}) collective-permute-start(bf16[512,256]{1,0:T(8,128)(2,1)S(1)} %reshape.205), channel_id=1, source_target_pairs={{0,2},{1,3},{2,0},{3,1},{4,6},{5,7},{6,4},{7,5},{8,10},{9,11},{10,... | collective-permute-start | bytes 786440 | tf_op jit(solution)/shard_map/ppermute | solution.py:26
  67.0 10.5 %collective-permute-start.4 = (bf16[512,256]{1,0:T(8,128)(2,1)S(1)}, bf16[512,256]{1,0:T(8,128)(2,1)S(1)}, u32[]{:S(2)}, u32[]{:S(2)}) collective-permute-start(bf16[512,256]{1,0:T(8,128)(2,1)S(1)} %reshape.205), channel_id=1, source_target_pairs={{0,1},{1,0},{2,3},{3,2},{4,5},{5,4},{6,7},{7,6},{8,9},{9,8},{10,11... | collective-permute-start | bytes 786440 | tf_op jit(solution)/shard_map/ppermute | solution.py:26
  76.8 18.6 %copy-start.2 = (s32[2]{0:T(128)}, s32[2]{0:T(128)S(1)}, u32[]{:S(2)}) copy-start(s32[2]{0:T(128)S(1)} %pad_add_fusion.where_ref) | copy-start | bytes 28
  76.9 5.1 collective-permute-start.6
  77.5 5.0 collective-permute-start.7
  82.8 27.1 %collective-permute-start.9 = (bf16[256,2048]{1,0:T(8,128)(2,1)}, bf16[256,2048]{1,0:T(8,128)(2,1)}, u32[]{:S(2)}, u32[]{:S(2)}) collective-permute-start(bf16[256,2048]{1,0:T(8,128)(2,1)} %fusion.40), channel_id=1, source_target_pairs={{0,2},{1,3},{2,0},{3,1},{4,6},{5,7},{6,4},{7,5},{8,10},{9,11},{10,... | collective-permute-start | bytes 3145736 | tf_op jit(solution)/shard_map/ppermute | solution.py:26
  83.4 26.5 %collective-permute-start.8 = (bf16[256,2048]{1,0:T(8,128)(2,1)}, bf16[256,2048]{1,0:T(8,128)(2,1)}, u32[]{:S(2)}, u32[]{:S(2)}) collective-permute-start(bf16[256,2048]{1,0:T(8,128)(2,1)} %fusion.40), channel_id=1, source_target_pairs={{0,1},{1,0},{2,3},{3,2},{4,5},{5,4},{6,7},{7,6},{8,9},{9,8},{10,11... | collective-permute-start | bytes 3145736 | tf_op jit(solution)/shard_map/ppermute | solution.py:26
  109.4 267.5 %reduce-scatter.4.cloned.1.call-start = ((), (), s32[]{:S(2)}) async-start(), calls=%async_computation.6 | async-start | bytes 10616832 | tf_op jit(solution)/shard_map/reduce_scatter | solution.py:80
  113.8 23.2 %collective-permute-start.10 = (bf16[256,2048]{1,0:T(8,128)(2,1)S(1)}, bf16[256,2048]{1,0:T(8,128)(2,1)S(1)}, u32[]{:S(2)}, u32[]{:S(2)}) collective-permute-start(bf16[256,2048]{1,0:T(8,128)(2,1)S(1)} %pad_maximum_fusion.13), channel_id=1, source_target_pairs={{0,1},{1,0},{2,3},{3,2},{4,5},{5,4},{6,7},{7,6},{8,9},{9,8},{10,11... | collective-permute-start | bytes 3145736 | tf_op jit(solution)/shard_map/ppermute | solution.py:26
  114.6 22.9 %collective-permute-start.12 = (bf16[256,2048]{1,0:T(8,128)(2,1)S(1)}, bf16[256,2048]{1,0:T(8,128)(2,1)S(1)}, u32[]{:S(2)}, u32[]{:S(2)}) collective-permute-start(bf16[256,2048]{1,0:T(8,128)(2,1)S(1)} %pad_maximum_fusion.14), channel_id=1, source_target_pairs={{0,2},{1,3},{2,0},{3,1},{4,6},{5,7},{6,4},{7,5},{8,10},{9,11},{10,... | collective-permute-start | bytes 3145736 | tf_op jit(solution)/shard_map/ppermute | solution.py:26
  138.0 14.9 %collective-permute-start.11 = (bf16[128,2048]{1,0:T(8,128)(2,1)S(1)}, bf16[128,2048]{1,0:T(8,128)(2,1)S(1)}, u32[]{:S(2)}, u32[]{:S(2)}) collective-permute-start(bf16[128,2048]{1,0:T(8,128)(2,1)S(1)} %get-tuple-element.131), channel_id=1, source_target_pairs={{0,2},{1,3},{2,0},{3,1},{4,6},{5,7},{6,4},{7,5},{8,10},{9,11},{10,... | collective-permute-start | bytes 1572872 | tf_op jit(solution)/shard_map/ppermute | solution.py:26
  139.6 14.8 %collective-permute-start.13 = (bf16[128,2048]{1,0:T(8,128)(2,1)S(1)}, bf16[128,2048]{1,0:T(8,128)(2,1)S(1)}, u32[]{:S(2)}, u32[]{:S(2)}) collective-permute-start(bf16[128,2048]{1,0:T(8,128)(2,1)S(1)} %get-tuple-element.132), channel_id=1, source_target_pairs={{0,1},{1,0},{2,3},{3,2},{4,5},{5,4},{6,7},{7,6},{8,9},{9,8},{10,11... | collective-permute-start | bytes 1572872 | tf_op jit(solution)/shard_map/ppermute | solution.py:26
  144.6 17.0 %collective-permute-start.14 = (bf16[128,2048]{1,0:T(8,128)(2,1)S(1)}, bf16[128,2048]{1,0:T(8,128)(2,1)S(1)}, u32[]{:S(2)}, u32[]{:S(2)}) collective-permute-start(bf16[128,2048]{1,0:T(8,128)(2,1)S(1)} %slice.479), channel_id=1, source_target_pairs={{0,1},{1,0},{2,3},{3,2},{4,5},{5,4},{6,7},{7,6},{8,9},{9,8},{10,11... | collective-permute-start | bytes 1572872 | tf_op jit(solution)/shard_map/ppermute | solution.py:26
  145.3 16.3 %collective-permute-start.15 = (bf16[128,2048]{1,0:T(8,128)(2,1)S(1)}, bf16[128,2048]{1,0:T(8,128)(2,1)S(1)}, u32[]{:S(2)}, u32[]{:S(2)}) collective-permute-start(bf16[128,2048]{1,0:T(8,128)(2,1)S(1)} %slice.480), channel_id=1, source_target_pairs={{0,2},{1,3},{2,0},{3,1},{4,6},{5,7},{6,4},{7,5},{8,10},{9,11},{10,... | collective-permute-start | bytes 1572872 | tf_op jit(solution)/shard_map/ppermute | solution.py:26
  163.9 21.4 %collective-permute-start.17 = (bf16[256,2048]{1,0:T(8,128)(2,1)}, bf16[256,2048]{1,0:T(8,128)(2,1)}, u32[]{:S(2)}, u32[]{:S(2)}) collective-permute-start(bf16[256,2048]{1,0:T(8,128)(2,1)} %multiply_convert_fusion.6), channel_id=1, source_target_pairs={{0,2},{1,3},{2,0},{3,1},{4,6},{5,7},{6,4},{7,5},{8,10},{9,11},{10,... | collective-permute-start | bytes 3145736 | tf_op jit(solution)/shard_map/ppermute | solution.py:26
  164.5 25.0 %collective-permute-start.16 = (bf16[256,2048]{1,0:T(8,128)(2,1)}, bf16[256,2048]{1,0:T(8,128)(2,1)}, u32[]{:S(2)}, u32[]{:S(2)}) collective-permute-start(bf16[256,2048]{1,0:T(8,128)(2,1)} %multiply_convert_fusion.6), channel_id=1, source_target_pairs={{0,1},{1,0},{2,3},{3,2},{4,5},{5,4},{6,7},{7,6},{8,9},{9,8},{10,11... | collective-permute-start | bytes 3145736 | tf_op jit(solution)/shard_map/ppermute | solution.py:26
  185.3 14.5 %copy-start.94 = (bf16[2048,2304]{0,1:T(8,128)(2,1)S(1)}, bf16[2048,2304]{0,1:T(8,128)(2,1)}, u32[]{:S(2)}) copy-start(bf16[2048,2304]{0,1:T(8,128)(2,1)} %all-gather.6.cloned.1.call-done) | copy-start | bytes 28311556
  186.6 10.2 %collective-permute-start.18 = (bf16[128,2048]{1,0:T(8,128)(2,1)S(1)}, bf16[128,2048]{1,0:T(8,128)(2,1)S(1)}, u32[]{:S(2)}, u32[]{:S(2)}) collective-permute-start(bf16[128,2048]{1,0:T(8,128)(2,1)S(1)} %slice.488), channel_id=1, source_target_pairs={{0,1},{1,0},{2,3},{3,2},{4,5},{5,4},{6,7},{7,6},{8,9},{9,8},{10,11... | collective-permute-start | bytes 1572872 | tf_op jit(solution)/shard_map/ppermute | solution.py:26
  190.6 9.2 %collective-permute-start.19 = (bf16[128,2048]{1,0:T(8,128)(2,1)S(1)}, bf16[128,2048]{1,0:T(8,128)(2,1)S(1)}, u32[]{:S(2)}, u32[]{:S(2)}) collective-permute-start(bf16[128,2048]{1,0:T(8,128)(2,1)S(1)} %slice.489), channel_id=1, source_target_pairs={{0,2},{1,3},{2,0},{3,1},{4,6},{5,7},{6,4},{7,5},{8,10},{9,11},{10,... | collective-permute-start | bytes 1572872 | tf_op jit(solution)/shard_map/ppermute | solution.py:26
  199.9 12.7 %copy-start.82 = (bf16[1024,2048]{1,0:T(8,128)(2,1)}, bf16[1024,2048]{1,0:T(8,128)(2,1)S(1)}, u32[]{:S(2)}) copy-start(bf16[1024,2048]{1,0:T(8,128)(2,1)S(1)} %constant_dynamic-update-slice_fusion.10) | copy-start | bytes 12582916
  232.8 206.6 %reduce-scatter.6.cloned.1.call-start = ((), (), s32[]{:S(2)}) async-start(), calls=%async_computation.7 | async-start | bytes 8847360 | tf_op jit(solution)/shard_map/reduce_scatter | solution.py:80
  244.6 14.3 %slice-start.9 = ((s8[6291456]{0:T(1024)(128)(4,1)}), s8[4194304]{0:T(1024)(128)(4,1)S(1)}, s32[]{:S(2)}) async-start(s8[6291456]{0:T(1024)(128)(4,1)} %bitcast.129), calls=%async_computation.18 | async-start | bytes 8388608
  258.9 8.0 %copy-start.19 = (bf16[1024,640]{0,1:T(8,128)(2,1)}, bf16[1024,640]{0,1:T(8,128)(2,1)S(1)}, u32[]{:S(2)}) copy-start(bf16[1024,640]{0,1:T(8,128)(2,1)S(1)} %get-tuple-element.107) | copy-start | bytes 3932164
  258.9 8.0 %copy-start.21 = (bf16[1024,640]{0,1:T(8,128)(2,1)}, bf16[1024,640]{0,1:T(8,128)(2,1)S(1)}, u32[]{:S(2)}) copy-start(bf16[1024,640]{0,1:T(8,128)(2,1)S(1)} %get-tuple-element.108) | copy-start | bytes 3932164
  258.9 27.0 %copy-start.58 = (bf16[1024,640]{0,1:T(8,128)(2,1)}, bf16[1024,640]{0,1:T(8,128)(2,1)S(1)}, u32[]{:S(2)}) copy-start(bf16[1024,640]{0,1:T(8,128)(2,1)S(1)} %get-tuple-element.62) | copy-start | bytes 3932164
  265.1 20.3 %collective-permute-start.21 = (bf16[256,2048]{1,0:T(8,128)(2,1)S(1)}, bf16[256,2048]{1,0:T(8,128)(2,1)S(1)}, u32[]{:S(2)}, u32[]{:S(2)}) collective-permute-start(bf16[256,2048]{1,0:T(8,128)(2,1)S(1)} %pad_maximum_fusion.16), channel_id=1, source_target_pairs={{0,2},{1,3},{2,0},{3,1},{4,6},{5,7},{6,4},{7,5},{8,10},{9,11},{10,... | collective-permute-start | bytes 3145736 | tf_op jit(solution)/shard_map/ppermute | solution.py:26
  265.7 20.2 %copy-start.81 = (bf16[1024,2048]{1,0:T(8,128)(2,1)S(1)}, bf16[1024,2048]{1,0:T(8,128)(2,1)}, u32[]{:S(2)}) copy-start(bf16[1024,2048]{1,0:T(8,128)(2,1)} %copy-done.79) | copy-start | bytes 12582916
  265.7 20.2 %collective-permute-start.20 = (bf16[256,2048]{1,0:T(8,128)(2,1)S(1)}, bf16[256,2048]{1,0:T(8,128)(2,1)S(1)}, u32[]{:S(2)}, u32[]{:S(2)}) collective-permute-start(bf16[256,2048]{1,0:T(8,128)(2,1)S(1)} %pad_maximum_fusion.15), channel_id=1, source_target_pairs={{0,1},{1,0},{2,3},{3,2},{4,5},{5,4},{6,7},{7,6},{8,9},{9,8},{10,11... | collective-permute-start | bytes 3145736 | tf_op jit(solution)/shard_map/ppermute | solution.py:26
  305.9 188.8 %reduce-scatter.8.cloned.1.call-start = ((), (), s32[]{:S(2)}) async-start(), calls=%async_computation.8 | async-start | bytes 5013504 | tf_op jit(solution)/shard_map/reduce_scatter | solution.py:80
  308.7 8.9 %slice-start.3 = ((s8[7864320]{0:T(1024)(128)(4,1)}), s8[4194304]{0:T(1024)(128)(4,1)S(1)}, s32[]{:S(2)}) async-start(s8[7864320]{0:T(1024)(128)(4,1)} %bitcast.98), calls=%async_computation.12 | async-start | bytes 8388608
  310.6 9.2 %collective-permute-start.22 = (bf16[128,2048]{1,0:T(8,128)(2,1)S(1)}, bf16[128,2048]{1,0:T(8,128)(2,1)S(1)}, u32[]{:S(2)}, u32[]{:S(2)}) collective-permute-start(bf16[128,2048]{1,0:T(8,128)(2,1)S(1)} %get-tuple-element.125), channel_id=1, source_target_pairs={{0,2},{1,3},{2,0},{3,1},{4,6},{5,7},{6,4},{7,5},{8,10},{9,11},{10,... | collective-permute-start | bytes 1572872 | tf_op jit(solution)/shard_map/ppermute | solution.py:26
  312.1 9.2 %collective-permute-start.23 = (bf16[128,2048]{1,0:T(8,128)(2,1)S(1)}, bf16[128,2048]{1,0:T(8,128)(2,1)S(1)}, u32[]{:S(2)}, u32[]{:S(2)}) collective-permute-start(bf16[128,2048]{1,0:T(8,128)(2,1)S(1)} %get-tuple-element.126), channel_id=1, source_target_pairs={{0,1},{1,0},{2,3},{3,2},{4,5},{5,4},{6,7},{7,6},{8,9},{9,8},{10,11... | collective-permute-start | bytes 1572872 | tf_op jit(solution)/shard_map/ppermute | solution.py:26
  325.8 20.6 %collective-permute-start.25 = (bf16[256,2048]{1,0:T(8,128)(2,1)}, bf16[256,2048]{1,0:T(8,128)(2,1)S(1)}, u32[]{:S(2)}, u32[]{:S(2)}) collective-permute-start(bf16[256,2048]{1,0:T(8,128)(2,1)} %get-tuple-element.103), channel_id=1, source_target_pairs={{0,2},{1,3},{2,0},{3,1},{4,6},{5,7},{6,4},{7,5},{8,10},{9,11},{10,... | collective-permute-start | bytes 3145736 | tf_op jit(solution)/shard_map/ppermute | solution.py:26
  326.5 23.7 %collective-permute-start.24 = (bf16[256,2048]{1,0:T(8,128)(2,1)}, bf16[256,2048]{1,0:T(8,128)(2,1)}, u32[]{:S(2)}, u32[]{:S(2)}) collective-permute-start(bf16[256,2048]{1,0:T(8,128)(2,1)} %get-tuple-element.103), channel_id=1, source_target_pairs={{0,1},{1,0},{2,3},{3,2},{4,5},{5,4},{6,7},{7,6},{8,9},{9,8},{10,11... | collective-permute-start | bytes 3145736 | tf_op jit(solution)/shard_map/ppermute | solution.py:26
  327.6 25.2 %copy-start.59 = (bf16[1024,640]{0,1:T(8,128)(2,1)S(1)}, bf16[1024,640]{0,1:T(8,128)(2,1)}, u32[]{:S(2)}) copy-start(bf16[1024,640]{0,1:T(8,128)(2,1)} %copy-done.58) | copy-start | bytes 3932164
  346.4 13.3 %collective-permute-start.26 = (bf16[128,2048]{1,0:T(8,128)(2,1)S(1)}, bf16[128,2048]{1,0:T(8,128)(2,1)S(1)}, u32[]{:S(2)}, u32[]{:S(2)}) collective-permute-start(bf16[128,2048]{1,0:T(8,128)(2,1)S(1)} %slice.630), channel_id=1, source_target_pairs={{0,1},{1,0},{2,3},{3,2},{4,5},{5,4},{6,7},{7,6},{8,9},{9,8},{10,11... | collective-permute-start | bytes 1572872 | tf_op jit(solution)/shard_map/ppermute | solution.py:26
  351.2 14.9 %collective-permute-start.27 = (bf16[128,2048]{1,0:T(8,128)(2,1)S(1)}, bf16[128,2048]{1,0:T(8,128)(2,1)S(1)}, u32[]{:S(2)}, u32[]{:S(2)}) collective-permute-start(bf16[128,2048]{1,0:T(8,128)(2,1)S(1)} %slice.631), channel_id=1, source_target_pairs={{0,2},{1,3},{2,0},{3,1},{4,6},{5,7},{6,4},{7,5},{8,10},{9,11},{10,... | collective-permute-start | bytes 1572872 | tf_op jit(solution)/shard_map/ppermute | solution.py:26
  357.5 8.8 %copy-start.43 = (bf16[768,2048]{1,0:T(8,128)(2,1)}, bf16[768,2048]{1,0:T(8,128)(2,1)S(1)}, u32[]{:S(2)}) copy-start(bf16[768,2048]{1,0:T(8,128)(2,1)S(1)} %add_convert_fusion) | copy-start | bytes 9437188
  367.4 31.0 %collective-permute-start.29 = (bf16[256,2048]{1,0:T(8,128)(2,1)}, bf16[256,2048]{1,0:T(8,128)(2,1)S(1)}, u32[]{:S(2)}, u32[]{:S(2)}) collective-permute-start(bf16[256,2048]{1,0:T(8,128)(2,1)} %pad_maximum_fusion.18), channel_id=1, source_target_pairs={{0,2},{1,3},{2,0},{3,1},{4,6},{5,7},{6,4},{7,5},{8,10},{9,11},{10,... | collective-permute-start | bytes 3145736 | tf_op jit(solution)/shard_map/ppermute | solution.py:26
  369.9 28.5 %collective-permute-start.28 = (bf16[256,2048]{1,0:T(8,128)(2,1)}, bf16[256,2048]{1,0:T(8,128)(2,1)}, u32[]{:S(2)}, u32[]{:S(2)}) collective-permute-start(bf16[256,2048]{1,0:T(8,128)(2,1)} %pad_maximum_fusion.17), channel_id=1, source_target_pairs={{0,1},{1,0},{2,3},{3,2},{4,5},{5,4},{6,7},{7,6},{8,9},{9,8},{10,11... | collective-permute-start | bytes 3145736 | tf_op jit(solution)/shard_map/ppermute | solution.py:26
  403.8 13.1 %collective-permute-start.32 = (bf16[512,256]{1,0:T(8,128)(2,1)S(1)}, bf16[512,256]{1,0:T(8,128)(2,1)S(1)}, u32[]{:S(2)}, u32[]{:S(2)}) collective-permute-start(bf16[512,256]{1,0:T(8,128)(2,1)S(1)} %pad_maximum_fusion.34), channel_id=1, source_target_pairs={{0,2},{1,3},{2,0},{3,1},{4,6},{5,7},{6,4},{7,5},{8,10},{9,11},{10,... | collective-permute-start | bytes 786440 | tf_op jit(solution)/shard_map/ppermute | solution.py:26
  403.9 11.4 %collective-permute-start.30 = (bf16[512,256]{1,0:T(8,128)(2,1)S(1)}, bf16[512,256]{1,0:T(8,128)(2,1)S(1)}, u32[]{:S(2)}, u32[]{:S(2)}) collective-permute-start(bf16[512,256]{1,0:T(8,128)(2,1)S(1)} %pad_maximum_fusion.33), channel_id=1, source_target_pairs={{0,1},{1,0},{2,3},{3,2},{4,5},{5,4},{6,7},{7,6},{8,9},{9,8},{10,11... | collective-permute-start | bytes 786440 | tf_op jit(solution)/shard_map/ppermute | solution.py:26
  415.4 5.0 collective-permute-start.31
  417.0 5.0 collective-permute-start.33
  438.1 13.4 %collective-permute-start.34 = (bf16[128,2048]{1,0:T(8,128)(2,1)}, bf16[128,2048]{1,0:T(8,128)(2,1)}, u32[]{:S(2)}, u32[]{:S(2)}) collective-permute-start(bf16[128,2048]{1,0:T(8,128)(2,1)} %get-tuple-element.119), channel_id=1, source_target_pairs={{0,2},{1,3},{2,0},{3,1},{4,6},{5,7},{6,4},{7,5},{8,10},{9,11},{10,... | collective-permute-start | bytes 1572872 | tf_op jit(solution)/shard_map/ppermute | solution.py:26
  438.7 12.8 %collective-permute-start.35 = (bf16[128,2048]{1,0:T(8,128)(2,1)}, bf16[128,2048]{1,0:T(8,128)(2,1)}, u32[]{:S(2)}, u32[]{:S(2)}) collective-permute-start(bf16[128,2048]{1,0:T(8,128)(2,1)} %get-tuple-element.120), channel_id=1, source_target_pairs={{0,1},{1,0},{2,3},{3,2},{4,5},{5,4},{6,7},{7,6},{8,9},{9,8},{10,11... | collective-permute-start | bytes 1572872 | tf_op jit(solution)/shard_map/ppermute | solution.py:26
  442.7 20.1 %collective-permute-start.38 = (bf16[256,2048]{1,0:T(8,128)(2,1)S(1)}, bf16[256,2048]{1,0:T(8,128)(2,1)S(1)}, u32[]{:S(2)}, u32[]{:S(2)}) collective-permute-start(bf16[256,2048]{1,0:T(8,128)(2,1)S(1)} %pad_maximum_fusion.20), channel_id=1, source_target_pairs={{0,2},{1,3},{2,0},{3,1},{4,6},{5,7},{6,4},{7,5},{8,10},{9,11},{10,... | collective-permute-start | bytes 3145736 | tf_op jit(solution)/shard_map/ppermute | solution.py:26
  444.8 19.1 %collective-permute-start.36 = (bf16[256,2048]{1,0:T(8,128)(2,1)S(1)}, bf16[256,2048]{1,0:T(8,128)(2,1)S(1)}, u32[]{:S(2)}, u32[]{:S(2)}) collective-permute-start(bf16[256,2048]{1,0:T(8,128)(2,1)S(1)} %pad_maximum_fusion.19), channel_id=1, source_target_pairs={{0,1},{1,0},{2,3},{3,2},{4,5},{5,4},{6,7},{7,6},{8,9},{9,8},{10,11... | collective-permute-start | bytes 3145736 | tf_op jit(solution)/shard_map/ppermute | solution.py:26
  454.6 10.5 %copy-start.49 = (bf16[256,640]{0,1:T(8,128)(2,1)S(1)}, bf16[256,640]{0,1:T(8,128)(2,1)}, u32[]{:S(2)}) copy-start(bf16[256,640]{0,1:T(8,128)(2,1)} %copy.55) | copy-start | bytes 983044
  454.6 10.5 %copy-start.51 = (bf16[256,640]{0,1:T(8,128)(2,1)S(1)}, bf16[256,640]{0,1:T(8,128)(2,1)}, u32[]{:S(2)}) copy-start(bf16[256,640]{0,1:T(8,128)(2,1)} %copy.56) | copy-start | bytes 983044
  454.6 10.5 %copy-start.91 = (f32[256]{0:T(256)S(1)}, f32[256]{0:T(256)}, u32[]{:S(2)}) copy-start(f32[256]{0:T(256)} %copy-done.90) | copy-start | bytes 3076
  475.1 11.6 %collective-permute-start.37 = (bf16[128,2048]{1,0:T(8,128)(2,1)}, bf16[128,2048]{1,0:T(8,128)(2,1)}, u32[]{:S(2)}, u32[]{:S(2)}) collective-permute-start(bf16[128,2048]{1,0:T(8,128)(2,1)} %get-tuple-element.113), channel_id=1, source_target_pairs={{0,2},{1,3},{2,0},{3,1},{4,6},{5,7},{6,4},{7,5},{8,10},{9,11},{10,... | collective-permute-start | bytes 1572872 | tf_op jit(solution)/shard_map/ppermute | solution.py:26
  476.3 11.6 %collective-permute-start.39 = (bf16[128,2048]{1,0:T(8,128)(2,1)}, bf16[128,2048]{1,0:T(8,128)(2,1)}, u32[]{:S(2)}, u32[]{:S(2)}) collective-permute-start(bf16[128,2048]{1,0:T(8,128)(2,1)} %get-tuple-element.114), channel_id=1, source_target_pairs={{0,1},{1,0},{2,3},{3,2},{4,5},{5,4},{6,7},{7,6},{8,9},{9,8},{10,11... | collective-permute-start | bytes 1572872 | tf_op jit(solution)/shard_map/ppermute | solution.py:26
  498.3 4.6 collective-permute-start.41
  499.2 4.6 collective-permute-start.40
  500.1 5.5 %collective-permute-start.42 = (f32[64,265]{1,0:T(8,128)S(1)}, f32[64,265]{1,0:T(8,128)S(1)}, u32[]{:S(2)}, u32[]{:S(2)}) collective-permute-start(f32[64,265]{1,0:T(8,128)S(1)} %pad_maximum_fusion.36), channel_id=1, source_target_pairs={{0,3},{1,2},{2,1},{3,0},{4,7},{5,6},{6,5},{7,4},{8,11},{9,10},{10,... | collective-permute-start | bytes 203528 | tf_op jit(solution)/shard_map/ppermute | solution.py:26
  (93 other events, 348.0 us)
Sparse Core Ops, SparseCore 0:
  15.9 48.3 all-gather.3
  66.5 89.9 all-gather.5
  158.6 76.3 all-gather.7
  237.2 97.6 reduce-scatter.3
  337.0 83.0 reduce-scatter.5
  425.8 49.8 reduce-scatter.7

commit v8 on v7

--- a/solution.py
+++ b/solution.py
@@ -58,17 +58,20 @@
 
 
 def finish_sums(own, rest, arrived):
-    arrived = [block.astype(f32) for block in arrived]
     if lax.axis_size("tensor") != 4:
-        return own + sum(arrived)
+        return own + sum(block.astype(f32) for block in arrived)
     rows = own.shape[0]
     half = rows // 2
     one, two = rows_of(rest, 0, rows), rows_of(rest, 1, rows)
     upper, lower = arrived
-    upper_far = hop((two[:half].astype(f32) + upper[half:]).astype(bf16), 2).astype(f32)
-    lower_near = hop((one[half:].astype(f32) + lower[half:]).astype(bf16), 1).astype(f32)
+    upper_far = hop((two[:half].astype(f32) + upper[half:].astype(f32)).astype(bf16), 2)
+    lower_near = hop((one[half:].astype(f32) + lower[half:].astype(f32)).astype(bf16), 1)
     return jnp.concatenate(
-        [own[:half] + upper[:half] + upper_far, own[half:] + lower[:half] + lower_near], axis=0
+        [
+            own[:half] + upper[:half].astype(f32) + upper_far.astype(f32),
+            own[half:] + lower[:half].astype(f32) + lower_near.astype(f32),
+        ],
+        axis=0,
     )
 
 
@@ -77,7 +80,7 @@
 
 
 def scatter_dp(partial):
-    return lax.psum_scatter(partial, "dp", scatter_dimension=0, tiled=True).astype(f32)
+    return lax.psum_scatter(partial, "dp", scatter_dimension=0, tiled=True)
 
 
 pick = functools.partial(lax.dynamic_index_in_dim, keepdims=False)
@@ -268,6 +271,53 @@
     )(where, qr, kvt, dmixed, lse, cos2, sin2, shared)
 
 
+def finish_kernel(first_ref, second_ref, gate_ref, up_ref, gain_ref, *out_refs):
+    gate_out, up_out, down_out, part_out = out_refs
+    gain, part, start = gain_ref[...], 0.0, 0
+    for sum_ref in (first_ref, second_ref):
+        width = sum_ref.shape[1] // 3
+        here = slice(start, start + width)
+        gate = sum_ref[:, :width].astype(f32)
+        up = sum_ref[:, width : 2 * width].astype(f32)
+        terms = gate_ref[:, here].astype(f32) * gate + up_ref[:, here].astype(f32) * up
+        part = part + jnp.sum(terms, axis=1, keepdims=True)
+        gate_out[:, here] = gate * gain
+        up_out[:, here] = up * gain
+        down_out[here, :] = sum_ref[:, 2 * width :].astype(f32).T
+        start += width
+    part_out[...] = part
+
+
+def finish_ff(parts, sums, gate_own, up_own, gain):
+    rows, ff = gate_own.shape
+    widths = [b - a for a, b in parts]
+    if rows % HD or any(width % HD for width in widths):
+        sums = [total.astype(f32) for total in sums]
+        gate = jnp.concatenate([t[:, :w] for t, w in zip(sums, widths)], axis=1)
+        up = jnp.concatenate([t[:, w : 2 * w] for t, w in zip(sums, widths)], axis=1)
+        down = jnp.concatenate([t[:, 2 * w :] for t, w in zip(sums, widths)], axis=1)
+        terms = gate * gate_own.astype(f32) + up * up_own.astype(f32)
+        return gate * gain, up * gain, down.T, jnp.sum(terms, axis=1, keepdims=True)
+    across = lambda width: pl.BlockSpec((HD, width), lambda i: (i, 0))
+    return pl.pallas_call(
+        finish_kernel,
+        name="finish_ff",
+        grid=(rows // HD,),
+        in_specs=[across(3 * w) for w in widths] + [across(ff), across(ff), across(1)],
+        out_specs=[across(ff), across(ff), pl.BlockSpec((ff, HD), lambda i: (0, i)), across(1)],
+        out_shape=(
+            jax.ShapeDtypeStruct((rows, ff), f32),
+            jax.ShapeDtypeStruct((rows, ff), f32),
+            jax.ShapeDtypeStruct((ff, rows), f32),
+            jax.ShapeDtypeStruct((rows, 1), f32),
+        ),
+        compiler_params=pltpu.CompilerParams(dimension_semantics=("arbitrary",)),
+        cost_estimate=pl.CostEstimate(
+            flops=8 * rows * ff, bytes_accessed=24 * rows * ff, transcendentals=0
+        ),
+    )(*sums, gate_own, up_own, gain)
+
+
 def inverse_norm(values):
     return lax.rsqrt(jnp.mean(values * values, axis=-1, keepdims=True) + eps)
 
@@ -433,33 +483,19 @@
         ],
         axis=1,
     ).reshape(-1, heads_width)
-    attn_sum = scatter_dp(attn_partial)
-    down_sent = [after(block, *kv_sent) for block in down_sent]
+    attn_sum = scatter_dp(attn_partial).astype(f32)
+    down_sent = [after(block, *qkv_sent) for block in down_sent]
     own_down = sum(
         dot(after(h[:rows], attn_partial), w, 1, 1) for h, w in zip(hidden, downs)
     )
     after_mlp = after_attn + finish_sums(own_down, down_rest, down_sent)
     output = (after_mlp * own_mask).astype(bf16)
     scaled_one = finish_sums(dot(qkv_back[:rows], qkv_full, 1, 1), qkv_rest, qkv_sent)
-    inv_one = inverse_norm(residual)
-    unit_one = residual * inv_one
-    input_grad = attn_top + inv_one * (
-        scaled_one - unit_one * jnp.mean(scaled_one * unit_one, axis=-1, keepdims=True)
-    )
-
     query_sum, project_sum = attn_sum[:shard_rows], attn_sum[shard_rows : 2 * shard_rows]
     kv_sum = attn_sum[2 * shard_rows :].reshape(kv_rows, 2 * HD)
-    ff_sums = [after(total, *qkv_sent) for total in ff_sums]
-    pair_sums = [total[:, : own.shape[1]] for own, total in zip(pair_own, ff_sums)]
-    down_sum = jnp.concatenate(
-        [total[:, own.shape[1] :] for own, total in zip(pair_own, ff_sums)], axis=1
-    )
-    gain_two_part = sum(
-        jnp.sum(own * total, axis=1, keepdims=True) for own, total in zip(pair_own, pair_sums)
-    )
-    scaled_sums = [total * gain_two for total in pair_sums]
-    grad_gate = jnp.concatenate([s[:, : b - a] for (a, b), s in zip(parts, scaled_sums)], axis=1)
-    grad_up = jnp.concatenate([s[:, b - a :] for (a, b), s in zip(parts, scaled_sums)], axis=1)
+    grad_gate, grad_up, grad_down, gain_two_part = finish_ff(
+        parts, ff_sums, w_gate, w_up, gain_two
+    )
     query_part = jnp.sum(qkv_own[:, :heads_width] * query_sum, axis=1, keepdims=True)
     kv_here = lax.dynamic_slice_in_dim(qkv_own[:, heads_width:], rank * kv_rows, kv_rows)
     gain_here = lax.dynamic_slice_in_dim(gain_one, rank * kv_rows, kv_rows)
@@ -470,6 +506,12 @@
             jnp.concatenate([query_part, gain_two_part], axis=1).reshape(kv_rows, -1),
         ],
         axis=1,
+    )
+    scaled_one = after(scaled_one, small)
+    inv_one = inverse_norm(residual)
+    unit_one = residual * inv_one
+    input_grad = attn_top + inv_one * (
+        scaled_one - unit_one * jnp.mean(scaled_one * unit_one, axis=-1, keepdims=True)
     )
     blocks = jnp.stack([small] + [hop(small, j) for j in range(1, ranks)], axis=0)
     sums = jnp.sum(blocks[:, :, 2 * HD + 1 :], axis=0).reshape(shard_rows, 2)
@@ -482,7 +524,7 @@
         project_sum.T,
         grad_gate,
         grad_up,
-        down_sum.T,
+        grad_down,
         sums[:, 0] + placed[:, 2 * HD],
         sums[:, 1],
     )

time: 521 us -> 513 us (0.985)
  local copies, waits for them, and re-layouts: 60.2 us -> 48.7 us
  matrix products: 122 us -> 132 us
  other arithmetic: 94.4 us -> 85.3 us
    unnamed x226 -> x162, local copies, waits for them, and re-layouts: 36.3 us -> 23.4 us
    dot_general x25, matrix products: 122 us -> 132 us  [dot(): lax.dot_general(a, b, (((ca,), (cb,)), ((), ())), preferred_element_type=...]
    convert_element_type x19 -> x7, other arithmetic: 17.9 us -> 8.66 us  [the longest x5 7.34 us: finish_sums(): (two[:half].astype(f32) + upper[half:].astype(f32)).astype(bf16)]
    concatenate x2, other arithmetic: 19.6 us -> 11.7 us  [partial(): jnp.concatenate([dot(normed_two, grads, 0, 0).astype(bf16), dot(top_all,...]
  transfers between devices with their start and end apart: 49 -> 49, of which waited for: 30 -> 27; matrix products, arithmetic and copies ran while one was open for 50% -> 49% of each run, Pallas kernels for 5% -> 6%
where the time goes in v8:
time: 513 us; the launch traced here: 504 us
  waiting for transfers between devices  133 us (26%)
  matrix products  132 us (26%)
  other arithmetic  85.3 us (17%)
  starting transfers between devices  50.6 us (10%)
  local copies, waits for them, and re-layouts  48.7 us (9%)
  Pallas kernels  29.2 us (6%)
  between operations  24.5 us (5%)
    dot_general x25, matrix products, dot(): lax.dot_general(a, b, (((ca,), (cb,)), ((), ())), preferred_element_type=...  132 us
    ppermute x43, waiting for transfers between devices, hop(): return lax.ppermute(value, 'tensor', [(i, i ^ step) for i in range(size)])  121 us
    ppermute x43, starting transfers between devices, hop(): return lax.ppermute(value, 'tensor', [(i, i ^ step) for i in range(size)])  49.2 us
    unnamed x162, local copies, waits for them, and re-layouts  23.4 us
    pallas_call x1, Pallas kernels, attend_back(): pl.pallas_call(attend_back_kernel, name='attend_back', grid_spec=pltpu.Pr...  13.7 us
    all_gather x3, waiting for transfers between devices, gather_dp(): return lax.all_gather(shard, 'dp', axis=0, tiled=True)  12.1 us
    concatenate x2, other arithmetic, partial(): jnp.concatenate([dot(normed_two, grads, 0, 0).astype(bf16), dot(top_all,...  11.7 us
    pallas_call x1, Pallas kernels, attend(): pl.pallas_call(attend_kernel, name='attend', grid_spec=pltpu.PrefetchScal...  11.4 us
  transfers between devices with their start and end apart: 49, of which 27 were waited for; matrix products, arithmetic and copies ran while one was open for 49% of the time, Pallas kernels for 6%

profile of v8, /device:TPU:0, one launch (start us, length us, event | category | flops | bytes accessed | tf_op | source)
XLA Modules:
  0.0 503.6 jit_solution(2165373217446121807)
XLA Ops:
  7.2 3.1 collective-permute-start.1
  22.0 3.1 fusion.81
  29.0 2.1 pad_maximum_fusion.9
  40.0 2.4 fusion.53
  43.6 4.7 collective-permute-done.2
  52.1 12.1 %all-gather.4.cloned.1.call-done = bf16[4352,512]{1,0:T(8,128)(2,1)} async-done(((bf16[544,512]{1,0:T(8,128)(2,1)}), bf16[4352,512]{1,0:T(8,128)(2,1)}) %all-gather.4.cloned.1.call-update) | async-done | bytes 4456464 | tf_op jit(solution)/shard_map/all_gather | solution.py:79
  78.2 3.8 collective-permute-done.6
  88.2 7.4 %fusion.65.q_ref.kv_ref = f32[1024,768]{1,0:T(8,128)} fusion(bf16[1024,2048]{1,0:T(8,128)(2,1)} %fusion.68, bf16[2048,256]{1,0:T(8,128)(2,1)S(1)} %bitcast.115, bf16[2048,512]{1,0:T(8,128)(2,1)S(1)} %bitcast.110), kind=kOutput, calls=%fused_computation.140 | convolution fusion | flops 3227516928 | bytes 10485760 | tf_op jit(solution)/shard_map/dot_general | solution.py:21
  95.6 11.4 %attend.1 = (bf16[1024,512]{1,0:T(8,128)(2,1)S(1)}, bf16[1024,256]{1,0:T(8,128)(2,1)S(1)}, bf16[1024,512]{1,0:T(8,128)(2,1)S(1)}, f32[1024,128]{1,0:T(8,128)S(1)}) custom-call(s32[2]{0:T(128)S(1)} %pad_add_fusion.where_ref, f32[1024,768]{1,0:T(8,128)} %fusion.65.q_ref.kv_ref, f32[1024,768]{1,0:T(8,128)} %fusion.65.q_ref.kv_ref, ...), custom_call_target="tpu_custom_call" | custom-call | flops 2147483648 | bytes 8388608 | tf_op jit(solution)/shard_map/attend/pallas_call | solution.py:202
  110.0 3.7 convolution_convert_fusion.2
  117.0 20.2 %collective-permute-done.12 = bf16[256,2048]{1,0:T(8,128)(2,1)S(1)} collective-permute-done((bf16[256,2048]{1,0:T(8,128)(2,1)S(1)}, bf16[256,2048]{1,0:T(8,128)(2,1)S(1)}, u32[]{:S(2)}, u32[]{:S(2)}) %collective-permute-start.12) | collective-permute-done | bytes 1048608 | tf_op jit(solution)/shard_map/ppermute | solution.py:26
  149.3 4.6 collective-permute-done.11
  155.4 6.2 %collective-permute-done.14 = bf16[128,2048]{1,0:T(8,128)(2,1)S(1)} collective-permute-done((bf16[128,2048]{1,0:T(8,128)(2,1)S(1)}, bf16[128,2048]{1,0:T(8,128)(2,1)S(1)}, u32[]{:S(2)}, u32[]{:S(2)}) %collective-permute-start.14) | collective-permute-done | bytes 524320 | tf_op jit(solution)/shard_map/ppermute | solution.py:26
  166.1 6.3 %fusion.27 = f32[1024,768]{0,1:T(8,128)S(1)} fusion(bf16[1024,2048]{1,0:T(8,128)(2,1)} %copy-done.53, bf16[2048,2304]{1,0:T(8,128)(2,1)} %all-gather.6.cloned.1.call-done), kind=kOutput, calls=%fused_computation.59 | convolution fusion | flops 3221225472 | bytes 10485760 | tf_op jit(solution)/shard_map/dot_general | solution.py:21
  172.4 12.9 %collective-permute-done.17 = bf16[256,2048]{1,0:T(8,128)(2,1)} collective-permute-done((bf16[256,2048]{1,0:T(8,128)(2,1)}, bf16[256,2048]{1,0:T(8,128)(2,1)}, u32[]{:S(2)}, u32[]{:S(2)}) %collective-permute-start.17) | collective-permute-done | bytes 1048608 | tf_op jit(solution)/shard_map/ppermute | solution.py:26
  193.8 3.8 collective-permute-done.18
  199.0 10.4 %fusion.4 = f32[1024,1536]{0,1:T(8,128)S(1)} fusion(bf16[1024,2048]{1,0:T(8,128)(2,1)S(1)} %constant_dynamic-update-slice_fusion.10, bf16[2048,2304]{1,0:T(8,128)(2,1)} %all-gather.6.cloned.1.call-done), kind=kOutput, calls=%fused_computation.10 | convolution fusion | flops 6442450944 | bytes 16777216 | tf_op jit(solution)/shard_map/dot_general | solution.py:21
  209.4 2.1 multiply_convert_fusion.1
  211.6 3.8 convolution_convert_fusion.4
  215.4 8.6 %convolution_convert_fusion.1 = bf16[2048,1536]{1,0:T(8,128)(2,1)S(1)} fusion(bf16[1024,2048]{1,0:T(8,128)(2,1)S(1)} %constant_dynamic-update-slice_fusion.10, bf16[1024,768]{0,1:T(8,128)(2,1)S(1)} %get-tuple-element.122, bf16[1024,768]{0,1:T(8,128)(2,1)S(1)} %get-tuple-element.121), kind=kOutput, calls=%fused_computation.3 | convolution fusion | flops 6451888128 | bytes 13631488 | tf_op jit(solution)/shard_map/dot_general | solution.py:21
  224.0 4.6 pad_maximum_fusion
  230.7 9.9 %fusion.2 = f32[768,2048]{1,0:T(8,128)} fusion(bf16[768,1536]{0,1:T(8,128)(2,1)S(1)} %pad_maximum_fusion.5, bf16[2048,2304]{1,0:T(8,128)(2,1)} %all-gather.6.cloned.1.call-done), kind=kOutput, calls=%fused_computation.8 | convolution fusion | flops 4831838208 | bytes 14942208 | tf_op jit(solution)/shard_map/dot_general | solution.py:21
  240.6 6.1 %fusion.43 = f32[1024,640]{0,1:T(8,128)S(1)} fusion(bf16[1024,2048]{1,0:T(8,128)(2,1)} %copy-done.53, bf16[2048,1920]{1,0:T(8,128)(2,1)} %all-gather.8.cloned.1.call-done), kind=kOutput, calls=%fused_computation.83 | convolution fusion | flops 2684354560 | bytes 9437184 | tf_op jit(solution)/shard_map/dot_general | solution.py:21
  247.5 6.0 %fusion.10 = f32[1024,1280]{0,1:T(8,128)S(1)} fusion(bf16[1024,2048]{1,0:T(8,128)(2,1)S(1)} %copy-done.57, bf16[2048,1920]{1,0:T(8,128)(2,1)S(1)} %copy-done.27), kind=kOutput, calls=%fused_computation.17 | convolution fusion | flops 5368709120 | bytes 14680064 | tf_op jit(solution)/shard_map/dot_general | solution.py:21
  255.4 7.9 %add_convert_fusion.1 = bf16[768,2048]{1,0:T(8,128)(2,1)S(1)} fusion(f32[768,2048]{1,0:T(8,128)} %fusion.2, bf16[2048,1920]{1,0:T(8,128)(2,1)S(1)} %copy-done.27, bf16[1024,640]{0,1:T(8,128)(2,1)S(1)} %get-tuple-element.124, bf16[1024,640]{0,1:T(8,128)(2,1)S(1)} %get-tuple-element.123), kind=kOutput, calls=%fused_computation.5 | convolution fusion | flops 4033609728 | bytes 17301504 | tf_op jit(solution)/shard_map/dot_general | solution.py:21
  268.4 17.2 %collective-permute-done.20 = bf16[256,2048]{1,0:T(8,128)(2,1)S(1)} collective-permute-done((bf16[256,2048]{1,0:T(8,128)(2,1)S(1)}, bf16[256,2048]{1,0:T(8,128)(2,1)S(1)}, u32[]{:S(2)}, u32[]{:S(2)}) %collective-permute-start.20) | collective-permute-done | bytes 1048608 | tf_op jit(solution)/shard_map/ppermute | solution.py:26
  285.9 4.8 convolution_convert_fusion.5
  290.8 7.4 %convolution_convert_fusion = bf16[2048,1280]{1,0:T(8,128)(2,1)} fusion(bf16[1024,2048]{1,0:T(8,128)(2,1)S(1)} %copy-done.58, bf16[1024,1280]{0,1:T(8,128)(2,1)S(1)} %pad_maximum_fusion.3), kind=kOutput, calls=%fused_computation.2 | convolution fusion | flops 5371330560 | bytes 12058624 | tf_op jit(solution)/shard_map/dot_general | solution.py:21
  298.2 7.1 %pad_maximum_fusion.1 = bf16[2048,1920]{1,0:T(8,128)(2,1)} fusion(bf16[2048,640]{1,0:T(8,128)(2,1)} %convolution_convert_fusion.5, bf16[2048,1280]{1,0:T(8,128)(2,1)} %convolution_convert_fusion), kind=kLoop, calls=%fused_computation.1 | loop fusion | flops 15728640 | bytes 15728640 | tf_op jit(solution)/shard_map/concatenate | solution.py:434
  307.1 2.1 add_convert_fusion.7
  311.3 5.1 %fusion = f32[256,2048]{1,0:T(8,128)S(1)} fusion(bf16[256,1536]{0,1:T(8,128)(2,1)S(1)} %pad_maximum_fusion.23, bf16[2048,2304]{1,0:T(8,128)(2,1)} %all-gather.6.cloned.1.call-done), kind=kOutput, calls=%fused_computation.6 | convolution fusion | flops 1610612736 | bytes 9175040 | tf_op jit(solution)/shard_map/dot_general | solution.py:21
  321.8 2.8 constant_dynamic-update-slice_fusion.19
  327.9 5.0 fusion.25
  332.9 12.6 %collective-permute-done.25 = bf16[256,2048]{1,0:T(8,128)(2,1)S(1)} collective-permute-done((bf16[256,2048]{1,0:T(8,128)(2,1)}, bf16[256,2048]{1,0:T(8,128)(2,1)S(1)}, u32[]{:S(2)}, u32[]{:S(2)}) %collective-permute-start.25) | collective-permute-done | bytes 1048608 | tf_op jit(solution)/shard_map/ppermute | solution.py:26
  347.4 3.2 collective-permute-done.24
  351.8 5.0 add_convert_fusion
  356.8 2.1 constant_dynamic-update-slice_fusion.18
  359.0 6.1 %collective-permute-done.27 = bf16[128,2048]{1,0:T(8,128)(2,1)S(1)} collective-permute-done((bf16[128,2048]{1,0:T(8,128)(2,1)S(1)}, bf16[128,2048]{1,0:T(8,128)(2,1)S(1)}, u32[]{:S(2)}, u32[]{:S(2)}) %collective-permute-start.27) | collective-permute-done | bytes 524320 | tf_op jit(solution)/shard_map/ppermute | solution.py:26
  366.3 2.5 collective-permute-start.28
  371.9 3.7 convolution_convert_fusion.6
  375.6 5.4 %convolution_convert_fusion.9.dm_ref = bf16[1024,512]{1,0:T(8,128)(2,1)S(1)} fusion(bf16[1024,2048]{1,0:T(8,128)(2,1)} %copy-done.52, bf16[2048,512]{1,0:T(8,128)(2,1)} %bitcast.102), kind=kOutput, calls=%fused_computation.89 | convolution fusion | flops 2148007936 | bytes 7340032 | tf_op jit(solution)/shard_map/dot_general | solution.py:21
  381.0 13.7 %attend_back.1 = (bf16[1024,512]{1,0:T(8,128)(2,1)S(1)}, bf16[1024,256]{1,0:T(8,128)(2,1)S(1)}) custom-call(s32[2]{0:T(128)S(1)} %copy-done.3, bf16[1024,512]{1,0:T(8,128)(2,1)S(1)} %get-tuple-element.58.qr_ref, bf16[1024,256]{1,0:T(8,128)(2,1)S(1)} %copy-done.5, bf16[1024,512]{1,0:T(8,128)(2,1)S(1)} %convolution_convert_fusion.9.dm_ref, ...), custom_call_target="tpu_custom_call" | custom-call | flops 5368709120 | bytes 8388608 | tf_op jit(solution)/shard_map/attend_back/pallas_call | solution.py:240
  394.8 4.2 convolution_convert_fusion.8
  399.2 2.0 collective-permute-start.32
  401.3 4.0 convolution_convert_fusion.3
  405.4 6.0 %convolution_convert_fusion.7 = bf16[2048,512]{1,0:T(8,128)(2,1)} fusion(bf16[1024,2048]{1,0:T(8,128)(2,1)} %fusion.68, bf16[1024,512]{1,0:T(8,128)(2,1)S(1)} %slice-done), kind=kOutput, calls=%fused_computation.40 | convolution fusion | flops 2148532224 | bytes 7340032 | tf_op jit(solution)/shard_map/dot_general | solution.py:21
  411.5 2.0 collective-permute-start.33
  413.6 2.9 collective-permute-done.33
  416.6 2.0 collective-permute-done.31
  418.8 3.6 pad_maximum_fusion.2
  430.9 3.6 fusion.64
  434.5 3.0 fusion.23
  437.5 8.4 %collective-permute-done.34 = bf16[256,2048]{1,0:T(8,128)(2,1)} collective-permute-done((bf16[256,2048]{1,0:T(8,128)(2,1)}, bf16[256,2048]{1,0:T(8,128)(2,1)}, u32[]{:S(2)}, u32[]{:S(2)}) %collective-permute-start.34) | collective-permute-done | bytes 1048608 | tf_op jit(solution)/shard_map/ppermute | solution.py:26
  445.9 2.3 collective-permute-done.35
  448.1 2.7 add_convert_fusion.3
  452.9 2.8 convolution_add_fusion
  455.8 4.1 finish_ff.1
  460.9 2.1 add_convert_fusion.5
  469.4 2.9 collective-permute-done.36
  472.9 3.0 fusion.58
  478.2 2.2 slice_bitcast_fusion
  484.9 2.0 copy.69
  486.9 2.2 fusion.33
  489.1 4.5 fusion.36
  (380 shorter events, 133.9 us)
Async XLA Ops:
  7.2 8.6 %copy-start.34 = (bf16[256,1408]{1,0:T(8,128)(2,1)S(1)}, bf16[256,1408]{1,0:T(8,128)(2,1)}, u32[]{:S(2)}) copy-start(bf16[256,1408]{1,0:T(8,128)(2,1)} %gate_ref.1) | copy-start | bytes 2162692
  7.2 57.1 %all-gather.4.cloned.1.call-start = ((), (), s32[]{:S(2)}) async-start(), calls=%async_computation.3 | async-start | bytes 5013504 | tf_op jit(solution)/shard_map/all_gather | solution.py:79
  7.2 27.9 %collective-permute-start.1 = (bf16[256,2048]{1,0:T(8,128)(2,1)}, bf16[256,2048]{1,0:T(8,128)(2,1)S(1)}, u32[]{:S(2)}, u32[]{:S(2)}) collective-permute-start(bf16[256,2048]{1,0:T(8,128)(2,1)} %param.12), channel_id=1, source_target_pairs={{0,2},{1,3},{2,0},{3,1},{4,6},{5,7},{6,4},{7,5},{8,10},{9,11},{10,... | collective-permute-start | bytes 3145736 | tf_op jit(solution)/shard_map/ppermute | solution.py:26
  10.3 25.4 %collective-permute-start = (bf16[256,2048]{1,0:T(8,128)(2,1)}, bf16[256,2048]{1,0:T(8,128)(2,1)}, u32[]{:S(2)}, u32[]{:S(2)}) collective-permute-start(bf16[256,2048]{1,0:T(8,128)(2,1)} %param.12), channel_id=1, source_target_pairs={{0,1},{1,0},{2,3},{3,2},{4,5},{5,4},{6,7},{7,6},{8,9},{9,8},{10,11... | collective-permute-start | bytes 3145736 | tf_op jit(solution)/shard_map/ppermute | solution.py:26
  15.7 150.4 %all-gather.6.cloned.1.call-start = ((), (), s32[]{:S(2)}) async-start(), calls=%async_computation.4 | async-start | bytes 10616832 | tf_op jit(solution)/shard_map/all_gather | solution.py:79
  18.0 9.9 %copy-start.64 = (f32[256]{0:T(256)}, f32[256]{0:T(256)S(1)}, u32[]{:S(2)}) copy-start(f32[256]{0:T(256)S(1)} %convert_element_type.348) | copy-start | bytes 3076
  35.1 13.2 %collective-permute-start.2 = (bf16[128,2048]{1,0:T(8,128)(2,1)S(1)}, bf16[128,2048]{1,0:T(8,128)(2,1)S(1)}, u32[]{:S(2)}, u32[]{:S(2)}) collective-permute-start(bf16[128,2048]{1,0:T(8,128)(2,1)S(1)} %slice.551), channel_id=1, source_target_pairs={{0,1},{1,0},{2,3},{3,2},{4,5},{5,4},{6,7},{7,6},{8,9},{9,8},{10,11... | collective-permute-start | bytes 1572872 | tf_op jit(solution)/shard_map/ppermute | solution.py:26
  36.8 12.9 %collective-permute-start.3 = (bf16[128,2048]{1,0:T(8,128)(2,1)S(1)}, bf16[128,2048]{1,0:T(8,128)(2,1)S(1)}, u32[]{:S(2)}, u32[]{:S(2)}) collective-permute-start(bf16[128,2048]{1,0:T(8,128)(2,1)S(1)} %slice.552), channel_id=1, source_target_pairs={{0,2},{1,3},{2,0},{3,1},{4,6},{5,7},{6,4},{7,5},{8,10},{9,11},{10,... | collective-permute-start | bytes 1572872 | tf_op jit(solution)/shard_map/ppermute | solution.py:26
  51.9 188.7 %all-gather.8.cloned.1.call-start = ((), (), s32[]{:S(2)}) async-start(), calls=%async_computation.5 | async-start | bytes 8847360 | tf_op jit(solution)/shard_map/all_gather | solution.py:79
  65.3 11.5 %collective-permute-start.5 = (bf16[512,256]{1,0:T(8,128)(2,1)S(1)}, bf16[512,256]{1,0:T(8,128)(2,1)S(1)}, u32[]{:S(2)}, u32[]{:S(2)}) collective-permute-start(bf16[512,256]{1,0:T(8,128)(2,1)S(1)} %reshape.192), channel_id=1, source_target_pairs={{0,2},{1,3},{2,0},{3,1},{4,6},{5,7},{6,4},{7,5},{8,10},{9,11},{10,... | collective-permute-start | bytes 786440 | tf_op jit(solution)/shard_map/ppermute | solution.py:26
  66.9 10.6 %collective-permute-start.4 = (bf16[512,256]{1,0:T(8,128)(2,1)S(1)}, bf16[512,256]{1,0:T(8,128)(2,1)S(1)}, u32[]{:S(2)}, u32[]{:S(2)}) collective-permute-start(bf16[512,256]{1,0:T(8,128)(2,1)S(1)} %reshape.192), channel_id=1, source_target_pairs={{0,1},{1,0},{2,3},{3,2},{4,5},{5,4},{6,7},{7,6},{8,9},{9,8},{10,11... | collective-permute-start | bytes 786440 | tf_op jit(solution)/shard_map/ppermute | solution.py:26
  76.8 18.8 %copy-start.2 = (s32[2]{0:T(128)}, s32[2]{0:T(128)S(1)}, u32[]{:S(2)}) copy-start(s32[2]{0:T(128)S(1)} %pad_add_fusion.where_ref) | copy-start | bytes 28
  76.9 5.1 %collective-permute-start.6 = (bf16[256,256]{1,0:T(8,128)(2,1)S(1)}, bf16[256,256]{1,0:T(8,128)(2,1)S(1)}, u32[]{:S(2)}, u32[]{:S(2)}) collective-permute-start(bf16[256,256]{1,0:T(8,128)(2,1)S(1)} %slice.557), channel_id=1, source_target_pairs={{0,1},{1,0},{2,3},{3,2},{4,5},{5,4},{6,7},{7,6},{8,9},{9,8},{10,11... | collective-permute-start | bytes 393224 | tf_op jit(solution)/shard_map/ppermute | solution.py:26
  77.5 5.0 collective-permute-start.7
  82.8 27.2 %collective-permute-start.9 = (bf16[256,2048]{1,0:T(8,128)(2,1)}, bf16[256,2048]{1,0:T(8,128)(2,1)}, u32[]{:S(2)}, u32[]{:S(2)}) collective-permute-start(bf16[256,2048]{1,0:T(8,128)(2,1)} %fusion.40), channel_id=1, source_target_pairs={{0,2},{1,3},{2,0},{3,1},{4,6},{5,7},{6,4},{7,5},{8,10},{9,11},{10,... | collective-permute-start | bytes 3145736 | tf_op jit(solution)/shard_map/ppermute | solution.py:26
  83.4 26.6 %collective-permute-start.8 = (bf16[256,2048]{1,0:T(8,128)(2,1)}, bf16[256,2048]{1,0:T(8,128)(2,1)}, u32[]{:S(2)}, u32[]{:S(2)}) collective-permute-start(bf16[256,2048]{1,0:T(8,128)(2,1)} %fusion.40), channel_id=1, source_target_pairs={{0,1},{1,0},{2,3},{3,2},{4,5},{5,4},{6,7},{7,6},{8,9},{9,8},{10,11... | collective-permute-start | bytes 3145736 | tf_op jit(solution)/shard_map/ppermute | solution.py:26
  109.6 266.1 %reduce-scatter.4.cloned.1.call-start = ((), (), s32[]{:S(2)}) async-start(), calls=%async_computation.6 | async-start | bytes 10616832 | tf_op jit(solution)/shard_map/reduce_scatter | solution.py:83
  114.0 23.3 %collective-permute-start.12 = (bf16[256,2048]{1,0:T(8,128)(2,1)S(1)}, bf16[256,2048]{1,0:T(8,128)(2,1)S(1)}, u32[]{:S(2)}, u32[]{:S(2)}) collective-permute-start(bf16[256,2048]{1,0:T(8,128)(2,1)S(1)} %pad_maximum_fusion.12), channel_id=1, source_target_pairs={{0,2},{1,3},{2,0},{3,1},{4,6},{5,7},{6,4},{7,5},{8,10},{9,11},{10,... | collective-permute-start | bytes 3145736 | tf_op jit(solution)/shard_map/ppermute | solution.py:26
  115.7 23.0 %collective-permute-start.10 = (bf16[256,2048]{1,0:T(8,128)(2,1)S(1)}, bf16[256,2048]{1,0:T(8,128)(2,1)S(1)}, u32[]{:S(2)}, u32[]{:S(2)}) collective-permute-start(bf16[256,2048]{1,0:T(8,128)(2,1)S(1)} %pad_maximum_fusion.11), channel_id=1, source_target_pairs={{0,1},{1,0},{2,3},{3,2},{4,5},{5,4},{6,7},{7,6},{8,9},{9,8},{10,11... | collective-permute-start | bytes 3145736 | tf_op jit(solution)/shard_map/ppermute | solution.py:26
  139.0 14.9 %collective-permute-start.11 = (bf16[128,2048]{1,0:T(8,128)(2,1)S(1)}, bf16[128,2048]{1,0:T(8,128)(2,1)S(1)}, u32[]{:S(2)}, u32[]{:S(2)}) collective-permute-start(bf16[128,2048]{1,0:T(8,128)(2,1)S(1)} %get-tuple-element.147), channel_id=1, source_target_pairs={{0,2},{1,3},{2,0},{3,1},{4,6},{5,7},{6,4},{7,5},{8,10},{9,11},{10,... | collective-permute-start | bytes 1572872 | tf_op jit(solution)/shard_map/ppermute | solution.py:26
  139.7 14.8 %collective-permute-start.13 = (bf16[128,2048]{1,0:T(8,128)(2,1)S(1)}, bf16[128,2048]{1,0:T(8,128)(2,1)S(1)}, u32[]{:S(2)}, u32[]{:S(2)}) collective-permute-start(bf16[128,2048]{1,0:T(8,128)(2,1)S(1)} %get-tuple-element.148), channel_id=1, source_target_pairs={{0,1},{1,0},{2,3},{3,2},{4,5},{5,4},{6,7},{7,6},{8,9},{9,8},{10,11... | collective-permute-start | bytes 1572872 | tf_op jit(solution)/shard_map/ppermute | solution.py:26
  143.7 17.8 %collective-permute-start.14 = (bf16[128,2048]{1,0:T(8,128)(2,1)S(1)}, bf16[128,2048]{1,0:T(8,128)(2,1)S(1)}, u32[]{:S(2)}, u32[]{:S(2)}) collective-permute-start(bf16[128,2048]{1,0:T(8,128)(2,1)S(1)} %slice.455), channel_id=1, source_target_pairs={{0,1},{1,0},{2,3},{3,2},{4,5},{5,4},{6,7},{7,6},{8,9},{9,8},{10,11... | collective-permute-start | bytes 1572872 | tf_op jit(solution)/shard_map/ppermute | solution.py:26
  145.3 16.3 %collective-permute-start.15 = (bf16[128,2048]{1,0:T(8,128)(2,1)S(1)}, bf16[128,2048]{1,0:T(8,128)(2,1)S(1)}, u32[]{:S(2)}, u32[]{:S(2)}) collective-permute-start(bf16[128,2048]{1,0:T(8,128)(2,1)S(1)} %slice.456), channel_id=1, source_target_pairs={{0,2},{1,3},{2,0},{3,1},{4,6},{5,7},{6,4},{7,5},{8,10},{9,11},{10,... | collective-permute-start | bytes 1572872 | tf_op jit(solution)/shard_map/ppermute | solution.py:26
  164.0 21.3 %collective-permute-start.17 = (bf16[256,2048]{1,0:T(8,128)(2,1)}, bf16[256,2048]{1,0:T(8,128)(2,1)}, u32[]{:S(2)}, u32[]{:S(2)}) collective-permute-start(bf16[256,2048]{1,0:T(8,128)(2,1)} %multiply_convert_fusion.6), channel_id=1, source_target_pairs={{0,2},{1,3},{2,0},{3,1},{4,6},{5,7},{6,4},{7,5},{8,10},{9,11},{10,... | collective-permute-start | bytes 3145736 | tf_op jit(solution)/shard_map/ppermute | solution.py:26
  165.4 23.2 %collective-permute-start.16 = (bf16[256,2048]{1,0:T(8,128)(2,1)}, bf16[256,2048]{1,0:T(8,128)(2,1)}, u32[]{:S(2)}, u32[]{:S(2)}) collective-permute-start(bf16[256,2048]{1,0:T(8,128)(2,1)} %multiply_convert_fusion.6), channel_id=1, source_target_pairs={{0,1},{1,0},{2,3},{3,2},{4,5},{5,4},{6,7},{7,6},{8,9},{9,8},{10,11... | collective-permute-start | bytes 3145736 | tf_op jit(solution)/shard_map/ppermute | solution.py:26
  186.4 11.2 %collective-permute-start.18 = (bf16[128,2048]{1,0:T(8,128)(2,1)S(1)}, bf16[128,2048]{1,0:T(8,128)(2,1)S(1)}, u32[]{:S(2)}, u32[]{:S(2)}) collective-permute-start(bf16[128,2048]{1,0:T(8,128)(2,1)S(1)} %slice.464), channel_id=1, source_target_pairs={{0,1},{1,0},{2,3},{3,2},{4,5},{5,4},{6,7},{7,6},{8,9},{9,8},{10,11... | collective-permute-start | bytes 1572872 | tf_op jit(solution)/shard_map/ppermute | solution.py:26
  189.7 9.2 %collective-permute-start.19 = (bf16[128,2048]{1,0:T(8,128)(2,1)S(1)}, bf16[128,2048]{1,0:T(8,128)(2,1)S(1)}, u32[]{:S(2)}, u32[]{:S(2)}) collective-permute-start(bf16[128,2048]{1,0:T(8,128)(2,1)S(1)} %slice.465), channel_id=1, source_target_pairs={{0,2},{1,3},{2,0},{3,1},{4,6},{5,7},{6,4},{7,5},{8,10},{9,11},{10,... | collective-permute-start | bytes 1572872 | tf_op jit(solution)/shard_map/ppermute | solution.py:26
  199.0 16.4 %copy-start.56 = (bf16[1024,2048]{1,0:T(8,128)(2,1)}, bf16[1024,2048]{1,0:T(8,128)(2,1)S(1)}, u32[]{:S(2)}) copy-start(bf16[1024,2048]{1,0:T(8,128)(2,1)S(1)} %constant_dynamic-update-slice_fusion.10) | copy-start | bytes 12582916
  228.7 193.8 %reduce-scatter.6.cloned.1.call-start = ((), (), s32[]{:S(2)}) async-start(), calls=%async_computation.7 | async-start | bytes 8847360 | tf_op jit(solution)/shard_map/reduce_scatter | solution.py:83
  255.4 12.8 %copy-start.20 = (bf16[1024,640]{0,1:T(8,128)(2,1)}, bf16[1024,640]{0,1:T(8,128)(2,1)S(1)}, u32[]{:S(2)}) copy-start(bf16[1024,640]{0,1:T(8,128)(2,1)S(1)} %get-tuple-element.123) | copy-start | bytes 3932164
  255.4 12.8 %copy-start.22 = (bf16[1024,640]{0,1:T(8,128)(2,1)}, bf16[1024,640]{0,1:T(8,128)(2,1)S(1)}, u32[]{:S(2)}) copy-start(bf16[1024,640]{0,1:T(8,128)(2,1)S(1)} %get-tuple-element.124) | copy-start | bytes 3932164
  255.4 30.5 %copy-start.41 = (bf16[1024,640]{0,1:T(8,128)(2,1)}, bf16[1024,640]{0,1:T(8,128)(2,1)S(1)}, u32[]{:S(2)}) copy-start(bf16[1024,640]{0,1:T(8,128)(2,1)S(1)} %get-tuple-element.65) | copy-start | bytes 3932164
  264.9 20.7 %collective-permute-start.20 = (bf16[256,2048]{1,0:T(8,128)(2,1)S(1)}, bf16[256,2048]{1,0:T(8,128)(2,1)S(1)}, u32[]{:S(2)}, u32[]{:S(2)}) collective-permute-start(bf16[256,2048]{1,0:T(8,128)(2,1)S(1)} %pad_maximum_fusion.13), channel_id=1, source_target_pairs={{0,1},{1,0},{2,3},{3,2},{4,5},{5,4},{6,7},{7,6},{8,9},{9,8},{10,11... | collective-permute-start | bytes 3145736 | tf_op jit(solution)/shard_map/ppermute | solution.py:26
  266.7 19.3 %copy-start.55 = (bf16[1024,2048]{1,0:T(8,128)(2,1)S(1)}, bf16[1024,2048]{1,0:T(8,128)(2,1)}, u32[]{:S(2)}) copy-start(bf16[1024,2048]{1,0:T(8,128)(2,1)} %copy-done.53) | copy-start | bytes 12582916
  266.7 19.3 %collective-permute-start.21 = (bf16[256,2048]{1,0:T(8,128)(2,1)S(1)}, bf16[256,2048]{1,0:T(8,128)(2,1)}, u32[]{:S(2)}, u32[]{:S(2)}) collective-permute-start(bf16[256,2048]{1,0:T(8,128)(2,1)S(1)} %pad_maximum_fusion.14), channel_id=1, source_target_pairs={{0,2},{1,3},{2,0},{3,1},{4,6},{5,7},{6,4},{7,5},{8,10},{9,11},{10,... | collective-permute-start | bytes 3145736 | tf_op jit(solution)/shard_map/ppermute | solution.py:26
  305.3 170.6 %reduce-scatter.8.cloned.1.call-start = ((), (), s32[]{:S(2)}) async-start(), calls=%async_computation.8 | async-start | bytes 5013504 | tf_op jit(solution)/shard_map/reduce_scatter | solution.py:83
  305.7 10.7 %slice-start.2 = ((s8[7864320]{0:T(1024)(128)(4,1)}), s8[4194304]{0:T(1024)(128)(4,1)S(1)}, s32[]{:S(2)}) async-start(s8[7864320]{0:T(1024)(128)(4,1)} %bitcast.104), calls=%async_computation.11 | async-start | bytes 8388608
  309.2 9.2 %collective-permute-start.22 = (bf16[128,2048]{1,0:T(8,128)(2,1)S(1)}, bf16[128,2048]{1,0:T(8,128)(2,1)S(1)}, u32[]{:S(2)}, u32[]{:S(2)}) collective-permute-start(bf16[128,2048]{1,0:T(8,128)(2,1)S(1)} %get-tuple-element.141), channel_id=1, source_target_pairs={{0,2},{1,3},{2,0},{3,1},{4,6},{5,7},{6,4},{7,5},{8,10},{9,11},{10,... | collective-permute-start | bytes 1572872 | tf_op jit(solution)/shard_map/ppermute | solution.py:26
  309.8 9.2 %collective-permute-start.23 = (bf16[128,2048]{1,0:T(8,128)(2,1)S(1)}, bf16[128,2048]{1,0:T(8,128)(2,1)S(1)}, u32[]{:S(2)}, u32[]{:S(2)}) collective-permute-start(bf16[128,2048]{1,0:T(8,128)(2,1)S(1)} %get-tuple-element.142), channel_id=1, source_target_pairs={{0,1},{1,0},{2,3},{3,2},{4,5},{5,4},{6,7},{7,6},{8,9},{9,8},{10,11... | collective-permute-start | bytes 1572872 | tf_op jit(solution)/shard_map/ppermute | solution.py:26
  324.6 20.9 %collective-permute-start.25 = (bf16[256,2048]{1,0:T(8,128)(2,1)}, bf16[256,2048]{1,0:T(8,128)(2,1)S(1)}, u32[]{:S(2)}, u32[]{:S(2)}) collective-permute-start(bf16[256,2048]{1,0:T(8,128)(2,1)} %get-tuple-element.119), channel_id=1, source_target_pairs={{0,2},{1,3},{2,0},{3,1},{4,6},{5,7},{6,4},{7,5},{8,10},{9,11},{10,... | collective-permute-start | bytes 3145736 | tf_op jit(solution)/shard_map/ppermute | solution.py:26
  326.1 24.5 %collective-permute-start.24 = (bf16[256,2048]{1,0:T(8,128)(2,1)}, bf16[256,2048]{1,0:T(8,128)(2,1)}, u32[]{:S(2)}, u32[]{:S(2)}) collective-permute-start(bf16[256,2048]{1,0:T(8,128)(2,1)} %get-tuple-element.119), channel_id=1, source_target_pairs={{0,1},{1,0},{2,3},{3,2},{4,5},{5,4},{6,7},{7,6},{8,9},{9,8},{10,11... | collective-permute-start | bytes 3145736 | tf_op jit(solution)/shard_map/ppermute | solution.py:26
  327.9 23.9 %copy-start.42 = (bf16[1024,640]{0,1:T(8,128)(2,1)S(1)}, bf16[1024,640]{0,1:T(8,128)(2,1)}, u32[]{:S(2)}) copy-start(bf16[1024,640]{0,1:T(8,128)(2,1)} %copy-done.41) | copy-start | bytes 3932164
  345.6 13.5 %collective-permute-start.26 = (bf16[128,2048]{1,0:T(8,128)(2,1)S(1)}, bf16[128,2048]{1,0:T(8,128)(2,1)S(1)}, u32[]{:S(2)}, u32[]{:S(2)}) collective-permute-start(bf16[128,2048]{1,0:T(8,128)(2,1)S(1)} %slice.598), channel_id=1, source_target_pairs={{0,1},{1,0},{2,3},{3,2},{4,5},{5,4},{6,7},{7,6},{8,9},{9,8},{10,11... | collective-permute-start | bytes 1572872 | tf_op jit(solution)/shard_map/ppermute | solution.py:26
  351.7 13.4 %collective-permute-start.27 = (bf16[128,2048]{1,0:T(8,128)(2,1)S(1)}, bf16[128,2048]{1,0:T(8,128)(2,1)S(1)}, u32[]{:S(2)}, u32[]{:S(2)}) collective-permute-start(bf16[128,2048]{1,0:T(8,128)(2,1)S(1)} %slice.599), channel_id=1, source_target_pairs={{0,2},{1,3},{2,0},{3,1},{4,6},{5,7},{6,4},{7,5},{8,10},{9,11},{10,... | collective-permute-start | bytes 1572872 | tf_op jit(solution)/shard_map/ppermute | solution.py:26
  366.3 28.4 %collective-permute-start.28 = (bf16[256,2048]{1,0:T(8,128)(2,1)}, bf16[256,2048]{1,0:T(8,128)(2,1)}, u32[]{:S(2)}, u32[]{:S(2)}) collective-permute-start(bf16[256,2048]{1,0:T(8,128)(2,1)} %pad_maximum_fusion.15), channel_id=1, source_target_pairs={{0,1},{1,0},{2,3},{3,2},{4,5},{5,4},{6,7},{7,6},{8,9},{9,8},{10,11... | collective-permute-start | bytes 3145736 | tf_op jit(solution)/shard_map/ppermute | solution.py:26
  369.8 24.9 %collective-permute-start.29 = (bf16[256,2048]{1,0:T(8,128)(2,1)}, bf16[256,2048]{1,0:T(8,128)(2,1)}, u32[]{:S(2)}, u32[]{:S(2)}) collective-permute-start(bf16[256,2048]{1,0:T(8,128)(2,1)} %pad_maximum_fusion.16), channel_id=1, source_target_pairs={{0,2},{1,3},{2,0},{3,1},{4,6},{5,7},{6,4},{7,5},{8,10},{9,11},{10,... | collective-permute-start | bytes 3145736 | tf_op jit(solution)/shard_map/ppermute | solution.py:26
  399.2 12.3 %collective-permute-start.32 = (bf16[512,256]{1,0:T(8,128)(2,1)S(1)}, bf16[512,256]{1,0:T(8,128)(2,1)S(1)}, u32[]{:S(2)}, u32[]{:S(2)}) collective-permute-start(bf16[512,256]{1,0:T(8,128)(2,1)S(1)} %pad_maximum_fusion.30), channel_id=1, source_target_pairs={{0,2},{1,3},{2,0},{3,1},{4,6},{5,7},{6,4},{7,5},{8,10},{9,11},{10,... | collective-permute-start | bytes 786440 | tf_op jit(solution)/shard_map/ppermute | solution.py:26
  401.2 12.3 %collective-permute-start.30 = (bf16[512,256]{1,0:T(8,128)(2,1)S(1)}, bf16[512,256]{1,0:T(8,128)(2,1)S(1)}, u32[]{:S(2)}, u32[]{:S(2)}) collective-permute-start(bf16[512,256]{1,0:T(8,128)(2,1)S(1)} %pad_maximum_fusion.29), channel_id=1, source_target_pairs={{0,1},{1,0},{2,3},{3,2},{4,5},{5,4},{6,7},{7,6},{8,9},{9,8},{10,11... | collective-permute-start | bytes 786440 | tf_op jit(solution)/shard_map/ppermute | solution.py:26
  411.5 5.0 collective-permute-start.33
  413.6 5.0 collective-permute-start.31
  425.3 20.6 %collective-permute-start.34 = (bf16[256,2048]{1,0:T(8,128)(2,1)}, bf16[256,2048]{1,0:T(8,128)(2,1)}, u32[]{:S(2)}, u32[]{:S(2)}) collective-permute-start(bf16[256,2048]{1,0:T(8,128)(2,1)} %pad_maximum_fusion.17), channel_id=1, source_target_pairs={{0,1},{1,0},{2,3},{3,2},{4,5},{5,4},{6,7},{7,6},{8,9},{9,8},{10,11... | collective-permute-start | bytes 3145736 | tf_op jit(solution)/shard_map/ppermute | solution.py:26
  426.4 21.8 %collective-permute-start.35 = (bf16[256,2048]{1,0:T(8,128)(2,1)}, bf16[256,2048]{1,0:T(8,128)(2,1)}, u32[]{:S(2)}, u32[]{:S(2)}) collective-permute-start(bf16[256,2048]{1,0:T(8,128)(2,1)} %pad_maximum_fusion.18), channel_id=1, source_target_pairs={{0,2},{1,3},{2,0},{3,1},{4,6},{5,7},{6,4},{7,5},{8,10},{9,11},{10,... | collective-permute-start | bytes 3145736 | tf_op jit(solution)/shard_map/ppermute | solution.py:26
  450.9 14.2 %collective-permute-start.38 = (bf16[128,2048]{1,0:T(8,128)(2,1)}, bf16[128,2048]{1,0:T(8,128)(2,1)S(1)}, u32[]{:S(2)}, u32[]{:S(2)}) collective-permute-start(bf16[128,2048]{1,0:T(8,128)(2,1)} %get-tuple-element.129), channel_id=1, source_target_pairs={{0,2},{1,3},{2,0},{3,1},{4,6},{5,7},{6,4},{7,5},{8,10},{9,11},{10,... | collective-permute-start | bytes 1572872 | tf_op jit(solution)/shard_map/ppermute | solution.py:26
  452.4 13.5 %collective-permute-start.39 = (bf16[128,2048]{1,0:T(8,128)(2,1)S(1)}, bf16[128,2048]{1,0:T(8,128)(2,1)}, u32[]{:S(2)}, u32[]{:S(2)}) collective-permute-start(bf16[128,2048]{1,0:T(8,128)(2,1)S(1)} %get-tuple-element.130), channel_id=1, source_target_pairs={{0,1},{1,0},{2,3},{3,2},{4,5},{5,4},{6,7},{7,6},{8,9},{9,8},{10,11... | collective-permute-start | bytes 1572872 | tf_op jit(solution)/shard_map/ppermute | solution.py:26
  463.0 9.2 %collective-permute-start.36 = (bf16[128,2048]{1,0:T(8,128)(2,1)S(1)}, bf16[128,2048]{1,0:T(8,128)(2,1)S(1)}, u32[]{:S(2)}, u32[]{:S(2)}) collective-permute-start(bf16[128,2048]{1,0:T(8,128)(2,1)S(1)} %get-tuple-element.131), channel_id=1, source_target_pairs={{0,2},{1,3},{2,0},{3,1},{4,6},{5,7},{6,4},{7,5},{8,10},{9,11},{10,... | collective-permute-start | bytes 1572872 | tf_op jit(solution)/shard_map/ppermute | solution.py:26
  463.6 9.3 %collective-permute-start.37 = (bf16[128,2048]{1,0:T(8,128)(2,1)S(1)}, bf16[128,2048]{1,0:T(8,128)(2,1)S(1)}, u32[]{:S(2)}, u32[]{:S(2)}) collective-permute-start(bf16[128,2048]{1,0:T(8,128)(2,1)S(1)} %get-tuple-element.132), channel_id=1, source_target_pairs={{0,1},{1,0},{2,3},{3,2},{4,5},{5,4},{6,7},{7,6},{8,9},{9,8},{10,11... | collective-permute-start | bytes 1572872 | tf_op jit(solution)/shard_map/ppermute | solution.py:26
  469.4 8.9 %copy-start.67 = (f32[256]{0:T(256)S(1)}, f32[256]{0:T(256)}, u32[]{:S(2)}) copy-start(f32[256]{0:T(256)} %copy-done.66) | copy-start | bytes 3076
  476.9 10.0 %copy-start.10 = (bf16[256,2048]{1,0:T(8,128)(2,1)S(1)}, bf16[256,2048]{1,0:T(8,128)(2,1)}, u32[]{:S(2)}) copy-start(bf16[256,2048]{1,0:T(8,128)(2,1)} %param.12) | copy-start | bytes 3145732
  476.9 10.0 %copy-start.63 = (f32[256]{0:T(256)S(1)}, f32[256]{0:T(256)}, u32[]{:S(2)}) copy-start(f32[256]{0:T(256)} %copy-done.62) | copy-start | bytes 3076
  480.4 8.7 %copy-start.13 = (f32[128,2048]{1,0:T(8,128)S(1)}, f32[128,2048]{1,0:T(8,128)}, u32[]{:S(2)}) copy-start(f32[128,2048]{1,0:T(8,128)} %copy-done.11) | copy-start | bytes 3145732
  480.4 8.7 %copy-start.16 = (f32[128,2048]{1,0:T(8,128)S(1)}, f32[128,2048]{1,0:T(8,128)}, u32[]{:S(2)}) copy-start(f32[128,2048]{1,0:T(8,128)} %copy-done.14) | copy-start | bytes 3145732
  481.4 12.3 %collective-permute-start.41 = (f32[64,265]{1,0:T(8,128)}, f32[64,265]{1,0:T(8,128)S(1)}, u32[]{:S(2)}, u32[]{:S(2)}) collective-permute-start(f32[64,265]{1,0:T(8,128)} %pad_maximum_fusion.32), channel_id=1, source_target_pairs={{0,2},{1,3},{2,0},{3,1},{4,6},{5,7},{6,4},{7,5},{8,10},{9,11},{10,... | collective-permute-start | bytes 203528 | tf_op jit(solution)/shard_map/ppermute | solution.py:26
  482.7 11.0 %collective-permute-start.40 = (f32[64,265]{1,0:T(8,128)}, f32[64,265]{1,0:T(8,128)}, u32[]{:S(2)}, u32[]{:S(2)}) collective-permute-start(f32[64,265]{1,0:T(8,128)} %pad_maximum_fusion.32), channel_id=1, source_target_pairs={{0,1},{1,0},{2,3},{3,2},{4,5},{5,4},{6,7},{7,6},{8,9},{9,8},{10,11... | collective-permute-start | bytes 203528 | tf_op jit(solution)/shard_map/ppermute | solution.py:26
  484.2 9.5 %collective-permute-start.42 = (f32[64,265]{1,0:T(8,128)}, f32[64,265]{1,0:T(8,128)}, u32[]{:S(2)}, u32[]{:S(2)}) collective-permute-start(f32[64,265]{1,0:T(8,128)} %pad_maximum_fusion.32), channel_id=1, source_target_pairs={{0,3},{1,2},{2,1},{3,0},{4,7},{5,6},{6,5},{7,4},{8,11},{9,10},{10,... | collective-permute-start | bytes 203528 | tf_op jit(solution)/shard_map/ppermute | solution.py:26
  (62 other events, 269.7 us)
Sparse Core Ops, SparseCore 0:
  15.8 48.3 all-gather.3
  66.5 89.4 all-gather.5
  158.2 76.1 all-gather.7
  236.5 97.9 reduce-scatter.3
  336.7 82.9 reduce-scatter.5
  422.6 50.1 reduce-scatter.7

commit v9 on v8

--- a/solution.py
+++ b/solution.py
@@ -288,6 +288,27 @@
     part_out[...] = part
 
 
+def finish_attn_kernel(sum_ref, query_ref, gain_ref, query_out, project_out, part_out):
+    rows = query_ref.shape[0]
+    total = sum_ref[:rows, :].astype(f32)
+    query_out[...] = total * gain_ref[...]
+    part_out[...] = jnp.sum(query_ref[...].astype(f32) * total, axis=1, keepdims=True)
+    project_out[...] = sum_ref[rows : 2 * rows, :].astype(f32).T
+
+
+def finish_attn(total, query_own, gain):
+    rows, width = query_own.shape
+    return pl.pallas_call(
+        finish_attn_kernel,
+        name="finish_attn",
+        out_shape=(
+            jax.ShapeDtypeStruct((rows, width), f32),
+            jax.ShapeDtypeStruct((width, rows), f32),
+            jax.ShapeDtypeStruct((rows, 1), f32),
+        ),
+    )(total, query_own, gain)
+
+
 def finish_ff(parts, sums, gate_own, up_own, gain):
     rows, ff = gate_own.shape
     widths = [b - a for a, b in parts]
@@ -377,8 +398,8 @@
     ]
 
     residual = layer_input.astype(f32)
-    near = near_blocks(layer_input)
-    inputs = all_blocks(layer_input, near)
+    x_own = after(layer_input, attn_shard)
+    inputs = all_blocks(x_own, near_blocks(x_own))
     attn_full = gather_dp(attn_shard)
 
     def norm(block):
@@ -483,7 +504,7 @@
         ],
         axis=1,
     ).reshape(-1, heads_width)
-    attn_sum = scatter_dp(attn_partial).astype(f32)
+    attn_sum = scatter_dp(attn_partial)
     down_sent = [after(block, *qkv_sent) for block in down_sent]
     own_down = sum(
         dot(after(h[:rows], attn_partial), w, 1, 1) for h, w in zip(hidden, downs)
@@ -491,12 +512,18 @@
     after_mlp = after_attn + finish_sums(own_down, down_rest, down_sent)
     output = (after_mlp * own_mask).astype(bf16)
     scaled_one = finish_sums(dot(qkv_back[:rows], qkv_full, 1, 1), qkv_rest, qkv_sent)
-    query_sum, project_sum = attn_sum[:shard_rows], attn_sum[shard_rows : 2 * shard_rows]
-    kv_sum = attn_sum[2 * shard_rows :].reshape(kv_rows, 2 * HD)
+    inv_one = inverse_norm(residual)
+    unit_one = residual * inv_one
+    input_grad = attn_top + inv_one * (
+        scaled_one - unit_one * jnp.mean(scaled_one * unit_one, axis=-1, keepdims=True)
+    )
+
     grad_gate, grad_up, grad_down, gain_two_part = finish_ff(
         parts, ff_sums, w_gate, w_up, gain_two
     )
-    query_part = jnp.sum(qkv_own[:, :heads_width] * query_sum, axis=1, keepdims=True)
+    attn_sum = after(attn_sum, output, input_grad, gain_two_part)
+    grad_query, grad_project, query_part = finish_attn(attn_sum, w_query, gain_one)
+    kv_sum = attn_sum[2 * shard_rows :].astype(f32).reshape(kv_rows, 2 * HD)
     kv_here = lax.dynamic_slice_in_dim(qkv_own[:, heads_width:], rank * kv_rows, kv_rows)
     gain_here = lax.dynamic_slice_in_dim(gain_one, rank * kv_rows, kv_rows)
     small = jnp.concatenate(
@@ -507,21 +534,15 @@
         ],
         axis=1,
     )
-    scaled_one = after(scaled_one, small)
-    inv_one = inverse_norm(residual)
-    unit_one = residual * inv_one
-    input_grad = attn_top + inv_one * (
-        scaled_one - unit_one * jnp.mean(scaled_one * unit_one, axis=-1, keepdims=True)
-    )
     blocks = jnp.stack([small] + [hop(small, j) for j in range(1, ranks)], axis=0)
     sums = jnp.sum(blocks[:, :, 2 * HD + 1 :], axis=0).reshape(shard_rows, 2)
     placed = jnp.concatenate([pick(blocks, order[j], 0) for j in range(ranks)], axis=0)
     return (
         output,
         input_grad,
-        query_sum * gain_one,
+        grad_query,
         placed[:, : 2 * HD],
-        project_sum.T,
+        grad_project,
         grad_gate,
         grad_up,
         grad_down,

time: 513 us -> 507 us (0.988)
  other arithmetic: 85.3 us -> 74.9 us
    ppermute x43, waiting for transfers between devices: 121 us -> 128 us  [hop(): return lax.ppermute(value, 'tensor', [(i, i ^ step) for i in range(size)])]
    unnamed x162 -> x157, local copies, waits for them, and re-layouts: 23.4 us -> 20.4 us
  transfers between devices with their start and end apart: 49 -> 49, of which waited for: 27 -> 31; matrix products, arithmetic and copies ran while one was open for 49% -> 48% of each run, Pallas kernels for 6% -> 6%
where the time goes in v9:
time: 507 us; the launch traced here: 498 us
  waiting for transfers between devices  136 us (27%)
  matrix products  132 us (26%)
  other arithmetic  74.9 us (15%)
  starting transfers between devices  52 us (10%)
  local copies, waits for them, and re-layouts  47.2 us (9%)
  Pallas kernels  31.4 us (6%)
  between operations  24.5 us (5%)
    dot_general x25, matrix products, dot(): lax.dot_general(a, b, (((ca,), (cb,)), ((), ())), preferred_element_type=...  132 us
    ppermute x43, waiting for transfers between devices, hop(): return lax.ppermute(value, 'tensor', [(i, i ^ step) for i in range(size)])  128 us
    ppermute x43, starting transfers between devices, hop(): return lax.ppermute(value, 'tensor', [(i, i ^ step) for i in range(size)])  50.6 us
    unnamed x157, local copies, waits for them, and re-layouts  20.4 us
    pallas_call x1, Pallas kernels, attend_back(): pl.pallas_call(attend_back_kernel, name='attend_back', grid_spec=pltpu.Pr...  13.7 us
    concatenate x2, other arithmetic, partial(): jnp.concatenate([dot(normed_two, grads, 0, 0).astype(bf16), dot(top_all,...  11.7 us
    pallas_call x1, Pallas kernels, attend(): pl.pallas_call(attend_kernel, name='attend', grid_spec=pltpu.PrefetchScal...  11.4 us
  transfers between devices with their start and end apart: 49, of which 31 were waited for; matrix products, arithmetic and copies ran while one was open for 48% of the time, Pallas kernels for 6%

profile of v9, /device:TPU:0, one launch (start us, length us, event | category | flops | bytes accessed | tf_op | source)
XLA Modules:
  0.0 498.0 jit_solution(8970741528805052667)
XLA Ops:
  11.3 3.1 collective-permute-start.1
  22.1 3.1 fusion.81
  29.1 2.1 pad_maximum_fusion.9
  35.1 2.4 collective-permute-done.1
  43.9 2.4 fusion.54
  47.5 3.3 collective-permute-done.2
  51.0 2.1 collective-permute-done.3
  55.5 7.7 %all-gather.4.cloned.1.call-done = bf16[4352,512]{1,0:T(8,128)(2,1)} async-done(((bf16[544,512]{1,0:T(8,128)(2,1)}), bf16[4352,512]{1,0:T(8,128)(2,1)}) %all-gather.4.cloned.1.call-update) | async-done | bytes 4456464 | tf_op jit(solution)/shard_map/all_gather | solution.py:79
  77.1 3.8 collective-permute-done.6
  87.1 7.4 %fusion.66.q_ref.kv_ref = f32[1024,768]{1,0:T(8,128)} fusion(bf16[1024,2048]{1,0:T(8,128)(2,1)} %fusion.69, bf16[2048,256]{1,0:T(8,128)(2,1)S(1)} %bitcast.113, bf16[2048,512]{1,0:T(8,128)(2,1)S(1)} %bitcast.108), kind=kOutput, calls=%fused_computation.143 | convolution fusion | flops 3227516928 | bytes 10485760 | tf_op jit(solution)/shard_map/dot_general | solution.py:21
  94.5 11.4 %attend.1 = (bf16[1024,512]{1,0:T(8,128)(2,1)S(1)}, bf16[1024,256]{1,0:T(8,128)(2,1)S(1)}, bf16[1024,512]{1,0:T(8,128)(2,1)S(1)}, f32[1024,128]{1,0:T(8,128)S(1)}) custom-call(s32[2]{0:T(128)S(1)} %pad_add_fusion.where_ref, f32[1024,768]{1,0:T(8,128)} %fusion.66.q_ref.kv_ref, f32[1024,768]{1,0:T(8,128)} %fusion.66.q_ref.kv_ref, ...), custom_call_target="tpu_custom_call" | custom-call | flops 2147483648 | bytes 8388608 | tf_op jit(solution)/shard_map/attend/pallas_call | solution.py:202
  109.0 3.7 convolution_convert_fusion.2
  116.0 20.3 %collective-permute-done.12 = bf16[256,2048]{1,0:T(8,128)(2,1)S(1)} collective-permute-done((bf16[256,2048]{1,0:T(8,128)(2,1)S(1)}, bf16[256,2048]{1,0:T(8,128)(2,1)S(1)}, u32[]{:S(2)}, u32[]{:S(2)}) %collective-permute-start.12) | collective-permute-done | bytes 1048608 | tf_op jit(solution)/shard_map/ppermute | solution.py:26
  148.3 4.6 collective-permute-done.11
  154.3 6.2 %collective-permute-done.14 = bf16[128,2048]{1,0:T(8,128)(2,1)S(1)} collective-permute-done((bf16[128,2048]{1,0:T(8,128)(2,1)S(1)}, bf16[128,2048]{1,0:T(8,128)(2,1)S(1)}, u32[]{:S(2)}, u32[]{:S(2)}) %collective-permute-start.14) | collective-permute-done | bytes 524320 | tf_op jit(solution)/shard_map/ppermute | solution.py:26
  165.1 6.3 %fusion.26 = f32[1024,768]{0,1:T(8,128)S(1)} fusion(bf16[1024,2048]{1,0:T(8,128)(2,1)} %copy-done.52, bf16[2048,2304]{1,0:T(8,128)(2,1)} %all-gather.6.cloned.1.call-done), kind=kOutput, calls=%fused_computation.60 | convolution fusion | flops 3221225472 | bytes 10485760 | tf_op jit(solution)/shard_map/dot_general | solution.py:21
  171.4 13.0 %collective-permute-done.17 = bf16[256,2048]{1,0:T(8,128)(2,1)} collective-permute-done((bf16[256,2048]{1,0:T(8,128)(2,1)}, bf16[256,2048]{1,0:T(8,128)(2,1)}, u32[]{:S(2)}, u32[]{:S(2)}) %collective-permute-start.17) | collective-permute-done | bytes 1048608 | tf_op jit(solution)/shard_map/ppermute | solution.py:26
  192.8 3.8 collective-permute-done.18
  198.0 10.4 %fusion.4 = f32[1024,1536]{0,1:T(8,128)S(1)} fusion(bf16[1024,2048]{1,0:T(8,128)(2,1)S(1)} %constant_dynamic-update-slice_fusion.10, bf16[2048,2304]{1,0:T(8,128)(2,1)} %all-gather.6.cloned.1.call-done), kind=kOutput, calls=%fused_computation.10 | convolution fusion | flops 6442450944 | bytes 16777216 | tf_op jit(solution)/shard_map/dot_general | solution.py:21
  208.4 2.1 multiply_convert_fusion.1
  210.5 3.8 convolution_convert_fusion.4
  214.3 8.6 %convolution_convert_fusion.1 = bf16[2048,1536]{1,0:T(8,128)(2,1)S(1)} fusion(bf16[1024,2048]{1,0:T(8,128)(2,1)S(1)} %constant_dynamic-update-slice_fusion.10, bf16[1024,768]{0,1:T(8,128)(2,1)S(1)} %get-tuple-element.102, bf16[1024,768]{0,1:T(8,128)(2,1)S(1)} %get-tuple-element.101), kind=kOutput, calls=%fused_computation.3 | convolution fusion | flops 6451888128 | bytes 13631488 | tf_op jit(solution)/shard_map/dot_general | solution.py:21
  223.0 4.6 pad_maximum_fusion
  229.6 9.9 %fusion.2 = f32[768,2048]{1,0:T(8,128)} fusion(bf16[768,1536]{0,1:T(8,128)(2,1)S(1)} %pad_maximum_fusion.5, bf16[2048,2304]{1,0:T(8,128)(2,1)} %all-gather.6.cloned.1.call-done), kind=kOutput, calls=%fused_computation.8 | convolution fusion | flops 4831838208 | bytes 14942208 | tf_op jit(solution)/shard_map/dot_general | solution.py:21
  239.5 6.1 %fusion.44 = f32[1024,640]{0,1:T(8,128)S(1)} fusion(bf16[1024,2048]{1,0:T(8,128)(2,1)} %copy-done.52, bf16[2048,1920]{1,0:T(8,128)(2,1)} %all-gather.8.cloned.1.call-done), kind=kOutput, calls=%fused_computation.86 | convolution fusion | flops 2684354560 | bytes 9437184 | tf_op jit(solution)/shard_map/dot_general | solution.py:21
  246.4 6.0 %fusion.10 = f32[1024,1280]{0,1:T(8,128)S(1)} fusion(bf16[1024,2048]{1,0:T(8,128)(2,1)S(1)} %copy-done.56, bf16[2048,1920]{1,0:T(8,128)(2,1)S(1)} %copy-done.27), kind=kOutput, calls=%fused_computation.17 | convolution fusion | flops 5368709120 | bytes 14680064 | tf_op jit(solution)/shard_map/dot_general | solution.py:21
  254.3 7.9 %add_convert_fusion.1 = bf16[768,2048]{1,0:T(8,128)(2,1)S(1)} fusion(f32[768,2048]{1,0:T(8,128)} %fusion.2, bf16[2048,1920]{1,0:T(8,128)(2,1)S(1)} %copy-done.27, bf16[1024,640]{0,1:T(8,128)(2,1)S(1)} %get-tuple-element.104, bf16[1024,640]{0,1:T(8,128)(2,1)S(1)} %get-tuple-element.103), kind=kOutput, calls=%fused_computation.5 | convolution fusion | flops 4033609728 | bytes 17301504 | tf_op jit(solution)/shard_map/dot_general | solution.py:21
  267.4 17.2 %collective-permute-done.20 = bf16[256,2048]{1,0:T(8,128)(2,1)S(1)} collective-permute-done((bf16[256,2048]{1,0:T(8,128)(2,1)S(1)}, bf16[256,2048]{1,0:T(8,128)(2,1)S(1)}, u32[]{:S(2)}, u32[]{:S(2)}) %collective-permute-start.20) | collective-permute-done | bytes 1048608 | tf_op jit(solution)/shard_map/ppermute | solution.py:26
  284.9 4.8 convolution_convert_fusion.5
  289.7 7.4 %convolution_convert_fusion = bf16[2048,1280]{1,0:T(8,128)(2,1)} fusion(bf16[1024,2048]{1,0:T(8,128)(2,1)S(1)} %copy-done.57, bf16[1024,1280]{0,1:T(8,128)(2,1)S(1)} %pad_maximum_fusion.3), kind=kOutput, calls=%fused_computation.2 | convolution fusion | flops 5371330560 | bytes 12058624 | tf_op jit(solution)/shard_map/dot_general | solution.py:21
  297.1 7.1 %pad_maximum_fusion.1 = bf16[2048,1920]{1,0:T(8,128)(2,1)} fusion(bf16[2048,640]{1,0:T(8,128)(2,1)} %convolution_convert_fusion.5, bf16[2048,1280]{1,0:T(8,128)(2,1)} %convolution_convert_fusion), kind=kLoop, calls=%fused_computation.1 | loop fusion | flops 15728640 | bytes 15728640 | tf_op jit(solution)/shard_map/concatenate | solution.py:455
  306.0 2.1 add_convert_fusion.7
  310.3 5.1 %fusion = f32[256,2048]{1,0:T(8,128)S(1)} fusion(bf16[256,1536]{0,1:T(8,128)(2,1)S(1)} %pad_maximum_fusion.23, bf16[2048,2304]{1,0:T(8,128)(2,1)} %all-gather.6.cloned.1.call-done), kind=kOutput, calls=%fused_computation.6 | convolution fusion | flops 1610612736 | bytes 9175040 | tf_op jit(solution)/shard_map/dot_general | solution.py:21
  320.7 2.8 constant_dynamic-update-slice_fusion.19
  326.8 5.0 %fusion.24 = f32[768,2048]{1,0:T(8,128)S(1)} fusion(bf16[2048,2304]{1,0:T(8,128)(2,1)} %all-gather.6.cloned.1.call-done, bf16[1024,768]{0,1:T(8,128)(2,1)} %copy-done.34), kind=kOutput, calls=%fused_computation.58 | convolution fusion | flops 2415919104 | bytes 10616832 | tf_op jit(solution)/shard_map/dot_general | solution.py:21
  331.8 12.7 %collective-permute-done.25 = bf16[256,2048]{1,0:T(8,128)(2,1)S(1)} collective-permute-done((bf16[256,2048]{1,0:T(8,128)(2,1)}, bf16[256,2048]{1,0:T(8,128)(2,1)S(1)}, u32[]{:S(2)}, u32[]{:S(2)}) %collective-permute-start.25) | collective-permute-done | bytes 1048608 | tf_op jit(solution)/shard_map/ppermute | solution.py:26
  346.4 3.2 collective-permute-done.24
  350.7 5.0 add_convert_fusion
  355.7 2.1 constant_dynamic-update-slice_fusion.18
  357.9 6.1 %collective-permute-done.27 = bf16[128,2048]{1,0:T(8,128)(2,1)S(1)} collective-permute-done((bf16[128,2048]{1,0:T(8,128)(2,1)S(1)}, bf16[128,2048]{1,0:T(8,128)(2,1)S(1)}, u32[]{:S(2)}, u32[]{:S(2)}) %collective-permute-start.27) | collective-permute-done | bytes 524320 | tf_op jit(solution)/shard_map/ppermute | solution.py:26
  365.3 2.4 collective-permute-start.28
  370.8 3.7 convolution_convert_fusion.6
  374.5 5.3 %convolution_convert_fusion.9.dm_ref = bf16[1024,512]{1,0:T(8,128)(2,1)S(1)} fusion(bf16[1024,2048]{1,0:T(8,128)(2,1)} %copy-done.51, bf16[2048,512]{1,0:T(8,128)(2,1)} %bitcast.100), kind=kOutput, calls=%fused_computation.92 | convolution fusion | flops 2148007936 | bytes 7340032 | tf_op jit(solution)/shard_map/dot_general | solution.py:21
  379.9 13.7 %attend_back.1 = (bf16[1024,512]{1,0:T(8,128)(2,1)S(1)}, bf16[1024,256]{1,0:T(8,128)(2,1)S(1)}) custom-call(s32[2]{0:T(128)S(1)} %copy-done.3, bf16[1024,512]{1,0:T(8,128)(2,1)S(1)} %get-tuple-element.63.qr_ref, bf16[1024,256]{1,0:T(8,128)(2,1)S(1)} %copy-done.5, bf16[1024,512]{1,0:T(8,128)(2,1)S(1)} %convolution_convert_fusion.9.dm_ref, ...), custom_call_target="tpu_custom_call" | custom-call | flops 5368709120 | bytes 8388608 | tf_op jit(solution)/shard_map/attend_back/pallas_call | solution.py:240
  393.8 4.2 convolution_convert_fusion.8
  400.2 4.0 convolution_convert_fusion.3
  404.3 6.0 %convolution_convert_fusion.7 = bf16[2048,512]{1,0:T(8,128)(2,1)} fusion(bf16[1024,2048]{1,0:T(8,128)(2,1)} %fusion.69, bf16[1024,512]{1,0:T(8,128)(2,1)S(1)} %slice-done), kind=kOutput, calls=%fused_computation.40 | convolution fusion | flops 2148532224 | bytes 7340032 | tf_op jit(solution)/shard_map/dot_general | solution.py:21
  410.4 2.0 collective-permute-start.33
  412.6 2.9 collective-permute-done.33
  415.5 2.0 collective-permute-done.31
  417.7 3.6 pad_maximum_fusion.2
  431.2 3.6 fusion.65
  434.7 3.0 fusion.22
  437.7 7.1 %collective-permute-done.34 = bf16[256,2048]{1,0:T(8,128)(2,1)} collective-permute-done((bf16[256,2048]{1,0:T(8,128)(2,1)}, bf16[256,2048]{1,0:T(8,128)(2,1)}, u32[]{:S(2)}, u32[]{:S(2)}) %collective-permute-start.34) | collective-permute-done | bytes 1048608 | tf_op jit(solution)/shard_map/ppermute | solution.py:26
  444.8 2.3 collective-permute-done.35
  447.1 2.9 add_convert_fusion.3
  452.0 2.8 convolution_add_fusion
  454.9 4.1 finish_ff.1
  460.0 2.1 add_convert_fusion.5
  464.2 2.1 fusion.57
  466.8 4.6 collective-permute-done.36
  474.0 2.3 fusion.31
  477.3 2.3 finish_attn.1
  486.6 2.4 collective-permute-done.42
  (376 shorter events, 135.8 us)
Async XLA Ops:
  7.2 8.7 %copy-start.33 = (bf16[256,1408]{1,0:T(8,128)(2,1)S(1)}, bf16[256,1408]{1,0:T(8,128)(2,1)}, u32[]{:S(2)}) copy-start(bf16[256,1408]{1,0:T(8,128)(2,1)} %gate_ref.1) | copy-start | bytes 2162692
  7.2 56.0 %all-gather.4.cloned.1.call-start = ((), (), s32[]{:S(2)}) async-start(), calls=%async_computation.3 | async-start | bytes 5013504 | tf_op jit(solution)/shard_map/all_gather | solution.py:79
  9.2 8.8 %copy-start.66 = (bf16[256]{0:T(256)(128)(2,1)S(1)}, bf16[256]{0:T(256)(128)(2,1)}, u32[]{:S(2)}) copy-start(bf16[256]{0:T(256)(128)(2,1)} %param.21) | copy-start | bytes 1540
  11.3 153.8 %all-gather.6.cloned.1.call-start = ((), (), s32[]{:S(2)}) async-start(), calls=%async_computation.4 | async-start | bytes 10616832 | tf_op jit(solution)/shard_map/all_gather | solution.py:79
  11.3 26.2 %collective-permute-start.1 = (bf16[256,2048]{1,0:T(8,128)(2,1)S(1)}, bf16[256,2048]{1,0:T(8,128)(2,1)S(1)}, u32[]{:S(2)}, u32[]{:S(2)}) collective-permute-start(bf16[256,2048]{1,0:T(8,128)(2,1)S(1)} %copy-done.8), channel_id=1, source_target_pairs={{0,2},{1,3},{2,0},{3,1},{4,6},{5,7},{6,4},{7,5},{8,10},{9,11},{10,... | collective-permute-start | bytes 3145736 | tf_op jit(solution)/shard_map/ppermute | solution.py:26
  14.4 25.0 %collective-permute-start = (bf16[256,2048]{1,0:T(8,128)(2,1)S(1)}, bf16[256,2048]{1,0:T(8,128)(2,1)}, u32[]{:S(2)}, u32[]{:S(2)}) collective-permute-start(bf16[256,2048]{1,0:T(8,128)(2,1)S(1)} %copy-done.8), channel_id=1, source_target_pairs={{0,1},{1,0},{2,3},{3,2},{4,5},{5,4},{6,7},{7,6},{8,9},{9,8},{10,11... | collective-permute-start | bytes 3145736 | tf_op jit(solution)/shard_map/ppermute | solution.py:26
  18.1 9.8 %copy-start.61 = (f32[256]{0:T(256)}, f32[256]{0:T(256)S(1)}, u32[]{:S(2)}) copy-start(f32[256]{0:T(256)S(1)} %convert_element_type.349) | copy-start | bytes 3076
  25.7 8.2 %copy-start.59 = (f32[1,256]{1,0:T(1,128)}, f32[1,256]{1,0:T(1,128)S(1)}, u32[]{:S(2)}) copy-start(f32[1,256]{1,0:T(1,128)S(1)} %compare_convert_fusion) | copy-start | bytes 3076
  37.6 13.3 %collective-permute-start.2 = (bf16[128,2048]{1,0:T(8,128)(2,1)S(1)}, bf16[128,2048]{1,0:T(8,128)(2,1)S(1)}, u32[]{:S(2)}, u32[]{:S(2)}) collective-permute-start(bf16[128,2048]{1,0:T(8,128)(2,1)S(1)} %slice.541), channel_id=1, source_target_pairs={{0,1},{1,0},{2,3},{3,2},{4,5},{5,4},{6,7},{7,6},{8,9},{9,8},{10,11... | collective-permute-start | bytes 1572872 | tf_op jit(solution)/shard_map/ppermute | solution.py:26
  40.5 12.7 %collective-permute-start.3 = (bf16[128,2048]{1,0:T(8,128)(2,1)S(1)}, bf16[128,2048]{1,0:T(8,128)(2,1)S(1)}, u32[]{:S(2)}, u32[]{:S(2)}) collective-permute-start(bf16[128,2048]{1,0:T(8,128)(2,1)S(1)} %slice.542), channel_id=1, source_target_pairs={{0,2},{1,3},{2,0},{3,1},{4,6},{5,7},{6,4},{7,5},{8,10},{9,11},{10,... | collective-permute-start | bytes 1572872 | tf_op jit(solution)/shard_map/ppermute | solution.py:26
  55.3 184.2 %all-gather.8.cloned.1.call-start = ((), (), s32[]{:S(2)}) async-start(), calls=%async_computation.5 | async-start | bytes 8847360 | tf_op jit(solution)/shard_map/all_gather | solution.py:79
  64.3 11.5 %collective-permute-start.5 = (bf16[512,256]{1,0:T(8,128)(2,1)S(1)}, bf16[512,256]{1,0:T(8,128)(2,1)S(1)}, u32[]{:S(2)}, u32[]{:S(2)}) collective-permute-start(bf16[512,256]{1,0:T(8,128)(2,1)S(1)} %reshape.203), channel_id=1, source_target_pairs={{0,2},{1,3},{2,0},{3,1},{4,6},{5,7},{6,4},{7,5},{8,10},{9,11},{10,... | collective-permute-start | bytes 786440 | tf_op jit(solution)/shard_map/ppermute | solution.py:26
  65.8 10.6 %collective-permute-start.4 = (bf16[512,256]{1,0:T(8,128)(2,1)S(1)}, bf16[512,256]{1,0:T(8,128)(2,1)S(1)}, u32[]{:S(2)}, u32[]{:S(2)}) collective-permute-start(bf16[512,256]{1,0:T(8,128)(2,1)S(1)} %reshape.203), channel_id=1, source_target_pairs={{0,1},{1,0},{2,3},{3,2},{4,5},{5,4},{6,7},{7,6},{8,9},{9,8},{10,11... | collective-permute-start | bytes 786440 | tf_op jit(solution)/shard_map/ppermute | solution.py:26
  75.8 18.7 %copy-start.2 = (s32[2]{0:T(128)}, s32[2]{0:T(128)S(1)}, u32[]{:S(2)}) copy-start(s32[2]{0:T(128)S(1)} %pad_add_fusion.where_ref) | copy-start | bytes 28
  75.8 5.1 %collective-permute-start.6 = (bf16[256,256]{1,0:T(8,128)(2,1)S(1)}, bf16[256,256]{1,0:T(8,128)(2,1)S(1)}, u32[]{:S(2)}, u32[]{:S(2)}) collective-permute-start(bf16[256,256]{1,0:T(8,128)(2,1)S(1)} %slice.545), channel_id=1, source_target_pairs={{0,1},{1,0},{2,3},{3,2},{4,5},{5,4},{6,7},{7,6},{8,9},{9,8},{10,11... | collective-permute-start | bytes 393224 | tf_op jit(solution)/shard_map/ppermute | solution.py:26
  76.4 5.0 %collective-permute-start.7 = (bf16[256,256]{1,0:T(8,128)(2,1)S(1)}, bf16[256,256]{1,0:T(8,128)(2,1)S(1)}, u32[]{:S(2)}, u32[]{:S(2)}) collective-permute-start(bf16[256,256]{1,0:T(8,128)(2,1)S(1)} %slice.546), channel_id=1, source_target_pairs={{0,2},{1,3},{2,0},{3,1},{4,6},{5,7},{6,4},{7,5},{8,10},{9,11},{10,... | collective-permute-start | bytes 393224 | tf_op jit(solution)/shard_map/ppermute | solution.py:26
  81.7 27.2 %collective-permute-start.9 = (bf16[256,2048]{1,0:T(8,128)(2,1)}, bf16[256,2048]{1,0:T(8,128)(2,1)}, u32[]{:S(2)}, u32[]{:S(2)}) collective-permute-start(bf16[256,2048]{1,0:T(8,128)(2,1)} %fusion.41), channel_id=1, source_target_pairs={{0,2},{1,3},{2,0},{3,1},{4,6},{5,7},{6,4},{7,5},{8,10},{9,11},{10,... | collective-permute-start | bytes 3145736 | tf_op jit(solution)/shard_map/ppermute | solution.py:26
  82.3 26.6 %collective-permute-start.8 = (bf16[256,2048]{1,0:T(8,128)(2,1)}, bf16[256,2048]{1,0:T(8,128)(2,1)}, u32[]{:S(2)}, u32[]{:S(2)}) collective-permute-start(bf16[256,2048]{1,0:T(8,128)(2,1)} %fusion.41), channel_id=1, source_target_pairs={{0,1},{1,0},{2,3},{3,2},{4,5},{5,4},{6,7},{7,6},{8,9},{9,8},{10,11... | collective-permute-start | bytes 3145736 | tf_op jit(solution)/shard_map/ppermute | solution.py:26
  107.5 7.7 %copy-start = (bf16[1024,512]{1,0:T(8,128)(2,1)}, bf16[1024,512]{1,0:T(8,128)(2,1)S(1)}, u32[]{:S(2)}) copy-start(bf16[1024,512]{1,0:T(8,128)(2,1)S(1)} %get-tuple-element.53) | copy-start | bytes 3145732
  108.5 266.1 %reduce-scatter.4.cloned.1.call-start = ((), (), s32[]{:S(2)}) async-start(), calls=%async_computation.6 | async-start | bytes 10616832 | tf_op jit(solution)/shard_map/reduce_scatter | solution.py:83
  112.9 23.3 %collective-permute-start.12 = (bf16[256,2048]{1,0:T(8,128)(2,1)S(1)}, bf16[256,2048]{1,0:T(8,128)(2,1)S(1)}, u32[]{:S(2)}, u32[]{:S(2)}) collective-permute-start(bf16[256,2048]{1,0:T(8,128)(2,1)S(1)} %pad_maximum_fusion.12), channel_id=1, source_target_pairs={{0,2},{1,3},{2,0},{3,1},{4,6},{5,7},{6,4},{7,5},{8,10},{9,11},{10,... | collective-permute-start | bytes 3145736 | tf_op jit(solution)/shard_map/ppermute | solution.py:26
  114.6 23.0 %collective-permute-start.10 = (bf16[256,2048]{1,0:T(8,128)(2,1)S(1)}, bf16[256,2048]{1,0:T(8,128)(2,1)S(1)}, u32[]{:S(2)}, u32[]{:S(2)}) collective-permute-start(bf16[256,2048]{1,0:T(8,128)(2,1)S(1)} %pad_maximum_fusion.11), channel_id=1, source_target_pairs={{0,1},{1,0},{2,3},{3,2},{4,5},{5,4},{6,7},{7,6},{8,9},{9,8},{10,11... | collective-permute-start | bytes 3145736 | tf_op jit(solution)/shard_map/ppermute | solution.py:26
  138.0 14.9 %collective-permute-start.11 = (bf16[128,2048]{1,0:T(8,128)(2,1)S(1)}, bf16[128,2048]{1,0:T(8,128)(2,1)S(1)}, u32[]{:S(2)}, u32[]{:S(2)}) collective-permute-start(bf16[128,2048]{1,0:T(8,128)(2,1)S(1)} %get-tuple-element.127), channel_id=1, source_target_pairs={{0,2},{1,3},{2,0},{3,1},{4,6},{5,7},{6,4},{7,5},{8,10},{9,11},{10,... | collective-permute-start | bytes 1572872 | tf_op jit(solution)/shard_map/ppermute | solution.py:26
  138.6 14.8 %collective-permute-start.13 = (bf16[128,2048]{1,0:T(8,128)(2,1)S(1)}, bf16[128,2048]{1,0:T(8,128)(2,1)S(1)}, u32[]{:S(2)}, u32[]{:S(2)}) collective-permute-start(bf16[128,2048]{1,0:T(8,128)(2,1)S(1)} %get-tuple-element.128), channel_id=1, source_target_pairs={{0,1},{1,0},{2,3},{3,2},{4,5},{5,4},{6,7},{7,6},{8,9},{9,8},{10,11... | collective-permute-start | bytes 1572872 | tf_op jit(solution)/shard_map/ppermute | solution.py:26
  142.6 17.9 %collective-permute-start.14 = (bf16[128,2048]{1,0:T(8,128)(2,1)S(1)}, bf16[128,2048]{1,0:T(8,128)(2,1)S(1)}, u32[]{:S(2)}, u32[]{:S(2)}) collective-permute-start(bf16[128,2048]{1,0:T(8,128)(2,1)S(1)} %slice.446), channel_id=1, source_target_pairs={{0,1},{1,0},{2,3},{3,2},{4,5},{5,4},{6,7},{7,6},{8,9},{9,8},{10,11... | collective-permute-start | bytes 1572872 | tf_op jit(solution)/shard_map/ppermute | solution.py:26
  144.2 16.4 %collective-permute-start.15 = (bf16[128,2048]{1,0:T(8,128)(2,1)S(1)}, bf16[128,2048]{1,0:T(8,128)(2,1)S(1)}, u32[]{:S(2)}, u32[]{:S(2)}) collective-permute-start(bf16[128,2048]{1,0:T(8,128)(2,1)S(1)} %slice.447), channel_id=1, source_target_pairs={{0,2},{1,3},{2,0},{3,1},{4,6},{5,7},{6,4},{7,5},{8,10},{9,11},{10,... | collective-permute-start | bytes 1572872 | tf_op jit(solution)/shard_map/ppermute | solution.py:26
  163.0 21.4 %collective-permute-start.17 = (bf16[256,2048]{1,0:T(8,128)(2,1)}, bf16[256,2048]{1,0:T(8,128)(2,1)}, u32[]{:S(2)}, u32[]{:S(2)}) collective-permute-start(bf16[256,2048]{1,0:T(8,128)(2,1)} %multiply_convert_fusion.6), channel_id=1, source_target_pairs={{0,2},{1,3},{2,0},{3,1},{4,6},{5,7},{6,4},{7,5},{8,10},{9,11},{10,... | collective-permute-start | bytes 3145736 | tf_op jit(solution)/shard_map/ppermute | solution.py:26
  164.4 23.2 %collective-permute-start.16 = (bf16[256,2048]{1,0:T(8,128)(2,1)}, bf16[256,2048]{1,0:T(8,128)(2,1)}, u32[]{:S(2)}, u32[]{:S(2)}) collective-permute-start(bf16[256,2048]{1,0:T(8,128)(2,1)} %multiply_convert_fusion.6), channel_id=1, source_target_pairs={{0,1},{1,0},{2,3},{3,2},{4,5},{5,4},{6,7},{7,6},{8,9},{9,8},{10,11... | collective-permute-start | bytes 3145736 | tf_op jit(solution)/shard_map/ppermute | solution.py:26
  185.4 11.2 %collective-permute-start.18 = (bf16[128,2048]{1,0:T(8,128)(2,1)S(1)}, bf16[128,2048]{1,0:T(8,128)(2,1)S(1)}, u32[]{:S(2)}, u32[]{:S(2)}) collective-permute-start(bf16[128,2048]{1,0:T(8,128)(2,1)S(1)} %slice.455), channel_id=1, source_target_pairs={{0,1},{1,0},{2,3},{3,2},{4,5},{5,4},{6,7},{7,6},{8,9},{9,8},{10,11... | collective-permute-start | bytes 1572872 | tf_op jit(solution)/shard_map/ppermute | solution.py:26
  188.7 9.2 %collective-permute-start.19 = (bf16[128,2048]{1,0:T(8,128)(2,1)S(1)}, bf16[128,2048]{1,0:T(8,128)(2,1)S(1)}, u32[]{:S(2)}, u32[]{:S(2)}) collective-permute-start(bf16[128,2048]{1,0:T(8,128)(2,1)S(1)} %slice.456), channel_id=1, source_target_pairs={{0,2},{1,3},{2,0},{3,1},{4,6},{5,7},{6,4},{7,5},{8,10},{9,11},{10,... | collective-permute-start | bytes 1572872 | tf_op jit(solution)/shard_map/ppermute | solution.py:26
  197.9 16.4 %copy-start.55 = (bf16[1024,2048]{1,0:T(8,128)(2,1)}, bf16[1024,2048]{1,0:T(8,128)(2,1)S(1)}, u32[]{:S(2)}) copy-start(bf16[1024,2048]{1,0:T(8,128)(2,1)S(1)} %constant_dynamic-update-slice_fusion.10) | copy-start | bytes 12582916
  227.6 193.8 %reduce-scatter.6.cloned.1.call-start = ((), (), s32[]{:S(2)}) async-start(), calls=%async_computation.7 | async-start | bytes 8847360 | tf_op jit(solution)/shard_map/reduce_scatter | solution.py:83
  254.3 12.8 %copy-start.19 = (bf16[1024,640]{0,1:T(8,128)(2,1)}, bf16[1024,640]{0,1:T(8,128)(2,1)S(1)}, u32[]{:S(2)}) copy-start(bf16[1024,640]{0,1:T(8,128)(2,1)S(1)} %get-tuple-element.103) | copy-start | bytes 3932164
  254.3 12.8 %copy-start.21 = (bf16[1024,640]{0,1:T(8,128)(2,1)}, bf16[1024,640]{0,1:T(8,128)(2,1)S(1)}, u32[]{:S(2)}) copy-start(bf16[1024,640]{0,1:T(8,128)(2,1)S(1)} %get-tuple-element.104) | copy-start | bytes 3932164
  254.3 30.5 %copy-start.41 = (bf16[1024,640]{0,1:T(8,128)(2,1)}, bf16[1024,640]{0,1:T(8,128)(2,1)S(1)}, u32[]{:S(2)}) copy-start(bf16[1024,640]{0,1:T(8,128)(2,1)S(1)} %get-tuple-element.70) | copy-start | bytes 3932164
  263.9 20.7 %collective-permute-start.20 = (bf16[256,2048]{1,0:T(8,128)(2,1)S(1)}, bf16[256,2048]{1,0:T(8,128)(2,1)S(1)}, u32[]{:S(2)}, u32[]{:S(2)}) collective-permute-start(bf16[256,2048]{1,0:T(8,128)(2,1)S(1)} %pad_maximum_fusion.13), channel_id=1, source_target_pairs={{0,1},{1,0},{2,3},{3,2},{4,5},{5,4},{6,7},{7,6},{8,9},{9,8},{10,11... | collective-permute-start | bytes 3145736 | tf_op jit(solution)/shard_map/ppermute | solution.py:26
  265.6 19.2 %copy-start.54 = (bf16[1024,2048]{1,0:T(8,128)(2,1)S(1)}, bf16[1024,2048]{1,0:T(8,128)(2,1)}, u32[]{:S(2)}) copy-start(bf16[1024,2048]{1,0:T(8,128)(2,1)} %copy-done.52) | copy-start | bytes 12582916
  265.7 19.2 %collective-permute-start.21 = (bf16[256,2048]{1,0:T(8,128)(2,1)S(1)}, bf16[256,2048]{1,0:T(8,128)(2,1)}, u32[]{:S(2)}, u32[]{:S(2)}) collective-permute-start(bf16[256,2048]{1,0:T(8,128)(2,1)S(1)} %pad_maximum_fusion.14), channel_id=1, source_target_pairs={{0,2},{1,3},{2,0},{3,1},{4,6},{5,7},{6,4},{7,5},{8,10},{9,11},{10,... | collective-permute-start | bytes 3145736 | tf_op jit(solution)/shard_map/ppermute | solution.py:26
  304.2 172.1 %reduce-scatter.8.cloned.1.call-start = ((), (), s32[]{:S(2)}) async-start(), calls=%async_computation.8 | async-start | bytes 5013504 | tf_op jit(solution)/shard_map/reduce_scatter | solution.py:83
  304.7 10.7 %slice-start.2 = ((s8[7864320]{0:T(1024)(128)(4,1)}), s8[4194304]{0:T(1024)(128)(4,1)S(1)}, s32[]{:S(2)}) async-start(s8[7864320]{0:T(1024)(128)(4,1)} %bitcast.102), calls=%async_computation.11 | async-start | bytes 8388608
  308.1 9.2 %collective-permute-start.22 = (bf16[128,2048]{1,0:T(8,128)(2,1)S(1)}, bf16[128,2048]{1,0:T(8,128)(2,1)S(1)}, u32[]{:S(2)}, u32[]{:S(2)}) collective-permute-start(bf16[128,2048]{1,0:T(8,128)(2,1)S(1)} %get-tuple-element.121), channel_id=1, source_target_pairs={{0,2},{1,3},{2,0},{3,1},{4,6},{5,7},{6,4},{7,5},{8,10},{9,11},{10,... | collective-permute-start | bytes 1572872 | tf_op jit(solution)/shard_map/ppermute | solution.py:26
  308.8 9.2 %collective-permute-start.23 = (bf16[128,2048]{1,0:T(8,128)(2,1)S(1)}, bf16[128,2048]{1,0:T(8,128)(2,1)S(1)}, u32[]{:S(2)}, u32[]{:S(2)}) collective-permute-start(bf16[128,2048]{1,0:T(8,128)(2,1)S(1)} %get-tuple-element.122), channel_id=1, source_target_pairs={{0,1},{1,0},{2,3},{3,2},{4,5},{5,4},{6,7},{7,6},{8,9},{9,8},{10,11... | collective-permute-start | bytes 1572872 | tf_op jit(solution)/shard_map/ppermute | solution.py:26
  323.5 20.9 %collective-permute-start.25 = (bf16[256,2048]{1,0:T(8,128)(2,1)}, bf16[256,2048]{1,0:T(8,128)(2,1)S(1)}, u32[]{:S(2)}, u32[]{:S(2)}) collective-permute-start(bf16[256,2048]{1,0:T(8,128)(2,1)} %get-tuple-element.99), channel_id=1, source_target_pairs={{0,2},{1,3},{2,0},{3,1},{4,6},{5,7},{6,4},{7,5},{8,10},{9,11},{10,... | collective-permute-start | bytes 3145736 | tf_op jit(solution)/shard_map/ppermute | solution.py:26
  325.0 24.5 %collective-permute-start.24 = (bf16[256,2048]{1,0:T(8,128)(2,1)}, bf16[256,2048]{1,0:T(8,128)(2,1)}, u32[]{:S(2)}, u32[]{:S(2)}) collective-permute-start(bf16[256,2048]{1,0:T(8,128)(2,1)} %get-tuple-element.99), channel_id=1, source_target_pairs={{0,1},{1,0},{2,3},{3,2},{4,5},{5,4},{6,7},{7,6},{8,9},{9,8},{10,11... | collective-permute-start | bytes 3145736 | tf_op jit(solution)/shard_map/ppermute | solution.py:26
  326.8 23.9 %copy-start.42 = (bf16[1024,640]{0,1:T(8,128)(2,1)S(1)}, bf16[1024,640]{0,1:T(8,128)(2,1)}, u32[]{:S(2)}) copy-start(bf16[1024,640]{0,1:T(8,128)(2,1)} %copy-done.41) | copy-start | bytes 3932164
  344.5 13.4 %collective-permute-start.26 = (bf16[128,2048]{1,0:T(8,128)(2,1)S(1)}, bf16[128,2048]{1,0:T(8,128)(2,1)S(1)}, u32[]{:S(2)}, u32[]{:S(2)}) collective-permute-start(bf16[128,2048]{1,0:T(8,128)(2,1)S(1)} %slice.586), channel_id=1, source_target_pairs={{0,1},{1,0},{2,3},{3,2},{4,5},{5,4},{6,7},{7,6},{8,9},{9,8},{10,11... | collective-permute-start | bytes 1572872 | tf_op jit(solution)/shard_map/ppermute | solution.py:26
  350.6 13.4 %collective-permute-start.27 = (bf16[128,2048]{1,0:T(8,128)(2,1)S(1)}, bf16[128,2048]{1,0:T(8,128)(2,1)S(1)}, u32[]{:S(2)}, u32[]{:S(2)}) collective-permute-start(bf16[128,2048]{1,0:T(8,128)(2,1)S(1)} %slice.587), channel_id=1, source_target_pairs={{0,2},{1,3},{2,0},{3,1},{4,6},{5,7},{6,4},{7,5},{8,10},{9,11},{10,... | collective-permute-start | bytes 1572872 | tf_op jit(solution)/shard_map/ppermute | solution.py:26
  355.7 8.5 %copy-start.31 = (bf16[768,2048]{1,0:T(8,128)(2,1)}, bf16[768,2048]{1,0:T(8,128)(2,1)S(1)}, u32[]{:S(2)}) copy-start(bf16[768,2048]{1,0:T(8,128)(2,1)S(1)} %add_convert_fusion) | copy-start | bytes 9437188
  365.3 28.3 %collective-permute-start.28 = (bf16[256,2048]{1,0:T(8,128)(2,1)}, bf16[256,2048]{1,0:T(8,128)(2,1)}, u32[]{:S(2)}, u32[]{:S(2)}) collective-permute-start(bf16[256,2048]{1,0:T(8,128)(2,1)} %pad_maximum_fusion.15), channel_id=1, source_target_pairs={{0,1},{1,0},{2,3},{3,2},{4,5},{5,4},{6,7},{7,6},{8,9},{9,8},{10,11... | collective-permute-start | bytes 3145736 | tf_op jit(solution)/shard_map/ppermute | solution.py:26
  368.7 24.9 %collective-permute-start.29 = (bf16[256,2048]{1,0:T(8,128)(2,1)}, bf16[256,2048]{1,0:T(8,128)(2,1)}, u32[]{:S(2)}, u32[]{:S(2)}) collective-permute-start(bf16[256,2048]{1,0:T(8,128)(2,1)} %pad_maximum_fusion.16), channel_id=1, source_target_pairs={{0,2},{1,3},{2,0},{3,1},{4,6},{5,7},{6,4},{7,5},{8,10},{9,11},{10,... | collective-permute-start | bytes 3145736 | tf_op jit(solution)/shard_map/ppermute | solution.py:26
  398.1 12.3 %collective-permute-start.32 = (bf16[512,256]{1,0:T(8,128)(2,1)S(1)}, bf16[512,256]{1,0:T(8,128)(2,1)S(1)}, u32[]{:S(2)}, u32[]{:S(2)}) collective-permute-start(bf16[512,256]{1,0:T(8,128)(2,1)S(1)} %pad_maximum_fusion.30), channel_id=1, source_target_pairs={{0,2},{1,3},{2,0},{3,1},{4,6},{5,7},{6,4},{7,5},{8,10},{9,11},{10,... | collective-permute-start | bytes 786440 | tf_op jit(solution)/shard_map/ppermute | solution.py:26
  400.1 12.3 %collective-permute-start.30 = (bf16[512,256]{1,0:T(8,128)(2,1)S(1)}, bf16[512,256]{1,0:T(8,128)(2,1)S(1)}, u32[]{:S(2)}, u32[]{:S(2)}) collective-permute-start(bf16[512,256]{1,0:T(8,128)(2,1)S(1)} %pad_maximum_fusion.29), channel_id=1, source_target_pairs={{0,1},{1,0},{2,3},{3,2},{4,5},{5,4},{6,7},{7,6},{8,9},{9,8},{10,11... | collective-permute-start | bytes 786440 | tf_op jit(solution)/shard_map/ppermute | solution.py:26
  410.2 7.5 %copy-start.36 = (bf16[2048,512]{1,0:T(8,128)(2,1)S(1)}, bf16[2048,512]{1,0:T(8,128)(2,1)}, u32[]{:S(2)}) copy-start(bf16[2048,512]{1,0:T(8,128)(2,1)} %convolution_convert_fusion.6) | copy-start | bytes 6291460
  410.4 5.0 %collective-permute-start.33 = (bf16[256,256]{1,0:T(8,128)(2,1)S(1)}, bf16[256,256]{1,0:T(8,128)(2,1)S(1)}, u32[]{:S(2)}, u32[]{:S(2)}) collective-permute-start(bf16[256,256]{1,0:T(8,128)(2,1)S(1)} %fusion.73), channel_id=1, source_target_pairs={{0,1},{1,0},{2,3},{3,2},{4,5},{5,4},{6,7},{7,6},{8,9},{9,8},{10,11... | collective-permute-start | bytes 393224 | tf_op jit(solution)/shard_map/ppermute | solution.py:26
  412.5 5.0 %collective-permute-start.31 = (bf16[256,256]{1,0:T(8,128)(2,1)S(1)}, bf16[256,256]{1,0:T(8,128)(2,1)S(1)}, u32[]{:S(2)}, u32[]{:S(2)}) collective-permute-start(bf16[256,256]{1,0:T(8,128)(2,1)S(1)} %fusion.74), channel_id=1, source_target_pairs={{0,2},{1,3},{2,0},{3,1},{4,6},{5,7},{6,4},{7,5},{8,10},{9,11},{10,... | collective-permute-start | bytes 393224 | tf_op jit(solution)/shard_map/ppermute | solution.py:26
  424.2 20.6 %collective-permute-start.34 = (bf16[256,2048]{1,0:T(8,128)(2,1)}, bf16[256,2048]{1,0:T(8,128)(2,1)}, u32[]{:S(2)}, u32[]{:S(2)}) collective-permute-start(bf16[256,2048]{1,0:T(8,128)(2,1)} %pad_maximum_fusion.17), channel_id=1, source_target_pairs={{0,1},{1,0},{2,3},{3,2},{4,5},{5,4},{6,7},{7,6},{8,9},{9,8},{10,11... | collective-permute-start | bytes 3145736 | tf_op jit(solution)/shard_map/ppermute | solution.py:26
  425.3 21.8 %collective-permute-start.35 = (bf16[256,2048]{1,0:T(8,128)(2,1)}, bf16[256,2048]{1,0:T(8,128)(2,1)}, u32[]{:S(2)}, u32[]{:S(2)}) collective-permute-start(bf16[256,2048]{1,0:T(8,128)(2,1)} %pad_maximum_fusion.18), channel_id=1, source_target_pairs={{0,2},{1,3},{2,0},{3,1},{4,6},{5,7},{6,4},{7,5},{8,10},{9,11},{10,... | collective-permute-start | bytes 3145736 | tf_op jit(solution)/shard_map/ppermute | solution.py:26
  450.0 14.2 %collective-permute-start.38 = (bf16[128,2048]{1,0:T(8,128)(2,1)}, bf16[128,2048]{1,0:T(8,128)(2,1)}, u32[]{:S(2)}, u32[]{:S(2)}) collective-permute-start(bf16[128,2048]{1,0:T(8,128)(2,1)} %get-tuple-element.109), channel_id=1, source_target_pairs={{0,2},{1,3},{2,0},{3,1},{4,6},{5,7},{6,4},{7,5},{8,10},{9,11},{10,... | collective-permute-start | bytes 1572872 | tf_op jit(solution)/shard_map/ppermute | solution.py:26
  451.5 12.7 %collective-permute-start.39 = (bf16[128,2048]{1,0:T(8,128)(2,1)}, bf16[128,2048]{1,0:T(8,128)(2,1)}, u32[]{:S(2)}, u32[]{:S(2)}) collective-permute-start(bf16[128,2048]{1,0:T(8,128)(2,1)} %get-tuple-element.110), channel_id=1, source_target_pairs={{0,1},{1,0},{2,3},{3,2},{4,5},{5,4},{6,7},{7,6},{8,9},{9,8},{10,11... | collective-permute-start | bytes 1572872 | tf_op jit(solution)/shard_map/ppermute | solution.py:26
  462.1 9.2 %collective-permute-start.36 = (bf16[128,2048]{1,0:T(8,128)(2,1)S(1)}, bf16[128,2048]{1,0:T(8,128)(2,1)S(1)}, u32[]{:S(2)}, u32[]{:S(2)}) collective-permute-start(bf16[128,2048]{1,0:T(8,128)(2,1)S(1)} %get-tuple-element.111), channel_id=1, source_target_pairs={{0,2},{1,3},{2,0},{3,1},{4,6},{5,7},{6,4},{7,5},{8,10},{9,11},{10,... | collective-permute-start | bytes 1572872 | tf_op jit(solution)/shard_map/ppermute | solution.py:26
  462.7 9.6 %collective-permute-start.37 = (bf16[128,2048]{1,0:T(8,128)(2,1)S(1)}, bf16[128,2048]{1,0:T(8,128)(2,1)S(1)}, u32[]{:S(2)}, u32[]{:S(2)}) collective-permute-start(bf16[128,2048]{1,0:T(8,128)(2,1)S(1)} %get-tuple-element.112), channel_id=1, source_target_pairs={{0,1},{1,0},{2,3},{3,2},{4,5},{5,4},{6,7},{7,6},{8,9},{9,8},{10,11... | collective-permute-start | bytes 1572872 | tf_op jit(solution)/shard_map/ppermute | solution.py:26
  480.9 4.6 collective-permute-start.41
  482.0 4.6 collective-permute-start.40
  483.5 5.5 %collective-permute-start.42 = (f32[64,265]{1,0:T(8,128)S(1)}, f32[64,265]{1,0:T(8,128)S(1)}, u32[]{:S(2)}, u32[]{:S(2)}) collective-permute-start(f32[64,265]{1,0:T(8,128)S(1)} %pad_maximum_fusion.32), channel_id=1, source_target_pairs={{0,3},{1,2},{2,1},{3,0},{4,7},{5,6},{6,5},{7,4},{8,11},{9,10},{10,... | collective-permute-start | bytes 203528 | tf_op jit(solution)/shard_map/ppermute | solution.py:26
  (60 other events, 252.9 us)
Sparse Core Ops, SparseCore 0:
  11.4 51.7 all-gather.3
  65.4 89.4 all-gather.5
  157.1 76.1 all-gather.7
  235.5 97.9 reduce-scatter.3
  335.6 83.0 reduce-scatter.5
  421.5 50.1 reduce-scatter.7

commit v10 on v9

--- a/solution.py
+++ b/solution.py
@@ -510,18 +510,11 @@
         dot(after(h[:rows], attn_partial), w, 1, 1) for h, w in zip(hidden, downs)
     )
     after_mlp = after_attn + finish_sums(own_down, down_rest, down_sent)
-    output = (after_mlp * own_mask).astype(bf16)
     scaled_one = finish_sums(dot(qkv_back[:rows], qkv_full, 1, 1), qkv_rest, qkv_sent)
-    inv_one = inverse_norm(residual)
-    unit_one = residual * inv_one
-    input_grad = attn_top + inv_one * (
-        scaled_one - unit_one * jnp.mean(scaled_one * unit_one, axis=-1, keepdims=True)
-    )
-
     grad_gate, grad_up, grad_down, gain_two_part = finish_ff(
         parts, ff_sums, w_gate, w_up, gain_two
     )
-    attn_sum = after(attn_sum, output, input_grad, gain_two_part)
+    attn_sum = after(attn_sum, scaled_one, gain_two_part)
     grad_query, grad_project, query_part = finish_attn(attn_sum, w_query, gain_one)
     kv_sum = attn_sum[2 * shard_rows :].astype(f32).reshape(kv_rows, 2 * HD)
     kv_here = lax.dynamic_slice_in_dim(qkv_own[:, heads_width:], rank * kv_rows, kv_rows)
@@ -533,6 +526,13 @@
             jnp.concatenate([query_part, gain_two_part], axis=1).reshape(kv_rows, -1),
         ],
         axis=1,
+    )
+    scaled_one, after_mlp = after(scaled_one, small), after(after_mlp, small)
+    output = (after_mlp * own_mask).astype(bf16)
+    inv_one = inverse_norm(residual)
+    unit_one = residual * inv_one
+    input_grad = attn_top + inv_one * (
+        scaled_one - unit_one * jnp.mean(scaled_one * unit_one, axis=-1, keepdims=True)
     )
     blocks = jnp.stack([small] + [hop(small, j) for j in range(1, ranks)], axis=0)
     sums = jnp.sum(blocks[:, :, 2 * HD + 1 :], axis=0).reshape(shard_rows, 2)

time: 507 us -> 510 us (level)
  other arithmetic: 74.9 us -> 82.8 us
  waiting for transfers between devices: 136 us -> 129 us
    ppermute x43, waiting for transfers between devices: 128 us -> 122 us  [hop(): return lax.ppermute(value, 'tensor', [(i, i ^ step) for i in range(size)])]
  transfers between devices with their start and end apart: 49 -> 49, of which waited for: 31 -> 28; matrix products, arithmetic and copies ran while one was open for 48% -> 49% of each run, Pallas kernels for 6% -> 6%
where the time goes in v10:
time: 510 us; the launch traced here: 500 us
  matrix products  132 us (26%)
  waiting for transfers between devices  129 us (25%)
  other arithmetic  82.8 us (16%)
  starting transfers between devices  52 us (10%)
  local copies, waits for them, and re-layouts  48 us (9%)
  Pallas kernels  31.4 us (6%)
  between operations  24.5 us (5%)
    dot_general x25, matrix products, dot(): lax.dot_general(a, b, (((ca,), (cb,)), ((), ())), preferred_element_type=...  132 us
    ppermute x43, waiting for transfers between devices, hop(): return lax.ppermute(value, 'tensor', [(i, i ^ step) for i in range(size)])  122 us
    ppermute x43, starting transfers between devices, hop(): return lax.ppermute(value, 'tensor', [(i, i ^ step) for i in range(size)])  50.6 us
    unnamed x157, local copies, waits for them, and re-layouts  21.2 us
    pallas_call x1, Pallas kernels, attend_back(): pl.pallas_call(attend_back_kernel, name='attend_back', grid_spec=pltpu.Pr...  13.7 us
    concatenate x2, other arithmetic, partial(): jnp.concatenate([dot(normed_two, grads, 0, 0).astype(bf16), dot(top_all,...  11.7 us
    pallas_call x1, Pallas kernels, attend(): pl.pallas_call(attend_kernel, name='attend', grid_spec=pltpu.PrefetchScal...  11.4 us
  transfers between devices with their start and end apart: 49, of which 28 were waited for; matrix products, arithmetic and copies ran while one was open for 49% of the time, Pallas kernels for 6%

profile of v10, /device:TPU:0, one launch (start us, length us, event | category | flops | bytes accessed | tf_op | source)
XLA Modules:
  0.0 500.2 jit_solution(809693465199885033)
XLA Ops:
  11.3 3.1 collective-permute-start.1
  22.1 3.1 fusion.79
  29.1 2.1 pad_maximum_fusion.9
  35.1 2.4 collective-permute-done.1
  43.9 2.4 fusion.52
  47.5 3.3 collective-permute-done.2
  51.0 2.1 collective-permute-done.3
  55.5 7.7 %all-gather.4.cloned.1.call-done = bf16[4352,512]{1,0:T(8,128)(2,1)} async-done(((bf16[544,512]{1,0:T(8,128)(2,1)}), bf16[4352,512]{1,0:T(8,128)(2,1)}) %all-gather.4.cloned.1.call-update) | async-done | bytes 4456464 | tf_op jit(solution)/shard_map/all_gather | solution.py:79
  77.1 3.8 collective-permute-done.6
  87.1 7.4 %fusion.64.q_ref.kv_ref = f32[1024,768]{1,0:T(8,128)} fusion(bf16[1024,2048]{1,0:T(8,128)(2,1)} %fusion.67, bf16[2048,256]{1,0:T(8,128)(2,1)S(1)} %bitcast.113, bf16[2048,512]{1,0:T(8,128)(2,1)S(1)} %bitcast.108), kind=kOutput, calls=%fused_computation.142 | convolution fusion | flops 3227516928 | bytes 10485760 | tf_op jit(solution)/shard_map/dot_general | solution.py:21
  94.5 11.4 %attend.1 = (bf16[1024,512]{1,0:T(8,128)(2,1)S(1)}, bf16[1024,256]{1,0:T(8,128)(2,1)S(1)}, bf16[1024,512]{1,0:T(8,128)(2,1)S(1)}, f32[1024,128]{1,0:T(8,128)S(1)}) custom-call(s32[2]{0:T(128)S(1)} %pad_add_fusion.where_ref, f32[1024,768]{1,0:T(8,128)} %fusion.64.q_ref.kv_ref, f32[1024,768]{1,0:T(8,128)} %fusion.64.q_ref.kv_ref, ...), custom_call_target="tpu_custom_call" | custom-call | flops 2147483648 | bytes 8388608 | tf_op jit(solution)/shard_map/attend/pallas_call | solution.py:202
  109.0 3.7 convolution_convert_fusion.2
  116.0 20.3 %collective-permute-done.12 = bf16[256,2048]{1,0:T(8,128)(2,1)S(1)} collective-permute-done((bf16[256,2048]{1,0:T(8,128)(2,1)S(1)}, bf16[256,2048]{1,0:T(8,128)(2,1)S(1)}, u32[]{:S(2)}, u32[]{:S(2)}) %collective-permute-start.12) | collective-permute-done | bytes 1048608 | tf_op jit(solution)/shard_map/ppermute | solution.py:26
  148.3 4.6 collective-permute-done.11
  154.3 6.2 %collective-permute-done.14 = bf16[128,2048]{1,0:T(8,128)(2,1)S(1)} collective-permute-done((bf16[128,2048]{1,0:T(8,128)(2,1)S(1)}, bf16[128,2048]{1,0:T(8,128)(2,1)S(1)}, u32[]{:S(2)}, u32[]{:S(2)}) %collective-permute-start.14) | collective-permute-done | bytes 524320 | tf_op jit(solution)/shard_map/ppermute | solution.py:26
  165.1 6.3 %fusion.26 = f32[1024,768]{0,1:T(8,128)S(1)} fusion(bf16[1024,2048]{1,0:T(8,128)(2,1)} %copy-done.53, bf16[2048,2304]{1,0:T(8,128)(2,1)} %all-gather.6.cloned.1.call-done), kind=kOutput, calls=%fused_computation.60 | convolution fusion | flops 3221225472 | bytes 10485760 | tf_op jit(solution)/shard_map/dot_general | solution.py:21
  171.4 13.0 %collective-permute-done.17 = bf16[256,2048]{1,0:T(8,128)(2,1)} collective-permute-done((bf16[256,2048]{1,0:T(8,128)(2,1)}, bf16[256,2048]{1,0:T(8,128)(2,1)}, u32[]{:S(2)}, u32[]{:S(2)}) %collective-permute-start.17) | collective-permute-done | bytes 1048608 | tf_op jit(solution)/shard_map/ppermute | solution.py:26
  192.8 3.8 collective-permute-done.18
  198.0 10.4 %fusion.4 = f32[1024,1536]{0,1:T(8,128)S(1)} fusion(bf16[1024,2048]{1,0:T(8,128)(2,1)S(1)} %constant_dynamic-update-slice_fusion.10, bf16[2048,2304]{1,0:T(8,128)(2,1)} %all-gather.6.cloned.1.call-done), kind=kOutput, calls=%fused_computation.10 | convolution fusion | flops 6442450944 | bytes 16777216 | tf_op jit(solution)/shard_map/dot_general | solution.py:21
  208.4 2.1 multiply_convert_fusion.1
  210.5 3.8 convolution_convert_fusion.4
  214.3 8.6 %convolution_convert_fusion.1 = bf16[2048,1536]{1,0:T(8,128)(2,1)S(1)} fusion(bf16[1024,2048]{1,0:T(8,128)(2,1)S(1)} %constant_dynamic-update-slice_fusion.10, bf16[1024,768]{0,1:T(8,128)(2,1)S(1)} %get-tuple-element.106, bf16[1024,768]{0,1:T(8,128)(2,1)S(1)} %get-tuple-element.105), kind=kOutput, calls=%fused_computation.3 | convolution fusion | flops 6451888128 | bytes 13631488 | tf_op jit(solution)/shard_map/dot_general | solution.py:21
  223.0 4.6 pad_maximum_fusion
  229.6 9.9 %fusion.2 = f32[768,2048]{1,0:T(8,128)} fusion(bf16[768,1536]{0,1:T(8,128)(2,1)S(1)} %pad_maximum_fusion.5, bf16[2048,2304]{1,0:T(8,128)(2,1)} %all-gather.6.cloned.1.call-done), kind=kOutput, calls=%fused_computation.8 | convolution fusion | flops 4831838208 | bytes 14942208 | tf_op jit(solution)/shard_map/dot_general | solution.py:21
  239.5 6.1 %fusion.42 = f32[1024,640]{0,1:T(8,128)S(1)} fusion(bf16[1024,2048]{1,0:T(8,128)(2,1)} %copy-done.53, bf16[2048,1920]{1,0:T(8,128)(2,1)} %all-gather.8.cloned.1.call-done), kind=kOutput, calls=%fused_computation.85 | convolution fusion | flops 2684354560 | bytes 9437184 | tf_op jit(solution)/shard_map/dot_general | solution.py:21
  246.4 6.0 %fusion.10 = f32[1024,1280]{0,1:T(8,128)S(1)} fusion(bf16[1024,2048]{1,0:T(8,128)(2,1)S(1)} %copy-done.57, bf16[2048,1920]{1,0:T(8,128)(2,1)S(1)} %copy-done.27), kind=kOutput, calls=%fused_computation.17 | convolution fusion | flops 5368709120 | bytes 14680064 | tf_op jit(solution)/shard_map/dot_general | solution.py:21
  254.3 7.9 %add_convert_fusion.1 = bf16[768,2048]{1,0:T(8,128)(2,1)S(1)} fusion(f32[768,2048]{1,0:T(8,128)} %fusion.2, bf16[2048,1920]{1,0:T(8,128)(2,1)S(1)} %copy-done.27, bf16[1024,640]{0,1:T(8,128)(2,1)S(1)} %get-tuple-element.108, bf16[1024,640]{0,1:T(8,128)(2,1)S(1)} %get-tuple-element.107), kind=kOutput, calls=%fused_computation.5 | convolution fusion | flops 4033609728 | bytes 17301504 | tf_op jit(solution)/shard_map/dot_general | solution.py:21
  267.4 17.2 %collective-permute-done.20 = bf16[256,2048]{1,0:T(8,128)(2,1)S(1)} collective-permute-done((bf16[256,2048]{1,0:T(8,128)(2,1)S(1)}, bf16[256,2048]{1,0:T(8,128)(2,1)S(1)}, u32[]{:S(2)}, u32[]{:S(2)}) %collective-permute-start.20) | collective-permute-done | bytes 1048608 | tf_op jit(solution)/shard_map/ppermute | solution.py:26
  284.9 4.8 convolution_convert_fusion.5
  289.7 7.4 %convolution_convert_fusion = bf16[2048,1280]{1,0:T(8,128)(2,1)} fusion(bf16[1024,2048]{1,0:T(8,128)(2,1)S(1)} %copy-done.58, bf16[1024,1280]{0,1:T(8,128)(2,1)S(1)} %pad_maximum_fusion.3), kind=kOutput, calls=%fused_computation.2 | convolution fusion | flops 5371330560 | bytes 12058624 | tf_op jit(solution)/shard_map/dot_general | solution.py:21
  297.1 7.1 %pad_maximum_fusion.1 = bf16[2048,1920]{1,0:T(8,128)(2,1)} fusion(bf16[2048,640]{1,0:T(8,128)(2,1)} %convolution_convert_fusion.5, bf16[2048,1280]{1,0:T(8,128)(2,1)} %convolution_convert_fusion), kind=kLoop, calls=%fused_computation.1 | loop fusion | flops 15728640 | bytes 15728640 | tf_op jit(solution)/shard_map/concatenate | solution.py:455
  306.0 2.1 add_convert_fusion.7
  310.3 5.1 %fusion = f32[256,2048]{1,0:T(8,128)S(1)} fusion(bf16[256,1536]{0,1:T(8,128)(2,1)S(1)} %pad_maximum_fusion.23, bf16[2048,2304]{1,0:T(8,128)(2,1)} %all-gather.6.cloned.1.call-done), kind=kOutput, calls=%fused_computation.6 | convolution fusion | flops 1610612736 | bytes 9175040 | tf_op jit(solution)/shard_map/dot_general | solution.py:21
  320.7 2.8 constant_dynamic-update-slice_fusion.19
  326.8 5.0 %fusion.24 = f32[768,2048]{1,0:T(8,128)S(1)} fusion(bf16[2048,2304]{1,0:T(8,128)(2,1)} %all-gather.6.cloned.1.call-done, bf16[1024,768]{0,1:T(8,128)(2,1)} %copy-done.34), kind=kOutput, calls=%fused_computation.58 | convolution fusion | flops 2415919104 | bytes 10616832 | tf_op jit(solution)/shard_map/dot_general | solution.py:21
  331.8 12.7 %collective-permute-done.25 = bf16[256,2048]{1,0:T(8,128)(2,1)S(1)} collective-permute-done((bf16[256,2048]{1,0:T(8,128)(2,1)}, bf16[256,2048]{1,0:T(8,128)(2,1)S(1)}, u32[]{:S(2)}, u32[]{:S(2)}) %collective-permute-start.25) | collective-permute-done | bytes 1048608 | tf_op jit(solution)/shard_map/ppermute | solution.py:26
  346.4 3.2 collective-permute-done.24
  350.7 5.0 add_convert_fusion
  355.7 2.1 constant_dynamic-update-slice_fusion.18
  357.9 6.1 %collective-permute-done.27 = bf16[128,2048]{1,0:T(8,128)(2,1)S(1)} collective-permute-done((bf16[128,2048]{1,0:T(8,128)(2,1)S(1)}, bf16[128,2048]{1,0:T(8,128)(2,1)S(1)}, u32[]{:S(2)}, u32[]{:S(2)}) %collective-permute-start.27) | collective-permute-done | bytes 524320 | tf_op jit(solution)/shard_map/ppermute | solution.py:26
  365.3 2.4 collective-permute-start.28
  370.8 3.7 convolution_convert_fusion.6
  374.5 5.3 %convolution_convert_fusion.9.dm_ref = bf16[1024,512]{1,0:T(8,128)(2,1)S(1)} fusion(bf16[1024,2048]{1,0:T(8,128)(2,1)} %copy-done.52, bf16[2048,512]{1,0:T(8,128)(2,1)} %bitcast.100), kind=kOutput, calls=%fused_computation.91 | convolution fusion | flops 2148007936 | bytes 7340032 | tf_op jit(solution)/shard_map/dot_general | solution.py:21
  379.9 13.7 %attend_back.1 = (bf16[1024,512]{1,0:T(8,128)(2,1)S(1)}, bf16[1024,256]{1,0:T(8,128)(2,1)S(1)}) custom-call(s32[2]{0:T(128)S(1)} %copy-done.3, bf16[1024,512]{1,0:T(8,128)(2,1)S(1)} %get-tuple-element.65.qr_ref, bf16[1024,256]{1,0:T(8,128)(2,1)S(1)} %copy-done.5, bf16[1024,512]{1,0:T(8,128)(2,1)S(1)} %convolution_convert_fusion.9.dm_ref, ...), custom_call_target="tpu_custom_call" | custom-call | flops 5368709120 | bytes 8388608 | tf_op jit(solution)/shard_map/attend_back/pallas_call | solution.py:240
  393.8 4.2 convolution_convert_fusion.8
  398.1 2.0 collective-permute-start.32
  400.2 4.0 convolution_convert_fusion.3
  404.3 6.0 %convolution_convert_fusion.7 = bf16[2048,512]{1,0:T(8,128)(2,1)} fusion(bf16[1024,2048]{1,0:T(8,128)(2,1)} %fusion.67, bf16[1024,512]{1,0:T(8,128)(2,1)S(1)} %slice-done), kind=kOutput, calls=%fused_computation.40 | convolution fusion | flops 2148532224 | bytes 7340032 | tf_op jit(solution)/shard_map/dot_general | solution.py:21
  410.4 2.0 collective-permute-start.33
  412.6 2.9 collective-permute-done.33
  415.5 2.0 collective-permute-done.31
  417.7 3.6 pad_maximum_fusion.2
  431.2 3.6 fusion.63
  434.8 3.0 fusion.22
  437.7 7.1 %collective-permute-done.34 = bf16[256,2048]{1,0:T(8,128)(2,1)} collective-permute-done((bf16[256,2048]{1,0:T(8,128)(2,1)}, bf16[256,2048]{1,0:T(8,128)(2,1)}, u32[]{:S(2)}, u32[]{:S(2)}) %collective-permute-start.34) | collective-permute-done | bytes 1048608 | tf_op jit(solution)/shard_map/ppermute | solution.py:26
  444.8 2.3 collective-permute-done.35
  447.1 2.7 add_convert_fusion.3
  451.9 2.8 convolution_add_fusion
  454.7 4.1 finish_ff.1
  459.8 2.1 add_convert_fusion.5
  468.3 2.9 collective-permute-done.36
  471.9 3.0 fusion.57
  476.8 2.3 finish_attn.1
  485.9 4.1 fusion.31
  (378 shorter events, 137.6 us)
Async XLA Ops:
  7.2 8.7 %copy-start.33 = (bf16[256,1408]{1,0:T(8,128)(2,1)S(1)}, bf16[256,1408]{1,0:T(8,128)(2,1)}, u32[]{:S(2)}) copy-start(bf16[256,1408]{1,0:T(8,128)(2,1)} %gate_ref.1) | copy-start | bytes 2162692
  7.2 56.0 %all-gather.4.cloned.1.call-start = ((), (), s32[]{:S(2)}) async-start(), calls=%async_computation.3 | async-start | bytes 5013504 | tf_op jit(solution)/shard_map/all_gather | solution.py:79
  9.2 8.8 %copy-start.66 = (bf16[256]{0:T(256)(128)(2,1)S(1)}, bf16[256]{0:T(256)(128)(2,1)}, u32[]{:S(2)}) copy-start(bf16[256]{0:T(256)(128)(2,1)} %param.21) | copy-start | bytes 1540
  11.3 153.8 %all-gather.6.cloned.1.call-start = ((), (), s32[]{:S(2)}) async-start(), calls=%async_computation.4 | async-start | bytes 10616832 | tf_op jit(solution)/shard_map/all_gather | solution.py:79
  11.3 26.2 %collective-permute-start.1 = (bf16[256,2048]{1,0:T(8,128)(2,1)S(1)}, bf16[256,2048]{1,0:T(8,128)(2,1)S(1)}, u32[]{:S(2)}, u32[]{:S(2)}) collective-permute-start(bf16[256,2048]{1,0:T(8,128)(2,1)S(1)} %copy-done.8), channel_id=1, source_target_pairs={{0,2},{1,3},{2,0},{3,1},{4,6},{5,7},{6,4},{7,5},{8,10},{9,11},{10,... | collective-permute-start | bytes 3145736 | tf_op jit(solution)/shard_map/ppermute | solution.py:26
  14.4 25.0 %collective-permute-start = (bf16[256,2048]{1,0:T(8,128)(2,1)S(1)}, bf16[256,2048]{1,0:T(8,128)(2,1)}, u32[]{:S(2)}, u32[]{:S(2)}) collective-permute-start(bf16[256,2048]{1,0:T(8,128)(2,1)S(1)} %copy-done.8), channel_id=1, source_target_pairs={{0,1},{1,0},{2,3},{3,2},{4,5},{5,4},{6,7},{7,6},{8,9},{9,8},{10,11... | collective-permute-start | bytes 3145736 | tf_op jit(solution)/shard_map/ppermute | solution.py:26
  18.1 9.8 %copy-start.62 = (f32[256]{0:T(256)}, f32[256]{0:T(256)S(1)}, u32[]{:S(2)}) copy-start(f32[256]{0:T(256)S(1)} %convert_element_type.349) | copy-start | bytes 3076
  37.6 13.3 %collective-permute-start.2 = (bf16[128,2048]{1,0:T(8,128)(2,1)S(1)}, bf16[128,2048]{1,0:T(8,128)(2,1)S(1)}, u32[]{:S(2)}, u32[]{:S(2)}) collective-permute-start(bf16[128,2048]{1,0:T(8,128)(2,1)S(1)} %slice.541), channel_id=1, source_target_pairs={{0,1},{1,0},{2,3},{3,2},{4,5},{5,4},{6,7},{7,6},{8,9},{9,8},{10,11... | collective-permute-start | bytes 1572872 | tf_op jit(solution)/shard_map/ppermute | solution.py:26
  40.5 12.7 %collective-permute-start.3 = (bf16[128,2048]{1,0:T(8,128)(2,1)S(1)}, bf16[128,2048]{1,0:T(8,128)(2,1)S(1)}, u32[]{:S(2)}, u32[]{:S(2)}) collective-permute-start(bf16[128,2048]{1,0:T(8,128)(2,1)S(1)} %slice.542), channel_id=1, source_target_pairs={{0,2},{1,3},{2,0},{3,1},{4,6},{5,7},{6,4},{7,5},{8,10},{9,11},{10,... | collective-permute-start | bytes 1572872 | tf_op jit(solution)/shard_map/ppermute | solution.py:26
  55.3 184.2 %all-gather.8.cloned.1.call-start = ((), (), s32[]{:S(2)}) async-start(), calls=%async_computation.5 | async-start | bytes 8847360 | tf_op jit(solution)/shard_map/all_gather | solution.py:79
  64.3 11.5 %collective-permute-start.5 = (bf16[512,256]{1,0:T(8,128)(2,1)S(1)}, bf16[512,256]{1,0:T(8,128)(2,1)S(1)}, u32[]{:S(2)}, u32[]{:S(2)}) collective-permute-start(bf16[512,256]{1,0:T(8,128)(2,1)S(1)} %reshape.203), channel_id=1, source_target_pairs={{0,2},{1,3},{2,0},{3,1},{4,6},{5,7},{6,4},{7,5},{8,10},{9,11},{10,... | collective-permute-start | bytes 786440 | tf_op jit(solution)/shard_map/ppermute | solution.py:26
  65.8 10.6 %collective-permute-start.4 = (bf16[512,256]{1,0:T(8,128)(2,1)S(1)}, bf16[512,256]{1,0:T(8,128)(2,1)S(1)}, u32[]{:S(2)}, u32[]{:S(2)}) collective-permute-start(bf16[512,256]{1,0:T(8,128)(2,1)S(1)} %reshape.203), channel_id=1, source_target_pairs={{0,1},{1,0},{2,3},{3,2},{4,5},{5,4},{6,7},{7,6},{8,9},{9,8},{10,11... | collective-permute-start | bytes 786440 | tf_op jit(solution)/shard_map/ppermute | solution.py:26
  75.8 18.7 %copy-start.2 = (s32[2]{0:T(128)}, s32[2]{0:T(128)S(1)}, u32[]{:S(2)}) copy-start(s32[2]{0:T(128)S(1)} %pad_add_fusion.where_ref) | copy-start | bytes 28
  75.8 5.1 %collective-permute-start.6 = (bf16[256,256]{1,0:T(8,128)(2,1)S(1)}, bf16[256,256]{1,0:T(8,128)(2,1)S(1)}, u32[]{:S(2)}, u32[]{:S(2)}) collective-permute-start(bf16[256,256]{1,0:T(8,128)(2,1)S(1)} %slice.545), channel_id=1, source_target_pairs={{0,1},{1,0},{2,3},{3,2},{4,5},{5,4},{6,7},{7,6},{8,9},{9,8},{10,11... | collective-permute-start | bytes 393224 | tf_op jit(solution)/shard_map/ppermute | solution.py:26
  76.4 5.0 %collective-permute-start.7 = (bf16[256,256]{1,0:T(8,128)(2,1)S(1)}, bf16[256,256]{1,0:T(8,128)(2,1)S(1)}, u32[]{:S(2)}, u32[]{:S(2)}) collective-permute-start(bf16[256,256]{1,0:T(8,128)(2,1)S(1)} %slice.546), channel_id=1, source_target_pairs={{0,2},{1,3},{2,0},{3,1},{4,6},{5,7},{6,4},{7,5},{8,10},{9,11},{10,... | collective-permute-start | bytes 393224 | tf_op jit(solution)/shard_map/ppermute | solution.py:26
  81.7 27.2 %collective-permute-start.9 = (bf16[256,2048]{1,0:T(8,128)(2,1)}, bf16[256,2048]{1,0:T(8,128)(2,1)}, u32[]{:S(2)}, u32[]{:S(2)}) collective-permute-start(bf16[256,2048]{1,0:T(8,128)(2,1)} %fusion.39), channel_id=1, source_target_pairs={{0,2},{1,3},{2,0},{3,1},{4,6},{5,7},{6,4},{7,5},{8,10},{9,11},{10,... | collective-permute-start | bytes 3145736 | tf_op jit(solution)/shard_map/ppermute | solution.py:26
  82.3 26.6 %collective-permute-start.8 = (bf16[256,2048]{1,0:T(8,128)(2,1)}, bf16[256,2048]{1,0:T(8,128)(2,1)}, u32[]{:S(2)}, u32[]{:S(2)}) collective-permute-start(bf16[256,2048]{1,0:T(8,128)(2,1)} %fusion.39), channel_id=1, source_target_pairs={{0,1},{1,0},{2,3},{3,2},{4,5},{5,4},{6,7},{7,6},{8,9},{9,8},{10,11... | collective-permute-start | bytes 3145736 | tf_op jit(solution)/shard_map/ppermute | solution.py:26
  108.5 266.1 %reduce-scatter.4.cloned.1.call-start = ((), (), s32[]{:S(2)}) async-start(), calls=%async_computation.6 | async-start | bytes 10616832 | tf_op jit(solution)/shard_map/reduce_scatter | solution.py:83
  112.9 23.3 %collective-permute-start.12 = (bf16[256,2048]{1,0:T(8,128)(2,1)S(1)}, bf16[256,2048]{1,0:T(8,128)(2,1)S(1)}, u32[]{:S(2)}, u32[]{:S(2)}) collective-permute-start(bf16[256,2048]{1,0:T(8,128)(2,1)S(1)} %pad_maximum_fusion.12), channel_id=1, source_target_pairs={{0,2},{1,3},{2,0},{3,1},{4,6},{5,7},{6,4},{7,5},{8,10},{9,11},{10,... | collective-permute-start | bytes 3145736 | tf_op jit(solution)/shard_map/ppermute | solution.py:26
  114.6 23.0 %collective-permute-start.10 = (bf16[256,2048]{1,0:T(8,128)(2,1)S(1)}, bf16[256,2048]{1,0:T(8,128)(2,1)S(1)}, u32[]{:S(2)}, u32[]{:S(2)}) collective-permute-start(bf16[256,2048]{1,0:T(8,128)(2,1)S(1)} %pad_maximum_fusion.11), channel_id=1, source_target_pairs={{0,1},{1,0},{2,3},{3,2},{4,5},{5,4},{6,7},{7,6},{8,9},{9,8},{10,11... | collective-permute-start | bytes 3145736 | tf_op jit(solution)/shard_map/ppermute | solution.py:26
  138.0 14.9 %collective-permute-start.11 = (bf16[128,2048]{1,0:T(8,128)(2,1)S(1)}, bf16[128,2048]{1,0:T(8,128)(2,1)S(1)}, u32[]{:S(2)}, u32[]{:S(2)}) collective-permute-start(bf16[128,2048]{1,0:T(8,128)(2,1)S(1)} %get-tuple-element.131), channel_id=1, source_target_pairs={{0,2},{1,3},{2,0},{3,1},{4,6},{5,7},{6,4},{7,5},{8,10},{9,11},{10,... | collective-permute-start | bytes 1572872 | tf_op jit(solution)/shard_map/ppermute | solution.py:26
  138.6 14.8 %collective-permute-start.13 = (bf16[128,2048]{1,0:T(8,128)(2,1)S(1)}, bf16[128,2048]{1,0:T(8,128)(2,1)S(1)}, u32[]{:S(2)}, u32[]{:S(2)}) collective-permute-start(bf16[128,2048]{1,0:T(8,128)(2,1)S(1)} %get-tuple-element.132), channel_id=1, source_target_pairs={{0,1},{1,0},{2,3},{3,2},{4,5},{5,4},{6,7},{7,6},{8,9},{9,8},{10,11... | collective-permute-start | bytes 1572872 | tf_op jit(solution)/shard_map/ppermute | solution.py:26
  142.6 17.9 %collective-permute-start.14 = (bf16[128,2048]{1,0:T(8,128)(2,1)S(1)}, bf16[128,2048]{1,0:T(8,128)(2,1)S(1)}, u32[]{:S(2)}, u32[]{:S(2)}) collective-permute-start(bf16[128,2048]{1,0:T(8,128)(2,1)S(1)} %slice.446), channel_id=1, source_target_pairs={{0,1},{1,0},{2,3},{3,2},{4,5},{5,4},{6,7},{7,6},{8,9},{9,8},{10,11... | collective-permute-start | bytes 1572872 | tf_op jit(solution)/shard_map/ppermute | solution.py:26
  144.2 16.4 %collective-permute-start.15 = (bf16[128,2048]{1,0:T(8,128)(2,1)S(1)}, bf16[128,2048]{1,0:T(8,128)(2,1)S(1)}, u32[]{:S(2)}, u32[]{:S(2)}) collective-permute-start(bf16[128,2048]{1,0:T(8,128)(2,1)S(1)} %slice.447), channel_id=1, source_target_pairs={{0,2},{1,3},{2,0},{3,1},{4,6},{5,7},{6,4},{7,5},{8,10},{9,11},{10,... | collective-permute-start | bytes 1572872 | tf_op jit(solution)/shard_map/ppermute | solution.py:26
  163.0 21.4 %collective-permute-start.17 = (bf16[256,2048]{1,0:T(8,128)(2,1)}, bf16[256,2048]{1,0:T(8,128)(2,1)}, u32[]{:S(2)}, u32[]{:S(2)}) collective-permute-start(bf16[256,2048]{1,0:T(8,128)(2,1)} %multiply_convert_fusion.7), channel_id=1, source_target_pairs={{0,2},{1,3},{2,0},{3,1},{4,6},{5,7},{6,4},{7,5},{8,10},{9,11},{10,... | collective-permute-start | bytes 3145736 | tf_op jit(solution)/shard_map/ppermute | solution.py:26
  164.4 23.2 %collective-permute-start.16 = (bf16[256,2048]{1,0:T(8,128)(2,1)}, bf16[256,2048]{1,0:T(8,128)(2,1)}, u32[]{:S(2)}, u32[]{:S(2)}) collective-permute-start(bf16[256,2048]{1,0:T(8,128)(2,1)} %multiply_convert_fusion.7), channel_id=1, source_target_pairs={{0,1},{1,0},{2,3},{3,2},{4,5},{5,4},{6,7},{7,6},{8,9},{9,8},{10,11... | collective-permute-start | bytes 3145736 | tf_op jit(solution)/shard_map/ppermute | solution.py:26
  185.4 11.2 %collective-permute-start.18 = (bf16[128,2048]{1,0:T(8,128)(2,1)S(1)}, bf16[128,2048]{1,0:T(8,128)(2,1)S(1)}, u32[]{:S(2)}, u32[]{:S(2)}) collective-permute-start(bf16[128,2048]{1,0:T(8,128)(2,1)S(1)} %slice.455), channel_id=1, source_target_pairs={{0,1},{1,0},{2,3},{3,2},{4,5},{5,4},{6,7},{7,6},{8,9},{9,8},{10,11... | collective-permute-start | bytes 1572872 | tf_op jit(solution)/shard_map/ppermute | solution.py:26
  188.7 9.2 %collective-permute-start.19 = (bf16[128,2048]{1,0:T(8,128)(2,1)S(1)}, bf16[128,2048]{1,0:T(8,128)(2,1)S(1)}, u32[]{:S(2)}, u32[]{:S(2)}) collective-permute-start(bf16[128,2048]{1,0:T(8,128)(2,1)S(1)} %slice.456), channel_id=1, source_target_pairs={{0,2},{1,3},{2,0},{3,1},{4,6},{5,7},{6,4},{7,5},{8,10},{9,11},{10,... | collective-permute-start | bytes 1572872 | tf_op jit(solution)/shard_map/ppermute | solution.py:26
  197.9 16.4 %copy-start.56 = (bf16[1024,2048]{1,0:T(8,128)(2,1)}, bf16[1024,2048]{1,0:T(8,128)(2,1)S(1)}, u32[]{:S(2)}) copy-start(bf16[1024,2048]{1,0:T(8,128)(2,1)S(1)} %constant_dynamic-update-slice_fusion.10) | copy-start | bytes 12582916
  227.6 193.8 %reduce-scatter.6.cloned.1.call-start = ((), (), s32[]{:S(2)}) async-start(), calls=%async_computation.7 | async-start | bytes 8847360 | tf_op jit(solution)/shard_map/reduce_scatter | solution.py:83
  254.3 12.8 %copy-start.20 = (bf16[1024,640]{0,1:T(8,128)(2,1)}, bf16[1024,640]{0,1:T(8,128)(2,1)S(1)}, u32[]{:S(2)}) copy-start(bf16[1024,640]{0,1:T(8,128)(2,1)S(1)} %get-tuple-element.107) | copy-start | bytes 3932164
  254.3 12.8 %copy-start.22 = (bf16[1024,640]{0,1:T(8,128)(2,1)}, bf16[1024,640]{0,1:T(8,128)(2,1)S(1)}, u32[]{:S(2)}) copy-start(bf16[1024,640]{0,1:T(8,128)(2,1)S(1)} %get-tuple-element.108) | copy-start | bytes 3932164
  254.3 30.5 %copy-start.41 = (bf16[1024,640]{0,1:T(8,128)(2,1)}, bf16[1024,640]{0,1:T(8,128)(2,1)S(1)}, u32[]{:S(2)}) copy-start(bf16[1024,640]{0,1:T(8,128)(2,1)S(1)} %get-tuple-element.72) | copy-start | bytes 3932164
  263.9 20.7 %collective-permute-start.20 = (bf16[256,2048]{1,0:T(8,128)(2,1)S(1)}, bf16[256,2048]{1,0:T(8,128)(2,1)S(1)}, u32[]{:S(2)}, u32[]{:S(2)}) collective-permute-start(bf16[256,2048]{1,0:T(8,128)(2,1)S(1)} %pad_maximum_fusion.13), channel_id=1, source_target_pairs={{0,1},{1,0},{2,3},{3,2},{4,5},{5,4},{6,7},{7,6},{8,9},{9,8},{10,11... | collective-permute-start | bytes 3145736 | tf_op jit(solution)/shard_map/ppermute | solution.py:26
  265.6 19.2 %copy-start.55 = (bf16[1024,2048]{1,0:T(8,128)(2,1)S(1)}, bf16[1024,2048]{1,0:T(8,128)(2,1)}, u32[]{:S(2)}) copy-start(bf16[1024,2048]{1,0:T(8,128)(2,1)} %copy-done.53) | copy-start | bytes 12582916
  265.7 19.2 %collective-permute-start.21 = (bf16[256,2048]{1,0:T(8,128)(2,1)S(1)}, bf16[256,2048]{1,0:T(8,128)(2,1)}, u32[]{:S(2)}, u32[]{:S(2)}) collective-permute-start(bf16[256,2048]{1,0:T(8,128)(2,1)S(1)} %pad_maximum_fusion.14), channel_id=1, source_target_pairs={{0,2},{1,3},{2,0},{3,1},{4,6},{5,7},{6,4},{7,5},{8,10},{9,11},{10,... | collective-permute-start | bytes 3145736 | tf_op jit(solution)/shard_map/ppermute | solution.py:26
  304.2 170.7 %reduce-scatter.8.cloned.1.call-start = ((), (), s32[]{:S(2)}) async-start(), calls=%async_computation.8 | async-start | bytes 5013504 | tf_op jit(solution)/shard_map/reduce_scatter | solution.py:83
  304.7 10.7 %slice-start.2 = ((s8[7864320]{0:T(1024)(128)(4,1)}), s8[4194304]{0:T(1024)(128)(4,1)S(1)}, s32[]{:S(2)}) async-start(s8[7864320]{0:T(1024)(128)(4,1)} %bitcast.102), calls=%async_computation.11 | async-start | bytes 8388608
  308.1 9.2 %collective-permute-start.22 = (bf16[128,2048]{1,0:T(8,128)(2,1)S(1)}, bf16[128,2048]{1,0:T(8,128)(2,1)S(1)}, u32[]{:S(2)}, u32[]{:S(2)}) collective-permute-start(bf16[128,2048]{1,0:T(8,128)(2,1)S(1)} %get-tuple-element.125), channel_id=1, source_target_pairs={{0,2},{1,3},{2,0},{3,1},{4,6},{5,7},{6,4},{7,5},{8,10},{9,11},{10,... | collective-permute-start | bytes 1572872 | tf_op jit(solution)/shard_map/ppermute | solution.py:26
  308.8 9.2 %collective-permute-start.23 = (bf16[128,2048]{1,0:T(8,128)(2,1)S(1)}, bf16[128,2048]{1,0:T(8,128)(2,1)S(1)}, u32[]{:S(2)}, u32[]{:S(2)}) collective-permute-start(bf16[128,2048]{1,0:T(8,128)(2,1)S(1)} %get-tuple-element.126), channel_id=1, source_target_pairs={{0,1},{1,0},{2,3},{3,2},{4,5},{5,4},{6,7},{7,6},{8,9},{9,8},{10,11... | collective-permute-start | bytes 1572872 | tf_op jit(solution)/shard_map/ppermute | solution.py:26
  323.5 20.9 %collective-permute-start.25 = (bf16[256,2048]{1,0:T(8,128)(2,1)}, bf16[256,2048]{1,0:T(8,128)(2,1)S(1)}, u32[]{:S(2)}, u32[]{:S(2)}) collective-permute-start(bf16[256,2048]{1,0:T(8,128)(2,1)} %get-tuple-element.103), channel_id=1, source_target_pairs={{0,2},{1,3},{2,0},{3,1},{4,6},{5,7},{6,4},{7,5},{8,10},{9,11},{10,... | collective-permute-start | bytes 3145736 | tf_op jit(solution)/shard_map/ppermute | solution.py:26
  325.0 24.5 %collective-permute-start.24 = (bf16[256,2048]{1,0:T(8,128)(2,1)}, bf16[256,2048]{1,0:T(8,128)(2,1)}, u32[]{:S(2)}, u32[]{:S(2)}) collective-permute-start(bf16[256,2048]{1,0:T(8,128)(2,1)} %get-tuple-element.103), channel_id=1, source_target_pairs={{0,1},{1,0},{2,3},{3,2},{4,5},{5,4},{6,7},{7,6},{8,9},{9,8},{10,11... | collective-permute-start | bytes 3145736 | tf_op jit(solution)/shard_map/ppermute | solution.py:26
  326.8 23.9 %copy-start.42 = (bf16[1024,640]{0,1:T(8,128)(2,1)S(1)}, bf16[1024,640]{0,1:T(8,128)(2,1)}, u32[]{:S(2)}) copy-start(bf16[1024,640]{0,1:T(8,128)(2,1)} %copy-done.41) | copy-start | bytes 3932164
  344.5 13.4 %collective-permute-start.26 = (bf16[128,2048]{1,0:T(8,128)(2,1)S(1)}, bf16[128,2048]{1,0:T(8,128)(2,1)S(1)}, u32[]{:S(2)}, u32[]{:S(2)}) collective-permute-start(bf16[128,2048]{1,0:T(8,128)(2,1)S(1)} %slice.586), channel_id=1, source_target_pairs={{0,1},{1,0},{2,3},{3,2},{4,5},{5,4},{6,7},{7,6},{8,9},{9,8},{10,11... | collective-permute-start | bytes 1572872 | tf_op jit(solution)/shard_map/ppermute | solution.py:26
  350.6 13.4 %collective-permute-start.27 = (bf16[128,2048]{1,0:T(8,128)(2,1)S(1)}, bf16[128,2048]{1,0:T(8,128)(2,1)S(1)}, u32[]{:S(2)}, u32[]{:S(2)}) collective-permute-start(bf16[128,2048]{1,0:T(8,128)(2,1)S(1)} %slice.587), channel_id=1, source_target_pairs={{0,2},{1,3},{2,0},{3,1},{4,6},{5,7},{6,4},{7,5},{8,10},{9,11},{10,... | collective-permute-start | bytes 1572872 | tf_op jit(solution)/shard_map/ppermute | solution.py:26
  355.7 8.5 %copy-start.31 = (bf16[768,2048]{1,0:T(8,128)(2,1)}, bf16[768,2048]{1,0:T(8,128)(2,1)S(1)}, u32[]{:S(2)}) copy-start(bf16[768,2048]{1,0:T(8,128)(2,1)S(1)} %add_convert_fusion) | copy-start | bytes 9437188
  365.3 28.3 %collective-permute-start.28 = (bf16[256,2048]{1,0:T(8,128)(2,1)}, bf16[256,2048]{1,0:T(8,128)(2,1)}, u32[]{:S(2)}, u32[]{:S(2)}) collective-permute-start(bf16[256,2048]{1,0:T(8,128)(2,1)} %pad_maximum_fusion.15), channel_id=1, source_target_pairs={{0,1},{1,0},{2,3},{3,2},{4,5},{5,4},{6,7},{7,6},{8,9},{9,8},{10,11... | collective-permute-start | bytes 3145736 | tf_op jit(solution)/shard_map/ppermute | solution.py:26
  368.7 24.9 %collective-permute-start.29 = (bf16[256,2048]{1,0:T(8,128)(2,1)}, bf16[256,2048]{1,0:T(8,128)(2,1)}, u32[]{:S(2)}, u32[]{:S(2)}) collective-permute-start(bf16[256,2048]{1,0:T(8,128)(2,1)} %pad_maximum_fusion.16), channel_id=1, source_target_pairs={{0,2},{1,3},{2,0},{3,1},{4,6},{5,7},{6,4},{7,5},{8,10},{9,11},{10,... | collective-permute-start | bytes 3145736 | tf_op jit(solution)/shard_map/ppermute | solution.py:26
  398.1 12.3 %collective-permute-start.32 = (bf16[512,256]{1,0:T(8,128)(2,1)S(1)}, bf16[512,256]{1,0:T(8,128)(2,1)S(1)}, u32[]{:S(2)}, u32[]{:S(2)}) collective-permute-start(bf16[512,256]{1,0:T(8,128)(2,1)S(1)} %pad_maximum_fusion.30), channel_id=1, source_target_pairs={{0,2},{1,3},{2,0},{3,1},{4,6},{5,7},{6,4},{7,5},{8,10},{9,11},{10,... | collective-permute-start | bytes 786440 | tf_op jit(solution)/shard_map/ppermute | solution.py:26
  400.1 12.3 %collective-permute-start.30 = (bf16[512,256]{1,0:T(8,128)(2,1)S(1)}, bf16[512,256]{1,0:T(8,128)(2,1)S(1)}, u32[]{:S(2)}, u32[]{:S(2)}) collective-permute-start(bf16[512,256]{1,0:T(8,128)(2,1)S(1)} %pad_maximum_fusion.29), channel_id=1, source_target_pairs={{0,1},{1,0},{2,3},{3,2},{4,5},{5,4},{6,7},{7,6},{8,9},{9,8},{10,11... | collective-permute-start | bytes 786440 | tf_op jit(solution)/shard_map/ppermute | solution.py:26
  410.4 5.0 %collective-permute-start.33 = (bf16[256,256]{1,0:T(8,128)(2,1)S(1)}, bf16[256,256]{1,0:T(8,128)(2,1)S(1)}, u32[]{:S(2)}, u32[]{:S(2)}) collective-permute-start(bf16[256,256]{1,0:T(8,128)(2,1)S(1)} %fusion.71), channel_id=1, source_target_pairs={{0,1},{1,0},{2,3},{3,2},{4,5},{5,4},{6,7},{7,6},{8,9},{9,8},{10,11... | collective-permute-start | bytes 393224 | tf_op jit(solution)/shard_map/ppermute | solution.py:26
  412.5 5.0 %collective-permute-start.31 = (bf16[256,256]{1,0:T(8,128)(2,1)S(1)}, bf16[256,256]{1,0:T(8,128)(2,1)S(1)}, u32[]{:S(2)}, u32[]{:S(2)}) collective-permute-start(bf16[256,256]{1,0:T(8,128)(2,1)S(1)} %fusion.72), channel_id=1, source_target_pairs={{0,2},{1,3},{2,0},{3,1},{4,6},{5,7},{6,4},{7,5},{8,10},{9,11},{10,... | collective-permute-start | bytes 393224 | tf_op jit(solution)/shard_map/ppermute | solution.py:26
  424.2 20.6 %collective-permute-start.34 = (bf16[256,2048]{1,0:T(8,128)(2,1)}, bf16[256,2048]{1,0:T(8,128)(2,1)}, u32[]{:S(2)}, u32[]{:S(2)}) collective-permute-start(bf16[256,2048]{1,0:T(8,128)(2,1)} %pad_maximum_fusion.17), channel_id=1, source_target_pairs={{0,1},{1,0},{2,3},{3,2},{4,5},{5,4},{6,7},{7,6},{8,9},{9,8},{10,11... | collective-permute-start | bytes 3145736 | tf_op jit(solution)/shard_map/ppermute | solution.py:26
  425.3 21.8 %collective-permute-start.35 = (bf16[256,2048]{1,0:T(8,128)(2,1)}, bf16[256,2048]{1,0:T(8,128)(2,1)}, u32[]{:S(2)}, u32[]{:S(2)}) collective-permute-start(bf16[256,2048]{1,0:T(8,128)(2,1)} %pad_maximum_fusion.18), channel_id=1, source_target_pairs={{0,2},{1,3},{2,0},{3,1},{4,6},{5,7},{6,4},{7,5},{8,10},{9,11},{10,... | collective-permute-start | bytes 3145736 | tf_op jit(solution)/shard_map/ppermute | solution.py:26
  449.8 14.2 %collective-permute-start.38 = (bf16[128,2048]{1,0:T(8,128)(2,1)}, bf16[128,2048]{1,0:T(8,128)(2,1)S(1)}, u32[]{:S(2)}, u32[]{:S(2)}) collective-permute-start(bf16[128,2048]{1,0:T(8,128)(2,1)} %get-tuple-element.113), channel_id=1, source_target_pairs={{0,2},{1,3},{2,0},{3,1},{4,6},{5,7},{6,4},{7,5},{8,10},{9,11},{10,... | collective-permute-start | bytes 1572872 | tf_op jit(solution)/shard_map/ppermute | solution.py:26
  451.3 13.5 %collective-permute-start.39 = (bf16[128,2048]{1,0:T(8,128)(2,1)S(1)}, bf16[128,2048]{1,0:T(8,128)(2,1)}, u32[]{:S(2)}, u32[]{:S(2)}) collective-permute-start(bf16[128,2048]{1,0:T(8,128)(2,1)S(1)} %get-tuple-element.114), channel_id=1, source_target_pairs={{0,1},{1,0},{2,3},{3,2},{4,5},{5,4},{6,7},{7,6},{8,9},{9,8},{10,11... | collective-permute-start | bytes 1572872 | tf_op jit(solution)/shard_map/ppermute | solution.py:26
  461.9 9.2 %collective-permute-start.36 = (bf16[128,2048]{1,0:T(8,128)(2,1)S(1)}, bf16[128,2048]{1,0:T(8,128)(2,1)S(1)}, u32[]{:S(2)}, u32[]{:S(2)}) collective-permute-start(bf16[128,2048]{1,0:T(8,128)(2,1)S(1)} %get-tuple-element.115), channel_id=1, source_target_pairs={{0,2},{1,3},{2,0},{3,1},{4,6},{5,7},{6,4},{7,5},{8,10},{9,11},{10,... | collective-permute-start | bytes 1572872 | tf_op jit(solution)/shard_map/ppermute | solution.py:26
  462.5 9.4 %collective-permute-start.37 = (bf16[128,2048]{1,0:T(8,128)(2,1)S(1)}, bf16[128,2048]{1,0:T(8,128)(2,1)S(1)}, u32[]{:S(2)}, u32[]{:S(2)}) collective-permute-start(bf16[128,2048]{1,0:T(8,128)(2,1)S(1)} %get-tuple-element.116), channel_id=1, source_target_pairs={{0,1},{1,0},{2,3},{3,2},{4,5},{5,4},{6,7},{7,6},{8,9},{9,8},{10,11... | collective-permute-start | bytes 1572872 | tf_op jit(solution)/shard_map/ppermute | solution.py:26
  468.3 15.5 %copy-start.10 = (bf16[256,2048]{1,0:T(8,128)(2,1)S(1)}, bf16[256,2048]{1,0:T(8,128)(2,1)}, u32[]{:S(2)}) copy-start(bf16[256,2048]{1,0:T(8,128)(2,1)} %param.12) | copy-start | bytes 3145732
  474.9 11.0 %copy-start.13 = (f32[128,2048]{1,0:T(8,128)S(1)}, f32[128,2048]{1,0:T(8,128)}, u32[]{:S(2)}) copy-start(f32[128,2048]{1,0:T(8,128)} %copy-done.11) | copy-start | bytes 3145732
  474.9 11.0 %copy-start.16 = (f32[128,2048]{1,0:T(8,128)S(1)}, f32[128,2048]{1,0:T(8,128)}, u32[]{:S(2)}) copy-start(f32[128,2048]{1,0:T(8,128)} %copy-done.14) | copy-start | bytes 3145732
  480.4 10.9 %collective-permute-start.41 = (f32[64,265]{1,0:T(8,128)S(1)}, f32[64,265]{1,0:T(8,128)S(1)}, u32[]{:S(2)}, u32[]{:S(2)}) collective-permute-start(f32[64,265]{1,0:T(8,128)S(1)} %pad_maximum_fusion.32), channel_id=1, source_target_pairs={{0,2},{1,3},{2,0},{3,1},{4,6},{5,7},{6,4},{7,5},{8,10},{9,11},{10,... | collective-permute-start | bytes 203528 | tf_op jit(solution)/shard_map/ppermute | solution.py:26
  481.7 9.6 %collective-permute-start.40 = (f32[64,265]{1,0:T(8,128)S(1)}, f32[64,265]{1,0:T(8,128)S(1)}, u32[]{:S(2)}, u32[]{:S(2)}) collective-permute-start(f32[64,265]{1,0:T(8,128)S(1)} %pad_maximum_fusion.32), channel_id=1, source_target_pairs={{0,1},{1,0},{2,3},{3,2},{4,5},{5,4},{6,7},{7,6},{8,9},{9,8},{10,11... | collective-permute-start | bytes 203528 | tf_op jit(solution)/shard_map/ppermute | solution.py:26
  483.2 8.1 %collective-permute-start.42 = (f32[64,265]{1,0:T(8,128)S(1)}, f32[64,265]{1,0:T(8,128)S(1)}, u32[]{:S(2)}, u32[]{:S(2)}) collective-permute-start(f32[64,265]{1,0:T(8,128)S(1)} %pad_maximum_fusion.32), channel_id=1, source_target_pairs={{0,3},{1,2},{2,1},{3,0},{4,7},{5,6},{6,5},{7,4},{8,11},{9,10},{10,... | collective-permute-start | bytes 203528 | tf_op jit(solution)/shard_map/ppermute | solution.py:26
  (60 other events, 259.6 us)
Sparse Core Ops, SparseCore 0:
  11.4 51.7 all-gather.3
  65.4 89.4 all-gather.5
  157.1 76.1 all-gather.7
  235.5 97.9 reduce-scatter.3
  335.6 83.0 reduce-scatter.5
  421.5 50.1 reduce-scatter.7

commit v11 on v9

--- a/solution.py
+++ b/solution.py
@@ -492,9 +492,9 @@
     kv_own, *kv_rest = (pick(kv_grads, order[j], 1).reshape(-1, 2 * HD) for j in range(ranks))
     kv_rest = jnp.concatenate(kv_rest, axis=0)
     kv_sent = send_sums(kv_rest)
-    qkv_rest = dot(after(qkv_back[rows:], kv_rest), qkv_full, 1, 1).astype(bf16)
+    qkv_rest = dot(after(qkv_back[rows:], *kv_sent), qkv_full, 1, 1).astype(bf16)
     qkv_sent = send_sums(after(qkv_rest, *kv_sent, ff_sums[1]))
-    query_back = after(qkv_back[:, :heads_width], qkv_rest)
+    query_back = after(qkv_back[:, :heads_width], kv_rest)
     kv_sum = finish_sums(kv_own.astype(f32), kv_rest, kv_sent).astype(bf16)
     attn_partial = jnp.concatenate(
         [

time: 507 us -> 506 us (level)
    unnamed x157 -> x155, local copies, waits for them, and re-layouts: 20.4 us -> 20.8 us
  transfers between devices with their start and end apart: 49 -> 49, of which waited for: 31 -> 32; matrix products, arithmetic and copies ran while one was open for 48% -> 48% of each run, Pallas kernels for 6% -> 6%
where the time goes in v11:
time: 506 us; the launch traced here: 499 us
  waiting for transfers between devices  134 us (26%)
  matrix products  134 us (26%)
  other arithmetic  74.9 us (15%)
  starting transfers between devices  51.6 us (10%)
  local copies, waits for them, and re-layouts  49.2 us (10%)
  Pallas kernels  31.4 us (6%)
  between operations  24.4 us (5%)
    dot_general x25, matrix products, dot(): lax.dot_general(a, b, (((ca,), (cb,)), ((), ())), preferred_element_type=...  134 us
    ppermute x43, waiting for transfers between devices, hop(): return lax.ppermute(value, 'tensor', [(i, i ^ step) for i in range(size)])  126 us
    ppermute x43, starting transfers between devices, hop(): return lax.ppermute(value, 'tensor', [(i, i ^ step) for i in range(size)])  50.2 us
    unnamed x155, local copies, waits for them, and re-layouts  20.8 us
    pallas_call x1, Pallas kernels, attend_back(): pl.pallas_call(attend_back_kernel, name='attend_back', grid_spec=pltpu.Pr...  13.6 us
    concatenate x2, other arithmetic, partial(): jnp.concatenate([dot(normed_two, grads, 0, 0).astype(bf16), dot(top_all,...  11.7 us
    pallas_call x1, Pallas kernels, attend(): pl.pallas_call(attend_kernel, name='attend', grid_spec=pltpu.PrefetchScal...  11.4 us
  transfers between devices with their start and end apart: 49, of which 32 were waited for; matrix products, arithmetic and copies ran while one was open for 48% of the time, Pallas kernels for 6%

profile of v11, /device:TPU:0, one launch (start us, length us, event | category | flops | bytes accessed | tf_op | source)
XLA Modules:
  0.0 499.1 jit_solution(4743287727216594591)
XLA Ops:
  11.3 3.1 collective-permute-start.1
  22.1 3.1 fusion.81
  29.1 2.1 pad_maximum_fusion.9
  35.1 2.4 collective-permute-done.1
  43.9 2.4 fusion.54
  47.6 3.3 collective-permute-done.2
  51.0 2.1 collective-permute-done.3
  55.6 7.6 %all-gather.4.cloned.1.call-done = bf16[4352,512]{1,0:T(8,128)(2,1)} async-done(((bf16[544,512]{1,0:T(8,128)(2,1)}), bf16[4352,512]{1,0:T(8,128)(2,1)}) %all-gather.4.cloned.1.call-update) | async-done | bytes 4456464 | tf_op jit(solution)/shard_map/all_gather | solution.py:79
  77.1 3.8 collective-permute-done.6
  87.2 7.4 %fusion.66.q_ref.kv_ref = f32[1024,768]{1,0:T(8,128)} fusion(bf16[1024,2048]{1,0:T(8,128)(2,1)} %fusion.69, bf16[2048,256]{1,0:T(8,128)(2,1)S(1)} %bitcast.113, bf16[2048,512]{1,0:T(8,128)(2,1)S(1)} %bitcast.108), kind=kOutput, calls=%fused_computation.143 | convolution fusion | flops 3227516928 | bytes 10485760 | tf_op jit(solution)/shard_map/dot_general | solution.py:21
  94.5 11.4 %attend.1 = (bf16[1024,512]{1,0:T(8,128)(2,1)S(1)}, bf16[1024,256]{1,0:T(8,128)(2,1)S(1)}, bf16[1024,512]{1,0:T(8,128)(2,1)S(1)}, f32[1024,128]{1,0:T(8,128)S(1)}) custom-call(s32[2]{0:T(128)S(1)} %pad_add_fusion.where_ref, f32[1024,768]{1,0:T(8,128)} %fusion.66.q_ref.kv_ref, f32[1024,768]{1,0:T(8,128)} %fusion.66.q_ref.kv_ref, ...), custom_call_target="tpu_custom_call" | custom-call | flops 2147483648 | bytes 8388608 | tf_op jit(solution)/shard_map/attend/pallas_call | solution.py:202
  109.0 3.7 convolution_convert_fusion.2
  116.0 20.2 %collective-permute-done.12 = bf16[256,2048]{1,0:T(8,128)(2,1)S(1)} collective-permute-done((bf16[256,2048]{1,0:T(8,128)(2,1)S(1)}, bf16[256,2048]{1,0:T(8,128)(2,1)S(1)}, u32[]{:S(2)}, u32[]{:S(2)}) %collective-permute-start.12) | collective-permute-done | bytes 1048608 | tf_op jit(solution)/shard_map/ppermute | solution.py:26
  148.3 4.6 collective-permute-done.11
  154.3 6.1 %collective-permute-done.14 = bf16[128,2048]{1,0:T(8,128)(2,1)S(1)} collective-permute-done((bf16[128,2048]{1,0:T(8,128)(2,1)S(1)}, bf16[128,2048]{1,0:T(8,128)(2,1)S(1)}, u32[]{:S(2)}, u32[]{:S(2)}) %collective-permute-start.14) | collective-permute-done | bytes 524320 | tf_op jit(solution)/shard_map/ppermute | solution.py:26
  165.1 6.3 %fusion.26 = f32[1024,768]{0,1:T(8,128)S(1)} fusion(bf16[1024,2048]{1,0:T(8,128)(2,1)} %copy-done.51, bf16[2048,2304]{1,0:T(8,128)(2,1)} %all-gather.6.cloned.1.call-done), kind=kOutput, calls=%fused_computation.60 | convolution fusion | flops 3221225472 | bytes 10485760 | tf_op jit(solution)/shard_map/dot_general | solution.py:21
  171.4 12.9 %collective-permute-done.17 = bf16[256,2048]{1,0:T(8,128)(2,1)} collective-permute-done((bf16[256,2048]{1,0:T(8,128)(2,1)}, bf16[256,2048]{1,0:T(8,128)(2,1)}, u32[]{:S(2)}, u32[]{:S(2)}) %collective-permute-start.17) | collective-permute-done | bytes 1048608 | tf_op jit(solution)/shard_map/ppermute | solution.py:26
  192.8 3.8 collective-permute-done.18
  198.1 10.4 %fusion.4 = f32[1024,1536]{0,1:T(8,128)S(1)} fusion(bf16[1024,2048]{1,0:T(8,128)(2,1)S(1)} %constant_dynamic-update-slice_fusion.10, bf16[2048,2304]{1,0:T(8,128)(2,1)} %all-gather.6.cloned.1.call-done), kind=kOutput, calls=%fused_computation.10 | convolution fusion | flops 6442450944 | bytes 16777216 | tf_op jit(solution)/shard_map/dot_general | solution.py:21
  208.5 2.1 multiply_convert_fusion.1
  210.6 3.8 convolution_convert_fusion.4
  214.4 8.6 %convolution_convert_fusion.1 = bf16[2048,1536]{1,0:T(8,128)(2,1)S(1)} fusion(bf16[1024,2048]{1,0:T(8,128)(2,1)S(1)} %constant_dynamic-update-slice_fusion.10, bf16[1024,768]{0,1:T(8,128)(2,1)S(1)} %get-tuple-element.102, bf16[1024,768]{0,1:T(8,128)(2,1)S(1)} %get-tuple-element.101), kind=kOutput, calls=%fused_computation.3 | convolution fusion | flops 6451888128 | bytes 13631488 | tf_op jit(solution)/shard_map/dot_general | solution.py:21
  223.1 4.6 pad_maximum_fusion
  229.7 9.9 %fusion.2 = f32[768,2048]{1,0:T(8,128)} fusion(bf16[768,1536]{0,1:T(8,128)(2,1)S(1)} %pad_maximum_fusion.5, bf16[2048,2304]{1,0:T(8,128)(2,1)} %all-gather.6.cloned.1.call-done), kind=kOutput, calls=%fused_computation.8 | convolution fusion | flops 4831838208 | bytes 14942208 | tf_op jit(solution)/shard_map/dot_general | solution.py:21
  239.6 6.0 %fusion.44 = f32[1024,640]{0,1:T(8,128)S(1)} fusion(bf16[1024,2048]{1,0:T(8,128)(2,1)} %copy-done.51, bf16[2048,1920]{1,0:T(8,128)(2,1)} %all-gather.8.cloned.1.call-done), kind=kOutput, calls=%fused_computation.86 | convolution fusion | flops 2684354560 | bytes 9437184 | tf_op jit(solution)/shard_map/dot_general | solution.py:21
  246.5 6.0 %fusion.10 = f32[1024,1280]{0,1:T(8,128)S(1)} fusion(bf16[1024,2048]{1,0:T(8,128)(2,1)S(1)} %copy-done.55, bf16[2048,1920]{1,0:T(8,128)(2,1)S(1)} %copy-done.27), kind=kOutput, calls=%fused_computation.17 | convolution fusion | flops 5368709120 | bytes 14680064 | tf_op jit(solution)/shard_map/dot_general | solution.py:21
  254.4 7.9 %add_convert_fusion.1 = bf16[768,2048]{1,0:T(8,128)(2,1)S(1)} fusion(f32[768,2048]{1,0:T(8,128)} %fusion.2, bf16[2048,1920]{1,0:T(8,128)(2,1)S(1)} %copy-done.27, bf16[1024,640]{0,1:T(8,128)(2,1)S(1)} %get-tuple-element.104, bf16[1024,640]{0,1:T(8,128)(2,1)S(1)} %get-tuple-element.103), kind=kOutput, calls=%fused_computation.5 | convolution fusion | flops 4033609728 | bytes 17301504 | tf_op jit(solution)/shard_map/dot_general | solution.py:21
  267.4 17.2 %collective-permute-done.20 = bf16[256,2048]{1,0:T(8,128)(2,1)S(1)} collective-permute-done((bf16[256,2048]{1,0:T(8,128)(2,1)S(1)}, bf16[256,2048]{1,0:T(8,128)(2,1)S(1)}, u32[]{:S(2)}, u32[]{:S(2)}) %collective-permute-start.20) | collective-permute-done | bytes 1048608 | tf_op jit(solution)/shard_map/ppermute | solution.py:26
  284.9 4.8 convolution_convert_fusion.5
  289.8 7.4 %convolution_convert_fusion = bf16[2048,1280]{1,0:T(8,128)(2,1)} fusion(bf16[1024,2048]{1,0:T(8,128)(2,1)S(1)} %copy-done.56, bf16[1024,1280]{0,1:T(8,128)(2,1)S(1)} %pad_maximum_fusion.3), kind=kOutput, calls=%fused_computation.2 | convolution fusion | flops 5371330560 | bytes 12058624 | tf_op jit(solution)/shard_map/dot_general | solution.py:21
  297.2 7.1 %pad_maximum_fusion.1 = bf16[2048,1920]{1,0:T(8,128)(2,1)} fusion(bf16[2048,640]{1,0:T(8,128)(2,1)} %convolution_convert_fusion.5, bf16[2048,1280]{1,0:T(8,128)(2,1)} %convolution_convert_fusion), kind=kLoop, calls=%fused_computation.1 | loop fusion | flops 15728640 | bytes 15728640 | tf_op jit(solution)/shard_map/concatenate | solution.py:455
  306.1 2.1 add_convert_fusion.7
  310.3 5.0 %fusion = f32[256,2048]{1,0:T(8,128)S(1)} fusion(bf16[256,1536]{0,1:T(8,128)(2,1)S(1)} %pad_maximum_fusion.23, bf16[2048,2304]{1,0:T(8,128)(2,1)} %all-gather.6.cloned.1.call-done), kind=kOutput, calls=%fused_computation.6 | convolution fusion | flops 1610612736 | bytes 9175040 | tf_op jit(solution)/shard_map/dot_general | solution.py:21
  320.7 2.8 constant_dynamic-update-slice_fusion.19
  326.9 5.0 %fusion.24 = f32[768,2048]{1,0:T(8,128)S(1)} fusion(bf16[2048,2304]{1,0:T(8,128)(2,1)} %all-gather.6.cloned.1.call-done, bf16[1024,768]{0,1:T(8,128)(2,1)} %copy-done.34), kind=kOutput, calls=%fused_computation.58 | convolution fusion | flops 2415919104 | bytes 10616832 | tf_op jit(solution)/shard_map/dot_general | solution.py:21
  331.9 12.7 %collective-permute-done.25 = bf16[256,2048]{1,0:T(8,128)(2,1)S(1)} collective-permute-done((bf16[256,2048]{1,0:T(8,128)(2,1)}, bf16[256,2048]{1,0:T(8,128)(2,1)S(1)}, u32[]{:S(2)}, u32[]{:S(2)}) %collective-permute-start.25) | collective-permute-done | bytes 1048608 | tf_op jit(solution)/shard_map/ppermute | solution.py:26
  346.4 3.2 collective-permute-done.24
  350.8 5.0 add_convert_fusion
  355.8 2.1 constant_dynamic-update-slice_fusion.18
  358.0 6.1 %collective-permute-done.27 = bf16[128,2048]{1,0:T(8,128)(2,1)S(1)} collective-permute-done((bf16[128,2048]{1,0:T(8,128)(2,1)S(1)}, bf16[128,2048]{1,0:T(8,128)(2,1)S(1)}, u32[]{:S(2)}, u32[]{:S(2)}) %collective-permute-start.27) | collective-permute-done | bytes 524320 | tf_op jit(solution)/shard_map/ppermute | solution.py:26
  365.3 2.3 collective-permute-start.28
  370.8 3.7 convolution_convert_fusion.6
  374.5 5.3 %convolution_convert_fusion.9.dm_ref = bf16[1024,512]{1,0:T(8,128)(2,1)S(1)} fusion(bf16[1024,2048]{1,0:T(8,128)(2,1)} %copy-done.50, bf16[2048,512]{1,0:T(8,128)(2,1)} %bitcast.100), kind=kOutput, calls=%fused_computation.92 | convolution fusion | flops 2148007936 | bytes 7340032 | tf_op jit(solution)/shard_map/dot_general | solution.py:21
  379.9 13.6 %attend_back.1 = (bf16[1024,512]{1,0:T(8,128)(2,1)S(1)}, bf16[1024,256]{1,0:T(8,128)(2,1)S(1)}) custom-call(s32[2]{0:T(128)S(1)} %copy-done.3, bf16[1024,512]{1,0:T(8,128)(2,1)S(1)} %get-tuple-element.63.qr_ref, bf16[1024,256]{1,0:T(8,128)(2,1)S(1)} %copy-done.5, bf16[1024,512]{1,0:T(8,128)(2,1)S(1)} %convolution_convert_fusion.9.dm_ref, ...), custom_call_target="tpu_custom_call" | custom-call | flops 5368709120 | bytes 8388608 | tf_op jit(solution)/shard_map/attend_back/pallas_call | solution.py:240
  393.7 4.1 convolution_convert_fusion.8
  398.0 2.0 collective-permute-start.32
  400.1 5.9 %convolution_convert_fusion.7 = bf16[2048,512]{1,0:T(8,128)(2,1)} fusion(bf16[1024,2048]{1,0:T(8,128)(2,1)} %fusion.69, bf16[1024,512]{1,0:T(8,128)(2,1)S(1)} %slice-done), kind=kOutput, calls=%fused_computation.40 | convolution fusion | flops 2148532224 | bytes 7340032 | tf_op jit(solution)/shard_map/dot_general | solution.py:21
  406.2 2.0 collective-permute-start.33
  408.5 2.7 collective-permute-done.33
  411.3 2.1 collective-permute-done.31
  413.5 3.6 pad_maximum_fusion.2
  418.7 5.6 %convolution_convert_fusion.3 = bf16[768,2048]{1,0:T(8,128)(2,1)} fusion(bf16[768,768]{1,0:T(8,128)(2,1)S(1)} %slice-done.1, bf16[2048,256]{1,0:T(8,128)(2,1)S(1)} %bitcast.115, bf16[2048,512]{1,0:T(8,128)(2,1)} %bitcast.109), kind=kOutput, calls=%fused_computation.20 | convolution fusion | flops 2423783424 | bytes 7471104 | tf_op jit(solution)/shard_map/dot_general | solution.py:21
  424.3 2.1 fusion.90
  433.9 3.6 fusion.65
  437.5 2.9 fusion.22
  440.5 4.4 collective-permute-done.34
  444.8 3.7 collective-permute-done.35
  448.5 2.9 add_convert_fusion.3
  453.9 2.8 convolution_add_fusion
  456.8 4.1 finish_ff.1
  461.9 2.1 add_convert_fusion.5
  469.7 3.5 collective-permute-done.36
  475.8 2.3 fusion.31
  479.2 2.3 finish_attn.1
  (374 shorter events, 138.7 us)
Async XLA Ops:
  7.2 8.7 %copy-start.33 = (bf16[256,1408]{1,0:T(8,128)(2,1)S(1)}, bf16[256,1408]{1,0:T(8,128)(2,1)}, u32[]{:S(2)}) copy-start(bf16[256,1408]{1,0:T(8,128)(2,1)} %gate_ref.1) | copy-start | bytes 2162692
  7.2 56.0 %all-gather.4.cloned.1.call-start = ((), (), s32[]{:S(2)}) async-start(), calls=%async_computation.3 | async-start | bytes 5013504 | tf_op jit(solution)/shard_map/all_gather | solution.py:79
  9.2 8.8 %copy-start.65 = (bf16[256]{0:T(256)(128)(2,1)S(1)}, bf16[256]{0:T(256)(128)(2,1)}, u32[]{:S(2)}) copy-start(bf16[256]{0:T(256)(128)(2,1)} %param.21) | copy-start | bytes 1540
  11.3 153.8 %all-gather.6.cloned.1.call-start = ((), (), s32[]{:S(2)}) async-start(), calls=%async_computation.4 | async-start | bytes 10616832 | tf_op jit(solution)/shard_map/all_gather | solution.py:79
  11.3 26.2 %collective-permute-start.1 = (bf16[256,2048]{1,0:T(8,128)(2,1)S(1)}, bf16[256,2048]{1,0:T(8,128)(2,1)S(1)}, u32[]{:S(2)}, u32[]{:S(2)}) collective-permute-start(bf16[256,2048]{1,0:T(8,128)(2,1)S(1)} %copy-done.8), channel_id=1, source_target_pairs={{0,2},{1,3},{2,0},{3,1},{4,6},{5,7},{6,4},{7,5},{8,10},{9,11},{10,... | collective-permute-start | bytes 3145736 | tf_op jit(solution)/shard_map/ppermute | solution.py:26
  14.4 25.0 %collective-permute-start = (bf16[256,2048]{1,0:T(8,128)(2,1)S(1)}, bf16[256,2048]{1,0:T(8,128)(2,1)}, u32[]{:S(2)}, u32[]{:S(2)}) collective-permute-start(bf16[256,2048]{1,0:T(8,128)(2,1)S(1)} %copy-done.8), channel_id=1, source_target_pairs={{0,1},{1,0},{2,3},{3,2},{4,5},{5,4},{6,7},{7,6},{8,9},{9,8},{10,11... | collective-permute-start | bytes 3145736 | tf_op jit(solution)/shard_map/ppermute | solution.py:26
  18.1 9.8 %copy-start.60 = (f32[256]{0:T(256)}, f32[256]{0:T(256)S(1)}, u32[]{:S(2)}) copy-start(f32[256]{0:T(256)S(1)} %convert_element_type.349) | copy-start | bytes 3076
  25.7 8.2 %copy-start.58 = (f32[1,256]{1,0:T(1,128)}, f32[1,256]{1,0:T(1,128)S(1)}, u32[]{:S(2)}) copy-start(f32[1,256]{1,0:T(1,128)S(1)} %compare_convert_fusion) | copy-start | bytes 3076
  37.6 13.3 %collective-permute-start.2 = (bf16[128,2048]{1,0:T(8,128)(2,1)S(1)}, bf16[128,2048]{1,0:T(8,128)(2,1)S(1)}, u32[]{:S(2)}, u32[]{:S(2)}) collective-permute-start(bf16[128,2048]{1,0:T(8,128)(2,1)S(1)} %slice.541), channel_id=1, source_target_pairs={{0,1},{1,0},{2,3},{3,2},{4,5},{5,4},{6,7},{7,6},{8,9},{9,8},{10,11... | collective-permute-start | bytes 1572872 | tf_op jit(solution)/shard_map/ppermute | solution.py:26
  40.5 12.7 %collective-permute-start.3 = (bf16[128,2048]{1,0:T(8,128)(2,1)S(1)}, bf16[128,2048]{1,0:T(8,128)(2,1)S(1)}, u32[]{:S(2)}, u32[]{:S(2)}) collective-permute-start(bf16[128,2048]{1,0:T(8,128)(2,1)S(1)} %slice.542), channel_id=1, source_target_pairs={{0,2},{1,3},{2,0},{3,1},{4,6},{5,7},{6,4},{7,5},{8,10},{9,11},{10,... | collective-permute-start | bytes 1572872 | tf_op jit(solution)/shard_map/ppermute | solution.py:26
  55.3 184.3 %all-gather.8.cloned.1.call-start = ((), (), s32[]{:S(2)}) async-start(), calls=%async_computation.5 | async-start | bytes 8847360 | tf_op jit(solution)/shard_map/all_gather | solution.py:79
  64.3 11.5 %collective-permute-start.5 = (bf16[512,256]{1,0:T(8,128)(2,1)S(1)}, bf16[512,256]{1,0:T(8,128)(2,1)S(1)}, u32[]{:S(2)}, u32[]{:S(2)}) collective-permute-start(bf16[512,256]{1,0:T(8,128)(2,1)S(1)} %reshape.203), channel_id=1, source_target_pairs={{0,2},{1,3},{2,0},{3,1},{4,6},{5,7},{6,4},{7,5},{8,10},{9,11},{10,... | collective-permute-start | bytes 786440 | tf_op jit(solution)/shard_map/ppermute | solution.py:26
  65.8 10.6 %collective-permute-start.4 = (bf16[512,256]{1,0:T(8,128)(2,1)S(1)}, bf16[512,256]{1,0:T(8,128)(2,1)S(1)}, u32[]{:S(2)}, u32[]{:S(2)}) collective-permute-start(bf16[512,256]{1,0:T(8,128)(2,1)S(1)} %reshape.203), channel_id=1, source_target_pairs={{0,1},{1,0},{2,3},{3,2},{4,5},{5,4},{6,7},{7,6},{8,9},{9,8},{10,11... | collective-permute-start | bytes 786440 | tf_op jit(solution)/shard_map/ppermute | solution.py:26
  75.8 18.8 %copy-start.2 = (s32[2]{0:T(128)}, s32[2]{0:T(128)S(1)}, u32[]{:S(2)}) copy-start(s32[2]{0:T(128)S(1)} %pad_add_fusion.where_ref) | copy-start | bytes 28
  75.8 5.1 %collective-permute-start.6 = (bf16[256,256]{1,0:T(8,128)(2,1)S(1)}, bf16[256,256]{1,0:T(8,128)(2,1)S(1)}, u32[]{:S(2)}, u32[]{:S(2)}) collective-permute-start(bf16[256,256]{1,0:T(8,128)(2,1)S(1)} %slice.545), channel_id=1, source_target_pairs={{0,1},{1,0},{2,3},{3,2},{4,5},{5,4},{6,7},{7,6},{8,9},{9,8},{10,11... | collective-permute-start | bytes 393224 | tf_op jit(solution)/shard_map/ppermute | solution.py:26
  76.4 5.0 %collective-permute-start.7 = (bf16[256,256]{1,0:T(8,128)(2,1)S(1)}, bf16[256,256]{1,0:T(8,128)(2,1)S(1)}, u32[]{:S(2)}, u32[]{:S(2)}) collective-permute-start(bf16[256,256]{1,0:T(8,128)(2,1)S(1)} %slice.546), channel_id=1, source_target_pairs={{0,2},{1,3},{2,0},{3,1},{4,6},{5,7},{6,4},{7,5},{8,10},{9,11},{10,... | collective-permute-start | bytes 393224 | tf_op jit(solution)/shard_map/ppermute | solution.py:26
  81.7 27.3 %collective-permute-start.9 = (bf16[256,2048]{1,0:T(8,128)(2,1)}, bf16[256,2048]{1,0:T(8,128)(2,1)}, u32[]{:S(2)}, u32[]{:S(2)}) collective-permute-start(bf16[256,2048]{1,0:T(8,128)(2,1)} %fusion.41), channel_id=1, source_target_pairs={{0,2},{1,3},{2,0},{3,1},{4,6},{5,7},{6,4},{7,5},{8,10},{9,11},{10,... | collective-permute-start | bytes 3145736 | tf_op jit(solution)/shard_map/ppermute | solution.py:26
  82.3 26.7 %collective-permute-start.8 = (bf16[256,2048]{1,0:T(8,128)(2,1)}, bf16[256,2048]{1,0:T(8,128)(2,1)}, u32[]{:S(2)}, u32[]{:S(2)}) collective-permute-start(bf16[256,2048]{1,0:T(8,128)(2,1)} %fusion.41), channel_id=1, source_target_pairs={{0,1},{1,0},{2,3},{3,2},{4,5},{5,4},{6,7},{7,6},{8,9},{9,8},{10,11... | collective-permute-start | bytes 3145736 | tf_op jit(solution)/shard_map/ppermute | solution.py:26
  107.5 7.7 %copy-start = (bf16[1024,512]{1,0:T(8,128)(2,1)}, bf16[1024,512]{1,0:T(8,128)(2,1)S(1)}, u32[]{:S(2)}) copy-start(bf16[1024,512]{1,0:T(8,128)(2,1)S(1)} %get-tuple-element.53) | copy-start | bytes 3145732
  108.5 266.0 %reduce-scatter.4.cloned.1.call-start = ((), (), s32[]{:S(2)}) async-start(), calls=%async_computation.6 | async-start | bytes 10616832 | tf_op jit(solution)/shard_map/reduce_scatter | solution.py:83
  113.0 23.2 %collective-permute-start.12 = (bf16[256,2048]{1,0:T(8,128)(2,1)S(1)}, bf16[256,2048]{1,0:T(8,128)(2,1)S(1)}, u32[]{:S(2)}, u32[]{:S(2)}) collective-permute-start(bf16[256,2048]{1,0:T(8,128)(2,1)S(1)} %pad_maximum_fusion.12), channel_id=1, source_target_pairs={{0,2},{1,3},{2,0},{3,1},{4,6},{5,7},{6,4},{7,5},{8,10},{9,11},{10,... | collective-permute-start | bytes 3145736 | tf_op jit(solution)/shard_map/ppermute | solution.py:26
  114.7 22.9 %collective-permute-start.10 = (bf16[256,2048]{1,0:T(8,128)(2,1)S(1)}, bf16[256,2048]{1,0:T(8,128)(2,1)S(1)}, u32[]{:S(2)}, u32[]{:S(2)}) collective-permute-start(bf16[256,2048]{1,0:T(8,128)(2,1)S(1)} %pad_maximum_fusion.11), channel_id=1, source_target_pairs={{0,1},{1,0},{2,3},{3,2},{4,5},{5,4},{6,7},{7,6},{8,9},{9,8},{10,11... | collective-permute-start | bytes 3145736 | tf_op jit(solution)/shard_map/ppermute | solution.py:26
  138.0 14.9 %collective-permute-start.11 = (bf16[128,2048]{1,0:T(8,128)(2,1)S(1)}, bf16[128,2048]{1,0:T(8,128)(2,1)S(1)}, u32[]{:S(2)}, u32[]{:S(2)}) collective-permute-start(bf16[128,2048]{1,0:T(8,128)(2,1)S(1)} %get-tuple-element.127), channel_id=1, source_target_pairs={{0,2},{1,3},{2,0},{3,1},{4,6},{5,7},{6,4},{7,5},{8,10},{9,11},{10,... | collective-permute-start | bytes 1572872 | tf_op jit(solution)/shard_map/ppermute | solution.py:26
  138.6 14.8 %collective-permute-start.13 = (bf16[128,2048]{1,0:T(8,128)(2,1)S(1)}, bf16[128,2048]{1,0:T(8,128)(2,1)S(1)}, u32[]{:S(2)}, u32[]{:S(2)}) collective-permute-start(bf16[128,2048]{1,0:T(8,128)(2,1)S(1)} %get-tuple-element.128), channel_id=1, source_target_pairs={{0,1},{1,0},{2,3},{3,2},{4,5},{5,4},{6,7},{7,6},{8,9},{9,8},{10,11... | collective-permute-start | bytes 1572872 | tf_op jit(solution)/shard_map/ppermute | solution.py:26
  142.7 17.8 %collective-permute-start.14 = (bf16[128,2048]{1,0:T(8,128)(2,1)S(1)}, bf16[128,2048]{1,0:T(8,128)(2,1)S(1)}, u32[]{:S(2)}, u32[]{:S(2)}) collective-permute-start(bf16[128,2048]{1,0:T(8,128)(2,1)S(1)} %slice.446), channel_id=1, source_target_pairs={{0,1},{1,0},{2,3},{3,2},{4,5},{5,4},{6,7},{7,6},{8,9},{9,8},{10,11... | collective-permute-start | bytes 1572872 | tf_op jit(solution)/shard_map/ppermute | solution.py:26
  144.2 16.3 %collective-permute-start.15 = (bf16[128,2048]{1,0:T(8,128)(2,1)S(1)}, bf16[128,2048]{1,0:T(8,128)(2,1)S(1)}, u32[]{:S(2)}, u32[]{:S(2)}) collective-permute-start(bf16[128,2048]{1,0:T(8,128)(2,1)S(1)} %slice.447), channel_id=1, source_target_pairs={{0,2},{1,3},{2,0},{3,1},{4,6},{5,7},{6,4},{7,5},{8,10},{9,11},{10,... | collective-permute-start | bytes 1572872 | tf_op jit(solution)/shard_map/ppermute | solution.py:26
  163.0 21.3 %collective-permute-start.17 = (bf16[256,2048]{1,0:T(8,128)(2,1)}, bf16[256,2048]{1,0:T(8,128)(2,1)}, u32[]{:S(2)}, u32[]{:S(2)}) collective-permute-start(bf16[256,2048]{1,0:T(8,128)(2,1)} %multiply_convert_fusion.6), channel_id=1, source_target_pairs={{0,2},{1,3},{2,0},{3,1},{4,6},{5,7},{6,4},{7,5},{8,10},{9,11},{10,... | collective-permute-start | bytes 3145736 | tf_op jit(solution)/shard_map/ppermute | solution.py:26
  164.4 23.3 %collective-permute-start.16 = (bf16[256,2048]{1,0:T(8,128)(2,1)}, bf16[256,2048]{1,0:T(8,128)(2,1)}, u32[]{:S(2)}, u32[]{:S(2)}) collective-permute-start(bf16[256,2048]{1,0:T(8,128)(2,1)} %multiply_convert_fusion.6), channel_id=1, source_target_pairs={{0,1},{1,0},{2,3},{3,2},{4,5},{5,4},{6,7},{7,6},{8,9},{9,8},{10,11... | collective-permute-start | bytes 3145736 | tf_op jit(solution)/shard_map/ppermute | solution.py:26
  185.4 11.2 %collective-permute-start.18 = (bf16[128,2048]{1,0:T(8,128)(2,1)S(1)}, bf16[128,2048]{1,0:T(8,128)(2,1)S(1)}, u32[]{:S(2)}, u32[]{:S(2)}) collective-permute-start(bf16[128,2048]{1,0:T(8,128)(2,1)S(1)} %slice.455), channel_id=1, source_target_pairs={{0,1},{1,0},{2,3},{3,2},{4,5},{5,4},{6,7},{7,6},{8,9},{9,8},{10,11... | collective-permute-start | bytes 1572872 | tf_op jit(solution)/shard_map/ppermute | solution.py:26
  188.7 9.2 %collective-permute-start.19 = (bf16[128,2048]{1,0:T(8,128)(2,1)S(1)}, bf16[128,2048]{1,0:T(8,128)(2,1)S(1)}, u32[]{:S(2)}, u32[]{:S(2)}) collective-permute-start(bf16[128,2048]{1,0:T(8,128)(2,1)S(1)} %slice.456), channel_id=1, source_target_pairs={{0,2},{1,3},{2,0},{3,1},{4,6},{5,7},{6,4},{7,5},{8,10},{9,11},{10,... | collective-permute-start | bytes 1572872 | tf_op jit(solution)/shard_map/ppermute | solution.py:26
  198.0 16.4 %copy-start.54 = (bf16[1024,2048]{1,0:T(8,128)(2,1)}, bf16[1024,2048]{1,0:T(8,128)(2,1)S(1)}, u32[]{:S(2)}) copy-start(bf16[1024,2048]{1,0:T(8,128)(2,1)S(1)} %constant_dynamic-update-slice_fusion.10) | copy-start | bytes 12582916
  227.7 196.7 %reduce-scatter.6.cloned.1.call-start = ((), (), s32[]{:S(2)}) async-start(), calls=%async_computation.7 | async-start | bytes 8847360 | tf_op jit(solution)/shard_map/reduce_scatter | solution.py:83
  254.4 12.8 %copy-start.19 = (bf16[1024,640]{0,1:T(8,128)(2,1)}, bf16[1024,640]{0,1:T(8,128)(2,1)S(1)}, u32[]{:S(2)}) copy-start(bf16[1024,640]{0,1:T(8,128)(2,1)S(1)} %get-tuple-element.103) | copy-start | bytes 3932164
  254.4 12.8 %copy-start.21 = (bf16[1024,640]{0,1:T(8,128)(2,1)}, bf16[1024,640]{0,1:T(8,128)(2,1)S(1)}, u32[]{:S(2)}) copy-start(bf16[1024,640]{0,1:T(8,128)(2,1)S(1)} %get-tuple-element.104) | copy-start | bytes 3932164
  254.4 30.5 %copy-start.40 = (bf16[1024,640]{0,1:T(8,128)(2,1)}, bf16[1024,640]{0,1:T(8,128)(2,1)S(1)}, u32[]{:S(2)}) copy-start(bf16[1024,640]{0,1:T(8,128)(2,1)S(1)} %get-tuple-element.70) | copy-start | bytes 3932164
  263.9 20.7 %collective-permute-start.20 = (bf16[256,2048]{1,0:T(8,128)(2,1)S(1)}, bf16[256,2048]{1,0:T(8,128)(2,1)S(1)}, u32[]{:S(2)}, u32[]{:S(2)}) collective-permute-start(bf16[256,2048]{1,0:T(8,128)(2,1)S(1)} %pad_maximum_fusion.13), channel_id=1, source_target_pairs={{0,1},{1,0},{2,3},{3,2},{4,5},{5,4},{6,7},{7,6},{8,9},{9,8},{10,11... | collective-permute-start | bytes 3145736 | tf_op jit(solution)/shard_map/ppermute | solution.py:26
  265.6 19.3 %copy-start.53 = (bf16[1024,2048]{1,0:T(8,128)(2,1)S(1)}, bf16[1024,2048]{1,0:T(8,128)(2,1)}, u32[]{:S(2)}) copy-start(bf16[1024,2048]{1,0:T(8,128)(2,1)} %copy-done.51) | copy-start | bytes 12582916
  265.6 19.3 %collective-permute-start.21 = (bf16[256,2048]{1,0:T(8,128)(2,1)S(1)}, bf16[256,2048]{1,0:T(8,128)(2,1)}, u32[]{:S(2)}, u32[]{:S(2)}) collective-permute-start(bf16[256,2048]{1,0:T(8,128)(2,1)S(1)} %pad_maximum_fusion.14), channel_id=1, source_target_pairs={{0,2},{1,3},{2,0},{3,1},{4,6},{5,7},{6,4},{7,5},{8,10},{9,11},{10,... | collective-permute-start | bytes 3145736 | tf_op jit(solution)/shard_map/ppermute | solution.py:26
  304.3 173.9 %reduce-scatter.8.cloned.1.call-start = ((), (), s32[]{:S(2)}) async-start(), calls=%async_computation.8 | async-start | bytes 5013504 | tf_op jit(solution)/shard_map/reduce_scatter | solution.py:83
  304.7 10.6 %slice-start.2 = ((s8[7864320]{0:T(1024)(128)(4,1)}), s8[4194304]{0:T(1024)(128)(4,1)S(1)}, s32[]{:S(2)}) async-start(s8[7864320]{0:T(1024)(128)(4,1)} %bitcast.102), calls=%async_computation.11 | async-start | bytes 8388608
  308.2 9.2 %collective-permute-start.22 = (bf16[128,2048]{1,0:T(8,128)(2,1)S(1)}, bf16[128,2048]{1,0:T(8,128)(2,1)S(1)}, u32[]{:S(2)}, u32[]{:S(2)}) collective-permute-start(bf16[128,2048]{1,0:T(8,128)(2,1)S(1)} %get-tuple-element.121), channel_id=1, source_target_pairs={{0,2},{1,3},{2,0},{3,1},{4,6},{5,7},{6,4},{7,5},{8,10},{9,11},{10,... | collective-permute-start | bytes 1572872 | tf_op jit(solution)/shard_map/ppermute | solution.py:26
  308.8 9.2 %collective-permute-start.23 = (bf16[128,2048]{1,0:T(8,128)(2,1)S(1)}, bf16[128,2048]{1,0:T(8,128)(2,1)S(1)}, u32[]{:S(2)}, u32[]{:S(2)}) collective-permute-start(bf16[128,2048]{1,0:T(8,128)(2,1)S(1)} %get-tuple-element.122), channel_id=1, source_target_pairs={{0,1},{1,0},{2,3},{3,2},{4,5},{5,4},{6,7},{7,6},{8,9},{9,8},{10,11... | collective-permute-start | bytes 1572872 | tf_op jit(solution)/shard_map/ppermute | solution.py:26
  323.5 21.0 %collective-permute-start.25 = (bf16[256,2048]{1,0:T(8,128)(2,1)}, bf16[256,2048]{1,0:T(8,128)(2,1)S(1)}, u32[]{:S(2)}, u32[]{:S(2)}) collective-permute-start(bf16[256,2048]{1,0:T(8,128)(2,1)} %get-tuple-element.99), channel_id=1, source_target_pairs={{0,2},{1,3},{2,0},{3,1},{4,6},{5,7},{6,4},{7,5},{8,10},{9,11},{10,... | collective-permute-start | bytes 3145736 | tf_op jit(solution)/shard_map/ppermute | solution.py:26
  325.0 24.5 %collective-permute-start.24 = (bf16[256,2048]{1,0:T(8,128)(2,1)}, bf16[256,2048]{1,0:T(8,128)(2,1)}, u32[]{:S(2)}, u32[]{:S(2)}) collective-permute-start(bf16[256,2048]{1,0:T(8,128)(2,1)} %get-tuple-element.99), channel_id=1, source_target_pairs={{0,1},{1,0},{2,3},{3,2},{4,5},{5,4},{6,7},{7,6},{8,9},{9,8},{10,11... | collective-permute-start | bytes 3145736 | tf_op jit(solution)/shard_map/ppermute | solution.py:26
  326.9 23.9 %copy-start.41 = (bf16[1024,640]{0,1:T(8,128)(2,1)S(1)}, bf16[1024,640]{0,1:T(8,128)(2,1)}, u32[]{:S(2)}) copy-start(bf16[1024,640]{0,1:T(8,128)(2,1)} %copy-done.40) | copy-start | bytes 3932164
  344.6 13.4 %collective-permute-start.26 = (bf16[128,2048]{1,0:T(8,128)(2,1)S(1)}, bf16[128,2048]{1,0:T(8,128)(2,1)S(1)}, u32[]{:S(2)}, u32[]{:S(2)}) collective-permute-start(bf16[128,2048]{1,0:T(8,128)(2,1)S(1)} %slice.586), channel_id=1, source_target_pairs={{0,1},{1,0},{2,3},{3,2},{4,5},{5,4},{6,7},{7,6},{8,9},{9,8},{10,11... | collective-permute-start | bytes 1572872 | tf_op jit(solution)/shard_map/ppermute | solution.py:26
  350.7 13.4 %collective-permute-start.27 = (bf16[128,2048]{1,0:T(8,128)(2,1)S(1)}, bf16[128,2048]{1,0:T(8,128)(2,1)S(1)}, u32[]{:S(2)}, u32[]{:S(2)}) collective-permute-start(bf16[128,2048]{1,0:T(8,128)(2,1)S(1)} %slice.587), channel_id=1, source_target_pairs={{0,2},{1,3},{2,0},{3,1},{4,6},{5,7},{6,4},{7,5},{8,10},{9,11},{10,... | collective-permute-start | bytes 1572872 | tf_op jit(solution)/shard_map/ppermute | solution.py:26
  355.8 8.5 %copy-start.31 = (bf16[768,2048]{1,0:T(8,128)(2,1)}, bf16[768,2048]{1,0:T(8,128)(2,1)S(1)}, u32[]{:S(2)}) copy-start(bf16[768,2048]{1,0:T(8,128)(2,1)S(1)} %add_convert_fusion) | copy-start | bytes 9437188
  365.3 28.3 %collective-permute-start.28 = (bf16[256,2048]{1,0:T(8,128)(2,1)}, bf16[256,2048]{1,0:T(8,128)(2,1)}, u32[]{:S(2)}, u32[]{:S(2)}) collective-permute-start(bf16[256,2048]{1,0:T(8,128)(2,1)} %pad_maximum_fusion.15), channel_id=1, source_target_pairs={{0,1},{1,0},{2,3},{3,2},{4,5},{5,4},{6,7},{7,6},{8,9},{9,8},{10,11... | collective-permute-start | bytes 3145736 | tf_op jit(solution)/shard_map/ppermute | solution.py:26
  368.7 24.9 %collective-permute-start.29 = (bf16[256,2048]{1,0:T(8,128)(2,1)}, bf16[256,2048]{1,0:T(8,128)(2,1)}, u32[]{:S(2)}, u32[]{:S(2)}) collective-permute-start(bf16[256,2048]{1,0:T(8,128)(2,1)} %pad_maximum_fusion.16), channel_id=1, source_target_pairs={{0,2},{1,3},{2,0},{3,1},{4,6},{5,7},{6,4},{7,5},{8,10},{9,11},{10,... | collective-permute-start | bytes 3145736 | tf_op jit(solution)/shard_map/ppermute | solution.py:26
  398.0 8.2 %collective-permute-start.32 = (bf16[512,256]{1,0:T(8,128)(2,1)S(1)}, bf16[512,256]{1,0:T(8,128)(2,1)S(1)}, u32[]{:S(2)}, u32[]{:S(2)}) collective-permute-start(bf16[512,256]{1,0:T(8,128)(2,1)S(1)} %pad_maximum_fusion.30), channel_id=1, source_target_pairs={{0,2},{1,3},{2,0},{3,1},{4,6},{5,7},{6,4},{7,5},{8,10},{9,11},{10,... | collective-permute-start | bytes 786440 | tf_op jit(solution)/shard_map/ppermute | solution.py:26
  400.0 8.2 %collective-permute-start.30 = (bf16[512,256]{1,0:T(8,128)(2,1)S(1)}, bf16[512,256]{1,0:T(8,128)(2,1)S(1)}, u32[]{:S(2)}, u32[]{:S(2)}) collective-permute-start(bf16[512,256]{1,0:T(8,128)(2,1)S(1)} %pad_maximum_fusion.29), channel_id=1, source_target_pairs={{0,1},{1,0},{2,3},{3,2},{4,5},{5,4},{6,7},{7,6},{8,9},{9,8},{10,11... | collective-permute-start | bytes 786440 | tf_op jit(solution)/shard_map/ppermute | solution.py:26
  406.0 7.5 %copy-start.36 = (bf16[2048,512]{1,0:T(8,128)(2,1)S(1)}, bf16[2048,512]{1,0:T(8,128)(2,1)}, u32[]{:S(2)}) copy-start(bf16[2048,512]{1,0:T(8,128)(2,1)} %convolution_convert_fusion.6) | copy-start | bytes 6291460
  406.2 5.0 %collective-permute-start.33 = (bf16[256,256]{1,0:T(8,128)(2,1)S(1)}, bf16[256,256]{1,0:T(8,128)(2,1)S(1)}, u32[]{:S(2)}, u32[]{:S(2)}) collective-permute-start(bf16[256,256]{1,0:T(8,128)(2,1)S(1)} %fusion.73), channel_id=1, source_target_pairs={{0,1},{1,0},{2,3},{3,2},{4,5},{5,4},{6,7},{7,6},{8,9},{9,8},{10,11... | collective-permute-start | bytes 393224 | tf_op jit(solution)/shard_map/ppermute | solution.py:26
  408.3 5.0 %collective-permute-start.31 = (bf16[256,256]{1,0:T(8,128)(2,1)S(1)}, bf16[256,256]{1,0:T(8,128)(2,1)S(1)}, u32[]{:S(2)}, u32[]{:S(2)}) collective-permute-start(bf16[256,256]{1,0:T(8,128)(2,1)S(1)} %fusion.74), channel_id=1, source_target_pairs={{0,2},{1,3},{2,0},{3,1},{4,6},{5,7},{6,4},{7,5},{8,10},{9,11},{10,... | collective-permute-start | bytes 393224 | tf_op jit(solution)/shard_map/ppermute | solution.py:26
  427.5 17.3 %collective-permute-start.34 = (bf16[256,2048]{1,0:T(8,128)(2,1)}, bf16[256,2048]{1,0:T(8,128)(2,1)}, u32[]{:S(2)}, u32[]{:S(2)}) collective-permute-start(bf16[256,2048]{1,0:T(8,128)(2,1)} %pad_maximum_fusion.17), channel_id=1, source_target_pairs={{0,1},{1,0},{2,3},{3,2},{4,5},{5,4},{6,7},{7,6},{8,9},{9,8},{10,11... | collective-permute-start | bytes 3145736 | tf_op jit(solution)/shard_map/ppermute | solution.py:26
  428.6 19.9 %collective-permute-start.35 = (bf16[256,2048]{1,0:T(8,128)(2,1)}, bf16[256,2048]{1,0:T(8,128)(2,1)}, u32[]{:S(2)}, u32[]{:S(2)}) collective-permute-start(bf16[256,2048]{1,0:T(8,128)(2,1)} %pad_maximum_fusion.18), channel_id=1, source_target_pairs={{0,2},{1,3},{2,0},{3,1},{4,6},{5,7},{6,4},{7,5},{8,10},{9,11},{10,... | collective-permute-start | bytes 3145736 | tf_op jit(solution)/shard_map/ppermute | solution.py:26
  451.4 14.2 %collective-permute-start.38 = (bf16[128,2048]{1,0:T(8,128)(2,1)}, bf16[128,2048]{1,0:T(8,128)(2,1)}, u32[]{:S(2)}, u32[]{:S(2)}) collective-permute-start(bf16[128,2048]{1,0:T(8,128)(2,1)} %get-tuple-element.109), channel_id=1, source_target_pairs={{0,2},{1,3},{2,0},{3,1},{4,6},{5,7},{6,4},{7,5},{8,10},{9,11},{10,... | collective-permute-start | bytes 1572872 | tf_op jit(solution)/shard_map/ppermute | solution.py:26
  452.6 14.5 %collective-permute-start.39 = (bf16[128,2048]{1,0:T(8,128)(2,1)}, bf16[128,2048]{1,0:T(8,128)(2,1)}, u32[]{:S(2)}, u32[]{:S(2)}) collective-permute-start(bf16[128,2048]{1,0:T(8,128)(2,1)} %get-tuple-element.110), channel_id=1, source_target_pairs={{0,1},{1,0},{2,3},{3,2},{4,5},{5,4},{6,7},{7,6},{8,9},{9,8},{10,11... | collective-permute-start | bytes 1572872 | tf_op jit(solution)/shard_map/ppermute | solution.py:26
  464.0 9.2 %collective-permute-start.36 = (bf16[128,2048]{1,0:T(8,128)(2,1)S(1)}, bf16[128,2048]{1,0:T(8,128)(2,1)S(1)}, u32[]{:S(2)}, u32[]{:S(2)}) collective-permute-start(bf16[128,2048]{1,0:T(8,128)(2,1)S(1)} %get-tuple-element.111), channel_id=1, source_target_pairs={{0,2},{1,3},{2,0},{3,1},{4,6},{5,7},{6,4},{7,5},{8,10},{9,11},{10,... | collective-permute-start | bytes 1572872 | tf_op jit(solution)/shard_map/ppermute | solution.py:26
  464.9 9.2 %collective-permute-start.37 = (bf16[128,2048]{1,0:T(8,128)(2,1)S(1)}, bf16[128,2048]{1,0:T(8,128)(2,1)S(1)}, u32[]{:S(2)}, u32[]{:S(2)}) collective-permute-start(bf16[128,2048]{1,0:T(8,128)(2,1)S(1)} %get-tuple-element.112), channel_id=1, source_target_pairs={{0,1},{1,0},{2,3},{3,2},{4,5},{5,4},{6,7},{7,6},{8,9},{9,8},{10,11... | collective-permute-start | bytes 1572872 | tf_op jit(solution)/shard_map/ppermute | solution.py:26
  482.8 4.6 collective-permute-start.41
  483.9 4.6 collective-permute-start.40
  484.7 5.5 %collective-permute-start.42 = (f32[64,265]{1,0:T(8,128)S(1)}, f32[64,265]{1,0:T(8,128)S(1)}, u32[]{:S(2)}, u32[]{:S(2)}) collective-permute-start(f32[64,265]{1,0:T(8,128)S(1)} %pad_maximum_fusion.32), channel_id=1, source_target_pairs={{0,3},{1,2},{2,1},{3,0},{4,7},{5,6},{6,5},{7,4},{8,11},{9,10},{10,... | collective-permute-start | bytes 203528 | tf_op jit(solution)/shard_map/ppermute | solution.py:26
  (59 other events, 238.0 us)
Sparse Core Ops, SparseCore 0:
  11.4 51.7 all-gather.3
  65.4 89.4 all-gather.5
  157.1 76.1 all-gather.7
  235.5 97.9 reduce-scatter.3
  335.6 83.0 reduce-scatter.5
  420.8 50.8 reduce-scatter.7
